TPU v7x, 512 devices: a whole 4x8x8 slice. The times are simulated.
512 devices in a mesh: dp: 128 (over y, z, core), term: 4 (over x).
Axes of the slice: x: 4, y: 8, z: 8, core: 2. Of those that a mesh axis runs over, the one named last changes fastest.
Arguments:
- hidden: bfloat16 [128, 256, 768], P('dp'), may hold values from -100 to 100, as said below
- segment_ids: int32 [128, 256], replicated, may hold values from 0 to 3, never falling along the last dimension, each value on 1 to 160 neighbouring positions
- block_lists: int32 [512, 128], replicated, may hold values from 0 to 255, all different within a row
- doc_ids: int32 [512], replicated, may hold values from 0 to 511, each once
- attn_gain: float32 [768], replicated, may hold values from 0.1 to 1.9
- qkv_weight: bfloat16 [3, 768, 768], P(None, None, 'term'), may hold values from -0.21875 to 0.21875
- attn_out: bfloat16 [768, 768], P('term'), may hold values from -0.21875 to 0.21875
- mlp_gain: float32 [768], replicated, may hold values from 0.1 to 1.9
- ffn_in: bfloat16 [2, 768, 1152], P(None, None, 'term'), may hold values from -0.21875 to 0.21875
- ffn_out: bfloat16 [1152, 768], P('term'), may hold values from -0.1875 to 0.1875
- final_gain: float32 [768], replicated, may hold values from 0.1 to 1.9
- head_dense: bfloat16 [768, 768], replicated, may hold values from -0.21875 to 0.21875
- head_gain: float32 [768], replicated, may hold values from 0.1 to 1.9
- decoder: bfloat16 [4, 8, 128, 8, 768], P('term', None, 'dp'), may hold values from -0.21875 to 0.21875
- decoder_bias: bfloat16 [4, 8, 128, 8], P('term', None, 'dp'), may hold values from -5 to 5
Outputs:
- postings: float32 [4, 8, 128, 8, 512], P('term', None, 'dp')
Inputs may be any that keep to these rules, and one draw needn't show every extreme that they name: `hidden`: every token has its own scale, and every feature its own scale. `segment_ids`: each row's numbers never fall and each of 0 to 3 appears; a passage has 1 to 160 tokens, and some passage of each row has exactly 160. `block_lists`: a passage lists 128 different blocks; every block is listed by some passage. `doc_ids`: each column appears once.
All inputs are finite; a program needn't handle non-finite values.
Results may differ from a plain program's by a relative error of at most 0.0035.
Values may be sent and summed in bfloat16 or wider, within the bound.
No kernel may reach another device: no remote copies, remote signals or barrier semaphores. Data moves between devices by JAX's collectives and lax.ppermute only.
A program may use at most 128 MiB of HBM per device.

v0:
```python
import jax
import jax.numpy as jnp
from jax import lax
from jax.sharding import PartitionSpec as P

BLOCK = 128
HALF_WIN = 64
PASS_DEV = 4
HEAD_DIM = 64


def layer_norm(values, gain_vec):
    average = jnp.mean(values, axis=-1, keepdims=True)
    centered = values - average
    spread = jnp.mean(centered * centered, axis=-1, keepdims=True)
    return centered * lax.rsqrt(spread + 1e-05) * gain_vec


def rotary(values, positions):
    half_dim = values.shape[-1] // 2
    frequency = 10000.0 ** (-2.0 * jnp.arange(half_dim, dtype=jnp.float32) / values.shape[-1])
    angles = positions.astype(jnp.float32)[:, None] * frequency[None, :]
    cosine = jnp.cos(angles)[:, None, :]
    sine_part = jnp.sin(angles)[:, None, :]
    first_half = values[..., :half_dim]
    second = values[..., half_dim:]
    return jnp.concatenate(
        [first_half * cosine - second * sine_part, second * cosine + first_half * sine_part],
        axis=-1,
    )


def head_block(residual, final_gain, head_dense, head_gain):
    normed_out = layer_norm(residual, final_gain).astype(jnp.bfloat16)
    dense_out = jnp.dot(normed_out, head_dense, preferred_element_type=jnp.float32)
    return layer_norm(jax.nn.gelu(dense_out, approximate=False), head_gain).astype(jnp.bfloat16)


def passage_maxima(activity, segments):
    return jnp.stack(
        [
            jnp.max(jnp.where(segments[..., None] == passage, activity, 0.0), axis=-2)
            for passage in range(PASS_DEV)
        ],
        axis=-2,
    )


def on_device(
    hidden,
    segment_ids,
    block_lists,
    doc_ids,
    attn_gain,
    qkv_weight,
    attn_out,
    mlp_gain,
    ffn_in,
    ffn_out,
    final_gain,
    head_dense,
    head_gain,
    decoder,
    decoder_bias,
):
    row_index = lax.axis_index("dp")
    dp_count = lax.axis_size("dp")
    tokens = hidden[0]
    length = tokens.shape[0]
    width = tokens.shape[1]
    segments = lax.dynamic_index_in_dim(segment_ids, row_index, 0, keepdims=False)
    token_index = jnp.arange(length, dtype=jnp.int32)
    positions = token_index - jnp.sum(
        (segments[None, :] < segments[:, None]).astype(jnp.int32), axis=1
    )
    allowed = (segments[:, None] == segments[None, :]) & (
        jnp.abs(token_index[:, None] - token_index[None, :]) <= HALF_WIN
    )
    normed = layer_norm(tokens.astype(jnp.float32), attn_gain).astype(jnp.bfloat16)
    head_width = qkv_weight.shape[2]
    local_heads = head_width // HEAD_DIM

    def project(which_slot):
        return jnp.dot(normed, qkv_weight[which_slot], preferred_element_type=jnp.float32).reshape(
            length, local_heads, HEAD_DIM
        )

    queries = rotary(project(0), positions).astype(jnp.bfloat16)
    key_rows = rotary(project(1), positions).astype(jnp.bfloat16)
    values = project(2).astype(jnp.bfloat16)
    scores = jnp.einsum(
        "qhd,khd->hqk", queries, key_rows, preferred_element_type=jnp.float32
    ) * HEAD_DIM ** (-0.5)
    raised = jnp.where(allowed[None], jnp.exp(scores), 0.0)
    probabilities = (raised / jnp.sum(raised, axis=-1, keepdims=True)).astype(jnp.bfloat16)
    context = jnp.einsum("hqk,khd->qhd", probabilities, values, preferred_element_type=jnp.float32)
    context = context.astype(jnp.bfloat16).reshape(length, head_width)
    partial_attn = jnp.dot(context, attn_out, preferred_element_type=jnp.float32)
    after_attn = tokens.astype(jnp.float32) + lax.psum(partial_attn, "term")
    mixed_in = layer_norm(after_attn, mlp_gain).astype(jnp.bfloat16)
    inner_up = jnp.dot(mixed_in, ffn_in[0], preferred_element_type=jnp.float32)
    gate_part = jnp.dot(mixed_in, ffn_in[1], preferred_element_type=jnp.float32)
    activated = (jax.nn.gelu(inner_up, approximate=False) * gate_part).astype(jnp.bfloat16)
    partial_ffn = jnp.dot(activated, ffn_out, preferred_element_type=jnp.float32)
    summed = lax.psum(partial_ffn, "term")
    headed = head_block(after_attn + summed, final_gain, head_dense, head_gain)
    groups = decoder.shape[1]
    span = decoder.shape[3]
    part_terms = dp_count * span
    range_width = groups * part_terms
    range_start = lax.axis_index("term") * range_width
    passages = block_lists.shape[0]
    rows_weight = lax.all_gather(decoder, "dp", axis=2, tiled=True)
    rows_bias = lax.all_gather(decoder_bias, "dp", axis=2, tiled=True)
    count = rows_weight.shape[2]
    flat_rows = rows_weight[0].reshape(groups * count * span, width)
    logits = lax.dot_general(
        headed, flat_rows, (((1,), (1,)), ((), ())), preferred_element_type=jnp.float32
    )
    logits = logits + rows_bias[0].reshape(groups * count * span).astype(jnp.float32)[None, :]
    activity = jnp.log1p(jnp.maximum(logits, 0.0))
    maxima = passage_maxima(activity, segments).reshape(PASS_DEV, groups, count, span)
    term_order = jnp.arange(range_width, dtype=jnp.int32)
    term_blocks = (range_start + term_order) // BLOCK
    own_lists = lax.dynamic_slice_in_dim(block_lists, row_index * PASS_DEV, PASS_DEV, 0)
    listed = jnp.any(own_lists[:, :, None] == term_blocks[None, None, :], axis=1).astype(
        jnp.float32
    )
    weighted = maxima * listed.reshape(PASS_DEV, groups, dp_count, span)
    received = lax.all_to_all(weighted, "dp", split_axis=2, concat_axis=0, tiled=True)
    own_weights = received[:, :, 0, :]
    placed = (
        jnp.zeros((groups, span, passages), jnp.float32)
        .at[:, :, doc_ids]
        .set(jnp.transpose(own_weights, (1, 2, 0)))
    )
    return placed[None, :, None]


def solution(mesh):
    in_specs = (
        P("dp", None, None),
        P(),
        P(),
        P(),
        P(),
        P(None, None, "term"),
        P("term", None),
        P(),
        P(None, None, "term"),
        P("term", None),
        P(),
        P(),
        P(),
        P("term", None, "dp", None, None),
        P("term", None, "dp", None),
    )
    out_specs = P("term", None, "dp", None, None)
    return jax.shard_map(
        on_device, mesh=mesh, in_specs=in_specs, out_specs=out_specs, check_vma=False
    )
```

profile of v0, /device:TPU:1, one launch (start us, length us, event | category | flops | bytes accessed | tf_op | source)
XLA Modules:
  0.0 268.6 jit_solution(5582998730450174788)
XLA Ops:
  7.4 0.8 constant_dynamic-slice_fusion
  8.5 1.1 convert_reduce_fusion
  9.6 1.2 fusion.9
  10.9 1.2 fusion.182
  13.2 1.2 fusion.3
  14.4 1.8 convolution_convert_fusion
  16.2 1.2 fusion.186
  17.5 58.9 %all-reduce.3.cloned.1.call-done = f32[256,768]{1,0:T(8,128)} async-done(((f32[256,768]{1,0:T(8,128)}), f32[256,768]{1,0:T(8,128)}) %all-reduce.3.cloned.1.call-update) | async-done | bytes 786448 | tf_op jit(solution)/shard_map/psum | solution.py:99
  76.4 1.4 fusion.140
  77.8 1.4 multiply_reduce_fusion.2
  79.4 1.3 fusion.24
  80.7 3.3 %fusion.5 = f32[256,768]{1,0:T(8,128)} fusion(bf16[288,768]{1,0:T(8,128)(2,1)S(1)} %copy-done.8, bf16[256,768]{1,0:T(8,128)(2,1)S(1)} %multiply_convert_fusion.2, bf16[2,768,288]{1,2,0:T(8,128)(2,1)} %param.23, f32[256,288]{0,1:T(8,128)S(1)} %fusion.24), kind=kOutput, calls=%fused_computation.19 | convolution fusion | flops 231358464 | bytes 2359296 | tf_op jit(solution)/shard_map/dot_general | solution.py:104
  84.1 0.5 all-gather.2.cloned.1.call-update
  84.6 53.9 %all_gather.7 = bf16[1,8,128,8]{3,1,0,2:T(8,128)(2,1)S(1)} all-gather(bf16[1,8,1,8]{3,1,0,2:T(8,128)(2,1)S(1)} %bitcast.86), channel_id=1, replica_groups=mesh['dp'=128,'term'=4] {'dp'}, dimensions={2}, use_global_device_ids=true | all-gather | bytes 16512 | tf_op jit(solution)/shard_map/all_gather | solution.py:114
  139.1 0.7 constant_dynamic-slice_fusion.1
  139.9 2.6 compare_reduce_fusion
  142.5 1.3 reduce_or.12
  143.8 1.3 fusion.180
  145.4 2.1 fusion.183
  147.8 36.3 %all-gather.2.cloned.1.call-done = bf16[1,8,128,8,768]{4,3,2,1,0:T(8,128)(2,1)} async-done(((bf16[1,8,1,8,768]{4,3,2,1,0:T(8,128)(2,1)}), bf16[1,8,128,8,768]{4,3,2,1,0:T(8,128)(2,1)}) %all-gather.2.cloned.1.call-update) | async-done | bytes 12582928 | tf_op jit(solution)/shard_map/all_gather | solution.py:113
  184.2 10.7 %select_reduce_fusion.3 = (f32[8192]{0:T(1024)S(1)}, f32[8192]{0:T(1024)S(1)}, f32[8192]{0:T(1024)S(1)}, f32[8192]{0:T(1024)S(1)}) fusion(pred[256]{0:T(512)(128)(4,1)S(1)} %get-tuple-element.25, pred[256]{0:T(512)(128)(4,1)S(1)} %get-tuple-element.23, pred[256]{0:T(512)(128)(4,1)S(1)} %get-tuple-element.24, pred[256]{0:T(512)(128)(4,1)S(1)} %get-tuple-element.22, ...), kind=kOutput, calls=%fused_computation.8 | convolution fusion | flops 3242950656 | bytes 13539328 | tf_op jit(solution)/shard_map/dot_general | solution.py:117
  195.8 1.1 stack.18
  196.9 1.4 maximum_select_fusion
  198.2 1.2 copy.48
  199.5 1.7 reshape.308
  201.2 9.3 %all-to-all-start = ((f32[128,1,256]{2,1,0:T(1,128)}), f32[128,1,256]{2,1,0:T(1,128)S(1)}, u32[]{:S(2)}, u32[]{:S(2)}) async-start(f32[128,1,256]{2,1,0:T(1,128)} %reshape.308), calls=%async_computation | async-start | bytes 262144 | tf_op jit(solution)/shard_map/all_to_all | solution.py:130
  210.5 12.2 %all-to-all-done = f32[128,1,256]{2,1,0:T(1,128)S(1)} async-done(((f32[128,1,256]{2,1,0:T(1,128)}), f32[128,1,256]{2,1,0:T(1,128)S(1)}, u32[]{:S(2)}, u32[]{:S(2)}) %all-to-all-start) | async-done | bytes 131104 | tf_op jit(solution)/shard_map/all_to_all | solution.py:130
  222.7 0.5 broadcast.282
  223.2 1.0 reduce.1
  224.1 2.5 reshape.309
  226.8 33.1 %scatter_fusion = f32[8,8,512]{1,0,2:T(8,128)S(1)} fusion(f32[8,8,512]{1,0,2:T(8,128)S(1)} %broadcast_in_dim.48, s32[512]{0:T(512)S(1)} %compare_select_fusion, f32[512,8,8]{2,1,0:T(8,128)} %bitcast.77), kind=kCustom, calls=%fused_computation | custom fusion | bytes 395264 | tf_op jit(solution)/shard_map/scatter | solution.py:135
  259.9 1.3 copy.45
  (58 shorter events, 3.8 us)
Async XLA Ops:
  7.4 138.0 %copy-start = (bf16[768,768]{1,0:T(8,128)(2,1)S(1)}, bf16[768,768]{1,0:T(8,128)(2,1)}, u32[]{:S(2)}) copy-start(bf16[768,768]{1,0:T(8,128)(2,1)} %param.26) | copy-start | bytes 3538948
  7.4 4.7 %copy-start.1 = (bf16[1,256,768]{2,1,0:T(8,128)(2,1)S(1)}, bf16[1,256,768]{2,1,0:T(8,128)(2,1)}, u32[]{:S(2)}) copy-start(bf16[1,256,768]{2,1,0:T(8,128)(2,1)} %param.15) | copy-start | bytes 1179652
  7.4 4.7 %copy-start.4 = (f32[768]{0:T(1024)S(1)}, f32[768]{0:T(1024)}, u32[]{:S(2)}) copy-start(f32[768]{0:T(1024)} %param.19) | copy-start | bytes 9220
  7.4 69.0 %all-reduce.3.cloned.1.call-start = ((), (), s32[]{:S(2)}) async-start(), calls=%async_computation.1 | async-start | bytes 1572864 | tf_op jit(solution)/shard_map/psum | solution.py:99
  13.2 3.1 %copy-start.3 = (bf16[192,768]{1,0:T(8,128)(2,1)S(1)}, bf16[192,768]{1,0:T(8,128)(2,1)}, u32[]{:S(2)}) copy-start(bf16[192,768]{1,0:T(8,128)(2,1)} %param.21) | copy-start | bytes 884740
  16.2 63.0 %copy-start.5 = (f32[768]{0:T(1024)S(1)}, f32[768]{0:T(1024)}, u32[]{:S(2)}) copy-start(f32[768]{0:T(1024)} %param.22) | copy-start | bytes 9220
  17.5 126.3 %all-reduce.5.cloned.1.call-start = ((), (), s32[]{:S(2)}) async-start(), calls=%async_computation.2 | async-start | bytes 1572864 | tf_op jit(solution)/shard_map/psum | solution.py:105
  76.4 2.8 %copy-start.2 = (f32[256,768]{1,0:T(8,128)S(1)}, f32[256,768]{1,0:T(8,128)}, u32[]{:S(2)}) copy-start(f32[256,768]{1,0:T(8,128)} %all-reduce.3.cloned.1.call-done) | copy-start | bytes 2359300
  77.7 3.0 %copy-start.8 = (bf16[288,768]{1,0:T(8,128)(2,1)S(1)}, bf16[288,768]{1,0:T(8,128)(2,1)}, u32[]{:S(2)}) copy-start(bf16[288,768]{1,0:T(8,128)(2,1)} %param.24) | copy-start | bytes 1327108
  80.7 3.9 %copy-start.6 = (bf16[1,8,1,8]{3,1,2,0:T(8,128)(2,1)S(1)}, bf16[1,8,1,8]{3,1,2,0:T(8,128)(2,1)}, u32[]{:S(2)}) copy-start(bf16[1,8,1,8]{3,1,2,0:T(8,128)(2,1)} %param.29) | copy-start | bytes 388
  84.0 100.1 %all-gather.2.cloned.1.call-start = ((), (), s32[]{:S(2)}) async-start(), calls=%async_computation.3 | async-start | bytes 12681216 | tf_op jit(solution)/shard_map/all_gather | solution.py:113
  139.9 5.5 %copy-start.9 = (f32[768]{0:T(1024)S(1)}, f32[768]{0:T(1024)}, u32[]{:S(2)}) copy-start(f32[768]{0:T(1024)} %param.25) | copy-start | bytes 9220
  145.4 38.8 %copy-start.10 = (f32[768]{0:T(1024)S(1)}, f32[768]{0:T(1024)}, u32[]{:S(2)}) copy-start(f32[768]{0:T(1024)} %param.27) | copy-start | bytes 9220
  199.4 11.0 %copy-start.7 = (s32[512]{0:T(512)S(1)}, s32[512]{0:T(512)}, u32[]{:S(2)}) copy-start(s32[512]{0:T(512)} %param.18) | copy-start | bytes 6148
  201.2 21.5 %all-to-all-start = ((f32[128,1,256]{2,1,0:T(1,128)}), f32[128,1,256]{2,1,0:T(1,128)S(1)}, u32[]{:S(2)}, u32[]{:S(2)}) async-start(f32[128,1,256]{2,1,0:T(1,128)} %reshape.308), calls=%async_computation | async-start | bytes 262144 | tf_op jit(solution)/shard_map/all_to_all | solution.py:130
Sparse Core Ops, SparseCore 0:
  17.6 58.7 all-reduce.2
  84.1 56.7 all-reduce.4
Sparse Core Ops, SparseCore 1:
  87.8 96.3 all-gather.1
where the time goes:
time: 271 us; the launch traced here: 269 us
  waiting for transfers between devices  108 us (40%)
  blocking collectives  53.9 us (20%)
  local copies, waits for them, and re-layouts  47.1 us (17%)
  matrix products  22.3 us (8%)
  between operations  15.2 us (6%)
  other arithmetic  12.8 us (5%)
  starting transfers between devices  9.34 us (3%)
    psum x1, waiting for transfers between devices, on_device(): after_attn = tokens.astype(jnp.float32) + lax.psum(partial_attn, 'term')  58.9 us
    all_gather x1, blocking collectives, on_device(): rows_bias = lax.all_gather(decoder_bias, 'dp', axis=2, tiled=True)  53.9 us
    all_gather x1, waiting for transfers between devices, on_device(): rows_weight = lax.all_gather(decoder, 'dp', axis=2, tiled=True)  36.3 us
    scatter x1, local copies, waits for them, and re-layouts, on_device(): placed = jnp.zeros((groups, span, passages), jnp.float32).at[:, :, doc_id...  33.1 us
    all_to_all x1, waiting for transfers between devices, on_device(): lax.all_to_all(weighted, 'dp', split_axis=2, concat_axis=0, tiled=True)  12.2 us
    dot_general x1, matrix products, on_device(): lax.dot_general(headed, flat_rows, (((1,), (1,)), ((), ())), preferred_el...  10.7 us
    all_to_all x1, starting transfers between devices, on_device(): lax.all_to_all(weighted, 'dp', split_axis=2, concat_axis=0, tiled=True)  9.25 us
  transfers between devices with their start and end apart: 4, of which 3 were waited for; matrix products, arithmetic and copies ran while one was open for 3% of the time, Pallas kernels for 0%

commit v1 on v0

v1 whole, which is shorter than its diff:
```python
import functools

import jax
import jax.numpy as jnp
import numpy as np
from jax import lax
from jax.experimental import pallas as pl
from jax.experimental.pallas import tpu as pltpu
from jax.sharding import Mesh
from jax.sharding import PartitionSpec as P

BLOCK = 128
HALF_WIN = 64
PASS_DEV = 4
HEAD_DIM = 64
HALF_HEAD = 32
LOWEST = -3.0e38

NT = (((1,), (1,)), ((), ()))
TN = (((0,), (0,)), ((), ()))


def rotary_table(length):
    frequency = 10000.0 ** (-2.0 * np.arange(HALF_HEAD, dtype=np.float64) / HEAD_DIM)
    angles = frequency[:, None] * np.arange(length, dtype=np.float64)[None, :]
    terms = []
    for whole in (np.cos(angles), np.sin(angles)):
        rest = whole.astype(np.float32)
        for _ in range(3):
            term = rest.astype(jnp.bfloat16)
            terms.append(term)
            rest = rest - term.astype(np.float32)
    return np.concatenate(terms, axis=0)


def layer_norm(values, gain_row):
    average = jnp.mean(values, axis=-1, keepdims=True)
    centered = values - average
    spread = jnp.mean(centered * centered, axis=-1, keepdims=True)
    return centered * lax.rsqrt(spread + 1e-05) * gain_row


def gelu(values):
    return 0.5 * values * (1.0 + lax.erf(values * np.float32(0.5**0.5)))


def matmul(left, right, dims):
    return lax.dot_general(left, right, dims, preferred_element_type=jnp.float32)


def attention_kernel(row_ref, hidden_ref, segment_ref, gain_ref, weight_ref, table_ref, out_ref):
    length = hidden_ref.shape[0]
    head_width = weight_ref.shape[1]
    segments = segment_ref[pl.ds(row_ref[0], 1), :]
    starts = jnp.zeros_like(segments)
    for passage in range(PASS_DEV - 1):
        held = jnp.sum((segments == passage).astype(jnp.int32), axis=1, keepdims=True)
        starts = starts + jnp.where(segments > passage, held, 0)
    lane = lax.broadcasted_iota(jnp.int32, (1, length), 1)
    positions = lane - starts
    sublane = lax.broadcasted_iota(jnp.int32, (length, length), 0)
    chosen = (sublane == positions).astype(jnp.float32).astype(jnp.bfloat16)
    parts = matmul(table_ref[...], chosen, (((1,), (0,)), ((), ())))
    part = [parts[i * HALF_HEAD : (i + 1) * HALF_HEAD] for i in range(6)]
    cosine = part[0] + part[1] + part[2]
    sine = part[3] + part[4] + part[5]
    lengths = jnp.zeros_like(segments)
    for passage in range(PASS_DEV):
        held = jnp.sum((segments == passage).astype(jnp.int32), axis=1, keepdims=True)
        lengths = jnp.where(segments == passage, held, lengths)
    low = jnp.maximum(starts, lane - HALF_WIN)
    high = jnp.minimum(starts + lengths - 1, lane + HALF_WIN)
    allowed = (sublane >= low) & (sublane <= high)

    normed = layer_norm(hidden_ref[...].astype(jnp.float32), gain_ref[...]).astype(jnp.bfloat16)
    queries = matmul(weight_ref[0], normed, NT)
    key_cols = matmul(weight_ref[1], normed, NT)
    values = matmul(weight_ref[2], normed, NT).astype(jnp.bfloat16)

    def rotate(block):
        first, second = block[:HALF_HEAD], block[HALF_HEAD:]
        turned = jnp.concatenate(
            [first * cosine - second * sine, second * cosine + first * sine], axis=0
        )
        return turned.astype(jnp.bfloat16)

    for head in range(head_width // HEAD_DIM):
        at = slice(head * HEAD_DIM, (head + 1) * HEAD_DIM)
        scores = matmul(rotate(key_cols[at]), rotate(queries[at]), TN) * np.float32(HEAD_DIM**-0.5)
        raised = jnp.where(allowed, jnp.exp(scores), 0.0)
        probabilities = (raised / jnp.sum(raised, axis=0, keepdims=True)).astype(jnp.bfloat16)
        context = matmul(values[at], probabilities, (((1,), (0,)), ((), ()))).astype(jnp.bfloat16)
        for copy in range(out_ref.shape[0]):
            out_ref[copy, at, :] = context


def inner_kernel(hidden_ref, context_ref, out_weight_ref, gain_ref, in_ref, after_ref, inner_ref):
    attended = matmul(context_ref[...], out_weight_ref[...], TN)
    after_attn = hidden_ref[...].astype(jnp.float32) + attended
    after_ref[...] = after_attn
    mixed = layer_norm(after_attn, gain_ref[...]).astype(jnp.bfloat16)
    inner_up = matmul(in_ref[0], mixed, NT)
    gate_part = matmul(in_ref[1], mixed, NT)
    activated = (gelu(inner_up) * gate_part).astype(jnp.bfloat16)
    for copy in range(inner_ref.shape[0]):
        inner_ref[copy] = activated


def head_kernel(after_ref, inner_ref, down_ref, final_ref, dense_ref, head_ref, out_ref):
    after_ffn = after_ref[...] + matmul(inner_ref[...], down_ref[...], TN)
    normed = layer_norm(after_ffn, final_ref[...]).astype(jnp.bfloat16)
    dense = matmul(normed, dense_ref[...], (((1,), (0,)), ((), ())))
    out_ref[...] = layer_norm(gelu(dense), head_ref[...]).astype(jnp.bfloat16)


def pool_kernel(
    row_ref, own_ref, core_ref, far_ref, far_core_ref, segment_ref, table_ref, out_ref, where_ref
):
    rows = (own_ref, core_ref, far_ref, far_core_ref)

    @pl.when(pl.program_id(0) == 0)
    def _():
        listed = [segment_ref[pl.ds(row_ref[r], 1), :] for r in range(len(rows))]
        stacked = jnp.concatenate(listed + listed, axis=0)
        columns = jnp.transpose(stacked)
        for r in range(len(rows)):
            where_ref[r] = jnp.broadcast_to(columns[:, r : r + 1], where_ref.shape[1:])

    width = where_ref.shape[2]
    terms = table_ref.shape[0]
    table = table_ref[...]
    maxima = []
    for r, row in enumerate(rows):
        logits = matmul(row[...], table, NT)
        for passage in range(PASS_DEV):
            inside = where_ref[r] == passage
            pieces = [
                jnp.max(
                    jnp.where(inside, logits[:, at : at + width], LOWEST), axis=0, keepdims=True
                )
                for at in range(0, terms, width)
            ]
            maxima.append(jnp.concatenate(pieces, axis=1))
    half = len(maxima) // 2
    low = jnp.concatenate(maxima[:half], axis=0)
    high = jnp.concatenate(maxima[half:], axis=0)
    own_terms = out_ref.shape[2] // 2
    for slot in range(out_ref.shape[0]):
        at = slice(slot * own_terms, (slot + 1) * own_terms)
        out_ref[slot] = jnp.concatenate([low[:, at], high[:, at]], axis=1)


def place_kernel(maxima_ref, bias_ref, listed_ref, docs_ref, out_ref):
    raw = maxima_ref[...] + bias_ref[...]
    weighted = jnp.log1p(jnp.maximum(raw, 0.0)) * listed_ref[...]
    own_terms, passages = out_ref.shape
    columns = lax.broadcasted_iota(jnp.int32, (weighted.shape[0], passages), 1)
    terms = []
    rest = weighted
    for _ in range(3):
        terms.append(rest.astype(jnp.bfloat16))
        rest = rest - terms[-1].astype(jnp.float32)
    placed = jnp.zeros((own_terms, passages), jnp.float32)
    for half in range(2):
        place = (docs_ref[half] == columns).astype(jnp.float32).astype(jnp.bfloat16)
        at = slice(half * own_terms, (half + 1) * own_terms)
        sums = [matmul(term, place, TN)[at] for term in terms]
        placed = placed + (sums[0] + sums[1] + sums[2])
    out_ref[...] = placed


def vmem():
    return pl.BlockSpec(memory_space=pltpu.VMEM)


def smem():
    return pl.BlockSpec(memory_space=pltpu.SMEM)


def grant(mib):
    return pltpu.CompilerParams(vmem_limit_bytes=mib << 20)


def cost(flops, nbytes):
    return pl.CostEstimate(flops=flops, bytes_accessed=nbytes, transcendentals=0)


def exchange(copies, axis):
    return lax.all_to_all(copies, axis, split_axis=0, concat_axis=0, tiled=True)


def gather_by_exchange(block, axis):
    return exchange(jnp.broadcast_to(block[None], (lax.axis_size(axis),) + block.shape), axis)


def swap(block, axis):
    return lax.ppermute(block, axis, [(0, 1), (1, 0)])


def on_device(
    hidden,
    segment_ids,
    block_lists,
    doc_ids,
    attn_gain,
    qkv_weight,
    attn_out,
    mlp_gain,
    ffn_in,
    ffn_out,
    final_gain,
    head_dense,
    head_gain,
    decoder,
    decoder_bias,
):
    near = ("y", "zh")
    slices = lax.axis_size(near)
    slice_index = lax.axis_index(near)
    near_row = lax.axis_index(("zl", "core"))
    rows_here = lax.axis_size(("zl", "core"))
    row_index = slice_index * rows_here + near_row
    tensor = lax.axis_size("term")
    tokens = hidden[0]
    length, width = tokens.shape
    groups, span = decoder.shape[1], decoder.shape[3]
    own_terms = groups * span
    head_width = qkv_weight.shape[2]
    hidden_units = ffn_in.shape[2]
    passages = block_lists.shape[0]
    near_rows = jnp.stack([jnp.bitwise_xor(near_row, d) for d in range(rows_here)])
    row_ids = slice_index * rows_here + near_rows

    own_slice = decoder.reshape(own_terms, width)
    part = gather_by_exchange(own_slice, "zh").reshape(-1, width)
    out_weight = gather_by_exchange(attn_out, "term").reshape(-1, width)

    context = pl.pallas_call(
        attention_kernel,
        out_shape=jax.ShapeDtypeStruct((tensor, head_width, length), jnp.bfloat16),
        in_specs=[smem()] + [vmem()] * 5,
        out_specs=vmem(),
        cost_estimate=cost(1200000000, 60000000),
        compiler_params=grant(20),
        name="attention",
    )(
        row_ids,
        tokens,
        segment_ids,
        attn_gain[None],
        jnp.swapaxes(qkv_weight, 1, 2),
        jnp.asarray(rotary_table(length)),
    )
    context, part, out_weight = lax.optimization_barrier((context, part, out_weight))
    table = lax.all_gather(part, "y", axis=0, tiled=True)
    all_context = exchange(context, "term").reshape(-1, length)
    down_weight = gather_by_exchange(ffn_out, "term").reshape(-1, width)
    after_attn, inner = pl.pallas_call(
        inner_kernel,
        out_shape=(
            jax.ShapeDtypeStruct((length, width), jnp.float32),
            jax.ShapeDtypeStruct((tensor, hidden_units, length), jnp.bfloat16),
        ),
        in_specs=[vmem()] * 5,
        out_specs=(vmem(), vmem()),
        cost_estimate=cost(600000000, 4000000),
        compiler_params=grant(20),
        name="inner",
    )(tokens, all_context, out_weight, mlp_gain[None], jnp.swapaxes(ffn_in, 1, 2))
    inner, down_weight = lax.optimization_barrier((inner, down_weight))
    all_inner = exchange(inner, "term").reshape(-1, length)
    headed = pl.pallas_call(
        head_kernel,
        out_shape=jax.ShapeDtypeStruct((length, width), jnp.bfloat16),
        in_specs=[vmem()] * 6,
        out_specs=vmem(),
        cost_estimate=cost(800000000, 5000000),
        compiler_params=grant(20),
        name="head",
    )(after_attn, all_inner, down_weight, final_gain[None], head_dense, head_gain[None])

    far = swap(headed, "zl")
    core = swap(headed, "core")
    far_core = swap(far, "core")
    terms_here = slices * own_terms
    step = 256
    pooled = pl.pallas_call(
        pool_kernel,
        out_shape=jax.ShapeDtypeStruct((slices, 2 * PASS_DEV, 2 * own_terms), jnp.float32),
        grid=(terms_here // step,),
        in_specs=[smem()]
        + [pl.BlockSpec((length, width), lambda j: (0, 0))] * rows_here
        + [
            pl.BlockSpec(segment_ids.shape, lambda j: (0, 0)),
            pl.BlockSpec((step, width), lambda j: (j, 0)),
        ],
        out_specs=pl.BlockSpec(
            (step // own_terms, 2 * PASS_DEV, 2 * own_terms), lambda j: (j, 0, 0)
        ),
        scratch_shapes=[pltpu.VMEM((rows_here, length, 128), jnp.int32)],
        cost_estimate=cost(3300000000, 6000000),
        compiler_params=grant(56),
        name="pool",
    )(row_ids, headed, core, far, far_core, segment_ids, table)
    received = exchange(pooled, near)

    bias = decoder_bias.reshape(1, own_terms).astype(jnp.float32)
    dp_count = slices * rows_here
    first_block = (lax.axis_index("term") * groups * dp_count * span + row_index * span) // BLOCK
    own_blocks = first_block + jnp.arange(groups, dtype=jnp.int32) * (dp_count * span // BLOCK)
    listed = jnp.any(block_lists[:, :, None] == own_blocks[None, None, :], axis=1)
    by_row = listed.astype(jnp.float32).reshape(slices, rows_here, PASS_DEV, groups)
    listed = jnp.stack([by_row[:, near_rows[d]] for d in range(rows_here)], axis=1)
    listed = jnp.repeat(listed, span, axis=3).reshape(slices, 2, 2 * PASS_DEV, own_terms)
    listed = jnp.transpose(listed, (0, 2, 1, 3)).reshape(slices * 2 * PASS_DEV, 2 * own_terms)
    docs = doc_ids.reshape(slices, rows_here, PASS_DEV)
    docs = jnp.stack([docs[:, near_rows[d]] for d in range(rows_here)], axis=1)
    docs = jnp.transpose(docs.reshape(slices, 2, 2 * PASS_DEV), (1, 0, 2)).reshape(2, -1, 1)
    placed = pl.pallas_call(
        place_kernel,
        out_shape=jax.ShapeDtypeStruct((own_terms, passages), jnp.float32),
        in_specs=[vmem()] * 4,
        out_specs=vmem(),
        cost_estimate=cost(200000000, 1000000),
        compiler_params=grant(16),
        name="place",
    )(
        received.reshape(-1, 2 * own_terms),
        jnp.concatenate([bias, bias], axis=1),
        listed,
        docs,
    )
    return placed.reshape(1, groups, 1, span, passages)


def solution(mesh):
    shape = (8, 4, 2, 2, mesh.devices.shape[1])
    fine = Mesh(mesh.devices.reshape(shape), ("y", "zh", "zl", "core", "term"))
    dp = ("y", "zh", "zl", "core")
    in_specs = (
        P(dp, None, None),
        P(),
        P(),
        P(),
        P(),
        P(None, None, "term"),
        P("term", None),
        P(),
        P(None, None, "term"),
        P("term", None),
        P(),
        P(),
        P(),
        P("term", None, dp, None, None),
        P("term", None, dp, None),
    )
    out_specs = P("term", None, dp, None, None)
    return jax.shard_map(
        on_device, mesh=fine, in_specs=in_specs, out_specs=out_specs, check_vma=False
    )
```

time: 271 us -> 169 us (0.62)
  waiting for transfers between devices: 108 us -> 36.9 us
  starting transfers between devices: 9.34 us -> 46.3 us
  local copies, waits for them, and re-layouts: 47.1 us -> 13.1 us
  blocking collectives: 53.9 us -> 30.2 us
  matrix products: 22.3 us -> 0 us
  Pallas kernels: 0 us -> 17 us
  other arithmetic: 12.8 us -> 9.96 us
    psum x2 -> x0, waiting for transfers between devices: 58.9 us -> none  [the longest x1 58.9 us: on_device(): after_attn = tokens.astype(jnp.float32) + lax.psum(partial_attn, 'term')]
    all_gather x1 -> x0, blocking collectives: 53.9 us -> none  [on_device(): rows_bias = lax.all_gather(decoder_bias, 'dp', axis=2, tiled=True)]
    all_gather x1, waiting for transfers between devices: 36.3 us -> 0.02 us  [on_device(): table = lax.all_gather(part, 'y', axis=0, tiled=True)]
    scatter x1 -> x0, local copies, waits for them, and re-layouts: 33.1 us -> none  [on_device(): placed = jnp.zeros((groups, span, passages), jnp.float32).at[:, :, doc_id...]
    all_to_all x0 -> x2, blocking collectives: none -> 30.2 us  [exchange(): return lax.all_to_all(copies, axis, split_axis=0, concat_axis=0, tiled=True)]
    ppermute x0 -> x3, starting transfers between devices: none -> 25.9 us  [swap(): return lax.ppermute(block, axis, [(0, 1), (1, 0)])]
    all_to_all x1 -> x4, waiting for transfers between devices: 12.2 us -> 36.8 us  [exchange(): return lax.all_to_all(copies, axis, split_axis=0, concat_axis=0, tiled=True)]
    dot_general x9 -> x0, matrix products: 22.3 us -> none  [the longest x1 10.7 us: on_device(): lax.dot_general(headed, flat_rows, (((1,), (1,)), ((), ())), preferred_el...]
  transfers between devices with their start and end apart: 4 -> 8, of which waited for: 3 -> 4; matrix products, arithmetic and copies ran while one was open for 3% -> 8% of each run, Pallas kernels for 0% -> 4%
where the time goes in v1:
time: 169 us; the launch traced here: 167 us
  starting transfers between devices  46.3 us (27%)
  waiting for transfers between devices  36.9 us (22%)
  blocking collectives  30.2 us (18%)
  Pallas kernels  17 us (10%)
  between operations  13.8 us (8%)
  local copies, waits for them, and re-layouts  13.1 us (8%)
  other arithmetic  9.96 us (6%)
    all_to_all x4, waiting for transfers between devices, exchange(): return lax.all_to_all(copies, axis, split_axis=0, concat_axis=0, tiled=True)  36.8 us
    all_to_all x2, blocking collectives, exchange(): return lax.all_to_all(copies, axis, split_axis=0, concat_axis=0, tiled=True)  30.2 us
    ppermute x3, starting transfers between devices, swap(): return lax.ppermute(block, axis, [(0, 1), (1, 0)])  25.9 us
    all_to_all x4, starting transfers between devices, exchange(): return lax.all_to_all(copies, axis, split_axis=0, concat_axis=0, tiled=True)  20.4 us
    pallas_call x1, Pallas kernels, on_device(): pl.pallas_call(pool_kernel, out_shape=jax.ShapeDtypeStruct((slices, 2 * P...  9.92 us
    reduce_or x1, other arithmetic, on_device(): jnp.any(block_lists[:, :, None] == own_blocks[None, None, :], axis=1)  9.76 us
    unnamed x40, local copies, waits for them, and re-layouts  5.93 us
    broadcast_in_dim x3, local copies, waits for them, and re-layouts, gather_by_exchange(): jnp.broadcast_to(block[None], (lax.axis_size(axis),) + block.shape)  5.46 us
  transfers between devices with their start and end apart: 8, of which 4 were waited for; matrix products, arithmetic and copies ran while one was open for 8% of the time, Pallas kernels for 4%

profile of v1, /device:TPU:1, one launch (start us, length us, event | category | flops | bytes accessed | tf_op | source)
XLA Modules:
  0.0 167.2 jit_solution(18152291718348856689)
XLA Ops:
  6.5 0.9 broadcast_in_dim.38
  7.5 21.6 %all_to_all.30 = bf16[4,64,768]{2,1,0:T(8,128)(2,1)} all-to-all(bf16[4,64,768]{2,1,0:T(8,128)(2,1)S(1)} %broadcast_in_dim.38), channel_id=1, replica_groups=mesh['y'=8,'zh'=4,'zl'=2,'core'=2,'term'=4] {'zh'}, dimensions={0} | all-to-all | bytes 786432 | tf_op jit(solution)/shard_map/all_to_all | solution.py:189
  29.1 2.2 %broadcast_in_dim.39 = bf16[4,192,768]{2,1,0:T(8,128)(2,1)} broadcast(bf16[192,768]{1,0:T(8,128)(2,1)} %param.22), dimensions={1,2} | broadcast | bytes 1474560 | tf_op jit(solution)/shard_map/broadcast_in_dim | solution.py:193
  31.3 4.0 %all-to-all-start.1 = ((bf16[4,192,768]{2,1,0:T(8,128)(2,1)}), bf16[4,192,768]{2,1,0:T(8,128)(2,1)S(1)}, u32[]{:S(2)}, u32[]{:S(2)}) async-start(bf16[4,192,768]{2,1,0:T(8,128)(2,1)} %broadcast_in_dim.39), calls=%async_computation.1 | async-start | bytes 2359296 | tf_op jit(solution)/shard_map/all_to_all | solution.py:189
  35.4 2.1 %attention.1 = bf16[4,192,256]{2,1,0:T(8,128)(2,1)S(1)} custom-call(s32[4]{0:T(128)S(1)} %add_add_fusion.row_ref, bf16[256,768]{1,0:T(8,128)(2,1)S(1)} %bitcast.33, s32[128,256]{1,0:T(8,128)S(1)} %copy-done.9, f32[1,768]{1,0:T(1,128)S(1)} %broadcast_in_dim.36.gain_ref, bf16[3,192,768]{2,1,0:T(8,128)(2,1)S(1)} %bitcast.36, bf16[192,256]{1,0:T(8,128)(2,1)S(1)} %copy-done.10), custom_call_target="tpu_custom_call" | custom-call | flops 1200000000 | bytes 60000000 | tf_op jit(solution)/shard_map/attention/pallas_call | solution.py:238
  37.6 9.3 %all-to-all-done.1 = bf16[4,192,768]{2,1,0:T(8,128)(2,1)S(1)} async-done(((bf16[4,192,768]{2,1,0:T(8,128)(2,1)}), bf16[4,192,768]{2,1,0:T(8,128)(2,1)S(1)}, u32[]{:S(2)}, u32[]{:S(2)}) %all-to-all-start.1) | async-done | bytes 1179680 | tf_op jit(solution)/shard_map/all_to_all | solution.py:189
  46.9 8.6 %all_to_all.31 = bf16[4,192,256]{2,1,0:T(8,128)(2,1)S(1)} all-to-all(bf16[4,192,256]{2,1,0:T(8,128)(2,1)S(1)} %attention.1), channel_id=1, replica_groups=mesh['y'=8,'zh'=4,'zl'=2,'core'=2,'term'=4] {'term'}, dimensions={0} | all-to-all | bytes 786432 | tf_op jit(solution)/shard_map/all_to_all | solution.py:189
  55.5 2.4 %broadcast_in_dim.41 = bf16[4,288,768]{2,1,0:T(8,128)(2,1)} broadcast(bf16[288,768]{1,0:T(8,128)(2,1)} %param.25), dimensions={1,2} | broadcast | bytes 2211840 | tf_op jit(solution)/shard_map/broadcast_in_dim | solution.py:193
  57.8 3.7 %all-to-all-start.3 = ((bf16[4,288,768]{2,1,0:T(8,128)(2,1)}), bf16[4,288,768]{2,1,0:T(8,128)(2,1)S(1)}, u32[]{:S(2)}, u32[]{:S(2)}) async-start(bf16[4,288,768]{2,1,0:T(8,128)(2,1)} %broadcast_in_dim.41), calls=%async_computation.3 | async-start | bytes 3538944 | tf_op jit(solution)/shard_map/all_to_all | solution.py:189
  61.6 1.2 copy-done.1
  62.7 1.0 copy-done.6
  63.7 1.3 inner.1
  65.0 0.9 copy-done.2
  66.0 0.8 copy-done.4
  66.8 10.3 %all-to-all-done.3 = bf16[4,288,768]{2,1,0:T(8,128)(2,1)S(1)} async-done(((bf16[4,288,768]{2,1,0:T(8,128)(2,1)}), bf16[4,288,768]{2,1,0:T(8,128)(2,1)S(1)}, u32[]{:S(2)}, u32[]{:S(2)}) %all-to-all-start.3) | async-done | bytes 1769504 | tf_op jit(solution)/shard_map/all_to_all | solution.py:189
  77.0 3.5 %all-to-all-start.4 = ((bf16[4,288,256]{2,1,0:T(8,128)(2,1)}), bf16[4,288,256]{2,1,0:T(8,128)(2,1)S(1)}, u32[]{:S(2)}, u32[]{:S(2)}) async-start(bf16[4,288,256]{2,1,0:T(8,128)(2,1)} %copy-done.4), calls=%async_computation.4 | async-start | bytes 1179648 | tf_op jit(solution)/shard_map/all_to_all | solution.py:189
  80.6 7.2 %all-to-all-done.4 = bf16[4,288,256]{2,1,0:T(8,128)(2,1)S(1)} async-done(((bf16[4,288,256]{2,1,0:T(8,128)(2,1)}), bf16[4,288,256]{2,1,0:T(8,128)(2,1)S(1)}, u32[]{:S(2)}, u32[]{:S(2)}) %all-to-all-start.4) | async-done | bytes 589856 | tf_op jit(solution)/shard_map/all_to_all | solution.py:189
  87.8 1.1 copy-done.3
  89.0 2.5 %head.1.own_ref = bf16[256,768]{1,0:T(8,128)(2,1)} custom-call(f32[256,768]{1,0:T(8,128)S(1)} %copy-done.3, bf16[1152,256]{1,0:T(8,128)(2,1)S(1)} %bitcast.30, bf16[1152,768]{1,0:T(8,128)(2,1)S(1)} %bitcast.28, f32[1,768]{1,0:T(1,128)S(1)} %broadcast_in_dim.42.final_ref, bf16[768,768]{1,0:T(8,128)(2,1)S(1)} %copy-done, f32[1,768]{1,0:T(1,128)S(1)} %broadcast_in_dim.43.head_ref), custom_call_target="tpu_custom_call" | custom-call | flops 800000000 | bytes 5000000 | tf_op jit(solution)/shard_map/head/pallas_call | solution.py:272
  91.5 11.7 %collective-permute-start.1 = (bf16[256,768]{1,0:T(8,128)(2,1)}, bf16[256,768]{1,0:T(8,128)(2,1)S(1)}, u32[]{:S(2)}, u32[]{:S(2)}) collective-permute-start(bf16[256,768]{1,0:T(8,128)(2,1)} %head.1.own_ref), channel_id=1, source_target_pairs={{0,8},{8,0},{1,9},{9,1},{2,10},{10,2},{3,11},{11,3},{4,12},{12,4},... | collective-permute-start | bytes 1179656 | tf_op jit(solution)/shard_map/ppermute | solution.py:197
  103.2 8.2 %collective-permute-start = (bf16[256,768]{1,0:T(8,128)(2,1)}, bf16[256,768]{1,0:T(8,128)(2,1)S(1)}, u32[]{:S(2)}, u32[]{:S(2)}) collective-permute-start(bf16[256,768]{1,0:T(8,128)(2,1)} %head.1.own_ref), channel_id=1, source_target_pairs={{0,4},{4,0},{1,5},{5,1},{2,6},{6,2},{3,7},{7,3},{8,12},{12,8},{9,1... | collective-permute-start | bytes 1179656 | tf_op jit(solution)/shard_map/ppermute | solution.py:197
  111.5 5.9 %collective-permute-start.2 = (bf16[256,768]{1,0:T(8,128)(2,1)S(1)}, bf16[256,768]{1,0:T(8,128)(2,1)S(1)}, u32[]{:S(2)}, u32[]{:S(2)}) collective-permute-start(bf16[256,768]{1,0:T(8,128)(2,1)S(1)} %collective-permute-done.1.far_ref), channel_id=1, source_target_pairs={{0,4},{4,0},{1,5},{5,1},{2,6},{6,2},{3,7},{7,3},{8,12},{12,8},{9,1... | collective-permute-start | bytes 1179656 | tf_op jit(solution)/shard_map/ppermute | solution.py:197
  117.4 9.8 %compare_reduce_fusion = pred[512,8]{1,0:T(8,128)(4,1)S(1)} fusion(s32[512,128]{1,0:T(8,128)} %param.18, s32[8]{0:T(128)S(1)} %multiply_add_fusion), kind=kLoop, calls=%fused_computation | loop fusion | flops 1044480 | bytes 266272 | tf_op jit(solution)/shard_map/reduce_or | solution.py:311
  127.6 0.1 reshape.68
  127.9 0.7 copy-done.18
  128.8 9.9 %pool.1 = f32[32,8,128]{2,1,0:T(8,128)} custom-call(s32[4]{0:T(128)} %copy-done.7, bf16[256,768]{1,0:T(8,128)(2,1)} %head.1.own_ref, bf16[256,768]{1,0:T(8,128)(2,1)} %copy-done.18, bf16[256,768]{1,0:T(8,128)(2,1)} %copy-done.17, bf16[256,768]{1,0:T(8,128)(2,1)} %copy-done.19, s32[128,256]{1,0:T(8,128)} %segment_ref.3, ...), custom_call_target="tpu_custom_call" | custom-call | flops 3300000000 | bytes 6000000 | tf_op jit(solution)/shard_map/pool/pallas_call | solution.py:287
  138.7 9.2 %all-to-all-start.5 = ((f32[32,8,128]{2,1,0:T(8,128)}), f32[32,8,128]{2,1,0:T(8,128)S(1)}, u32[]{:S(2)}, u32[]{:S(2)}) async-start(f32[32,8,128]{2,1,0:T(8,128)} %pool.1), calls=%async_computation.5 | async-start | bytes 262144 | tf_op jit(solution)/shard_map/all_to_all | solution.py:189
  148.1 0.3 copy.45
  148.3 0.2 reshape.67.listed_ref
  148.9 0.1 reshape.73.docs_ref
  149.1 10.0 %all-to-all-done.5 = f32[32,8,128]{2,1,0:T(8,128)S(1)} async-done(((f32[32,8,128]{2,1,0:T(8,128)}), f32[32,8,128]{2,1,0:T(8,128)S(1)}, u32[]{:S(2)}, u32[]{:S(2)}) %all-to-all-start.5) | async-done | bytes 131104 | tf_op jit(solution)/shard_map/all_to_all | solution.py:189
  159.2 1.2 place.1
  (63 shorter events, 1.4 us)
Async XLA Ops:
  29.1 6.2 %copy-start.11 = (f32[768]{0:T(1024)S(1)}, f32[768]{0:T(1024)}, u32[]{:S(2)}) copy-start(f32[768]{0:T(1024)} %param.20) | copy-start | bytes 9220
  29.1 6.3 %copy-start.5 = (bf16[1,256,768]{2,1,0:T(8,128)(2,1)S(1)}, bf16[1,256,768]{2,1,0:T(8,128)(2,1)}, u32[]{:S(2)}) copy-start(bf16[1,256,768]{2,1,0:T(8,128)(2,1)} %param.16) | copy-start | bytes 1179652
  29.1 6.3 %copy-start.8 = (bf16[3,768,192]{1,2,0:T(8,128)(2,1)S(1)}, bf16[3,768,192]{1,2,0:T(8,128)(2,1)}, u32[]{:S(2)}) copy-start(bf16[3,768,192]{1,2,0:T(8,128)(2,1)} %param.21) | copy-start | bytes 2654212
  29.1 6.3 %copy-start.9 = (s32[128,256]{1,0:T(8,128)S(1)}, s32[128,256]{1,0:T(8,128)}, u32[]{:S(2)}) copy-start(s32[128,256]{1,0:T(8,128)} %segment_ref.3) | copy-start | bytes 393220
  29.1 6.3 %copy-start.10 = (bf16[192,256]{1,0:T(8,128)(2,1)S(1)}, bf16[192,256]{1,0:T(8,128)(2,1)}, u32[]{:S(2)}) copy-start(bf16[192,256]{1,0:T(8,128)(2,1)} %constant.54.clone.table_ref) | copy-start | bytes 294916
  31.3 15.6 %all-to-all-start.1 = ((bf16[4,192,768]{2,1,0:T(8,128)(2,1)}), bf16[4,192,768]{2,1,0:T(8,128)(2,1)S(1)}, u32[]{:S(2)}, u32[]{:S(2)}) async-start(bf16[4,192,768]{2,1,0:T(8,128)(2,1)} %broadcast_in_dim.39), calls=%async_computation.1 | async-start | bytes 2359296 | tf_op jit(solution)/shard_map/all_to_all | solution.py:189
  35.3 92.6 %all-gather.2.cloned.1.call-start = ((), (), s32[]{:S(2)}) async-start(), calls=%async_computation.6 | async-start | bytes 3538944 | tf_op jit(solution)/shard_map/all_gather | solution.py:255
  35.4 2.2 %copy-start.7 = (s32[4]{0:T(128)}, s32[4]{0:T(128)S(1)}, u32[]{:S(2)}) copy-start(s32[4]{0:T(128)S(1)} %add_add_fusion.row_ref) | copy-start | bytes 52
  57.8 3.7 %copy-start.12 = (f32[768]{0:T(1024)S(1)}, f32[768]{0:T(1024)}, u32[]{:S(2)}) copy-start(f32[768]{0:T(1024)} %param.23) | copy-start | bytes 9220
  57.8 19.2 %all-to-all-start.3 = ((bf16[4,288,768]{2,1,0:T(8,128)(2,1)}), bf16[4,288,768]{2,1,0:T(8,128)(2,1)S(1)}, u32[]{:S(2)}, u32[]{:S(2)}) async-start(bf16[4,288,768]{2,1,0:T(8,128)(2,1)} %broadcast_in_dim.41), calls=%async_computation.3 | async-start | bytes 3538944 | tf_op jit(solution)/shard_map/all_to_all | solution.py:189
  61.6 1.2 copy-start.1
  62.7 1.0 copy-start.6
  63.7 16.8 %copy-start.13 = (f32[768]{0:T(1024)S(1)}, f32[768]{0:T(1024)}, u32[]{:S(2)}) copy-start(f32[768]{0:T(1024)} %param.26) | copy-start | bytes 9220
  63.7 16.8 %copy-start.14 = (f32[768]{0:T(1024)S(1)}, f32[768]{0:T(1024)}, u32[]{:S(2)}) copy-start(f32[768]{0:T(1024)} %param.28) | copy-start | bytes 9220
  65.0 0.9 copy-start.2
  66.0 0.8 copy-start.4
  66.8 21.1 %copy-start = (bf16[768,768]{1,0:T(8,128)(2,1)S(1)}, bf16[768,768]{1,0:T(8,128)(2,1)}, u32[]{:S(2)}) copy-start(bf16[768,768]{1,0:T(8,128)(2,1)} %dense_ref.1) | copy-start | bytes 3538948
  77.0 10.8 %all-to-all-start.4 = ((bf16[4,288,256]{2,1,0:T(8,128)(2,1)}), bf16[4,288,256]{2,1,0:T(8,128)(2,1)S(1)}, u32[]{:S(2)}, u32[]{:S(2)}) async-start(bf16[4,288,256]{2,1,0:T(8,128)(2,1)} %copy-done.4), calls=%async_computation.4 | async-start | bytes 1179648 | tf_op jit(solution)/shard_map/all_to_all | solution.py:189
  87.8 1.1 copy-start.3
  89.0 38.6 %copy-start.15 = (s32[512]{0:T(512)S(1)}, s32[512]{0:T(512)}, u32[]{:S(2)}) copy-start(s32[512]{0:T(512)} %param.19) | copy-start | bytes 6148
  91.5 20.0 %collective-permute-start.1 = (bf16[256,768]{1,0:T(8,128)(2,1)}, bf16[256,768]{1,0:T(8,128)(2,1)S(1)}, u32[]{:S(2)}, u32[]{:S(2)}) collective-permute-start(bf16[256,768]{1,0:T(8,128)(2,1)} %head.1.own_ref), channel_id=1, source_target_pairs={{0,8},{8,0},{1,9},{9,1},{2,10},{10,2},{3,11},{11,3},{4,12},{12,4},... | collective-permute-start | bytes 1179656 | tf_op jit(solution)/shard_map/ppermute | solution.py:197
  103.2 24.6 %collective-permute-start = (bf16[256,768]{1,0:T(8,128)(2,1)}, bf16[256,768]{1,0:T(8,128)(2,1)S(1)}, u32[]{:S(2)}, u32[]{:S(2)}) collective-permute-start(bf16[256,768]{1,0:T(8,128)(2,1)} %head.1.own_ref), channel_id=1, source_target_pairs={{0,4},{4,0},{1,5},{5,1},{2,6},{6,2},{3,7},{7,3},{8,12},{12,8},{9,1... | collective-permute-start | bytes 1179656 | tf_op jit(solution)/shard_map/ppermute | solution.py:197
  111.5 16.5 %copy-start.17 = (bf16[256,768]{1,0:T(8,128)(2,1)}, bf16[256,768]{1,0:T(8,128)(2,1)S(1)}, u32[]{:S(2)}) copy-start(bf16[256,768]{1,0:T(8,128)(2,1)S(1)} %collective-permute-done.1.far_ref) | copy-start | bytes 1179652
  111.5 16.4 %collective-permute-start.2 = (bf16[256,768]{1,0:T(8,128)(2,1)S(1)}, bf16[256,768]{1,0:T(8,128)(2,1)S(1)}, u32[]{:S(2)}, u32[]{:S(2)}) collective-permute-start(bf16[256,768]{1,0:T(8,128)(2,1)S(1)} %collective-permute-done.1.far_ref), channel_id=1, source_target_pairs={{0,4},{4,0},{1,5},{5,1},{2,6},{6,2},{3,7},{7,3},{8,12},{12,8},{9,1... | collective-permute-start | bytes 1179656 | tf_op jit(solution)/shard_map/ppermute | solution.py:197
  127.8 20.1 %copy-start.16 = (bf16[1,8,1,8]{3,1,2,0:T(8,128)(2,1)S(1)}, bf16[1,8,1,8]{3,1,2,0:T(8,128)(2,1)}, u32[]{:S(2)}) copy-start(bf16[1,8,1,8]{3,1,2,0:T(8,128)(2,1)} %param.30) | copy-start | bytes 388
  127.9 0.8 copy-start.18
  127.9 0.9 copy-start.19
  138.7 20.5 %all-to-all-start.5 = ((f32[32,8,128]{2,1,0:T(8,128)}), f32[32,8,128]{2,1,0:T(8,128)S(1)}, u32[]{:S(2)}, u32[]{:S(2)}) async-start(f32[32,8,128]{2,1,0:T(8,128)} %pool.1), calls=%async_computation.5 | async-start | bytes 262144 | tf_op jit(solution)/shard_map/all_to_all | solution.py:189
Sparse Core Ops, SparseCore 0:
  47.0 50.1 all-gather.1

commit v2 on v1

--- a/solution.py
+++ b/solution.py
@@ -14,7 +14,10 @@
 PASS_DEV = 4
 HEAD_DIM = 64
 HALF_HEAD = 32
+SPAN = 8
+NEAR = 4
 LOWEST = -3.0e38
+NEAR_AT, TERM_AT, BLOCK_AT, STRIDE_AT = 4, 5, 6, 7
 
 NT = (((1,), (1,)), ((), ()))
 TN = (((0,), (0,)), ((), ()))
@@ -48,7 +51,10 @@
     return lax.dot_general(left, right, dims, preferred_element_type=jnp.float32)
 
 
-def attention_kernel(row_ref, hidden_ref, segment_ref, gain_ref, weight_ref, table_ref, out_ref):
+def attention_kernel(
+    row_ref, hidden_ref, segment_ref, gain_ref, weight_ref, table_ref, out_weight_ref, out_ref
+):
+    out_weight = out_weight_ref[...]
     length = hidden_ref.shape[0]
     head_width = weight_ref.shape[1]
     segments = segment_ref[pl.ds(row_ref[0], 1), :]
@@ -91,11 +97,14 @@
         probabilities = (raised / jnp.sum(raised, axis=0, keepdims=True)).astype(jnp.bfloat16)
         context = matmul(values[at], probabilities, (((1,), (0,)), ((), ()))).astype(jnp.bfloat16)
         for copy in range(out_ref.shape[0]):
-            out_ref[copy, at, :] = context
-
-
-def inner_kernel(hidden_ref, context_ref, out_weight_ref, gain_ref, in_ref, after_ref, inner_ref):
-    attended = matmul(context_ref[...], out_weight_ref[...], TN)
+            out_ref[copy, at, :length] = context
+    for copy in range(out_ref.shape[0]):
+        out_ref[copy, :, length:] = out_weight
+
+
+def inner_kernel(hidden_ref, merged_ref, gain_ref, in_ref, after_ref, inner_ref):
+    length = hidden_ref.shape[0]
+    attended = matmul(merged_ref[:, :length], merged_ref[:, length:], TN)
     after_attn = hidden_ref[...].astype(jnp.float32) + attended
     after_ref[...] = after_attn
     mixed = layer_norm(after_attn, gain_ref[...]).astype(jnp.bfloat16)
@@ -106,53 +115,91 @@
         inner_ref[copy] = activated
 
 
-def head_kernel(after_ref, inner_ref, down_ref, final_ref, dense_ref, head_ref, out_ref):
-    after_ffn = after_ref[...] + matmul(inner_ref[...], down_ref[...], TN)
+def head_kernel(
+    ids_ref, after_ref, inner_ref, *refs
+):
+    downs, (final_ref, dense_ref, head_ref, out_ref) = refs[:-4], refs[-4:]
+    after_ffn = after_ref[...]
+    for d, down_ref in enumerate(downs):
+        shard = jnp.bitwise_xor(ids_ref[TERM_AT], d)
+        after_ffn = after_ffn + matmul(inner_ref[shard], down_ref[...], TN)
     normed = layer_norm(after_ffn, final_ref[...]).astype(jnp.bfloat16)
     dense = matmul(normed, dense_ref[...], (((1,), (0,)), ((), ())))
     out_ref[...] = layer_norm(gelu(dense), head_ref[...]).astype(jnp.bfloat16)
 
 
+def prep_kernel(ids_ref, segment_ref, list_ref, docs_ref, bounds_ref, mask_ref):
+    segments = segment_ref[...]
+    slot = lax.broadcasted_iota(jnp.int32, bounds_ref.shape, 1)
+    bounds = jnp.zeros(bounds_ref.shape, jnp.int32)
+    for passage in range(1, PASS_DEV + 1):
+        before = jnp.sum((segments < passage).astype(jnp.int32), axis=1, keepdims=True)
+        bounds = jnp.where(slot == passage, before, bounds)
+    bounds_ref[...] = bounds
+    own_terms, passages = mask_ref.shape
+    groups = own_terms // SPAN
+    stride = ids_ref[STRIDE_AT]
+    blocks = list_ref[...] - ids_ref[BLOCK_AT]
+    bits = jnp.zeros(blocks.shape, jnp.float32)
+    for group in range(groups):
+        bits = jnp.where(blocks == group * stride, np.float32(2**group), bits)
+    ones = jnp.ones((SPAN, bits.shape[1]), jnp.bfloat16)
+    codes = matmul(ones, bits.astype(jnp.bfloat16), NT).astype(jnp.bfloat16)
+    columns = lax.broadcasted_iota(jnp.int32, (passages, passages), 1)
+    place = (docs_ref[...] == columns).astype(jnp.float32).astype(jnp.bfloat16)
+    placed = matmul(codes, place, (((1,), (0,)), ((), ()))).astype(jnp.int32)
+    for group in range(groups):
+        held = jnp.bitwise_and(lax.shift_right_logical(placed, group), 1)
+        mask_ref[group * SPAN : (group + 1) * SPAN, :] = held.astype(jnp.float32)
+
+
 def pool_kernel(
-    row_ref, own_ref, core_ref, far_ref, far_core_ref, segment_ref, table_ref, out_ref, where_ref
+    ids_ref, bounds_ref, own_ref, core_ref, far_ref, far_core_ref, table_ref, out_ref, rows_ref, logits_ref
 ):
     rows = (own_ref, core_ref, far_ref, far_core_ref)
+    length = own_ref.shape[0]
 
     @pl.when(pl.program_id(0) == 0)
     def _():
-        listed = [segment_ref[pl.ds(row_ref[r], 1), :] for r in range(len(rows))]
-        stacked = jnp.concatenate(listed + listed, axis=0)
-        columns = jnp.transpose(stacked)
-        for r in range(len(rows)):
-            where_ref[r] = jnp.broadcast_to(columns[:, r : r + 1], where_ref.shape[1:])
-
-    width = where_ref.shape[2]
-    terms = table_ref.shape[0]
-    table = table_ref[...]
+        for r, row in enumerate(rows):
+            rows_ref[r * length : (r + 1) * length, :] = row[...]
+
+    logits_ref[...] = matmul(rows_ref[...], table_ref[...], NT)
+    tile = 8
+    sublane = lax.broadcasted_iota(jnp.int32, (tile, logits_ref.shape[1]), 0)
     maxima = []
-    for r, row in enumerate(rows):
-        logits = matmul(row[...], table, NT)
+    for r in range(len(rows)):
         for passage in range(PASS_DEV):
-            inside = where_ref[r] == passage
-            pieces = [
-                jnp.max(
-                    jnp.where(inside, logits[:, at : at + width], LOWEST), axis=0, keepdims=True
-                )
-                for at in range(0, terms, width)
-            ]
-            maxima.append(jnp.concatenate(pieces, axis=1))
+            first = bounds_ref[ids_ref[r], passage]
+            end = bounds_ref[ids_ref[r], passage + 1]
+            first_tile = lax.shift_right_logical(first, 3)
+            last_tile = lax.shift_right_logical(end - 1, 3)
+
+            def load(t):
+                return logits_ref[pl.ds(pl.multiple_of(r * length + t * tile, tile), tile), :]
+
+            def inside(t):
+                token = sublane + t * tile
+                return jnp.where((token >= first) & (token < end), load(t), LOWEST)
+
+            held = jnp.maximum(inside(first_tile), inside(last_tile))
+            held = lax.fori_loop(
+                first_tile + 1, last_tile, lambda t, m: jnp.maximum(m, load(t)), held
+            )
+            maxima.append(jnp.max(held, axis=0, keepdims=True))
     half = len(maxima) // 2
     low = jnp.concatenate(maxima[:half], axis=0)
     high = jnp.concatenate(maxima[half:], axis=0)
     own_terms = out_ref.shape[2] // 2
     for slot in range(out_ref.shape[0]):
         at = slice(slot * own_terms, (slot + 1) * own_terms)
-        out_ref[slot] = jnp.concatenate([low[:, at], high[:, at]], axis=1)
-
-
-def place_kernel(maxima_ref, bias_ref, listed_ref, docs_ref, out_ref):
+        to = slot - slot % NEAR + jnp.bitwise_xor(ids_ref[NEAR_AT], slot % NEAR)
+        out_ref[to] = jnp.concatenate([low[:, at], high[:, at]], axis=1)
+
+
+def place_kernel(maxima_ref, bias_ref, mask_ref, docs_ref, out_ref):
     raw = maxima_ref[...] + bias_ref[...]
-    weighted = jnp.log1p(jnp.maximum(raw, 0.0)) * listed_ref[...]
+    weighted = jnp.log1p(jnp.maximum(raw, 0.0))
     own_terms, passages = out_ref.shape
     columns = lax.broadcasted_iota(jnp.int32, (weighted.shape[0], passages), 1)
     terms = []
@@ -166,7 +213,7 @@
         at = slice(half * own_terms, (half + 1) * own_terms)
         sums = [matmul(term, place, TN)[at] for term in terms]
         placed = placed + (sums[0] + sums[1] + sums[2])
-    out_ref[...] = placed
+    out_ref[...] = placed * mask_ref[...]
 
 
 def vmem():
@@ -189,12 +236,12 @@
     return lax.all_to_all(copies, axis, split_axis=0, concat_axis=0, tiled=True)
 
 
-def gather_by_exchange(block, axis):
-    return exchange(jnp.broadcast_to(block[None], (lax.axis_size(axis),) + block.shape), axis)
-
-
-def swap(block, axis):
-    return lax.ppermute(block, axis, [(0, 1), (1, 0)])
+def swap(block, axis, d=1):
+    return lax.ppermute(block, axis, [(i, i ^ d) for i in range(lax.axis_size(axis))])
+
+
+def others(block, axis):
+    return [swap(block, axis, d) for d in range(1, lax.axis_size(axis))]
 
 
 def on_device(
@@ -231,88 +278,102 @@
     near_rows = jnp.stack([jnp.bitwise_xor(near_row, d) for d in range(rows_here)])
     row_ids = slice_index * rows_here + near_rows
 
-    own_slice = decoder.reshape(own_terms, width)
-    part = gather_by_exchange(own_slice, "zh").reshape(-1, width)
-    out_weight = gather_by_exchange(attn_out, "term").reshape(-1, width)
-
-    context = pl.pallas_call(
+    dp_count = slices * rows_here
+    first_block = (lax.axis_index("term") * groups * dp_count * span + row_index * span) // BLOCK
+    scalars = [
+        lax.axis_index("zh"),
+        lax.axis_index("term"),
+        first_block,
+        jnp.int32(dp_count * span // BLOCK),
+    ]
+    ids = jnp.concatenate([row_ids, jnp.stack(scalars)])
+
+    merged = pl.pallas_call(
         attention_kernel,
-        out_shape=jax.ShapeDtypeStruct((tensor, head_width, length), jnp.bfloat16),
-        in_specs=[smem()] + [vmem()] * 5,
+        out_shape=jax.ShapeDtypeStruct((tensor, head_width, length + width), jnp.bfloat16),
+        in_specs=[smem()] + [vmem()] * 6,
         out_specs=vmem(),
-        cost_estimate=cost(1200000000, 60000000),
         compiler_params=grant(20),
+        cost_estimate=cost(1200000000, 2000000),
         name="attention",
     )(
-        row_ids,
+        ids,
         tokens,
         segment_ids,
         attn_gain[None],
         jnp.swapaxes(qkv_weight, 1, 2),
         jnp.asarray(rotary_table(length)),
+        attn_out,
     )
-    context, part, out_weight = lax.optimization_barrier((context, part, out_weight))
+    own_slice = decoder.reshape(own_terms, width)
+    own_slice, merged = lax.optimization_barrier((own_slice, merged))
+    part = jnp.concatenate([own_slice] + others(own_slice, "zh"), axis=0)
+    merged = exchange(merged, "term").reshape(-1, length + width)
+    merged, ffn_out = lax.optimization_barrier((merged, ffn_out))
     table = lax.all_gather(part, "y", axis=0, tiled=True)
-    all_context = exchange(context, "term").reshape(-1, length)
-    down_weight = gather_by_exchange(ffn_out, "term").reshape(-1, width)
     after_attn, inner = pl.pallas_call(
         inner_kernel,
         out_shape=(
             jax.ShapeDtypeStruct((length, width), jnp.float32),
             jax.ShapeDtypeStruct((tensor, hidden_units, length), jnp.bfloat16),
         ),
-        in_specs=[vmem()] * 5,
+        in_specs=[vmem()] * 4,
         out_specs=(vmem(), vmem()),
+        compiler_params=grant(20),
         cost_estimate=cost(600000000, 4000000),
+        name="inner",
+    )(tokens, merged, mlp_gain[None], jnp.swapaxes(ffn_in, 1, 2))
+    downs = [ffn_out] + others(ffn_out, "term")
+    bounds, mask = pl.pallas_call(
+        prep_kernel,
+        out_shape=(
+            jax.ShapeDtypeStruct((segment_ids.shape[0], 2 * PASS_DEV), jnp.int32),
+            jax.ShapeDtypeStruct((own_terms, passages), jnp.float32),
+        ),
+        in_specs=[smem()] + [vmem()] * 3,
+        out_specs=(vmem(), vmem()),
         compiler_params=grant(20),
-        name="inner",
-    )(tokens, all_context, out_weight, mlp_gain[None], jnp.swapaxes(ffn_in, 1, 2))
-    inner, down_weight = lax.optimization_barrier((inner, down_weight))
-    all_inner = exchange(inner, "term").reshape(-1, length)
+        cost_estimate=cost(1000000, 1000000),
+        name="prep",
+    )(ids, segment_ids, block_lists, doc_ids[:, None])
+    all_inner = exchange(inner, "term")
+    all_inner, bounds, mask = lax.optimization_barrier((all_inner, bounds, mask))
     headed = pl.pallas_call(
         head_kernel,
         out_shape=jax.ShapeDtypeStruct((length, width), jnp.bfloat16),
-        in_specs=[vmem()] * 6,
+        in_specs=[smem()] + [vmem()] * (5 + tensor),
         out_specs=vmem(),
+        compiler_params=grant(20),
         cost_estimate=cost(800000000, 5000000),
-        compiler_params=grant(20),
         name="head",
-    )(after_attn, all_inner, down_weight, final_gain[None], head_dense, head_gain[None])
+    )(ids, after_attn, all_inner, *downs, final_gain[None], head_dense, head_gain[None])
 
     far = swap(headed, "zl")
     core = swap(headed, "core")
     far_core = swap(far, "core")
     terms_here = slices * own_terms
-    step = 256
+    step = terms_here // 2
     pooled = pl.pallas_call(
         pool_kernel,
         out_shape=jax.ShapeDtypeStruct((slices, 2 * PASS_DEV, 2 * own_terms), jnp.float32),
         grid=(terms_here // step,),
-        in_specs=[smem()]
+        in_specs=[smem(), smem()]
         + [pl.BlockSpec((length, width), lambda j: (0, 0))] * rows_here
-        + [
-            pl.BlockSpec(segment_ids.shape, lambda j: (0, 0)),
-            pl.BlockSpec((step, width), lambda j: (j, 0)),
-        ],
+        + [pl.BlockSpec((step, width), lambda j: (j, 0))],
         out_specs=pl.BlockSpec(
             (step // own_terms, 2 * PASS_DEV, 2 * own_terms), lambda j: (j, 0, 0)
         ),
-        scratch_shapes=[pltpu.VMEM((rows_here, length, 128), jnp.int32)],
+        scratch_shapes=[
+            pltpu.VMEM((rows_here * length, width), jnp.bfloat16),
+            pltpu.VMEM((rows_here * length, step), jnp.float32),
+        ],
+        compiler_params=grant(56),
         cost_estimate=cost(3300000000, 6000000),
-        compiler_params=grant(56),
         name="pool",
-    )(row_ids, headed, core, far, far_core, segment_ids, table)
+    )(ids, bounds, headed, core, far, far_core, table)
     received = exchange(pooled, near)
 
     bias = decoder_bias.reshape(1, own_terms).astype(jnp.float32)
-    dp_count = slices * rows_here
-    first_block = (lax.axis_index("term") * groups * dp_count * span + row_index * span) // BLOCK
-    own_blocks = first_block + jnp.arange(groups, dtype=jnp.int32) * (dp_count * span // BLOCK)
-    listed = jnp.any(block_lists[:, :, None] == own_blocks[None, None, :], axis=1)
-    by_row = listed.astype(jnp.float32).reshape(slices, rows_here, PASS_DEV, groups)
-    listed = jnp.stack([by_row[:, near_rows[d]] for d in range(rows_here)], axis=1)
-    listed = jnp.repeat(listed, span, axis=3).reshape(slices, 2, 2 * PASS_DEV, own_terms)
-    listed = jnp.transpose(listed, (0, 2, 1, 3)).reshape(slices * 2 * PASS_DEV, 2 * own_terms)
     docs = doc_ids.reshape(slices, rows_here, PASS_DEV)
     docs = jnp.stack([docs[:, near_rows[d]] for d in range(rows_here)], axis=1)
     docs = jnp.transpose(docs.reshape(slices, 2, 2 * PASS_DEV), (1, 0, 2)).reshape(2, -1, 1)
@@ -327,7 +388,7 @@
     )(
         received.reshape(-1, 2 * own_terms),
         jnp.concatenate([bias, bias], axis=1),
-        listed,
+        mask,
         docs,
     )
     return placed.reshape(1, groups, 1, span, passages)

time: 169 us -> 163 us (0.964)
  blocking collectives: 30.2 us -> 0 us
  waiting for transfers between devices: 36.9 us -> 54.8 us
  starting transfers between devices: 46.3 us -> 61.2 us
  other arithmetic: 9.96 us -> 0.94 us
  Pallas kernels: 17 us -> 19.3 us
    all_to_all x2 -> x0, blocking collectives: 30.2 us -> none  [exchange(): return lax.all_to_all(copies, axis, split_axis=0, concat_axis=0, tiled=True)]
    ppermute x3 -> x9, waiting for transfers between devices: 0.01 us -> 24.2 us  [swap(): lax.ppermute(block, axis, [(i, i ^ d) for i in range(lax.axis_size(axis))])]
    ppermute x3 -> x9, starting transfers between devices: 25.9 us -> 44.2 us  [swap(): lax.ppermute(block, axis, [(i, i ^ d) for i in range(lax.axis_size(axis))])]
    reduce_or x1 -> x0, other arithmetic: 9.76 us -> none  [on_device(): jnp.any(block_lists[:, :, None] == own_blocks[None, None, :], axis=1)]
    all_to_all x4 -> x3, waiting for transfers between devices: 36.8 us -> 30.5 us  [exchange(): return lax.all_to_all(copies, axis, split_axis=0, concat_axis=0, tiled=True)]
    broadcast_in_dim x4 -> x1, local copies, waits for them, and re-layouts: 5.51 us -> 0.14 us  [on_device(): doc_ids[:, None]]
    unnamed x40 -> x50, local copies, waits for them, and re-layouts: 5.93 us -> 9.71 us
    all_to_all x4 -> x3, starting transfers between devices: 20.4 us -> 17 us  [exchange(): return lax.all_to_all(copies, axis, split_axis=0, concat_axis=0, tiled=True)]
  transfers between devices with their start and end apart: 8 -> 13, of which waited for: 4 -> 7; matrix products, arithmetic and copies ran while one was open for 8% -> 1% of each run, Pallas kernels for 4% -> 4%
where the time goes in v2:
time: 163 us; the launch traced here: 162 us
  starting transfers between devices  61.2 us (38%)
  waiting for transfers between devices  54.8 us (34%)
  Pallas kernels  19.3 us (12%)
  between operations  13.7 us (8%)
  local copies, waits for them, and re-layouts  11.5 us (7%)
    ppermute x9, starting transfers between devices, swap(): lax.ppermute(block, axis, [(i, i ^ d) for i in range(lax.axis_size(axis))])  44.2 us
    all_to_all x3, waiting for transfers between devices, exchange(): return lax.all_to_all(copies, axis, split_axis=0, concat_axis=0, tiled=True)  30.5 us
    ppermute x9, waiting for transfers between devices, swap(): lax.ppermute(block, axis, [(i, i ^ d) for i in range(lax.axis_size(axis))])  24.2 us
    all_to_all x3, starting transfers between devices, exchange(): return lax.all_to_all(copies, axis, split_axis=0, concat_axis=0, tiled=True)  17 us
    unnamed x50, local copies, waits for them, and re-layouts  9.71 us
    pallas_call x1, Pallas kernels, on_device(): pl.pallas_call(pool_kernel, out_shape=jax.ShapeDtypeStruct((slices, 2 * P...  8.18 us
    pallas_call x1, Pallas kernels, on_device(): pl.pallas_call(head_kernel, out_shape=jax.ShapeDtypeStruct((length, width...  4.43 us
    pallas_call x1, Pallas kernels, on_device(): pl.pallas_call(attention_kernel, out_shape=jax.ShapeDtypeStruct((tensor,...  3.29 us
  transfers between devices with their start and end apart: 13, of which 7 were waited for; matrix products, arithmetic and copies ran while one was open for 1% of the time, Pallas kernels for 4%

profile of v2, /device:TPU:1, one launch (start us, length us, event | category | flops | bytes accessed | tf_op | source)
XLA Modules:
  0.0 161.5 jit_solution(6366754672654666218)
XLA Ops:
  7.4 1.0 copy-done.4
  8.4 0.9 copy-done.7
  9.3 1.2 copy-done.10
  10.5 1.0 copy-done.11
  11.4 0.9 copy-done.15
  12.3 3.3 %attention.1 = bf16[4,192,1024]{2,1,0:T(8,128)(2,1)} custom-call(s32[8]{0:T(128)S(1)} %concatenate.11.row_ref.ids_ref, bf16[256,768]{1,0:T(8,128)(2,1)S(1)} %bitcast.26, s32[128,256]{1,0:T(8,128)S(1)} %copy-done.7, f32[1,768]{1,0:T(1,128)S(1)} %broadcast_in_dim.15.gain_ref, bf16[3,192,768]{2,1,0:T(8,128)(2,1)S(1)} %bitcast.29, ...), custom_call_target="tpu_custom_call" | custom-call | flops 1200000000 | bytes 2000000 | tf_op jit(solution)/shard_map/attention/pallas_call | solution.py:291
  15.6 11.5 %collective-permute-start.8 = (bf16[64,768]{1,0:T(8,128)(2,1)S(1)}, bf16[64,768]{1,0:T(8,128)(2,1)S(1)}, u32[]{:S(2)}, u32[]{:S(2)}) collective-permute-start(bf16[64,768]{1,0:T(8,128)(2,1)S(1)} %bitcast.30), channel_id=1, source_target_pairs={{0,48},{16,32},{32,16},{48,0},{1,49},{17,33},{33,17},{49,1},{2,50}... | collective-permute-start | bytes 294920 | tf_op jit(solution)/shard_map/ppermute | solution.py:240
  27.1 1.9 %collective-permute-start.7 = (bf16[64,768]{1,0:T(8,128)(2,1)S(1)}, bf16[64,768]{1,0:T(8,128)(2,1)S(1)}, u32[]{:S(2)}, u32[]{:S(2)}) collective-permute-start(bf16[64,768]{1,0:T(8,128)(2,1)S(1)} %bitcast.31), channel_id=1, source_target_pairs={{0,32},{16,48},{32,0},{48,16},{1,33},{17,49},{33,1},{49,17},{2,34}... | collective-permute-start | bytes 294920 | tf_op jit(solution)/shard_map/ppermute | solution.py:240
  29.0 4.0 %collective-permute-start.6 = (bf16[64,768]{1,0:T(8,128)(2,1)S(1)}, bf16[64,768]{1,0:T(8,128)(2,1)S(1)}, u32[]{:S(2)}, u32[]{:S(2)}) collective-permute-start(bf16[64,768]{1,0:T(8,128)(2,1)S(1)} %bitcast.32), channel_id=1, source_target_pairs={{0,16},{16,0},{32,48},{48,32},{1,17},{17,1},{33,49},{49,33},{2,18}... | collective-permute-start | bytes 294920 | tf_op jit(solution)/shard_map/ppermute | solution.py:240
  33.0 6.9 %collective-permute-done.7 = bf16[64,768]{1,0:T(8,128)(2,1)S(1)} collective-permute-done((bf16[64,768]{1,0:T(8,128)(2,1)S(1)}, bf16[64,768]{1,0:T(8,128)(2,1)S(1)}, u32[]{:S(2)}, u32[]{:S(2)}) %collective-permute-start.7) | collective-permute-done | bytes 98336 | tf_op jit(solution)/shard_map/ppermute | solution.py:240
  40.0 1.6 collective-permute-done.6
  42.4 4.2 %all-to-all-start = ((bf16[4,192,1024]{2,1,0:T(8,128)(2,1)}), bf16[4,192,1024]{2,1,0:T(8,128)(2,1)S(1)}, u32[]{:S(2)}, u32[]{:S(2)}) async-start(bf16[4,192,1024]{2,1,0:T(8,128)(2,1)} %attention.1), calls=%async_computation | async-start | bytes 3145728 | tf_op jit(solution)/shard_map/all_to_all | solution.py:236
  46.5 20.0 %all-to-all-done = bf16[4,192,1024]{2,1,0:T(8,128)(2,1)S(1)} async-done(((bf16[4,192,1024]{2,1,0:T(8,128)(2,1)}), bf16[4,192,1024]{2,1,0:T(8,128)(2,1)S(1)}, u32[]{:S(2)}, u32[]{:S(2)}) %all-to-all-start) | async-done | bytes 1572896 | tf_op jit(solution)/shard_map/all_to_all | solution.py:236
  66.5 1.0 copy-done.5
  67.6 1.3 inner.1
  69.7 3.6 %all-to-all-start.1 = ((bf16[4,288,256]{2,1,0:T(8,128)(2,1)}), bf16[4,288,256]{2,1,0:T(8,128)(2,1)S(1)}, u32[]{:S(2)}, u32[]{:S(2)}) async-start(bf16[4,288,256]{2,1,0:T(8,128)(2,1)} %copy-done.2), calls=%async_computation.1 | async-start | bytes 1179648 | tf_op jit(solution)/shard_map/all_to_all | solution.py:236
  73.3 3.3 %collective-permute-start = (bf16[288,768]{1,0:T(8,128)(2,1)}, bf16[288,768]{1,0:T(8,128)(2,1)}, u32[]{:S(2)}, u32[]{:S(2)}) collective-permute-start(bf16[288,768]{1,0:T(8,128)(2,1)} %refs_0_), channel_id=1, source_target_pairs={{0,1},{1,0},{2,3},{3,2},{4,5},{5,4},{6,7},{7,6},{8,9},{9,8},{10,11... | collective-permute-start | bytes 1327112 | tf_op jit(solution)/shard_map/ppermute | solution.py:240
  76.6 4.3 %collective-permute-start.1 = (bf16[288,768]{1,0:T(8,128)(2,1)}, bf16[288,768]{1,0:T(8,128)(2,1)}, u32[]{:S(2)}, u32[]{:S(2)}) collective-permute-start(bf16[288,768]{1,0:T(8,128)(2,1)} %refs_0_), channel_id=1, source_target_pairs={{0,2},{1,3},{2,0},{3,1},{4,6},{5,7},{6,4},{7,5},{8,10},{9,11},{10,... | collective-permute-start | bytes 1327112 | tf_op jit(solution)/shard_map/ppermute | solution.py:240
  81.0 2.0 %collective-permute-start.2 = (bf16[288,768]{1,0:T(8,128)(2,1)}, bf16[288,768]{1,0:T(8,128)(2,1)}, u32[]{:S(2)}, u32[]{:S(2)}) collective-permute-start(bf16[288,768]{1,0:T(8,128)(2,1)} %refs_0_), channel_id=1, source_target_pairs={{0,3},{1,2},{2,1},{3,0},{4,7},{5,6},{6,5},{7,4},{8,11},{9,10},{10,... | collective-permute-start | bytes 1327112 | tf_op jit(solution)/shard_map/ppermute | solution.py:240
  83.1 0.9 copy-done.8
  84.0 1.0 prep.1
  86.3 3.6 %collective-permute-done.refs_1_ = bf16[288,768]{1,0:T(8,128)(2,1)} collective-permute-done((bf16[288,768]{1,0:T(8,128)(2,1)}, bf16[288,768]{1,0:T(8,128)(2,1)}, u32[]{:S(2)}, u32[]{:S(2)}) %collective-permute-start) | collective-permute-done | bytes 442400 | tf_op jit(solution)/shard_map/ppermute | solution.py:240
  89.9 11.0 %collective-permute-done.1.refs_2_ = bf16[288,768]{1,0:T(8,128)(2,1)} collective-permute-done((bf16[288,768]{1,0:T(8,128)(2,1)}, bf16[288,768]{1,0:T(8,128)(2,1)}, u32[]{:S(2)}, u32[]{:S(2)}) %collective-permute-start.1) | collective-permute-done | bytes 442400 | tf_op jit(solution)/shard_map/ppermute | solution.py:240
  101.0 4.4 %head.1.own_ref = bf16[256,768]{1,0:T(8,128)(2,1)} custom-call(s32[8]{0:T(128)S(1)} %concatenate.11.row_ref.ids_ref, f32[256,768]{1,0:T(8,128)S(1)} %get-tuple-element.22.after_ref, bf16[4,288,256]{2,1,0:T(8,128)(2,1)S(1)} %all-to-all-done.1.inner_ref, bf16[288,768]{1,0:T(8,128)(2,1)S(1)} %copy-done.3, bf16[288,768]{1,0:T(8,128)(2,1)} %collective-permute-done.refs_1_, ...), custom_call_target="tpu_custom_call" | custom-call | flops 800000000 | bytes 5000000 | tf_op jit(solution)/shard_map/head/pallas_call | solution.py:341
  105.4 1.9 %collective-permute-start.4 = (bf16[256,768]{1,0:T(8,128)(2,1)}, bf16[256,768]{1,0:T(8,128)(2,1)S(1)}, u32[]{:S(2)}, u32[]{:S(2)}) collective-permute-start(bf16[256,768]{1,0:T(8,128)(2,1)} %head.1.own_ref), channel_id=1, source_target_pairs={{0,8},{8,0},{1,9},{9,1},{2,10},{10,2},{3,11},{11,3},{4,12},{12,4},... | collective-permute-start | bytes 1179656 | tf_op jit(solution)/shard_map/ppermute | solution.py:240
  107.3 7.4 %collective-permute-start.3 = (bf16[256,768]{1,0:T(8,128)(2,1)}, bf16[256,768]{1,0:T(8,128)(2,1)S(1)}, u32[]{:S(2)}, u32[]{:S(2)}) collective-permute-start(bf16[256,768]{1,0:T(8,128)(2,1)} %head.1.own_ref), channel_id=1, source_target_pairs={{0,4},{4,0},{1,5},{5,1},{2,6},{6,2},{3,7},{7,3},{8,12},{12,8},{9,1... | collective-permute-start | bytes 1179656 | tf_op jit(solution)/shard_map/ppermute | solution.py:240
  114.7 7.9 %collective-permute-start.5 = (bf16[256,768]{1,0:T(8,128)(2,1)S(1)}, bf16[256,768]{1,0:T(8,128)(2,1)S(1)}, u32[]{:S(2)}, u32[]{:S(2)}) collective-permute-start(bf16[256,768]{1,0:T(8,128)(2,1)S(1)} %collective-permute-done.4.far_ref), channel_id=1, source_target_pairs={{0,4},{4,0},{1,5},{5,1},{2,6},{6,2},{3,7},{7,3},{8,12},{12,8},{9,1... | collective-permute-start | bytes 1179656 | tf_op jit(solution)/shard_map/ppermute | solution.py:240
  122.9 1.1 collective-permute-done.5.far_core_ref
  124.7 8.2 %pool.1 = f32[32,8,128]{2,1,0:T(8,128)} custom-call(s32[8]{0:T(128)} %copy-done.9, s32[128,8]{1,0:T(8,128)} %copy-done.14, bf16[256,768]{1,0:T(8,128)(2,1)} %head.1.own_ref, bf16[256,768]{1,0:T(8,128)(2,1)} %copy-done.23, bf16[256,768]{1,0:T(8,128)(2,1)} %copy-done.22, bf16[256,768]{1,0:T(8,128)(2,1)} %copy-done.24, ...), custom_call_target="tpu_custom_call" | custom-call | flops 3300000000 | bytes 6000000 | tf_op jit(solution)/shard_map/pool/pallas_call | solution.py:356
  132.9 9.3 %all-to-all-start.2 = ((f32[32,8,128]{2,1,0:T(8,128)}), f32[32,8,128]{2,1,0:T(8,128)S(1)}, u32[]{:S(2)}, u32[]{:S(2)}) async-start(f32[32,8,128]{2,1,0:T(8,128)} %pool.1), calls=%async_computation.2 | async-start | bytes 262144 | tf_op jit(solution)/shard_map/all_to_all | solution.py:236
  143.0 10.5 %all-to-all-done.2 = f32[32,8,128]{2,1,0:T(8,128)S(1)} async-done(((f32[32,8,128]{2,1,0:T(8,128)}), f32[32,8,128]{2,1,0:T(8,128)S(1)}, u32[]{:S(2)}, u32[]{:S(2)}) %all-to-all-start.2) | async-done | bytes 131104 | tf_op jit(solution)/shard_map/all_to_all | solution.py:236
  153.5 1.2 place.1
  (70 shorter events, 5.6 us)
Async XLA Ops:
  6.5 117.5 %all-gather.2.cloned.1.call-start = ((), (), s32[]{:S(2)}) async-start(), calls=%async_computation.3 | async-start | bytes 3538944 | tf_op jit(solution)/shard_map/all_gather | solution.py:313
  7.4 93.5 %copy-start.9 = (s32[8]{0:T(128)}, s32[8]{0:T(128)S(1)}, u32[]{:S(2)}) copy-start(s32[8]{0:T(128)S(1)} %concatenate.11.row_ref.ids_ref) | copy-start | bytes 100
  7.4 1.0 copy-start.4
  9.3 1.2 copy-start.10
  10.5 1.0 copy-start.11
  12.3 3.3 %copy-start.16 = (bf16[1,8,1,8,768]{4,3,2,1,0:T(8,128)(2,1)S(1)}, bf16[1,8,1,8,768]{4,3,2,1,0:T(8,128)(2,1)}, u32[]{:S(2)}) copy-start(bf16[1,8,1,8,768]{4,3,2,1,0:T(8,128)(2,1)} %param.29) | copy-start | bytes 294916
  15.6 17.4 %collective-permute-start.8 = (bf16[64,768]{1,0:T(8,128)(2,1)S(1)}, bf16[64,768]{1,0:T(8,128)(2,1)S(1)}, u32[]{:S(2)}, u32[]{:S(2)}) collective-permute-start(bf16[64,768]{1,0:T(8,128)(2,1)S(1)} %bitcast.30), channel_id=1, source_target_pairs={{0,48},{16,32},{32,16},{48,0},{1,49},{17,33},{33,17},{49,1},{2,50}... | collective-permute-start | bytes 294920 | tf_op jit(solution)/shard_map/ppermute | solution.py:240
  27.1 12.8 %collective-permute-start.7 = (bf16[64,768]{1,0:T(8,128)(2,1)S(1)}, bf16[64,768]{1,0:T(8,128)(2,1)S(1)}, u32[]{:S(2)}, u32[]{:S(2)}) collective-permute-start(bf16[64,768]{1,0:T(8,128)(2,1)S(1)} %bitcast.31), channel_id=1, source_target_pairs={{0,32},{16,48},{32,0},{48,16},{1,33},{17,49},{33,1},{49,17},{2,34}... | collective-permute-start | bytes 294920 | tf_op jit(solution)/shard_map/ppermute | solution.py:240
  29.0 12.5 %collective-permute-start.6 = (bf16[64,768]{1,0:T(8,128)(2,1)S(1)}, bf16[64,768]{1,0:T(8,128)(2,1)S(1)}, u32[]{:S(2)}, u32[]{:S(2)}) collective-permute-start(bf16[64,768]{1,0:T(8,128)(2,1)S(1)} %bitcast.32), channel_id=1, source_target_pairs={{0,16},{16,0},{32,48},{48,32},{1,17},{17,1},{33,49},{49,33},{2,18}... | collective-permute-start | bytes 294920 | tf_op jit(solution)/shard_map/ppermute | solution.py:240
  42.4 4.2 %copy-start.18 = (f32[768]{0:T(1024)S(1)}, f32[768]{0:T(1024)}, u32[]{:S(2)}) copy-start(f32[768]{0:T(1024)} %param.23) | copy-start | bytes 9220
  42.4 24.2 %copy-start.1 = (bf16[2,768,288]{1,2,0:T(8,128)(2,1)S(1)}, bf16[2,768,288]{1,2,0:T(8,128)(2,1)}, u32[]{:S(2)}) copy-start(bf16[2,768,288]{1,2,0:T(8,128)(2,1)} %param.24) | copy-start | bytes 2654212
  42.4 24.2 %all-to-all-start = ((bf16[4,192,1024]{2,1,0:T(8,128)(2,1)}), bf16[4,192,1024]{2,1,0:T(8,128)(2,1)S(1)}, u32[]{:S(2)}, u32[]{:S(2)}) async-start(bf16[4,192,1024]{2,1,0:T(8,128)(2,1)} %attention.1), calls=%async_computation | async-start | bytes 3145728 | tf_op jit(solution)/shard_map/all_to_all | solution.py:236
  66.5 1.0 copy-start.5
  67.5 15.4 %copy-start.17 = (s32[512]{0:T(512)S(1)}, s32[512]{0:T(512)}, u32[]{:S(2)}) copy-start(s32[512]{0:T(512)} %param.19) | copy-start | bytes 6148
  67.5 15.5 %copy-start.19 = (f32[768]{0:T(1024)S(1)}, f32[768]{0:T(1024)}, u32[]{:S(2)}) copy-start(f32[768]{0:T(1024)} %param.26) | copy-start | bytes 9220
  67.5 15.6 %copy-start.20 = (f32[768]{0:T(1024)S(1)}, f32[768]{0:T(1024)}, u32[]{:S(2)}) copy-start(f32[768]{0:T(1024)} %param.28) | copy-start | bytes 9220
  67.5 15.6 %copy-start.6 = (s32[512,128]{1,0:T(8,128)S(1)}, s32[512,128]{1,0:T(8,128)}, u32[]{:S(2)}) copy-start(s32[512,128]{1,0:T(8,128)} %list_ref.1) | copy-start | bytes 786436
  69.7 31.3 %copy-start = (bf16[768,768]{1,0:T(8,128)(2,1)S(1)}, bf16[768,768]{1,0:T(8,128)(2,1)}, u32[]{:S(2)}) copy-start(bf16[768,768]{1,0:T(8,128)(2,1)} %refs_5_.1) | copy-start | bytes 3538948
  69.7 31.3 %copy-start.3 = (bf16[288,768]{1,0:T(8,128)(2,1)S(1)}, bf16[288,768]{1,0:T(8,128)(2,1)}, u32[]{:S(2)}) copy-start(bf16[288,768]{1,0:T(8,128)(2,1)} %refs_0_) | copy-start | bytes 1327108
  69.7 16.6 %all-to-all-start.1 = ((bf16[4,288,256]{2,1,0:T(8,128)(2,1)}), bf16[4,288,256]{2,1,0:T(8,128)(2,1)S(1)}, u32[]{:S(2)}, u32[]{:S(2)}) async-start(bf16[4,288,256]{2,1,0:T(8,128)(2,1)} %copy-done.2), calls=%async_computation.1 | async-start | bytes 1179648 | tf_op jit(solution)/shard_map/all_to_all | solution.py:236
  73.3 16.6 %collective-permute-start = (bf16[288,768]{1,0:T(8,128)(2,1)}, bf16[288,768]{1,0:T(8,128)(2,1)}, u32[]{:S(2)}, u32[]{:S(2)}) collective-permute-start(bf16[288,768]{1,0:T(8,128)(2,1)} %refs_0_), channel_id=1, source_target_pairs={{0,1},{1,0},{2,3},{3,2},{4,5},{5,4},{6,7},{7,6},{8,9},{9,8},{10,11... | collective-permute-start | bytes 1327112 | tf_op jit(solution)/shard_map/ppermute | solution.py:240
  76.6 24.3 %collective-permute-start.1 = (bf16[288,768]{1,0:T(8,128)(2,1)}, bf16[288,768]{1,0:T(8,128)(2,1)}, u32[]{:S(2)}, u32[]{:S(2)}) collective-permute-start(bf16[288,768]{1,0:T(8,128)(2,1)} %refs_0_), channel_id=1, source_target_pairs={{0,2},{1,3},{2,0},{3,1},{4,6},{5,7},{6,4},{7,5},{8,10},{9,11},{10,... | collective-permute-start | bytes 1327112 | tf_op jit(solution)/shard_map/ppermute | solution.py:240
  81.0 20.0 %collective-permute-start.2 = (bf16[288,768]{1,0:T(8,128)(2,1)}, bf16[288,768]{1,0:T(8,128)(2,1)}, u32[]{:S(2)}, u32[]{:S(2)}) collective-permute-start(bf16[288,768]{1,0:T(8,128)(2,1)} %refs_0_), channel_id=1, source_target_pairs={{0,3},{1,2},{2,1},{3,0},{4,7},{5,6},{6,5},{7,4},{8,11},{9,10},{10,... | collective-permute-start | bytes 1327112 | tf_op jit(solution)/shard_map/ppermute | solution.py:240
  83.1 0.9 copy-start.8
  105.4 9.3 %collective-permute-start.4 = (bf16[256,768]{1,0:T(8,128)(2,1)}, bf16[256,768]{1,0:T(8,128)(2,1)S(1)}, u32[]{:S(2)}, u32[]{:S(2)}) collective-permute-start(bf16[256,768]{1,0:T(8,128)(2,1)} %head.1.own_ref), channel_id=1, source_target_pairs={{0,8},{8,0},{1,9},{9,1},{2,10},{10,2},{3,11},{11,3},{4,12},{12,4},... | collective-permute-start | bytes 1179656 | tf_op jit(solution)/shard_map/ppermute | solution.py:240
  107.3 15.5 %collective-permute-start.3 = (bf16[256,768]{1,0:T(8,128)(2,1)}, bf16[256,768]{1,0:T(8,128)(2,1)S(1)}, u32[]{:S(2)}, u32[]{:S(2)}) collective-permute-start(bf16[256,768]{1,0:T(8,128)(2,1)} %head.1.own_ref), channel_id=1, source_target_pairs={{0,4},{4,0},{1,5},{5,1},{2,6},{6,2},{3,7},{7,3},{8,12},{12,8},{9,1... | collective-permute-start | bytes 1179656 | tf_op jit(solution)/shard_map/ppermute | solution.py:240
  114.7 9.3 %copy-start.22 = (bf16[256,768]{1,0:T(8,128)(2,1)}, bf16[256,768]{1,0:T(8,128)(2,1)S(1)}, u32[]{:S(2)}) copy-start(bf16[256,768]{1,0:T(8,128)(2,1)S(1)} %collective-permute-done.4.far_ref) | copy-start | bytes 1179652
  114.7 9.3 %collective-permute-start.5 = (bf16[256,768]{1,0:T(8,128)(2,1)S(1)}, bf16[256,768]{1,0:T(8,128)(2,1)S(1)}, u32[]{:S(2)}, u32[]{:S(2)}) collective-permute-start(bf16[256,768]{1,0:T(8,128)(2,1)S(1)} %collective-permute-done.4.far_ref), channel_id=1, source_target_pairs={{0,4},{4,0},{1,5},{5,1},{2,6},{6,2},{3,7},{7,3},{8,12},{12,8},{9,1... | collective-permute-start | bytes 1179656 | tf_op jit(solution)/shard_map/ppermute | solution.py:240
  122.8 19.4 %copy-start.21 = (bf16[1,8,1,8]{3,1,2,0:T(8,128)(2,1)S(1)}, bf16[1,8,1,8]{3,1,2,0:T(8,128)(2,1)}, u32[]{:S(2)}) copy-start(bf16[1,8,1,8]{3,1,2,0:T(8,128)(2,1)} %param.30) | copy-start | bytes 388
  122.8 30.7 %copy-start.13 = (f32[64,512]{1,0:T(8,128)S(1)}, f32[64,512]{1,0:T(8,128)}, u32[]{:S(2)}) copy-start(f32[64,512]{1,0:T(8,128)} %copy-done.12) | copy-start | bytes 393220
  122.9 1.1 copy-start.23
  132.9 20.6 %all-to-all-start.2 = ((f32[32,8,128]{2,1,0:T(8,128)}), f32[32,8,128]{2,1,0:T(8,128)S(1)}, u32[]{:S(2)}, u32[]{:S(2)}) async-start(f32[32,8,128]{2,1,0:T(8,128)} %pool.1), calls=%async_computation.2 | async-start | bytes 262144 | tf_op jit(solution)/shard_map/all_to_all | solution.py:236
  (6 other events, 4.6 us)
Sparse Core Ops, SparseCore 0:
  42.5 46.0 all-gather.1

commit v3 on v2

--- a/solution.py
+++ b/solution.py
@@ -102,7 +102,7 @@
         out_ref[copy, :, length:] = out_weight
 
 
-def inner_kernel(hidden_ref, merged_ref, gain_ref, in_ref, after_ref, inner_ref):
+def ffn_kernel(hidden_ref, merged_ref, gain_ref, in_ref, down_ref, after_ref, out_ref):
     length = hidden_ref.shape[0]
     attended = matmul(merged_ref[:, :length], merged_ref[:, length:], TN)
     after_attn = hidden_ref[...].astype(jnp.float32) + attended
@@ -111,18 +111,15 @@
     inner_up = matmul(in_ref[0], mixed, NT)
     gate_part = matmul(in_ref[1], mixed, NT)
     activated = (gelu(inner_up) * gate_part).astype(jnp.bfloat16)
-    for copy in range(inner_ref.shape[0]):
-        inner_ref[copy] = activated
-
-
-def head_kernel(
-    ids_ref, after_ref, inner_ref, *refs
-):
-    downs, (final_ref, dense_ref, head_ref, out_ref) = refs[:-4], refs[-4:]
+    partial = matmul(activated, down_ref[...], TN).astype(jnp.bfloat16)
+    for copy in range(out_ref.shape[0]):
+        out_ref[copy] = partial
+
+
+def head_kernel(after_ref, partial_ref, final_ref, dense_ref, head_ref, out_ref):
     after_ffn = after_ref[...]
-    for d, down_ref in enumerate(downs):
-        shard = jnp.bitwise_xor(ids_ref[TERM_AT], d)
-        after_ffn = after_ffn + matmul(inner_ref[shard], down_ref[...], TN)
+    for shard in range(partial_ref.shape[0]):
+        after_ffn = after_ffn + partial_ref[shard].astype(jnp.float32)
     normed = layer_norm(after_ffn, final_ref[...]).astype(jnp.bfloat16)
     dense = matmul(normed, dense_ref[...], (((1,), (0,)), ((), ())))
     out_ref[...] = layer_norm(gelu(dense), head_ref[...]).astype(jnp.bfloat16)
@@ -273,7 +270,6 @@
     groups, span = decoder.shape[1], decoder.shape[3]
     own_terms = groups * span
     head_width = qkv_weight.shape[2]
-    hidden_units = ffn_in.shape[2]
     passages = block_lists.shape[0]
     near_rows = jnp.stack([jnp.bitwise_xor(near_row, d) for d in range(rows_here)])
     row_ids = slice_index * rows_here + near_rows
@@ -306,24 +302,23 @@
         attn_out,
     )
     own_slice = decoder.reshape(own_terms, width)
-    own_slice, merged = lax.optimization_barrier((own_slice, merged))
-    part = jnp.concatenate([own_slice] + others(own_slice, "zh"), axis=0)
+    pieces = others(own_slice, "zh")
+    pieces, merged = lax.optimization_barrier((pieces, merged))
+    part = jnp.concatenate([own_slice] + pieces, axis=0)
     merged = exchange(merged, "term").reshape(-1, length + width)
-    merged, ffn_out = lax.optimization_barrier((merged, ffn_out))
     table = lax.all_gather(part, "y", axis=0, tiled=True)
-    after_attn, inner = pl.pallas_call(
-        inner_kernel,
+    after_attn, partial = pl.pallas_call(
+        ffn_kernel,
         out_shape=(
             jax.ShapeDtypeStruct((length, width), jnp.float32),
-            jax.ShapeDtypeStruct((tensor, hidden_units, length), jnp.bfloat16),
+            jax.ShapeDtypeStruct((tensor, length, width), jnp.bfloat16),
         ),
-        in_specs=[vmem()] * 4,
+        in_specs=[vmem()] * 5,
         out_specs=(vmem(), vmem()),
         compiler_params=grant(20),
-        cost_estimate=cost(600000000, 4000000),
-        name="inner",
-    )(tokens, merged, mlp_gain[None], jnp.swapaxes(ffn_in, 1, 2))
-    downs = [ffn_out] + others(ffn_out, "term")
+        cost_estimate=cost(700000000, 4000000),
+        name="ffn",
+    )(tokens, merged, mlp_gain[None], jnp.swapaxes(ffn_in, 1, 2), ffn_out)
     bounds, mask = pl.pallas_call(
         prep_kernel,
         out_shape=(
@@ -336,17 +331,17 @@
         cost_estimate=cost(1000000, 1000000),
         name="prep",
     )(ids, segment_ids, block_lists, doc_ids[:, None])
-    all_inner = exchange(inner, "term")
-    all_inner, bounds, mask = lax.optimization_barrier((all_inner, bounds, mask))
+    partials = exchange(partial, "term")
+    partials, bounds, mask = lax.optimization_barrier((partials, bounds, mask))
     headed = pl.pallas_call(
         head_kernel,
         out_shape=jax.ShapeDtypeStruct((length, width), jnp.bfloat16),
-        in_specs=[smem()] + [vmem()] * (5 + tensor),
+        in_specs=[vmem()] * 5,
         out_specs=vmem(),
         compiler_params=grant(20),
         cost_estimate=cost(800000000, 5000000),
         name="head",
-    )(ids, after_attn, all_inner, *downs, final_gain[None], head_dense, head_gain[None])
+    )(after_attn, partials, final_gain[None], head_dense, head_gain[None])
 
     far = swap(headed, "zl")
     core = swap(headed, "core")

time: 163 us -> 141 us (0.87)
  starting transfers between devices: 61.2 us -> 50 us
  waiting for transfers between devices: 54.8 us -> 47.8 us
  Pallas kernels: 19.3 us -> 17.4 us
    ppermute x9 -> x6, waiting for transfers between devices: 24.2 us -> 1.61 us  [swap(): lax.ppermute(block, axis, [(i, i ^ d) for i in range(lax.axis_size(axis))])]
    all_to_all x3, waiting for transfers between devices: 30.5 us -> 46.1 us  [exchange(): return lax.all_to_all(copies, axis, split_axis=0, concat_axis=0, tiled=True)]
    ppermute x9 -> x6, starting transfers between devices: 44.2 us -> 32.2 us  [swap(): lax.ppermute(block, axis, [(i, i ^ d) for i in range(lax.axis_size(axis))])]
    pallas_call x1, Pallas kernels: 4.43 us -> 1.04 us  [on_device(): pl.pallas_call(head_kernel, out_shape=jax.ShapeDtypeStruct((length, width...]
  transfers between devices with their start and end apart: 13 -> 10, of which waited for: 7 -> 5; matrix products, arithmetic and copies ran while one was open for 1% -> 1% of each run, Pallas kernels for 4% -> 6%
where the time goes in v3:
time: 141 us; the launch traced here: 140 us
  starting transfers between devices  50 us (35%)
  waiting for transfers between devices  47.8 us (34%)
  Pallas kernels  17.4 us (12%)
  between operations  13.8 us (10%)
  local copies, waits for them, and re-layouts  10.1 us (7%)
    all_to_all x3, waiting for transfers between devices, exchange(): return lax.all_to_all(copies, axis, split_axis=0, concat_axis=0, tiled=True)  46.1 us
    ppermute x6, starting transfers between devices, swap(): lax.ppermute(block, axis, [(i, i ^ d) for i in range(lax.axis_size(axis))])  32.2 us
    all_to_all x3, starting transfers between devices, exchange(): return lax.all_to_all(copies, axis, split_axis=0, concat_axis=0, tiled=True)  17.8 us
    unnamed x50, local copies, waits for them, and re-layouts  8.39 us
    pallas_call x1, Pallas kernels, on_device(): pl.pallas_call(pool_kernel, out_shape=jax.ShapeDtypeStruct((slices, 2 * P...  8.19 us
    pallas_call x1, Pallas kernels, on_device(): pl.pallas_call(attention_kernel, out_shape=jax.ShapeDtypeStruct((tensor,...  3.29 us
  transfers between devices with their start and end apart: 10, of which 5 were waited for; matrix products, arithmetic and copies ran while one was open for 1% of the time, Pallas kernels for 6%

profile of v3, /device:TPU:1, one launch (start us, length us, event | category | flops | bytes accessed | tf_op | source)
XLA Modules:
  0.0 140.1 jit_solution(6249139915436343703)
XLA Ops:
  6.5 6.6 %collective-permute-start = (bf16[64,768]{1,0:T(8,128)(2,1)}, bf16[64,768]{1,0:T(8,128)(2,1)S(1)}, u32[]{:S(2)}, u32[]{:S(2)}) collective-permute-start(bf16[64,768]{1,0:T(8,128)(2,1)} %bitcast.30), channel_id=1, source_target_pairs={{0,16},{16,0},{32,48},{48,32},{1,17},{17,1},{33,49},{49,33},{2,18}... | collective-permute-start | bytes 294920 | tf_op jit(solution)/shard_map/ppermute | solution.py:237
  13.2 8.8 %collective-permute-start.1 = (bf16[64,768]{1,0:T(8,128)(2,1)}, bf16[64,768]{1,0:T(8,128)(2,1)S(1)}, u32[]{:S(2)}, u32[]{:S(2)}) collective-permute-start(bf16[64,768]{1,0:T(8,128)(2,1)} %bitcast.31), channel_id=1, source_target_pairs={{0,32},{16,48},{32,0},{48,16},{1,33},{17,49},{33,1},{49,17},{2,34}... | collective-permute-start | bytes 294920 | tf_op jit(solution)/shard_map/ppermute | solution.py:237
  22.0 1.9 %collective-permute-start.2 = (bf16[64,768]{1,0:T(8,128)(2,1)}, bf16[64,768]{1,0:T(8,128)(2,1)S(1)}, u32[]{:S(2)}, u32[]{:S(2)}) collective-permute-start(bf16[64,768]{1,0:T(8,128)(2,1)} %bitcast.32), channel_id=1, source_target_pairs={{0,48},{16,32},{32,16},{48,0},{1,49},{17,33},{33,17},{49,1},{2,50}... | collective-permute-start | bytes 294920 | tf_op jit(solution)/shard_map/ppermute | solution.py:237
  24.0 0.7 broadcast_in_dim.15.gain_ref
  24.8 1.0 copy-done.6
  25.8 0.9 copy-done.9
  26.7 1.2 copy-done.12
  27.9 1.0 copy-done.13
  28.9 0.9 copy-done.15
  29.8 3.3 %attention.1 = bf16[4,192,1024]{2,1,0:T(8,128)(2,1)} custom-call(s32[8]{0:T(128)S(1)} %concatenate.11.row_ref.ids_ref, bf16[256,768]{1,0:T(8,128)(2,1)S(1)} %bitcast.26, s32[128,256]{1,0:T(8,128)S(1)} %copy-done.9, f32[1,768]{1,0:T(1,128)S(1)} %broadcast_in_dim.15.gain_ref, bf16[3,192,768]{2,1,0:T(8,128)(2,1)S(1)} %bitcast.29, ...), custom_call_target="tpu_custom_call" | custom-call | flops 1200000000 | bytes 2000000 | tf_op jit(solution)/shard_map/attention/pallas_call | solution.py:287
  33.1 0.8 pad_maximum_fusion
  33.9 4.2 %all-to-all-start = ((bf16[4,192,1024]{2,1,0:T(8,128)(2,1)}), bf16[4,192,1024]{2,1,0:T(8,128)(2,1)S(1)}, u32[]{:S(2)}, u32[]{:S(2)}) async-start(bf16[4,192,1024]{2,1,0:T(8,128)(2,1)} %attention.1), calls=%async_computation | async-start | bytes 3145728 | tf_op jit(solution)/shard_map/all_to_all | solution.py:233
  38.1 19.2 %all-to-all-done = bf16[4,192,1024]{2,1,0:T(8,128)(2,1)S(1)} async-done(((bf16[4,192,1024]{2,1,0:T(8,128)(2,1)}), bf16[4,192,1024]{2,1,0:T(8,128)(2,1)S(1)}, u32[]{:S(2)}, u32[]{:S(2)}) %all-to-all-start) | async-done | bytes 1572896 | tf_op jit(solution)/shard_map/all_to_all | solution.py:233
  57.3 2.7 %ffn.1 = (f32[256,768]{1,0:T(8,128)S(1)}, bf16[4,256,768]{2,1,0:T(8,128)(2,1)}) custom-call(bf16[256,768]{1,0:T(8,128)(2,1)S(1)} %bitcast.27, bf16[768,1024]{1,0:T(8,128)(2,1)S(1)} %bitcast.24, f32[1,768]{1,0:T(1,128)S(1)} %broadcast_in_dim.16.gain_ref, bf16[2,288,768]{2,1,0:T(8,128)(2,1)S(1)} %bitcast.25, bf16[288,768]{1,0:T(8,128)(2,1)S(1)} %copy-done.4), custom_call_target="tpu_custom_call" | custom-call | flops 700000000 | bytes 4000000 | tf_op jit(solution)/shard_map/ffn/pallas_call | solution.py:310
  60.1 0.9 copy-done.2
  61.0 3.7 %all-to-all-start.1 = ((bf16[4,256,768]{2,1,0:T(8,128)(2,1)}), bf16[4,256,768]{2,1,0:T(8,128)(2,1)S(1)}, u32[]{:S(2)}, u32[]{:S(2)}) async-start(bf16[4,256,768]{2,1,0:T(8,128)(2,1)} %get-tuple-element.17), calls=%async_computation.1 | async-start | bytes 3145728 | tf_op jit(solution)/shard_map/all_to_all | solution.py:233
  64.9 1.0 prep.1
  66.0 0.6 copy-done.14
  66.6 16.4 %all-to-all-done.1.partial_ref = bf16[4,256,768]{2,1,0:T(8,128)(2,1)S(1)} async-done(((bf16[4,256,768]{2,1,0:T(8,128)(2,1)}), bf16[4,256,768]{2,1,0:T(8,128)(2,1)S(1)}, u32[]{:S(2)}, u32[]{:S(2)}) %all-to-all-start.1) | async-done | bytes 1572896 | tf_op jit(solution)/shard_map/all_to_all | solution.py:233
  83.0 1.1 copy-done.3
  84.1 1.0 head.1.own_ref
  85.2 3.1 %collective-permute-start.4 = (bf16[256,768]{1,0:T(8,128)(2,1)S(1)}, bf16[256,768]{1,0:T(8,128)(2,1)S(1)}, u32[]{:S(2)}, u32[]{:S(2)}) collective-permute-start(bf16[256,768]{1,0:T(8,128)(2,1)S(1)} %head.1.own_ref), channel_id=1, source_target_pairs={{0,8},{8,0},{1,9},{9,1},{2,10},{10,2},{3,11},{11,3},{4,12},{12,4},... | collective-permute-start | bytes 1179656 | tf_op jit(solution)/shard_map/ppermute | solution.py:237
  88.3 5.6 %collective-permute-start.3 = (bf16[256,768]{1,0:T(8,128)(2,1)S(1)}, bf16[256,768]{1,0:T(8,128)(2,1)S(1)}, u32[]{:S(2)}, u32[]{:S(2)}) collective-permute-start(bf16[256,768]{1,0:T(8,128)(2,1)S(1)} %head.1.own_ref), channel_id=1, source_target_pairs={{0,4},{4,0},{1,5},{5,1},{2,6},{6,2},{3,7},{7,3},{8,12},{12,8},{9,1... | collective-permute-start | bytes 1179656 | tf_op jit(solution)/shard_map/ppermute | solution.py:237
  93.8 0.5 collective-permute-done.4.far_ref
  94.3 6.2 %collective-permute-start.5 = (bf16[256,768]{1,0:T(8,128)(2,1)S(1)}, bf16[256,768]{1,0:T(8,128)(2,1)S(1)}, u32[]{:S(2)}, u32[]{:S(2)}) collective-permute-start(bf16[256,768]{1,0:T(8,128)(2,1)S(1)} %collective-permute-done.4.far_ref), channel_id=1, source_target_pairs={{0,4},{4,0},{1,5},{5,1},{2,6},{6,2},{3,7},{7,3},{8,12},{12,8},{9,1... | collective-permute-start | bytes 1179656 | tf_op jit(solution)/shard_map/ppermute | solution.py:237
  100.7 1.1 collective-permute-done.5.far_core_ref
  101.9 0.7 copy-done.24
  102.6 8.2 %pool.1 = f32[32,8,128]{2,1,0:T(8,128)} custom-call(s32[8]{0:T(128)} %copy-done.11, s32[128,8]{1,0:T(8,128)} %copy-done.14, bf16[256,768]{1,0:T(8,128)(2,1)} %copy-done.5, bf16[256,768]{1,0:T(8,128)(2,1)} %copy-done.23, bf16[256,768]{1,0:T(8,128)(2,1)} %copy-done.22, bf16[256,768]{1,0:T(8,128)(2,1)} %copy-done.24, ...), custom_call_target="tpu_custom_call" | custom-call | flops 3300000000 | bytes 6000000 | tf_op jit(solution)/shard_map/pool/pallas_call | solution.py:351
  110.8 10.0 %all-to-all-start.2 = ((f32[32,8,128]{2,1,0:T(8,128)}), f32[32,8,128]{2,1,0:T(8,128)S(1)}, u32[]{:S(2)}, u32[]{:S(2)}) async-start(f32[32,8,128]{2,1,0:T(8,128)} %pool.1), calls=%async_computation.2 | async-start | bytes 262144 | tf_op jit(solution)/shard_map/all_to_all | solution.py:233
  121.3 0.1 reshape.43.docs_ref
  121.5 10.5 %all-to-all-done.2 = f32[32,8,128]{2,1,0:T(8,128)S(1)} async-done(((f32[32,8,128]{2,1,0:T(8,128)}), f32[32,8,128]{2,1,0:T(8,128)S(1)}, u32[]{:S(2)}, u32[]{:S(2)}) %all-to-all-start.2) | async-done | bytes 131104 | tf_op jit(solution)/shard_map/all_to_all | solution.py:233
  132.0 1.2 place.1
  (64 shorter events, 1.2 us)
Async XLA Ops:
  6.5 95.3 %all-gather.2.cloned.1.call-start = ((), (), s32[]{:S(2)}) async-start(), calls=%async_computation.3 | async-start | bytes 3538944 | tf_op jit(solution)/shard_map/all_gather | solution.py:309
  6.5 26.5 %collective-permute-start = (bf16[64,768]{1,0:T(8,128)(2,1)}, bf16[64,768]{1,0:T(8,128)(2,1)S(1)}, u32[]{:S(2)}, u32[]{:S(2)}) collective-permute-start(bf16[64,768]{1,0:T(8,128)(2,1)} %bitcast.30), channel_id=1, source_target_pairs={{0,16},{16,0},{32,48},{48,32},{1,17},{17,1},{33,49},{49,33},{2,18}... | collective-permute-start | bytes 294920 | tf_op jit(solution)/shard_map/ppermute | solution.py:237
  13.2 19.9 %collective-permute-start.1 = (bf16[64,768]{1,0:T(8,128)(2,1)}, bf16[64,768]{1,0:T(8,128)(2,1)S(1)}, u32[]{:S(2)}, u32[]{:S(2)}) collective-permute-start(bf16[64,768]{1,0:T(8,128)(2,1)} %bitcast.31), channel_id=1, source_target_pairs={{0,32},{16,48},{32,0},{48,16},{1,33},{17,49},{33,1},{49,17},{2,34}... | collective-permute-start | bytes 294920 | tf_op jit(solution)/shard_map/ppermute | solution.py:237
  22.0 11.0 %collective-permute-start.2 = (bf16[64,768]{1,0:T(8,128)(2,1)}, bf16[64,768]{1,0:T(8,128)(2,1)S(1)}, u32[]{:S(2)}, u32[]{:S(2)}) collective-permute-start(bf16[64,768]{1,0:T(8,128)(2,1)} %bitcast.32), channel_id=1, source_target_pairs={{0,48},{16,32},{32,16},{48,0},{1,49},{17,33},{33,17},{49,1},{2,50}... | collective-permute-start | bytes 294920 | tf_op jit(solution)/shard_map/ppermute | solution.py:237
  24.8 40.1 %copy-start.11 = (s32[8]{0:T(128)}, s32[8]{0:T(128)S(1)}, u32[]{:S(2)}) copy-start(s32[8]{0:T(128)S(1)} %concatenate.11.row_ref.ids_ref) | copy-start | bytes 100
  24.8 1.0 copy-start.6
  25.8 0.9 copy-start.9
  26.7 1.2 copy-start.12
  27.9 1.0 copy-start.13
  29.8 3.3 %copy-start.16 = (bf16[1,8,1,8,768]{4,3,2,1,0:T(8,128)(2,1)S(1)}, bf16[1,8,1,8,768]{4,3,2,1,0:T(8,128)(2,1)}, u32[]{:S(2)}) copy-start(bf16[1,8,1,8,768]{4,3,2,1,0:T(8,128)(2,1)} %param.29) | copy-start | bytes 294916
  33.9 4.2 %copy-start.18 = (f32[768]{0:T(1024)S(1)}, f32[768]{0:T(1024)}, u32[]{:S(2)}) copy-start(f32[768]{0:T(1024)} %param.23) | copy-start | bytes 9220
  33.9 23.4 %copy-start.1 = (bf16[2,768,288]{1,2,0:T(8,128)(2,1)S(1)}, bf16[2,768,288]{1,2,0:T(8,128)(2,1)}, u32[]{:S(2)}) copy-start(bf16[2,768,288]{1,2,0:T(8,128)(2,1)} %param.24) | copy-start | bytes 2654212
  33.9 23.4 %copy-start.4 = (bf16[288,768]{1,0:T(8,128)(2,1)S(1)}, bf16[288,768]{1,0:T(8,128)(2,1)}, u32[]{:S(2)}) copy-start(bf16[288,768]{1,0:T(8,128)(2,1)} %down_ref.1) | copy-start | bytes 1327108
  33.9 23.4 %copy-start.7 = (bf16[1,256,768]{2,1,0:T(8,128)(2,1)S(1)}, bf16[1,256,768]{2,1,0:T(8,128)(2,1)}, u32[]{:S(2)}) copy-start(bf16[1,256,768]{2,1,0:T(8,128)(2,1)} %param.16) | copy-start | bytes 1179652
  33.9 23.4 %all-to-all-start = ((bf16[4,192,1024]{2,1,0:T(8,128)(2,1)}), bf16[4,192,1024]{2,1,0:T(8,128)(2,1)S(1)}, u32[]{:S(2)}, u32[]{:S(2)}) async-start(bf16[4,192,1024]{2,1,0:T(8,128)(2,1)} %attention.1), calls=%async_computation | async-start | bytes 3145728 | tf_op jit(solution)/shard_map/all_to_all | solution.py:233
  60.1 0.9 copy-start.2
  61.0 3.8 %copy-start.17 = (s32[512]{0:T(512)S(1)}, s32[512]{0:T(512)}, u32[]{:S(2)}) copy-start(s32[512]{0:T(512)} %param.19) | copy-start | bytes 6148
  61.0 3.9 %copy-start.19 = (f32[768]{0:T(1024)S(1)}, f32[768]{0:T(1024)}, u32[]{:S(2)}) copy-start(f32[768]{0:T(1024)} %param.26) | copy-start | bytes 9220
  61.0 3.9 %copy-start.20 = (f32[768]{0:T(1024)S(1)}, f32[768]{0:T(1024)}, u32[]{:S(2)}) copy-start(f32[768]{0:T(1024)} %param.28) | copy-start | bytes 9220
  61.0 4.0 %copy-start.8 = (s32[512,128]{1,0:T(8,128)S(1)}, s32[512,128]{1,0:T(8,128)}, u32[]{:S(2)}) copy-start(s32[512,128]{1,0:T(8,128)} %list_ref.1) | copy-start | bytes 786436
  61.0 4.0 %copy-start.10 = (s32[128,256]{1,0:T(8,128)S(1)}, s32[128,256]{1,0:T(8,128)}, u32[]{:S(2)}) copy-start(s32[128,256]{1,0:T(8,128)} %segment_ref.3) | copy-start | bytes 393220
  61.0 22.0 %copy-start = (bf16[768,768]{1,0:T(8,128)(2,1)S(1)}, bf16[768,768]{1,0:T(8,128)(2,1)}, u32[]{:S(2)}) copy-start(bf16[768,768]{1,0:T(8,128)(2,1)} %dense_ref.1) | copy-start | bytes 3538948
  61.0 22.0 %all-to-all-start.1 = ((bf16[4,256,768]{2,1,0:T(8,128)(2,1)}), bf16[4,256,768]{2,1,0:T(8,128)(2,1)S(1)}, u32[]{:S(2)}, u32[]{:S(2)}) async-start(bf16[4,256,768]{2,1,0:T(8,128)(2,1)} %get-tuple-element.17), calls=%async_computation.1 | async-start | bytes 3145728 | tf_op jit(solution)/shard_map/all_to_all | solution.py:233
  83.0 1.1 copy-start.3
  85.2 16.7 %copy-start.5 = (bf16[256,768]{1,0:T(8,128)(2,1)}, bf16[256,768]{1,0:T(8,128)(2,1)S(1)}, u32[]{:S(2)}) copy-start(bf16[256,768]{1,0:T(8,128)(2,1)S(1)} %head.1.own_ref) | copy-start | bytes 1179652
  85.2 9.1 %collective-permute-start.4 = (bf16[256,768]{1,0:T(8,128)(2,1)S(1)}, bf16[256,768]{1,0:T(8,128)(2,1)S(1)}, u32[]{:S(2)}, u32[]{:S(2)}) collective-permute-start(bf16[256,768]{1,0:T(8,128)(2,1)S(1)} %head.1.own_ref), channel_id=1, source_target_pairs={{0,8},{8,0},{1,9},{9,1},{2,10},{10,2},{3,11},{11,3},{4,12},{12,4},... | collective-permute-start | bytes 1179656 | tf_op jit(solution)/shard_map/ppermute | solution.py:237
  88.3 12.4 %collective-permute-start.3 = (bf16[256,768]{1,0:T(8,128)(2,1)S(1)}, bf16[256,768]{1,0:T(8,128)(2,1)S(1)}, u32[]{:S(2)}, u32[]{:S(2)}) collective-permute-start(bf16[256,768]{1,0:T(8,128)(2,1)S(1)} %head.1.own_ref), channel_id=1, source_target_pairs={{0,4},{4,0},{1,5},{5,1},{2,6},{6,2},{3,7},{7,3},{8,12},{12,8},{9,1... | collective-permute-start | bytes 1179656 | tf_op jit(solution)/shard_map/ppermute | solution.py:237
  94.3 7.5 %copy-start.22 = (bf16[256,768]{1,0:T(8,128)(2,1)}, bf16[256,768]{1,0:T(8,128)(2,1)S(1)}, u32[]{:S(2)}) copy-start(bf16[256,768]{1,0:T(8,128)(2,1)S(1)} %collective-permute-done.4.far_ref) | copy-start | bytes 1179652
  94.3 7.5 %collective-permute-start.5 = (bf16[256,768]{1,0:T(8,128)(2,1)S(1)}, bf16[256,768]{1,0:T(8,128)(2,1)S(1)}, u32[]{:S(2)}, u32[]{:S(2)}) collective-permute-start(bf16[256,768]{1,0:T(8,128)(2,1)S(1)} %collective-permute-done.4.far_ref), channel_id=1, source_target_pairs={{0,4},{4,0},{1,5},{5,1},{2,6},{6,2},{3,7},{7,3},{8,12},{12,8},{9,1... | collective-permute-start | bytes 1179656 | tf_op jit(solution)/shard_map/ppermute | solution.py:237
  100.7 20.1 %copy-start.21 = (bf16[1,8,1,8]{3,1,2,0:T(8,128)(2,1)S(1)}, bf16[1,8,1,8]{3,1,2,0:T(8,128)(2,1)}, u32[]{:S(2)}) copy-start(bf16[1,8,1,8]{3,1,2,0:T(8,128)(2,1)} %param.30) | copy-start | bytes 388
  100.7 1.2 copy-start.23
  110.8 21.3 %all-to-all-start.2 = ((f32[32,8,128]{2,1,0:T(8,128)}), f32[32,8,128]{2,1,0:T(8,128)S(1)}, u32[]{:S(2)}, u32[]{:S(2)}) async-start(f32[32,8,128]{2,1,0:T(8,128)} %pool.1), calls=%async_computation.2 | async-start | bytes 262144 | tf_op jit(solution)/shard_map/all_to_all | solution.py:233
  (3 other events, 2.3 us)
Sparse Core Ops, SparseCore 0:
  34.0 47.1 all-gather.1

commit v4 on v3

--- a/solution.py
+++ b/solution.py
@@ -15,9 +15,8 @@
 HEAD_DIM = 64
 HALF_HEAD = 32
 SPAN = 8
-NEAR = 4
 LOWEST = -3.0e38
-NEAR_AT, TERM_AT, BLOCK_AT, STRIDE_AT = 4, 5, 6, 7
+TERM_AT, BLOCK_AT, STRIDE_AT, CORE_AT = 4, 5, 6, 7
 
 NT = (((1,), (1,)), ((), ()))
 TN = (((0,), (0,)), ((), ()))
@@ -52,12 +51,35 @@
 
 
 def attention_kernel(
-    row_ref, hidden_ref, segment_ref, gain_ref, weight_ref, table_ref, out_weight_ref, out_ref
+    ids_ref,
+    gain_ref,
+    hidden_hbm,
+    segment_hbm,
+    weight_hbm,
+    table_hbm,
+    out_ref,
+    hidden_ref,
+    segment_ref,
+    weight_ref,
+    table_ref,
+    sems,
 ):
-    out_weight = out_weight_ref[...]
     length = hidden_ref.shape[0]
+    row = ids_ref[0]
+    tile = pl.multiple_of(lax.shift_left(lax.shift_right_logical(row, 3), 3), 8)
+    copies = [
+        pltpu.make_async_copy(hidden_hbm, hidden_ref, sems.at[0]),
+        pltpu.make_async_copy(segment_hbm.at[pl.ds(tile, 8), :], segment_ref, sems.at[1]),
+        pltpu.make_async_copy(table_hbm, table_ref, sems.at[2]),
+    ] + [
+        pltpu.make_async_copy(weight_hbm.at[slot], weight_ref.at[slot], sems.at[3 + slot])
+        for slot in range(3)
+    ]
+    for copy in copies:
+        copy.start()
+    copies[1].wait()
     head_width = weight_ref.shape[1]
-    segments = segment_ref[pl.ds(row_ref[0], 1), :]
+    segments = segment_ref[pl.ds(row - tile, 1), :]
     starts = jnp.zeros_like(segments)
     for passage in range(PASS_DEV - 1):
         held = jnp.sum((segments == passage).astype(jnp.int32), axis=1, keepdims=True)
@@ -65,6 +87,7 @@
     lane = lax.broadcasted_iota(jnp.int32, (1, length), 1)
     positions = lane - starts
     sublane = lax.broadcasted_iota(jnp.int32, (length, length), 0)
+    copies[2].wait()
     chosen = (sublane == positions).astype(jnp.float32).astype(jnp.bfloat16)
     parts = matmul(table_ref[...], chosen, (((1,), (0,)), ((), ())))
     part = [parts[i * HALF_HEAD : (i + 1) * HALF_HEAD] for i in range(6)]
@@ -78,7 +101,10 @@
     high = jnp.minimum(starts + lengths - 1, lane + HALF_WIN)
     allowed = (sublane >= low) & (sublane <= high)
 
+    copies[0].wait()
     normed = layer_norm(hidden_ref[...].astype(jnp.float32), gain_ref[...]).astype(jnp.bfloat16)
+    for copy in copies[3:]:
+        copy.wait()
     queries = matmul(weight_ref[0], normed, NT)
     key_cols = matmul(weight_ref[1], normed, NT)
     values = matmul(weight_ref[2], normed, NT).astype(jnp.bfloat16)
@@ -97,15 +123,33 @@
         probabilities = (raised / jnp.sum(raised, axis=0, keepdims=True)).astype(jnp.bfloat16)
         context = matmul(values[at], probabilities, (((1,), (0,)), ((), ()))).astype(jnp.bfloat16)
         for copy in range(out_ref.shape[0]):
-            out_ref[copy, at, :length] = context
-    for copy in range(out_ref.shape[0]):
-        out_ref[copy, :, length:] = out_weight
-
-
-def ffn_kernel(hidden_ref, merged_ref, gain_ref, in_ref, down_ref, after_ref, out_ref):
-    length = hidden_ref.shape[0]
-    attended = matmul(merged_ref[:, :length], merged_ref[:, length:], TN)
-    after_attn = hidden_ref[...].astype(jnp.float32) + attended
+            out_ref[copy, at, :] = context
+
+
+def ffn_kernel(
+    ids_ref,
+    hidden_ref,
+    context_ref,
+    gain_ref,
+    in_ref,
+    down_ref,
+    own_weight_ref,
+    mine_ref,
+    other_ref,
+    after_ref,
+    out_ref,
+):
+    own = ids_ref[TERM_AT]
+    after_attn = hidden_ref[...].astype(jnp.float32)
+    after_attn = after_attn + matmul(context_ref[own], own_weight_ref[...], TN)
+    half = own_weight_ref.shape[0] // 2
+    for d in range(1, context_ref.shape[0]):
+        shard = jnp.bitwise_xor(own, d)
+        at = slice((d - 1) * half, d * half)
+        for core, ref in ((ids_ref[CORE_AT], mine_ref), (1 - ids_ref[CORE_AT], other_ref)):
+            first = pl.multiple_of(core * half, half)
+            context = context_ref[shard, pl.ds(first, half), :]
+            after_attn = after_attn + matmul(context, ref[at, :], TN)
     after_ref[...] = after_attn
     mixed = layer_norm(after_attn, gain_ref[...]).astype(jnp.bfloat16)
     inner_up = matmul(in_ref[0], mixed, NT)
@@ -150,25 +194,18 @@
         mask_ref[group * SPAN : (group + 1) * SPAN, :] = held.astype(jnp.float32)
 
 
-def pool_kernel(
-    ids_ref, bounds_ref, own_ref, core_ref, far_ref, far_core_ref, table_ref, out_ref, rows_ref, logits_ref
-):
-    rows = (own_ref, core_ref, far_ref, far_core_ref)
-    length = own_ref.shape[0]
-
-    @pl.when(pl.program_id(0) == 0)
-    def _():
-        for r, row in enumerate(rows):
-            rows_ref[r * length : (r + 1) * length, :] = row[...]
-
-    logits_ref[...] = matmul(rows_ref[...], table_ref[...], NT)
+def passage_maxima(ids_ref, bounds_ref, first_row, rows, table_ref, logits_ref):
+    length = rows[0].shape[0]
+    stacked = jnp.concatenate([row[...] for row in rows], axis=0)
+    logits_ref[...] = matmul(stacked, table_ref[...], NT)
     tile = 8
     sublane = lax.broadcasted_iota(jnp.int32, (tile, logits_ref.shape[1]), 0)
     maxima = []
     for r in range(len(rows)):
+        row = ids_ref[first_row + r]
         for passage in range(PASS_DEV):
-            first = bounds_ref[ids_ref[r], passage]
-            end = bounds_ref[ids_ref[r], passage + 1]
+            first = bounds_ref[row, passage]
+            end = bounds_ref[row, passage + 1]
             first_tile = lax.shift_right_logical(first, 3)
             last_tile = lax.shift_right_logical(end - 1, 3)
 
@@ -184,14 +221,24 @@
                 first_tile + 1, last_tile, lambda t, m: jnp.maximum(m, load(t)), held
             )
             maxima.append(jnp.max(held, axis=0, keepdims=True))
-    half = len(maxima) // 2
-    low = jnp.concatenate(maxima[:half], axis=0)
-    high = jnp.concatenate(maxima[half:], axis=0)
+    return jnp.concatenate(maxima, axis=0)
+
+
+def near_pool_kernel(ids_ref, bounds_ref, own_ref, core_ref, table_ref, low_ref, logits_ref):
+    rows = (own_ref, core_ref)
+    low_ref[...] = passage_maxima(ids_ref, bounds_ref, 0, rows, table_ref, logits_ref)
+
+
+def far_pool_kernel(
+    ids_ref, bounds_ref, far_ref, far_core_ref, table_ref, low_ref, out_ref, logits_ref
+):
+    rows = (far_ref, far_core_ref)
+    high = passage_maxima(ids_ref, bounds_ref, len(rows), rows, table_ref, logits_ref)
+    low = low_ref[...]
     own_terms = out_ref.shape[2] // 2
     for slot in range(out_ref.shape[0]):
         at = slice(slot * own_terms, (slot + 1) * own_terms)
-        to = slot - slot % NEAR + jnp.bitwise_xor(ids_ref[NEAR_AT], slot % NEAR)
-        out_ref[to] = jnp.concatenate([low[:, at], high[:, at]], axis=1)
+        out_ref[slot] = jnp.concatenate([low[:, at], high[:, at]], axis=1)
 
 
 def place_kernel(maxima_ref, bias_ref, mask_ref, docs_ref, out_ref):
@@ -217,6 +264,10 @@
     return pl.BlockSpec(memory_space=pltpu.VMEM)
 
 
+def hbm():
+    return pl.BlockSpec(memory_space=pltpu.HBM)
+
+
 def smem():
     return pl.BlockSpec(memory_space=pltpu.SMEM)
 
@@ -231,6 +282,10 @@
 
 def exchange(copies, axis):
     return lax.all_to_all(copies, axis, split_axis=0, concat_axis=0, tiled=True)
+
+
+def gather_by_exchange(block, axis):
+    return exchange(jnp.broadcast_to(block[None], (lax.axis_size(axis),) + block.shape), axis)
 
 
 def swap(block, axis, d=1):
@@ -277,48 +332,62 @@
     dp_count = slices * rows_here
     first_block = (lax.axis_index("term") * groups * dp_count * span + row_index * span) // BLOCK
     scalars = [
-        lax.axis_index("zh"),
         lax.axis_index("term"),
         first_block,
         jnp.int32(dp_count * span // BLOCK),
+        lax.axis_index("core"),
     ]
     ids = jnp.concatenate([row_ids, jnp.stack(scalars)])
 
-    merged = pl.pallas_call(
+    own_slice = decoder.reshape(own_terms, width)
+    part = gather_by_exchange(own_slice, "zh").reshape(-1, width)
+    half = head_width // 2
+    own_half = lax.dynamic_slice_in_dim(attn_out, lax.axis_index("core") * half, half, 0)
+    pieces = others(own_half, "term")
+    rotary = jnp.asarray(rotary_table(length))
+    context = pl.pallas_call(
         attention_kernel,
-        out_shape=jax.ShapeDtypeStruct((tensor, head_width, length + width), jnp.bfloat16),
-        in_specs=[smem()] + [vmem()] * 6,
+        out_shape=jax.ShapeDtypeStruct((tensor, head_width, length), jnp.bfloat16),
+        in_specs=[smem(), vmem()] + [hbm()] * 4,
         out_specs=vmem(),
-        compiler_params=grant(20),
+        scratch_shapes=[
+            pltpu.VMEM((length, width), jnp.bfloat16),
+            pltpu.VMEM((8, length), jnp.int32),
+            pltpu.VMEM((3, head_width, width), jnp.bfloat16),
+            pltpu.VMEM(rotary.shape, jnp.bfloat16),
+            pltpu.SemaphoreType.DMA((6,)),
+        ],
+        compiler_params=grant(60),
         cost_estimate=cost(1200000000, 2000000),
         name="attention",
-    )(
-        ids,
-        tokens,
-        segment_ids,
-        attn_gain[None],
-        jnp.swapaxes(qkv_weight, 1, 2),
-        jnp.asarray(rotary_table(length)),
-        attn_out,
-    )
-    own_slice = decoder.reshape(own_terms, width)
-    pieces = others(own_slice, "zh")
-    pieces, merged = lax.optimization_barrier((pieces, merged))
-    part = jnp.concatenate([own_slice] + pieces, axis=0)
-    merged = exchange(merged, "term").reshape(-1, length + width)
+    )(ids, attn_gain[None], tokens, segment_ids, jnp.swapaxes(qkv_weight, 1, 2), rotary)
+    part, pieces, context = lax.optimization_barrier((part, pieces, context))
+    mine = jnp.concatenate(pieces, axis=0)
+    other = swap(mine, "core")
     table = lax.all_gather(part, "y", axis=0, tiled=True)
+    all_context = exchange(context, "term")
     after_attn, partial = pl.pallas_call(
         ffn_kernel,
         out_shape=(
             jax.ShapeDtypeStruct((length, width), jnp.float32),
             jax.ShapeDtypeStruct((tensor, length, width), jnp.bfloat16),
         ),
-        in_specs=[vmem()] * 5,
+        in_specs=[smem()] + [vmem()] * 8,
         out_specs=(vmem(), vmem()),
         compiler_params=grant(20),
         cost_estimate=cost(700000000, 4000000),
         name="ffn",
-    )(tokens, merged, mlp_gain[None], jnp.swapaxes(ffn_in, 1, 2), ffn_out)
+    )(
+        ids,
+        tokens,
+        all_context,
+        mlp_gain[None],
+        jnp.swapaxes(ffn_in, 1, 2),
+        ffn_out,
+        attn_out,
+        mine,
+        other,
+    )
     bounds, mask = pl.pallas_call(
         prep_kernel,
         out_shape=(
@@ -347,25 +416,27 @@
     core = swap(headed, "core")
     far_core = swap(far, "core")
     terms_here = slices * own_terms
-    step = terms_here // 2
+    logits = pltpu.VMEM((2 * length, terms_here), jnp.float32)
+    low = pl.pallas_call(
+        near_pool_kernel,
+        out_shape=jax.ShapeDtypeStruct((2 * PASS_DEV, terms_here), jnp.float32),
+        in_specs=[smem(), smem()] + [vmem()] * 3,
+        out_specs=vmem(),
+        scratch_shapes=[logits],
+        compiler_params=grant(20),
+        cost_estimate=cost(1600000000, 4000000),
+        name="near_pool",
+    )(ids, bounds, headed, core, table)
     pooled = pl.pallas_call(
-        pool_kernel,
+        far_pool_kernel,
         out_shape=jax.ShapeDtypeStruct((slices, 2 * PASS_DEV, 2 * own_terms), jnp.float32),
-        grid=(terms_here // step,),
-        in_specs=[smem(), smem()]
-        + [pl.BlockSpec((length, width), lambda j: (0, 0))] * rows_here
-        + [pl.BlockSpec((step, width), lambda j: (j, 0))],
-        out_specs=pl.BlockSpec(
-            (step // own_terms, 2 * PASS_DEV, 2 * own_terms), lambda j: (j, 0, 0)
-        ),
-        scratch_shapes=[
-            pltpu.VMEM((rows_here * length, width), jnp.bfloat16),
-            pltpu.VMEM((rows_here * length, step), jnp.float32),
-        ],
-        compiler_params=grant(56),
-        cost_estimate=cost(3300000000, 6000000),
-        name="pool",
-    )(ids, bounds, headed, core, far, far_core, table)
+        in_specs=[smem(), smem()] + [vmem()] * 4,
+        out_specs=vmem(),
+        scratch_shapes=[logits],
+        compiler_params=grant(20),
+        cost_estimate=cost(1600000000, 4000000),
+        name="far_pool",
+    )(ids, bounds, far, far_core, table, low)
     received = exchange(pooled, near)
 
     bias = decoder_bias.reshape(1, own_terms).astype(jnp.float32)

time: 141 us -> 141 us (level)
  waiting for transfers between devices: 47.8 us -> 39.3 us
  starting transfers between devices: 50 us -> 56.4 us
  Pallas kernels: 17.4 us -> 20.4 us
    all_to_all x3 -> x4, starting transfers between devices: 17.8 us -> 30.8 us  [exchange(): return lax.all_to_all(copies, axis, split_axis=0, concat_axis=0, tiled=True)]
    all_to_all x3 -> x4, waiting for transfers between devices: 46.1 us -> 36.1 us  [exchange(): return lax.all_to_all(copies, axis, split_axis=0, concat_axis=0, tiled=True)]
    ppermute x6 -> x7, starting transfers between devices: 32.2 us -> 25.6 us  [swap(): lax.ppermute(block, axis, [(i, i ^ d) for i in range(lax.axis_size(axis))])]
    unnamed x50 -> x44, local copies, waits for them, and re-layouts: 8.39 us -> 5.41 us
    broadcast_in_dim x0 -> x1, local copies, waits for them, and re-layouts: none -> 1.68 us  [gather_by_exchange(): jnp.broadcast_to(block[None], (lax.axis_size(axis),) + block.shape)]
    ppermute x6 -> x7, waiting for transfers between devices: 1.61 us -> 3.11 us  [swap(): lax.ppermute(block, axis, [(i, i ^ d) for i in range(lax.axis_size(axis))])]
    pallas_call x1 -> x2, Pallas kernels: 8.19 us -> 8.87 us  [the longest x1 4.81 us: on_device(): pl.pallas_call(far_pool_kernel, out_shape=jax.ShapeDtypeStruct((slices, 2...]
  transfers between devices with their start and end apart: 10 -> 12, of which waited for: 5 -> 4; matrix products, arithmetic and copies ran while one was open for 1% -> 2% of each run, Pallas kernels for 6% -> 10%
where the time goes in v4:
time: 141 us; the launch traced here: 140 us
  starting transfers between devices  56.4 us (40%)
  waiting for transfers between devices  39.3 us (28%)
  Pallas kernels  20.4 us (14%)
  between operations  13.9 us (10%)
  local copies, waits for them, and re-layouts  10.2 us (7%)
    all_to_all x4, waiting for transfers between devices, exchange(): return lax.all_to_all(copies, axis, split_axis=0, concat_axis=0, tiled=True)  36.1 us
    all_to_all x4, starting transfers between devices, exchange(): return lax.all_to_all(copies, axis, split_axis=0, concat_axis=0, tiled=True)  30.8 us
    ppermute x7, starting transfers between devices, swap(): lax.ppermute(block, axis, [(i, i ^ d) for i in range(lax.axis_size(axis))])  25.6 us
    unnamed x44, local copies, waits for them, and re-layouts  5.41 us
    pallas_call x1, Pallas kernels, on_device(): pl.pallas_call(far_pool_kernel, out_shape=jax.ShapeDtypeStruct((slices, 2...  4.81 us
    pallas_call x1, Pallas kernels, on_device(): pl.pallas_call(attention_kernel, out_shape=jax.ShapeDtypeStruct((tensor,...  4.32 us
    pallas_call x1, Pallas kernels, on_device(): pl.pallas_call(near_pool_kernel, out_shape=jax.ShapeDtypeStruct((2 * PASS...  4.06 us
    pallas_call x1, Pallas kernels, on_device(): pl.pallas_call(ffn_kernel, out_shape=(jax.ShapeDtypeStruct((length, width...  4 us
  transfers between devices with their start and end apart: 12, of which 4 were waited for; matrix products, arithmetic and copies ran while one was open for 2% of the time, Pallas kernels for 10%

profile of v4, /device:TPU:1, one launch (start us, length us, event | category | flops | bytes accessed | tf_op | source)
XLA Modules:
  0.0 140.4 jit_solution(7368318096401513252)
XLA Ops:
  6.5 1.7 %broadcast_in_dim.23 = bf16[4,64,768]{2,1,0:T(8,128)(2,1)} broadcast(bf16[64,768]{1,0:T(8,128)(2,1)} %bitcast.29), dimensions={1,2} | broadcast | bytes 491520 | tf_op jit(solution)/shard_map/broadcast_in_dim | solution.py:288
  8.2 10.8 %all-to-all-start = ((bf16[4,64,768]{2,1,0:T(8,128)(2,1)}), bf16[4,64,768]{2,1,0:T(8,128)(2,1)S(1)}, u32[]{:S(2)}, u32[]{:S(2)}) async-start(bf16[4,64,768]{2,1,0:T(8,128)(2,1)} %broadcast_in_dim.23), calls=%async_computation | async-start | bytes 786432 | tf_op jit(solution)/shard_map/all_to_all | solution.py:284
  19.1 0.9 constant_dynamic-slice_fusion.4
  20.0 3.1 %collective-permute-start = (bf16[96,768]{1,0:T(8,128)(2,1)S(1)}, bf16[96,768]{1,0:T(8,128)(2,1)S(1)}, u32[]{:S(2)}, u32[]{:S(2)}) collective-permute-start(bf16[96,768]{1,0:T(8,128)(2,1)S(1)} %constant_dynamic-slice_fusion.4), channel_id=1, source_target_pairs={{0,1},{1,0},{2,3},{3,2},{4,5},{5,4},{6,7},{7,6},{8,9},{9,8},{10,11... | collective-permute-start | bytes 442376 | tf_op jit(solution)/shard_map/ppermute | solution.py:292
  23.1 4.4 %collective-permute-start.1 = (bf16[96,768]{1,0:T(8,128)(2,1)S(1)}, bf16[96,768]{1,0:T(8,128)(2,1)S(1)}, u32[]{:S(2)}, u32[]{:S(2)}) collective-permute-start(bf16[96,768]{1,0:T(8,128)(2,1)S(1)} %constant_dynamic-slice_fusion.4), channel_id=1, source_target_pairs={{0,2},{1,3},{2,0},{3,1},{4,6},{5,7},{6,4},{7,5},{8,10},{9,11},{10,... | collective-permute-start | bytes 442376 | tf_op jit(solution)/shard_map/ppermute | solution.py:292
  27.5 2.1 %collective-permute-start.2 = (bf16[96,768]{1,0:T(8,128)(2,1)S(1)}, bf16[96,768]{1,0:T(8,128)(2,1)S(1)}, u32[]{:S(2)}, u32[]{:S(2)}) collective-permute-start(bf16[96,768]{1,0:T(8,128)(2,1)S(1)} %constant_dynamic-slice_fusion.4), channel_id=1, source_target_pairs={{0,3},{1,2},{2,1},{3,0},{4,7},{5,6},{6,5},{7,4},{8,11},{9,10},{10,... | collective-permute-start | bytes 442376 | tf_op jit(solution)/shard_map/ppermute | solution.py:292
  29.7 0.6 broadcast_in_dim.24.gain_ref
  30.3 0.7 concatenate.11.ids_ref
  31.0 4.3 %attention.1 = bf16[4,192,256]{2,1,0:T(8,128)(2,1)} custom-call(s32[8]{0:T(128)} %concatenate.11.ids_ref, f32[1,768]{1,0:T(1,128)} %broadcast_in_dim.24.gain_ref, bf16[256,768]{1,0:T(8,128)(2,1)} %bitcast.25, s32[128,256]{1,0:T(8,128)} %segment_ref.1, bf16[3,192,768]{2,1,0:T(8,128)(2,1)} %bitcast.32, bf16[192,256]{1,0:T(8,128)(2,1)} %constant.57.clone.table_hbm), custom_call_target="tpu_custom_call" | custom-call | flops 1200000000 | bytes 2000000 | tf_op jit(solution)/shard_map/attention/pallas_call | solution.py:348
  35.4 0.7 copy-done.14
  36.2 3.8 %collective-permute-start.3 = (bf16[288,768]{1,0:T(8,128)(2,1)S(1)}, bf16[288,768]{1,0:T(8,128)(2,1)S(1)}, u32[]{:S(2)}, u32[]{:S(2)}) collective-permute-start(bf16[288,768]{1,0:T(8,128)(2,1)S(1)} %constant_dynamic-update-slice_fusion.mine_ref), channel_id=1, source_target_pairs={{0,4},{4,0},{1,5},{5,1},{2,6},{6,2},{3,7},{7,3},{8,12},{12,8},{9,1... | collective-permute-start | bytes 1327112 | tf_op jit(solution)/shard_map/ppermute | solution.py:292
  40.0 3.7 %all-to-all-start.1 = ((bf16[4,192,256]{2,1,0:T(8,128)(2,1)}), bf16[4,192,256]{2,1,0:T(8,128)(2,1)S(1)}, u32[]{:S(2)}, u32[]{:S(2)}) async-start(bf16[4,192,256]{2,1,0:T(8,128)(2,1)} %attention.1), calls=%async_computation.1 | async-start | bytes 786432 | tf_op jit(solution)/shard_map/all_to_all | solution.py:284
  43.7 7.9 %all-to-all-done.1.context_ref = bf16[4,192,256]{2,1,0:T(8,128)(2,1)S(1)} async-done(((bf16[4,192,256]{2,1,0:T(8,128)(2,1)}), bf16[4,192,256]{2,1,0:T(8,128)(2,1)S(1)}, u32[]{:S(2)}, u32[]{:S(2)}) %all-to-all-start.1) | async-done | bytes 393248 | tf_op jit(solution)/shard_map/all_to_all | solution.py:284
  51.7 4.0 %ffn.1 = (f32[256,768]{1,0:T(8,128)S(1)}, bf16[4,256,768]{2,1,0:T(8,128)(2,1)}) custom-call(s32[8]{0:T(128)S(1)} %copy-done.9, bf16[256,768]{1,0:T(8,128)(2,1)S(1)} %bitcast.26, bf16[4,192,256]{2,1,0:T(8,128)(2,1)S(1)} %all-to-all-done.1.context_ref, f32[1,768]{1,0:T(1,128)S(1)} %broadcast_in_dim.25.gain_ref, bf16[2,288,768]{2,1,0:T(8,128)(2,1)S(1)} %bitcast.24, ...), custom_call_target="tpu_custom_call" | custom-call | flops 700000000 | bytes 4000000 | tf_op jit(solution)/shard_map/ffn/pallas_call | solution.py:369
  55.7 0.9 copy-done.2
  56.6 3.7 %all-to-all-start.2 = ((bf16[4,256,768]{2,1,0:T(8,128)(2,1)}), bf16[4,256,768]{2,1,0:T(8,128)(2,1)S(1)}, u32[]{:S(2)}, u32[]{:S(2)}) async-start(bf16[4,256,768]{2,1,0:T(8,128)(2,1)} %get-tuple-element.21), calls=%async_computation.2 | async-start | bytes 3145728 | tf_op jit(solution)/shard_map/all_to_all | solution.py:284
  60.6 1.0 prep.1
  61.6 0.6 copy-done.12
  62.2 17.7 %all-to-all-done.2.partial_ref = bf16[4,256,768]{2,1,0:T(8,128)(2,1)S(1)} async-done(((bf16[4,256,768]{2,1,0:T(8,128)(2,1)}), bf16[4,256,768]{2,1,0:T(8,128)(2,1)S(1)}, u32[]{:S(2)}, u32[]{:S(2)}) %all-to-all-start.2) | async-done | bytes 1572896 | tf_op jit(solution)/shard_map/all_to_all | solution.py:284
  79.9 1.1 copy-done.3
  81.1 1.0 head.1.own_ref
  82.1 3.1 %collective-permute-start.4 = (bf16[256,768]{1,0:T(8,128)(2,1)S(1)}, bf16[256,768]{1,0:T(8,128)(2,1)S(1)}, u32[]{:S(2)}, u32[]{:S(2)}) collective-permute-start(bf16[256,768]{1,0:T(8,128)(2,1)S(1)} %head.1.own_ref), channel_id=1, source_target_pairs={{0,8},{8,0},{1,9},{9,1},{2,10},{10,2},{3,11},{11,3},{4,12},{12,4},... | collective-permute-start | bytes 1179656 | tf_op jit(solution)/shard_map/ppermute | solution.py:292
  85.2 4.2 %collective-permute-start.6 = (bf16[256,768]{1,0:T(8,128)(2,1)S(1)}, bf16[256,768]{1,0:T(8,128)(2,1)S(1)}, u32[]{:S(2)}, u32[]{:S(2)}) collective-permute-start(bf16[256,768]{1,0:T(8,128)(2,1)S(1)} %head.1.own_ref), channel_id=1, source_target_pairs={{0,4},{4,0},{1,5},{5,1},{2,6},{6,2},{3,7},{7,3},{8,12},{12,8},{9,1... | collective-permute-start | bytes 1179656 | tf_op jit(solution)/shard_map/ppermute | solution.py:292
  89.5 3.1 %collective-permute-done.4.far_ref = bf16[256,768]{1,0:T(8,128)(2,1)S(1)} collective-permute-done((bf16[256,768]{1,0:T(8,128)(2,1)S(1)}, bf16[256,768]{1,0:T(8,128)(2,1)S(1)}, u32[]{:S(2)}, u32[]{:S(2)}) %collective-permute-start.4) | collective-permute-done | bytes 393248 | tf_op jit(solution)/shard_map/ppermute | solution.py:292
  92.6 4.9 %collective-permute-start.5 = (bf16[256,768]{1,0:T(8,128)(2,1)S(1)}, bf16[256,768]{1,0:T(8,128)(2,1)S(1)}, u32[]{:S(2)}, u32[]{:S(2)}) collective-permute-start(bf16[256,768]{1,0:T(8,128)(2,1)S(1)} %collective-permute-done.4.far_ref), channel_id=1, source_target_pairs={{0,4},{4,0},{1,5},{5,1},{2,6},{6,2},{3,7},{7,3},{8,12},{12,8},{9,1... | collective-permute-start | bytes 1179656 | tf_op jit(solution)/shard_map/ppermute | solution.py:292
  97.7 1.9 %copy-done.10 = bf16[2048,768]{1,0:T(8,128)(2,1)S(1)} copy-done((bf16[2048,768]{1,0:T(8,128)(2,1)S(1)}, bf16[2048,768]{1,0:T(8,128)(2,1)}, u32[]{:S(2)}) %copy-start.10) | copy-done | bytes 3145752
  99.6 4.1 %near_pool.1.low_ref = f32[8,2048]{1,0:T(8,128)S(1)} custom-call(s32[8]{0:T(128)S(1)} %copy-done.9, s32[128,8]{1,0:T(8,128)S(1)} %copy-done.13, bf16[256,768]{1,0:T(8,128)(2,1)S(1)} %head.1.own_ref, bf16[256,768]{1,0:T(8,128)(2,1)S(1)} %collective-permute-done.6.core_ref, bf16[2048,768]{1,0:T(8,128)(2,1)S(1)} %copy-done.10), custom_call_target="tpu_custom_call" | custom-call | flops 1600000000 | bytes 4000000 | tf_op jit(solution)/shard_map/near_pool/pallas_call | solution.py:420
  103.7 4.8 %far_pool.1 = f32[32,8,128]{2,1,0:T(8,128)} custom-call(s32[8]{0:T(128)S(1)} %copy-done.9, s32[128,8]{1,0:T(8,128)S(1)} %copy-done.13, bf16[256,768]{1,0:T(8,128)(2,1)S(1)} %collective-permute-done.4.far_ref, bf16[256,768]{1,0:T(8,128)(2,1)S(1)} %collective-permute-done.5.far_core_ref, bf16[2048,768]{1,0:T(8,128)(2,1)S(1)} %copy-done.11, ...), custom_call_target="tpu_custom_call" | custom-call | flops 1600000000 | bytes 4000000 | tf_op jit(solution)/shard_map/far_pool/pallas_call | solution.py:430
  108.5 12.6 %all-to-all-start.3 = ((f32[32,8,128]{2,1,0:T(8,128)}), f32[32,8,128]{2,1,0:T(8,128)S(1)}, u32[]{:S(2)}, u32[]{:S(2)}) async-start(f32[32,8,128]{2,1,0:T(8,128)} %far_pool.1), calls=%async_computation.3 | async-start | bytes 262144 | tf_op jit(solution)/shard_map/all_to_all | solution.py:284
  121.5 0.1 reshape.40.docs_ref
  121.8 10.5 %all-to-all-done.3 = f32[32,8,128]{2,1,0:T(8,128)S(1)} async-done(((f32[32,8,128]{2,1,0:T(8,128)}), f32[32,8,128]{2,1,0:T(8,128)S(1)}, u32[]{:S(2)}, u32[]{:S(2)}) %all-to-all-start.3) | async-done | bytes 131104 | tf_op jit(solution)/shard_map/all_to_all | solution.py:284
  132.4 1.2 place.1
  (65 shorter events, 1.2 us)
Async XLA Ops:
  6.5 23.2 %copy-start.16 = (f32[768]{0:T(1024)S(1)}, f32[768]{0:T(1024)}, u32[]{:S(2)}) copy-start(f32[768]{0:T(1024)} %param.20) | copy-start | bytes 9220
  8.2 27.2 %all-to-all-start = ((bf16[4,64,768]{2,1,0:T(8,128)(2,1)}), bf16[4,64,768]{2,1,0:T(8,128)(2,1)S(1)}, u32[]{:S(2)}, u32[]{:S(2)}) async-start(bf16[4,64,768]{2,1,0:T(8,128)(2,1)} %broadcast_in_dim.23), calls=%async_computation | async-start | bytes 786432 | tf_op jit(solution)/shard_map/all_to_all | solution.py:284
  19.1 78.6 %all-gather.2.cloned.1.call-start = ((), (), s32[]{:S(2)}) async-start(), calls=%async_computation.4 | async-start | bytes 3538944 | tf_op jit(solution)/shard_map/all_gather | solution.py:367
  20.0 15.4 %collective-permute-start = (bf16[96,768]{1,0:T(8,128)(2,1)S(1)}, bf16[96,768]{1,0:T(8,128)(2,1)S(1)}, u32[]{:S(2)}, u32[]{:S(2)}) collective-permute-start(bf16[96,768]{1,0:T(8,128)(2,1)S(1)} %constant_dynamic-slice_fusion.4), channel_id=1, source_target_pairs={{0,1},{1,0},{2,3},{3,2},{4,5},{5,4},{6,7},{7,6},{8,9},{9,8},{10,11... | collective-permute-start | bytes 442376 | tf_op jit(solution)/shard_map/ppermute | solution.py:292
  23.1 12.3 %collective-permute-start.1 = (bf16[96,768]{1,0:T(8,128)(2,1)S(1)}, bf16[96,768]{1,0:T(8,128)(2,1)S(1)}, u32[]{:S(2)}, u32[]{:S(2)}) collective-permute-start(bf16[96,768]{1,0:T(8,128)(2,1)S(1)} %constant_dynamic-slice_fusion.4), channel_id=1, source_target_pairs={{0,2},{1,3},{2,0},{3,1},{4,6},{5,7},{6,4},{7,5},{8,10},{9,11},{10,... | collective-permute-start | bytes 442376 | tf_op jit(solution)/shard_map/ppermute | solution.py:292
  27.5 7.9 %collective-permute-start.2 = (bf16[96,768]{1,0:T(8,128)(2,1)S(1)}, bf16[96,768]{1,0:T(8,128)(2,1)S(1)}, u32[]{:S(2)}, u32[]{:S(2)}) collective-permute-start(bf16[96,768]{1,0:T(8,128)(2,1)S(1)} %constant_dynamic-slice_fusion.4), channel_id=1, source_target_pairs={{0,3},{1,2},{2,1},{3,0},{4,7},{5,6},{6,5},{7,4},{8,11},{9,10},{10,... | collective-permute-start | bytes 442376 | tf_op jit(solution)/shard_map/ppermute | solution.py:292
  35.3 8.4 %copy-start.17 = (f32[768]{0:T(1024)S(1)}, f32[768]{0:T(1024)}, u32[]{:S(2)}) copy-start(f32[768]{0:T(1024)} %param.23) | copy-start | bytes 9220
  35.3 16.3 %copy-start.1 = (bf16[2,768,288]{1,2,0:T(8,128)(2,1)S(1)}, bf16[2,768,288]{1,2,0:T(8,128)(2,1)}, u32[]{:S(2)}) copy-start(bf16[2,768,288]{1,2,0:T(8,128)(2,1)} %param.24) | copy-start | bytes 2654212
  35.3 16.3 %copy-start.4 = (bf16[192,768]{1,0:T(8,128)(2,1)S(1)}, bf16[192,768]{1,0:T(8,128)(2,1)}, u32[]{:S(2)}) copy-start(bf16[192,768]{1,0:T(8,128)(2,1)} %own_weight_ref.1) | copy-start | bytes 884740
  35.3 16.3 %copy-start.5 = (bf16[288,768]{1,0:T(8,128)(2,1)S(1)}, bf16[288,768]{1,0:T(8,128)(2,1)}, u32[]{:S(2)}) copy-start(bf16[288,768]{1,0:T(8,128)(2,1)} %down_ref.1) | copy-start | bytes 1327108
  35.3 16.3 %copy-start.6 = (bf16[1,256,768]{2,1,0:T(8,128)(2,1)S(1)}, bf16[1,256,768]{2,1,0:T(8,128)(2,1)}, u32[]{:S(2)}) copy-start(bf16[1,256,768]{2,1,0:T(8,128)(2,1)} %param.16) | copy-start | bytes 1179652
  35.3 16.3 %copy-start.9 = (s32[8]{0:T(128)S(1)}, s32[8]{0:T(128)}, u32[]{:S(2)}) copy-start(s32[8]{0:T(128)} %concatenate.11.ids_ref) | copy-start | bytes 100
  35.4 0.8 copy-start.14
  36.2 15.4 %collective-permute-start.3 = (bf16[288,768]{1,0:T(8,128)(2,1)S(1)}, bf16[288,768]{1,0:T(8,128)(2,1)S(1)}, u32[]{:S(2)}, u32[]{:S(2)}) collective-permute-start(bf16[288,768]{1,0:T(8,128)(2,1)S(1)} %constant_dynamic-update-slice_fusion.mine_ref), channel_id=1, source_target_pairs={{0,4},{4,0},{1,5},{5,1},{2,6},{6,2},{3,7},{7,3},{8,12},{12,8},{9,1... | collective-permute-start | bytes 1327112 | tf_op jit(solution)/shard_map/ppermute | solution.py:292
  40.0 11.6 %all-to-all-start.1 = ((bf16[4,192,256]{2,1,0:T(8,128)(2,1)}), bf16[4,192,256]{2,1,0:T(8,128)(2,1)S(1)}, u32[]{:S(2)}, u32[]{:S(2)}) async-start(bf16[4,192,256]{2,1,0:T(8,128)(2,1)} %attention.1), calls=%async_computation.1 | async-start | bytes 786432 | tf_op jit(solution)/shard_map/all_to_all | solution.py:284
  55.7 0.9 copy-start.2
  56.6 3.8 %copy-start.15 = (s32[512]{0:T(512)S(1)}, s32[512]{0:T(512)}, u32[]{:S(2)}) copy-start(s32[512]{0:T(512)} %param.19) | copy-start | bytes 6148
  56.6 3.9 %copy-start.18 = (f32[768]{0:T(1024)S(1)}, f32[768]{0:T(1024)}, u32[]{:S(2)}) copy-start(f32[768]{0:T(1024)} %param.26) | copy-start | bytes 9220
  56.6 3.9 %copy-start.19 = (f32[768]{0:T(1024)S(1)}, f32[768]{0:T(1024)}, u32[]{:S(2)}) copy-start(f32[768]{0:T(1024)} %param.28) | copy-start | bytes 9220
  56.6 4.0 %copy-start.7 = (s32[512,128]{1,0:T(8,128)S(1)}, s32[512,128]{1,0:T(8,128)}, u32[]{:S(2)}) copy-start(s32[512,128]{1,0:T(8,128)} %list_ref.1) | copy-start | bytes 786436
  56.6 4.0 %copy-start.8 = (s32[128,256]{1,0:T(8,128)S(1)}, s32[128,256]{1,0:T(8,128)}, u32[]{:S(2)}) copy-start(s32[128,256]{1,0:T(8,128)} %segment_ref.1) | copy-start | bytes 393220
  56.6 23.3 %copy-start = (bf16[768,768]{1,0:T(8,128)(2,1)S(1)}, bf16[768,768]{1,0:T(8,128)(2,1)}, u32[]{:S(2)}) copy-start(bf16[768,768]{1,0:T(8,128)(2,1)} %dense_ref.1) | copy-start | bytes 3538948
  56.6 23.3 %all-to-all-start.2 = ((bf16[4,256,768]{2,1,0:T(8,128)(2,1)}), bf16[4,256,768]{2,1,0:T(8,128)(2,1)S(1)}, u32[]{:S(2)}, u32[]{:S(2)}) async-start(bf16[4,256,768]{2,1,0:T(8,128)(2,1)} %get-tuple-element.21), calls=%async_computation.2 | async-start | bytes 3145728 | tf_op jit(solution)/shard_map/all_to_all | solution.py:284
  79.9 1.1 copy-start.3
  81.1 16.6 %copy-start.13 = (s32[128,8]{1,0:T(8,128)S(1)}, s32[128,8]{1,0:T(8,128)}, u32[]{:S(2)}) copy-start(s32[128,8]{1,0:T(8,128)} %copy-done.12) | copy-start | bytes 12292
  82.1 10.4 %collective-permute-start.4 = (bf16[256,768]{1,0:T(8,128)(2,1)S(1)}, bf16[256,768]{1,0:T(8,128)(2,1)S(1)}, u32[]{:S(2)}, u32[]{:S(2)}) collective-permute-start(bf16[256,768]{1,0:T(8,128)(2,1)S(1)} %head.1.own_ref), channel_id=1, source_target_pairs={{0,8},{8,0},{1,9},{9,1},{2,10},{10,2},{3,11},{11,3},{4,12},{12,4},... | collective-permute-start | bytes 1179656 | tf_op jit(solution)/shard_map/ppermute | solution.py:292
  85.2 12.4 %collective-permute-start.6 = (bf16[256,768]{1,0:T(8,128)(2,1)S(1)}, bf16[256,768]{1,0:T(8,128)(2,1)S(1)}, u32[]{:S(2)}, u32[]{:S(2)}) collective-permute-start(bf16[256,768]{1,0:T(8,128)(2,1)S(1)} %head.1.own_ref), channel_id=1, source_target_pairs={{0,4},{4,0},{1,5},{5,1},{2,6},{6,2},{3,7},{7,3},{8,12},{12,8},{9,1... | collective-permute-start | bytes 1179656 | tf_op jit(solution)/shard_map/ppermute | solution.py:292
  92.6 11.1 %collective-permute-start.5 = (bf16[256,768]{1,0:T(8,128)(2,1)S(1)}, bf16[256,768]{1,0:T(8,128)(2,1)S(1)}, u32[]{:S(2)}, u32[]{:S(2)}) collective-permute-start(bf16[256,768]{1,0:T(8,128)(2,1)S(1)} %collective-permute-done.4.far_ref), channel_id=1, source_target_pairs={{0,4},{4,0},{1,5},{5,1},{2,6},{6,2},{3,7},{7,3},{8,12},{12,8},{9,1... | collective-permute-start | bytes 1179656 | tf_op jit(solution)/shard_map/ppermute | solution.py:292
  97.7 1.9 %copy-start.10 = (bf16[2048,768]{1,0:T(8,128)(2,1)S(1)}, bf16[2048,768]{1,0:T(8,128)(2,1)}, u32[]{:S(2)}) copy-start(bf16[2048,768]{1,0:T(8,128)(2,1)} %all-gather.2.cloned.1.call-done.table_ref) | copy-start | bytes 9437188
  99.6 4.1 %copy-start.11 = (bf16[2048,768]{1,0:T(8,128)(2,1)S(1)}, bf16[2048,768]{1,0:T(8,128)(2,1)}, u32[]{:S(2)}) copy-start(bf16[2048,768]{1,0:T(8,128)(2,1)} %all-gather.2.cloned.1.call-done.table_ref) | copy-start | bytes 9437188
  103.6 18.0 %copy-start.20 = (bf16[1,8,1,8]{3,1,2,0:T(8,128)(2,1)S(1)}, bf16[1,8,1,8]{3,1,2,0:T(8,128)(2,1)}, u32[]{:S(2)}) copy-start(bf16[1,8,1,8]{3,1,2,0:T(8,128)(2,1)} %param.30) | copy-start | bytes 388
  108.5 23.9 %all-to-all-start.3 = ((f32[32,8,128]{2,1,0:T(8,128)}), f32[32,8,128]{2,1,0:T(8,128)S(1)}, u32[]{:S(2)}, u32[]{:S(2)}) async-start(f32[32,8,128]{2,1,0:T(8,128)} %far_pool.1), calls=%async_computation.3 | async-start | bytes 262144 | tf_op jit(solution)/shard_map/all_to_all | solution.py:284
  (1 other events, 0.6 us)
Sparse Core Ops, SparseCore 0:
  36.3 49.2 all-gather.1

commit v5 on v4

--- a/solution.py
+++ b/solution.py
@@ -57,11 +57,13 @@
     segment_hbm,
     weight_hbm,
     table_hbm,
+    out_weight_hbm,
     out_ref,
     hidden_ref,
     segment_ref,
     weight_ref,
     table_ref,
+    half_ref,
     sems,
 ):
     length = hidden_ref.shape[0]
@@ -75,6 +77,9 @@
         pltpu.make_async_copy(weight_hbm.at[slot], weight_ref.at[slot], sems.at[3 + slot])
         for slot in range(3)
     ]
+    half = half_ref.shape[0]
+    own_rows = pl.ds(pl.multiple_of(ids_ref[CORE_AT] * half, half), half)
+    copies.append(pltpu.make_async_copy(out_weight_hbm.at[own_rows, :], half_ref, sems.at[6]))
     for copy in copies:
         copy.start()
     copies[1].wait()
@@ -103,7 +108,7 @@
 
     copies[0].wait()
     normed = layer_norm(hidden_ref[...].astype(jnp.float32), gain_ref[...]).astype(jnp.bfloat16)
-    for copy in copies[3:]:
+    for copy in copies[3:6]:
         copy.wait()
     queries = matmul(weight_ref[0], normed, NT)
     key_cols = matmul(weight_ref[1], normed, NT)
@@ -124,40 +129,42 @@
         context = matmul(values[at], probabilities, (((1,), (0,)), ((), ()))).astype(jnp.bfloat16)
         for copy in range(out_ref.shape[0]):
             out_ref[copy, at, :] = context
+    copies[6].wait()
+    for column in range(half_ref.shape[1] // length):
+        block = half_ref[:, column * length : (column + 1) * length]
+        at = slice(head_width + column * half, head_width + (column + 1) * half)
+        for copy in range(out_ref.shape[0]):
+            out_ref[copy, at, :] = block
 
 
 def ffn_kernel(
-    ids_ref,
-    hidden_ref,
-    context_ref,
-    gain_ref,
-    in_ref,
-    down_ref,
-    own_weight_ref,
-    mine_ref,
-    other_ref,
-    after_ref,
-    out_ref,
+    ids_ref, hidden_ref, merged_ref, other_ref, gain_ref, in_ref, down_ref, after_ref, out_ref, weight_ref, all_ref
 ):
-    own = ids_ref[TERM_AT]
-    after_attn = hidden_ref[...].astype(jnp.float32)
-    after_attn = after_attn + matmul(context_ref[own], own_weight_ref[...], TN)
-    half = own_weight_ref.shape[0] // 2
-    for d in range(1, context_ref.shape[0]):
-        shard = jnp.bitwise_xor(own, d)
-        at = slice((d - 1) * half, d * half)
-        for core, ref in ((ids_ref[CORE_AT], mine_ref), (1 - ids_ref[CORE_AT], other_ref)):
-            first = pl.multiple_of(core * half, half)
-            context = context_ref[shard, pl.ds(first, half), :]
-            after_attn = after_attn + matmul(context, ref[at, :], TN)
-    after_ref[...] = after_attn
+    length, width = hidden_ref.shape
+    shards = merged_ref.shape[0]
+    head_width = width // shards
+    half = head_width // 2
+    for shard in range(shards):
+        for column in range(width // length):
+            to = slice(column * length, (column + 1) * length)
+            at = slice(column * half, (column + 1) * half)
+            mine = merged_ref[shard, head_width + column * half : head_width + (column + 1) * half]
+            for core, block in (
+                (ids_ref[CORE_AT], mine),
+                (1 - ids_ref[CORE_AT], other_ref[shard, at, :]),
+            ):
+                first = pl.multiple_of(shard * head_width + core * half, half)
+                weight_ref[pl.ds(first, half), to] = block
+    context = jnp.concatenate([merged_ref[shard, :head_width] for shard in range(shards)], axis=0)
+    after_attn = hidden_ref[...].astype(jnp.float32) + matmul(context, weight_ref[...], TN)
+    all_ref[...] = after_attn
+    share = after_ref.shape[0]
+    after_ref[...] = all_ref[pl.ds(pl.multiple_of(ids_ref[TERM_AT] * share, share), share), :]
     mixed = layer_norm(after_attn, gain_ref[...]).astype(jnp.bfloat16)
     inner_up = matmul(in_ref[0], mixed, NT)
     gate_part = matmul(in_ref[1], mixed, NT)
     activated = (gelu(inner_up) * gate_part).astype(jnp.bfloat16)
-    partial = matmul(activated, down_ref[...], TN).astype(jnp.bfloat16)
-    for copy in range(out_ref.shape[0]):
-        out_ref[copy] = partial
+    out_ref[...] = matmul(activated, down_ref[...], TN).astype(jnp.bfloat16)
 
 
 def head_kernel(after_ref, partial_ref, final_ref, dense_ref, head_ref, out_ref):
@@ -166,7 +173,9 @@
         after_ffn = after_ffn + partial_ref[shard].astype(jnp.float32)
     normed = layer_norm(after_ffn, final_ref[...]).astype(jnp.bfloat16)
     dense = matmul(normed, dense_ref[...], (((1,), (0,)), ((), ())))
-    out_ref[...] = layer_norm(gelu(dense), head_ref[...]).astype(jnp.bfloat16)
+    headed = layer_norm(gelu(dense), head_ref[...]).astype(jnp.bfloat16)
+    for copy in range(out_ref.shape[0]):
+        out_ref[copy] = headed
 
 
 def prep_kernel(ids_ref, segment_ref, list_ref, docs_ref, bounds_ref, mask_ref):
@@ -341,53 +350,48 @@
 
     own_slice = decoder.reshape(own_terms, width)
     part = gather_by_exchange(own_slice, "zh").reshape(-1, width)
+    rotary = jnp.asarray(rotary_table(length))
     half = head_width // 2
-    own_half = lax.dynamic_slice_in_dim(attn_out, lax.axis_index("core") * half, half, 0)
-    pieces = others(own_half, "term")
-    rotary = jnp.asarray(rotary_table(length))
-    context = pl.pallas_call(
+    chunk = head_width + half * width // length
+    merged = pl.pallas_call(
         attention_kernel,
-        out_shape=jax.ShapeDtypeStruct((tensor, head_width, length), jnp.bfloat16),
-        in_specs=[smem(), vmem()] + [hbm()] * 4,
+        out_shape=jax.ShapeDtypeStruct((tensor, chunk, length), jnp.bfloat16),
+        in_specs=[smem(), vmem()] + [hbm()] * 5,
         out_specs=vmem(),
         scratch_shapes=[
             pltpu.VMEM((length, width), jnp.bfloat16),
             pltpu.VMEM((8, length), jnp.int32),
             pltpu.VMEM((3, head_width, width), jnp.bfloat16),
             pltpu.VMEM(rotary.shape, jnp.bfloat16),
-            pltpu.SemaphoreType.DMA((6,)),
+            pltpu.VMEM((half, width), jnp.bfloat16),
+            pltpu.SemaphoreType.DMA((7,)),
         ],
         compiler_params=grant(60),
         cost_estimate=cost(1200000000, 2000000),
         name="attention",
-    )(ids, attn_gain[None], tokens, segment_ids, jnp.swapaxes(qkv_weight, 1, 2), rotary)
-    part, pieces, context = lax.optimization_barrier((part, pieces, context))
-    mine = jnp.concatenate(pieces, axis=0)
-    other = swap(mine, "core")
+    )(
+        ids, attn_gain[None], tokens, segment_ids, jnp.swapaxes(qkv_weight, 1, 2), rotary, attn_out
+    )
+    part, merged = lax.optimization_barrier((part, merged))
     table = lax.all_gather(part, "y", axis=0, tiled=True)
-    all_context = exchange(context, "term")
+    merged = exchange(merged, "term")
+    other = swap(merged[:, head_width:], "core")
     after_attn, partial = pl.pallas_call(
         ffn_kernel,
         out_shape=(
-            jax.ShapeDtypeStruct((length, width), jnp.float32),
-            jax.ShapeDtypeStruct((tensor, length, width), jnp.bfloat16),
+            jax.ShapeDtypeStruct((length // tensor, width), jnp.float32),
+            jax.ShapeDtypeStruct((length, width), jnp.bfloat16),
         ),
-        in_specs=[smem()] + [vmem()] * 8,
+        in_specs=[smem()] + [vmem()] * 6,
         out_specs=(vmem(), vmem()),
+        scratch_shapes=[
+            pltpu.VMEM((width, width), jnp.bfloat16),
+            pltpu.VMEM((length, width), jnp.float32),
+        ],
         compiler_params=grant(20),
         cost_estimate=cost(700000000, 4000000),
         name="ffn",
-    )(
-        ids,
-        tokens,
-        all_context,
-        mlp_gain[None],
-        jnp.swapaxes(ffn_in, 1, 2),
-        ffn_out,
-        attn_out,
-        mine,
-        other,
-    )
+    )(ids, tokens, merged, other, mlp_gain[None], jnp.swapaxes(ffn_in, 1, 2), ffn_out)
     bounds, mask = pl.pallas_call(
         prep_kernel,
         out_shape=(
@@ -400,17 +404,19 @@
         cost_estimate=cost(1000000, 1000000),
         name="prep",
     )(ids, segment_ids, block_lists, doc_ids[:, None])
-    partials = exchange(partial, "term")
+    partials = exchange(partial.reshape(tensor, -1, width), "term")
     partials, bounds, mask = lax.optimization_barrier((partials, bounds, mask))
     headed = pl.pallas_call(
         head_kernel,
-        out_shape=jax.ShapeDtypeStruct((length, width), jnp.bfloat16),
+        out_shape=jax.ShapeDtypeStruct((tensor, length // tensor, width), jnp.bfloat16),
         in_specs=[vmem()] * 5,
         out_specs=vmem(),
         compiler_params=grant(20),
         cost_estimate=cost(800000000, 5000000),
         name="head",
     )(after_attn, partials, final_gain[None], head_dense, head_gain[None])
+
+    headed = exchange(headed, "term").reshape(length, width)
 
     far = swap(headed, "zl")
     core = swap(headed, "core")

time: 141 us -> 136 us (0.965)
  blocking collectives: 0 us -> 22.7 us
  waiting for transfers between devices: 39.3 us -> 24.8 us
  starting transfers between devices: 56.4 us -> 45.9 us
  local copies, waits for them, and re-layouts: 10.2 us -> 8.15 us
    all_to_all x0 -> x2, blocking collectives: none -> 22.7 us  [exchange(): return lax.all_to_all(copies, axis, split_axis=0, concat_axis=0, tiled=True)]
    all_to_all x4 -> x3, waiting for transfers between devices: 36.1 us -> 20.2 us  [exchange(): return lax.all_to_all(copies, axis, split_axis=0, concat_axis=0, tiled=True)]
    all_to_all x4 -> x3, starting transfers between devices: 30.8 us -> 22.5 us  [exchange(): return lax.all_to_all(copies, axis, split_axis=0, concat_axis=0, tiled=True)]
    ppermute x7 -> x4, starting transfers between devices: 25.6 us -> 23.5 us  [swap(): lax.ppermute(block, axis, [(i, i ^ d) for i in range(lax.axis_size(axis))])]
    unnamed x44 -> x36, local copies, waits for them, and re-layouts: 5.41 us -> 3.54 us
    ppermute x7 -> x4, waiting for transfers between devices: 3.11 us -> 4.53 us  [swap(): lax.ppermute(block, axis, [(i, i ^ d) for i in range(lax.axis_size(axis))])]
  transfers between devices with their start and end apart: 12 -> 8, of which waited for: 4 -> 5; matrix products, arithmetic and copies ran while one was open for 2% -> 2% of each run, Pallas kernels for 10% -> 10%
where the time goes in v5:
time: 136 us; the launch traced here: 135 us
  starting transfers between devices  45.9 us (34%)
  waiting for transfers between devices  24.8 us (18%)
  blocking collectives  22.7 us (17%)
  Pallas kernels  19.4 us (14%)
  between operations  13.7 us (10%)
  local copies, waits for them, and re-layouts  8.15 us (6%)
    ppermute x4, starting transfers between devices, swap(): lax.ppermute(block, axis, [(i, i ^ d) for i in range(lax.axis_size(axis))])  23.5 us
    all_to_all x2, blocking collectives, exchange(): return lax.all_to_all(copies, axis, split_axis=0, concat_axis=0, tiled=True)  22.7 us
    all_to_all x3, starting transfers between devices, exchange(): return lax.all_to_all(copies, axis, split_axis=0, concat_axis=0, tiled=True)  22.5 us
    all_to_all x3, waiting for transfers between devices, exchange(): return lax.all_to_all(copies, axis, split_axis=0, concat_axis=0, tiled=True)  20.2 us
    pallas_call x1, Pallas kernels, on_device(): pl.pallas_call(far_pool_kernel, out_shape=jax.ShapeDtypeStruct((slices, 2...  4.81 us
    pallas_call x1, Pallas kernels, on_device(): pl.pallas_call(attention_kernel, out_shape=jax.ShapeDtypeStruct((tensor,...  4.68 us
    ppermute x4, waiting for transfers between devices, swap(): lax.ppermute(block, axis, [(i, i ^ d) for i in range(lax.axis_size(axis))])  4.53 us
    pallas_call x1, Pallas kernels, on_device(): pl.pallas_call(near_pool_kernel, out_shape=jax.ShapeDtypeStruct((2 * PASS...  4.08 us
  transfers between devices with their start and end apart: 8, of which 5 were waited for; matrix products, arithmetic and copies ran while one was open for 2% of the time, Pallas kernels for 10%

profile of v5, /device:TPU:1, one launch (start us, length us, event | category | flops | bytes accessed | tf_op | source)
XLA Modules:
  0.0 134.9 jit_solution(6833159593817992255)
XLA Ops:
  6.5 1.7 %broadcast_in_dim.23 = bf16[4,64,768]{2,1,0:T(8,128)(2,1)} broadcast(bf16[64,768]{1,0:T(8,128)(2,1)} %bitcast.34), dimensions={1,2} | broadcast | bytes 491520 | tf_op jit(solution)/shard_map/broadcast_in_dim | solution.py:297
  8.2 10.8 %all-to-all-start = ((bf16[4,64,768]{2,1,0:T(8,128)(2,1)}), bf16[4,64,768]{2,1,0:T(8,128)(2,1)S(1)}, u32[]{:S(2)}, u32[]{:S(2)}) async-start(bf16[4,64,768]{2,1,0:T(8,128)(2,1)} %broadcast_in_dim.23), calls=%async_computation | async-start | bytes 786432 | tf_op jit(solution)/shard_map/all_to_all | solution.py:293
  19.0 1.3 broadcast_in_dim.24.gain_ref
  20.4 0.7 concatenate.8.ids_ref
  21.1 4.7 %attention.1 = bf16[4,480,256]{2,1,0:T(8,128)(2,1)} custom-call(s32[8]{0:T(128)} %concatenate.8.ids_ref, f32[1,768]{1,0:T(1,128)} %broadcast_in_dim.24.gain_ref, bf16[256,768]{1,0:T(8,128)(2,1)} %bitcast.30, s32[128,256]{1,0:T(8,128)} %segment_ref.1, bf16[3,192,768]{2,1,0:T(8,128)(2,1)} %bitcast.37, bf16[192,256]{1,0:T(8,128)(2,1)} %constant.53.clone.table_hbm, ...), custom_call_target="tpu_custom_call" | custom-call | flops 1200000000 | bytes 2000000 | tf_op jit(solution)/shard_map/attention/pallas_call | solution.py:356
  25.8 3.2 %all-to-all-done = bf16[4,64,768]{2,1,0:T(8,128)(2,1)S(1)} async-done(((bf16[4,64,768]{2,1,0:T(8,128)(2,1)}), bf16[4,64,768]{2,1,0:T(8,128)(2,1)S(1)}, u32[]{:S(2)}, u32[]{:S(2)}) %all-to-all-start) | async-done | bytes 393248 | tf_op jit(solution)/shard_map/all_to_all | solution.py:293
  28.9 0.8 copy-done.12
  29.7 13.4 %all_to_all.25.merged_ref = bf16[4,480,256]{2,1,0:T(8,128)(2,1)S(1)} all-to-all(bf16[4,480,256]{2,1,0:T(8,128)(2,1)} %attention.1), channel_id=1, replica_groups=mesh['y'=8,'zh'=4,'zl'=2,'core'=2,'term'=4] {'term'}, dimensions={0} | all-to-all | bytes 1966080 | tf_op jit(solution)/shard_map/all_to_all | solution.py:293
  43.2 8.0 %collective-permute-start = (bf16[4,288,256]{2,1,0:T(8,128)(2,1)S(1)}, bf16[4,288,256]{2,1,0:T(8,128)(2,1)S(1)}, u32[]{:S(2)}, u32[]{:S(2)}) collective-permute-start(bf16[4,288,256]{2,1,0:T(8,128)(2,1)S(1)} %slice.4), channel_id=1, source_target_pairs={{0,4},{4,0},{1,5},{5,1},{2,6},{6,2},{3,7},{7,3},{8,12},{12,8},{9,1... | collective-permute-start | bytes 1769480 | tf_op jit(solution)/shard_map/ppermute | solution.py:301
  51.3 1.6 %collective-permute-done.other_ref = bf16[4,288,256]{2,1,0:T(8,128)(2,1)S(1)} collective-permute-done((bf16[4,288,256]{2,1,0:T(8,128)(2,1)S(1)}, bf16[4,288,256]{2,1,0:T(8,128)(2,1)S(1)}, u32[]{:S(2)}, u32[]{:S(2)}) %collective-permute-start) | collective-permute-done | bytes 589856 | tf_op jit(solution)/shard_map/ppermute | solution.py:301
  52.9 2.9 %ffn.1 = (f32[64,768]{1,0:T(8,128)S(1)}, bf16[256,768]{1,0:T(8,128)(2,1)}) custom-call(s32[8]{0:T(128)S(1)} %copy-done.5, bf16[256,768]{1,0:T(8,128)(2,1)S(1)} %bitcast.31, bf16[4,480,256]{2,1,0:T(8,128)(2,1)S(1)} %all_to_all.25.merged_ref, bf16[4,288,256]{2,1,0:T(8,128)(2,1)S(1)} %collective-permute-done.other_ref, f32[1,768]{1,0:T(1,128)S(1)} %broadcast_in_dim.25.gain_ref, ...), custom_call_target="tpu_custom_call" | custom-call | flops 700000000 | bytes 4000000 | tf_op jit(solution)/shard_map/ffn/pallas_call | solution.py:379
  55.8 3.5 %all-to-all-start.2 = ((bf16[4,64,768]{2,1,0:T(8,128)(2,1)}), bf16[4,64,768]{2,1,0:T(8,128)(2,1)S(1)}, u32[]{:S(2)}, u32[]{:S(2)}) async-start(bf16[4,64,768]{2,1,0:T(8,128)(2,1)} %bitcast.12), calls=%async_computation.2 | async-start | bytes 786432 | tf_op jit(solution)/shard_map/all_to_all | solution.py:293
  59.3 0.1 copy.23.docs_ref
  59.5 1.0 prep.1
  60.5 6.6 %all-to-all-done.2.partial_ref = bf16[4,64,768]{2,1,0:T(8,128)(2,1)S(1)} async-done(((bf16[4,64,768]{2,1,0:T(8,128)(2,1)}), bf16[4,64,768]{2,1,0:T(8,128)(2,1)S(1)}, u32[]{:S(2)}, u32[]{:S(2)}) %all-to-all-start.2) | async-done | bytes 393248 | tf_op jit(solution)/shard_map/all_to_all | solution.py:293
  67.1 0.7 head.1
  67.8 9.3 %all_to_all.26 = bf16[4,64,768]{2,1,0:T(8,128)(2,1)S(1)} all-to-all(bf16[4,64,768]{2,1,0:T(8,128)(2,1)S(1)} %head.1), channel_id=1, replica_groups=mesh['y'=8,'zh'=4,'zl'=2,'core'=2,'term'=4] {'term'}, dimensions={0} | all-to-all | bytes 786432 | tf_op jit(solution)/shard_map/all_to_all | solution.py:293
  77.1 6.5 %collective-permute-start.1 = (bf16[256,768]{1,0:T(8,128)(2,1)S(1)}, bf16[256,768]{1,0:T(8,128)(2,1)S(1)}, u32[]{:S(2)}, u32[]{:S(2)}) collective-permute-start(bf16[256,768]{1,0:T(8,128)(2,1)S(1)} %bitcast.27), channel_id=1, source_target_pairs={{0,8},{8,0},{1,9},{9,1},{2,10},{10,2},{3,11},{11,3},{4,12},{12,4},... | collective-permute-start | bytes 1179656 | tf_op jit(solution)/shard_map/ppermute | solution.py:301
  83.6 4.3 %collective-permute-start.3 = (bf16[256,768]{1,0:T(8,128)(2,1)S(1)}, bf16[256,768]{1,0:T(8,128)(2,1)S(1)}, u32[]{:S(2)}, u32[]{:S(2)}) collective-permute-start(bf16[256,768]{1,0:T(8,128)(2,1)S(1)} %bitcast.28), channel_id=1, source_target_pairs={{0,4},{4,0},{1,5},{5,1},{2,6},{6,2},{3,7},{7,3},{8,12},{12,8},{9,1... | collective-permute-start | bytes 1179656 | tf_op jit(solution)/shard_map/ppermute | solution.py:301
  87.9 2.9 %collective-permute-done.1.far_ref = bf16[256,768]{1,0:T(8,128)(2,1)S(1)} collective-permute-done((bf16[256,768]{1,0:T(8,128)(2,1)S(1)}, bf16[256,768]{1,0:T(8,128)(2,1)S(1)}, u32[]{:S(2)}, u32[]{:S(2)}) %collective-permute-start.1) | collective-permute-done | bytes 393248 | tf_op jit(solution)/shard_map/ppermute | solution.py:301
  90.8 4.7 %collective-permute-start.2 = (bf16[256,768]{1,0:T(8,128)(2,1)S(1)}, bf16[256,768]{1,0:T(8,128)(2,1)S(1)}, u32[]{:S(2)}, u32[]{:S(2)}) collective-permute-start(bf16[256,768]{1,0:T(8,128)(2,1)S(1)} %collective-permute-done.1.far_ref), channel_id=1, source_target_pairs={{0,4},{4,0},{1,5},{5,1},{2,6},{6,2},{3,7},{7,3},{8,12},{12,8},{9,1... | collective-permute-start | bytes 1179656 | tf_op jit(solution)/shard_map/ppermute | solution.py:301
  95.5 0.1 reshape.44
  95.7 1.9 %copy-done.6 = bf16[2048,768]{1,0:T(8,128)(2,1)S(1)} copy-done((bf16[2048,768]{1,0:T(8,128)(2,1)S(1)}, bf16[2048,768]{1,0:T(8,128)(2,1)}, u32[]{:S(2)}) %copy-start.6) | copy-done | bytes 3145752
  97.6 0.8 copy-done.10
  98.5 4.1 %near_pool.1.low_ref = f32[8,2048]{1,0:T(8,128)S(1)} custom-call(s32[8]{0:T(128)S(1)} %copy-done.5, s32[128,8]{1,0:T(8,128)S(1)} %copy-done.10, bf16[256,768]{1,0:T(8,128)(2,1)S(1)} %bitcast.29, bf16[256,768]{1,0:T(8,128)(2,1)S(1)} %collective-permute-done.3.core_ref, bf16[2048,768]{1,0:T(8,128)(2,1)S(1)} %copy-done.6), custom_call_target="tpu_custom_call" | custom-call | flops 1600000000 | bytes 4000000 | tf_op jit(solution)/shard_map/near_pool/pallas_call | solution.py:426
  102.6 4.8 %far_pool.1 = f32[32,8,128]{2,1,0:T(8,128)} custom-call(s32[8]{0:T(128)S(1)} %copy-done.5, s32[128,8]{1,0:T(8,128)S(1)} %copy-done.11, bf16[256,768]{1,0:T(8,128)(2,1)S(1)} %collective-permute-done.1.far_ref, bf16[256,768]{1,0:T(8,128)(2,1)S(1)} %collective-permute-done.2.far_core_ref, bf16[2048,768]{1,0:T(8,128)(2,1)S(1)} %copy-done.7, ...), custom_call_target="tpu_custom_call" | custom-call | flops 1600000000 | bytes 4000000 | tf_op jit(solution)/shard_map/far_pool/pallas_call | solution.py:436
  107.4 8.2 %all-to-all-start.4 = ((f32[32,8,128]{2,1,0:T(8,128)}), f32[32,8,128]{2,1,0:T(8,128)S(1)}, u32[]{:S(2)}, u32[]{:S(2)}) async-start(f32[32,8,128]{2,1,0:T(8,128)} %far_pool.1), calls=%async_computation.4 | async-start | bytes 262144 | tf_op jit(solution)/shard_map/all_to_all | solution.py:293
  115.9 0.1 copy.28
  116.0 0.1 reshape.48.docs_ref
  116.2 0.1 convert_element_type.12
  116.4 10.5 %all-to-all-done.4 = f32[32,8,128]{2,1,0:T(8,128)S(1)} async-done(((f32[32,8,128]{2,1,0:T(8,128)}), f32[32,8,128]{2,1,0:T(8,128)S(1)}, u32[]{:S(2)}, u32[]{:S(2)}) %all-to-all-start.4) | async-done | bytes 131104 | tf_op jit(solution)/shard_map/all_to_all | solution.py:293
  126.9 1.2 place.1
  (50 shorter events, 0.7 us)
Async XLA Ops:
  8.2 20.7 %all-to-all-start = ((bf16[4,64,768]{2,1,0:T(8,128)(2,1)}), bf16[4,64,768]{2,1,0:T(8,128)(2,1)S(1)}, u32[]{:S(2)}, u32[]{:S(2)}) async-start(bf16[4,64,768]{2,1,0:T(8,128)(2,1)} %broadcast_in_dim.23), calls=%async_computation | async-start | bytes 786432 | tf_op jit(solution)/shard_map/all_to_all | solution.py:293
  19.0 76.7 %all-gather.2.cloned.1.call-start = ((), (), s32[]{:S(2)}) async-start(), calls=%async_computation.5 | async-start | bytes 3538944 | tf_op jit(solution)/shard_map/all_gather | solution.py:376
  21.1 30.2 %copy-start.14 = (f32[768]{0:T(1024)S(1)}, f32[768]{0:T(1024)}, u32[]{:S(2)}) copy-start(f32[768]{0:T(1024)} %param.23) | copy-start | bytes 9220
  21.1 31.8 %copy-start = (bf16[2,768,288]{1,2,0:T(8,128)(2,1)S(1)}, bf16[2,768,288]{1,2,0:T(8,128)(2,1)}, u32[]{:S(2)}) copy-start(bf16[2,768,288]{1,2,0:T(8,128)(2,1)} %param.24) | copy-start | bytes 2654212
  21.1 31.8 %copy-start.1 = (bf16[288,768]{1,0:T(8,128)(2,1)S(1)}, bf16[288,768]{1,0:T(8,128)(2,1)}, u32[]{:S(2)}) copy-start(bf16[288,768]{1,0:T(8,128)(2,1)} %down_ref.1) | copy-start | bytes 1327108
  21.1 31.8 %copy-start.2 = (bf16[1,256,768]{2,1,0:T(8,128)(2,1)S(1)}, bf16[1,256,768]{2,1,0:T(8,128)(2,1)}, u32[]{:S(2)}) copy-start(bf16[1,256,768]{2,1,0:T(8,128)(2,1)} %param.16) | copy-start | bytes 1179652
  21.1 31.8 %copy-start.5 = (s32[8]{0:T(128)S(1)}, s32[8]{0:T(128)}, u32[]{:S(2)}) copy-start(s32[8]{0:T(128)} %concatenate.8.ids_ref) | copy-start | bytes 100
  28.9 0.8 copy-start.12
  29.7 29.6 %copy-start.13 = (s32[512]{0:T(512)S(1)}, s32[512]{0:T(512)}, u32[]{:S(2)}) copy-start(s32[512]{0:T(512)} %param.19) | copy-start | bytes 6148
  43.2 16.3 %copy-start.15 = (f32[768]{0:T(1024)S(1)}, f32[768]{0:T(1024)}, u32[]{:S(2)}) copy-start(f32[768]{0:T(1024)} %param.26) | copy-start | bytes 9220
  43.2 16.3 %copy-start.16 = (f32[768]{0:T(1024)S(1)}, f32[768]{0:T(1024)}, u32[]{:S(2)}) copy-start(f32[768]{0:T(1024)} %param.28) | copy-start | bytes 9220
  43.2 16.3 %copy-start.3 = (s32[512,128]{1,0:T(8,128)S(1)}, s32[512,128]{1,0:T(8,128)}, u32[]{:S(2)}) copy-start(s32[512,128]{1,0:T(8,128)} %list_ref.1) | copy-start | bytes 786436
  43.2 16.3 %copy-start.4 = (s32[128,256]{1,0:T(8,128)S(1)}, s32[128,256]{1,0:T(8,128)}, u32[]{:S(2)}) copy-start(s32[128,256]{1,0:T(8,128)} %segment_ref.1) | copy-start | bytes 393220
  43.2 23.9 %copy-start.8 = (bf16[768,768]{1,0:T(8,128)(2,1)S(1)}, bf16[768,768]{1,0:T(8,128)(2,1)}, u32[]{:S(2)}) copy-start(bf16[768,768]{1,0:T(8,128)(2,1)} %dense_ref.1) | copy-start | bytes 3538948
  43.2 9.6 %collective-permute-start = (bf16[4,288,256]{2,1,0:T(8,128)(2,1)S(1)}, bf16[4,288,256]{2,1,0:T(8,128)(2,1)S(1)}, u32[]{:S(2)}, u32[]{:S(2)}) collective-permute-start(bf16[4,288,256]{2,1,0:T(8,128)(2,1)S(1)} %slice.4), channel_id=1, source_target_pairs={{0,4},{4,0},{1,5},{5,1},{2,6},{6,2},{3,7},{7,3},{8,12},{12,8},{9,1... | collective-permute-start | bytes 1769480 | tf_op jit(solution)/shard_map/ppermute | solution.py:301
  55.8 11.3 %all-to-all-start.2 = ((bf16[4,64,768]{2,1,0:T(8,128)(2,1)}), bf16[4,64,768]{2,1,0:T(8,128)(2,1)S(1)}, u32[]{:S(2)}, u32[]{:S(2)}) async-start(bf16[4,64,768]{2,1,0:T(8,128)(2,1)} %bitcast.12), calls=%async_computation.2 | async-start | bytes 786432 | tf_op jit(solution)/shard_map/all_to_all | solution.py:293
  60.5 16.6 %copy-start.9 = (s32[128,8]{1,0:T(8,128)}, s32[128,8]{1,0:T(8,128)S(1)}, u32[]{:S(2)}) copy-start(s32[128,8]{1,0:T(8,128)S(1)} %get-tuple-element.18.bounds_ref) | copy-start | bytes 12292
  77.1 25.5 %copy-start.11 = (s32[128,8]{1,0:T(8,128)S(1)}, s32[128,8]{1,0:T(8,128)}, u32[]{:S(2)}) copy-start(s32[128,8]{1,0:T(8,128)} %copy-done.9) | copy-start | bytes 12292
  77.1 13.8 %collective-permute-start.1 = (bf16[256,768]{1,0:T(8,128)(2,1)S(1)}, bf16[256,768]{1,0:T(8,128)(2,1)S(1)}, u32[]{:S(2)}, u32[]{:S(2)}) collective-permute-start(bf16[256,768]{1,0:T(8,128)(2,1)S(1)} %bitcast.27), channel_id=1, source_target_pairs={{0,8},{8,0},{1,9},{9,1},{2,10},{10,2},{3,11},{11,3},{4,12},{12,4},... | collective-permute-start | bytes 1179656 | tf_op jit(solution)/shard_map/ppermute | solution.py:301
  83.6 12.1 %collective-permute-start.3 = (bf16[256,768]{1,0:T(8,128)(2,1)S(1)}, bf16[256,768]{1,0:T(8,128)(2,1)S(1)}, u32[]{:S(2)}, u32[]{:S(2)}) collective-permute-start(bf16[256,768]{1,0:T(8,128)(2,1)S(1)} %bitcast.28), channel_id=1, source_target_pairs={{0,4},{4,0},{1,5},{5,1},{2,6},{6,2},{3,7},{7,3},{8,12},{12,8},{9,1... | collective-permute-start | bytes 1179656 | tf_op jit(solution)/shard_map/ppermute | solution.py:301
  90.8 11.7 %collective-permute-start.2 = (bf16[256,768]{1,0:T(8,128)(2,1)S(1)}, bf16[256,768]{1,0:T(8,128)(2,1)S(1)}, u32[]{:S(2)}, u32[]{:S(2)}) collective-permute-start(bf16[256,768]{1,0:T(8,128)(2,1)S(1)} %collective-permute-done.1.far_ref), channel_id=1, source_target_pairs={{0,4},{4,0},{1,5},{5,1},{2,6},{6,2},{3,7},{7,3},{8,12},{12,8},{9,1... | collective-permute-start | bytes 1179656 | tf_op jit(solution)/shard_map/ppermute | solution.py:301
  95.7 1.9 %copy-start.6 = (bf16[2048,768]{1,0:T(8,128)(2,1)S(1)}, bf16[2048,768]{1,0:T(8,128)(2,1)}, u32[]{:S(2)}) copy-start(bf16[2048,768]{1,0:T(8,128)(2,1)} %all-gather.2.cloned.1.call-done.table_ref) | copy-start | bytes 9437188
  97.6 0.8 copy-start.10
  98.5 4.1 %copy-start.7 = (bf16[2048,768]{1,0:T(8,128)(2,1)S(1)}, bf16[2048,768]{1,0:T(8,128)(2,1)}, u32[]{:S(2)}) copy-start(bf16[2048,768]{1,0:T(8,128)(2,1)} %all-gather.2.cloned.1.call-done.table_ref) | copy-start | bytes 9437188
  102.5 13.6 %copy-start.17 = (bf16[1,8,1,8]{3,1,2,0:T(8,128)(2,1)S(1)}, bf16[1,8,1,8]{3,1,2,0:T(8,128)(2,1)}, u32[]{:S(2)}) copy-start(bf16[1,8,1,8]{3,1,2,0:T(8,128)(2,1)} %param.30) | copy-start | bytes 388
  107.4 19.5 %all-to-all-start.4 = ((f32[32,8,128]{2,1,0:T(8,128)}), f32[32,8,128]{2,1,0:T(8,128)S(1)}, u32[]{:S(2)}, u32[]{:S(2)}) async-start(f32[32,8,128]{2,1,0:T(8,128)} %far_pool.1), calls=%async_computation.4 | async-start | bytes 262144 | tf_op jit(solution)/shard_map/all_to_all | solution.py:293
Sparse Core Ops, SparseCore 0:
  29.8 48.0 all-gather.1

commit v6 on v5

--- a/solution.py
+++ b/solution.py
@@ -15,8 +15,9 @@
 HEAD_DIM = 64
 HALF_HEAD = 32
 SPAN = 8
+NEAR = 4
 LOWEST = -3.0e38
-TERM_AT, BLOCK_AT, STRIDE_AT, CORE_AT = 4, 5, 6, 7
+TERM_AT, BLOCK_AT, STRIDE_AT, CORE_AT, NEAR_AT = 4, 5, 6, 7, 8
 
 NT = (((1,), (1,)), ((), ()))
 TN = (((0,), (0,)), ((), ()))
@@ -51,14 +52,14 @@
 
 
 def attention_kernel(
-    ids_ref,
-    gain_ref,
+    gain_hbm,
     hidden_hbm,
     segment_hbm,
     weight_hbm,
     table_hbm,
     out_weight_hbm,
     out_ref,
+    gain_ref,
     hidden_ref,
     segment_ref,
     weight_ref,
@@ -67,7 +68,9 @@
     sems,
 ):
     length = hidden_ref.shape[0]
-    row = ids_ref[0]
+    row = lax.axis_index("y")
+    for axis in ("zh", "zl", "core"):
+        row = row * lax.axis_size(axis) + lax.axis_index(axis)
     tile = pl.multiple_of(lax.shift_left(lax.shift_right_logical(row, 3), 3), 8)
     copies = [
         pltpu.make_async_copy(hidden_hbm, hidden_ref, sems.at[0]),
@@ -78,8 +81,9 @@
         for slot in range(3)
     ]
     half = half_ref.shape[0]
-    own_rows = pl.ds(pl.multiple_of(ids_ref[CORE_AT] * half, half), half)
+    own_rows = pl.ds(pl.multiple_of(lax.axis_index("core") * half, half), half)
     copies.append(pltpu.make_async_copy(out_weight_hbm.at[own_rows, :], half_ref, sems.at[6]))
+    copies.append(pltpu.make_async_copy(gain_hbm, gain_ref, sems.at[7]))
     for copy in copies:
         copy.start()
     copies[1].wait()
@@ -107,7 +111,9 @@
     allowed = (sublane >= low) & (sublane <= high)
 
     copies[0].wait()
-    normed = layer_norm(hidden_ref[...].astype(jnp.float32), gain_ref[...]).astype(jnp.bfloat16)
+    copies[7].wait()
+    gain = gain_ref[...].reshape(1, -1)
+    normed = layer_norm(hidden_ref[...].astype(jnp.float32), gain).astype(jnp.bfloat16)
     for copy in copies[3:6]:
         copy.wait()
     queries = matmul(weight_ref[0], normed, NT)
@@ -247,7 +253,8 @@
     own_terms = out_ref.shape[2] // 2
     for slot in range(out_ref.shape[0]):
         at = slice(slot * own_terms, (slot + 1) * own_terms)
-        out_ref[slot] = jnp.concatenate([low[:, at], high[:, at]], axis=1)
+        to = slot - slot % NEAR + jnp.bitwise_xor(ids_ref[NEAR_AT], slot % NEAR)
+        out_ref[to] = jnp.concatenate([low[:, at], high[:, at]], axis=1)
 
 
 def place_kernel(maxima_ref, bias_ref, mask_ref, docs_ref, out_ref):
@@ -291,10 +298,6 @@
 
 def exchange(copies, axis):
     return lax.all_to_all(copies, axis, split_axis=0, concat_axis=0, tiled=True)
-
-
-def gather_by_exchange(block, axis):
-    return exchange(jnp.broadcast_to(block[None], (lax.axis_size(axis),) + block.shape), axis)
 
 
 def swap(block, axis, d=1):
@@ -345,34 +348,35 @@
         first_block,
         jnp.int32(dp_count * span // BLOCK),
         lax.axis_index("core"),
+        lax.axis_index("zh"),
     ]
     ids = jnp.concatenate([row_ids, jnp.stack(scalars)])
 
     own_slice = decoder.reshape(own_terms, width)
-    part = gather_by_exchange(own_slice, "zh").reshape(-1, width)
+    pieces = others(own_slice, "zh")
     rotary = jnp.asarray(rotary_table(length))
     half = head_width // 2
     chunk = head_width + half * width // length
     merged = pl.pallas_call(
         attention_kernel,
         out_shape=jax.ShapeDtypeStruct((tensor, chunk, length), jnp.bfloat16),
-        in_specs=[smem(), vmem()] + [hbm()] * 5,
+        in_specs=[hbm()] * 6,
         out_specs=vmem(),
         scratch_shapes=[
+            pltpu.VMEM((width,), jnp.float32),
             pltpu.VMEM((length, width), jnp.bfloat16),
             pltpu.VMEM((8, length), jnp.int32),
             pltpu.VMEM((3, head_width, width), jnp.bfloat16),
             pltpu.VMEM(rotary.shape, jnp.bfloat16),
             pltpu.VMEM((half, width), jnp.bfloat16),
-            pltpu.SemaphoreType.DMA((7,)),
+            pltpu.SemaphoreType.DMA((8,)),
         ],
         compiler_params=grant(60),
         cost_estimate=cost(1200000000, 2000000),
         name="attention",
-    )(
-        ids, attn_gain[None], tokens, segment_ids, jnp.swapaxes(qkv_weight, 1, 2), rotary, attn_out
-    )
-    part, merged = lax.optimization_barrier((part, merged))
+    )(attn_gain, tokens, segment_ids, jnp.swapaxes(qkv_weight, 1, 2), rotary, attn_out)
+    pieces, merged = lax.optimization_barrier((pieces, merged))
+    part = jnp.concatenate([own_slice] + pieces, axis=0)
     table = lax.all_gather(part, "y", axis=0, tiled=True)
     merged = exchange(merged, "term")
     other = swap(merged[:, head_width:], "core")
@@ -420,7 +424,6 @@
 
     far = swap(headed, "zl")
     core = swap(headed, "core")
-    far_core = swap(far, "core")
     terms_here = slices * own_terms
     logits = pltpu.VMEM((2 * length, terms_here), jnp.float32)
     low = pl.pallas_call(
@@ -433,6 +436,8 @@
         cost_estimate=cost(1600000000, 4000000),
         name="near_pool",
     )(ids, bounds, headed, core, table)
+    far, low = lax.optimization_barrier((far, low))
+    far_core = swap(far, "core")
     pooled = pl.pallas_call(
         far_pool_kernel,
         out_shape=jax.ShapeDtypeStruct((slices, 2 * PASS_DEV, 2 * own_terms), jnp.float32),

time: 136 us -> 146 us (1.074)
  local copies, waits for them, and re-layouts: 8.15 us -> 15.9 us
  blocking collectives: 22.7 us -> 27.2 us
  waiting for transfers between devices: 24.8 us -> 22.7 us
    all_to_all x3 -> x2, starting transfers between devices: 22.5 us -> 14.5 us  [exchange(): return lax.all_to_all(copies, axis, split_axis=0, concat_axis=0, tiled=True)]
    ppermute x4 -> x7, starting transfers between devices: 23.5 us -> 31 us  [swap(): lax.ppermute(block, axis, [(i, i ^ d) for i in range(lax.axis_size(axis))])]
    all_to_all x3 -> x2, waiting for transfers between devices: 20.2 us -> 14 us  [exchange(): return lax.all_to_all(copies, axis, split_axis=0, concat_axis=0, tiled=True)]
    unnamed x36 -> x34, local copies, waits for them, and re-layouts: 3.54 us -> 9.46 us
    all_to_all x2, blocking collectives: 22.7 us -> 27.2 us  [exchange(): return lax.all_to_all(copies, axis, split_axis=0, concat_axis=0, tiled=True)]
    ppermute x4 -> x7, waiting for transfers between devices: 4.53 us -> 8.66 us  [swap(): lax.ppermute(block, axis, [(i, i ^ d) for i in range(lax.axis_size(axis))])]
    broadcast_in_dim x2 -> x0, local copies, waits for them, and re-layouts: 2.93 us -> none  [the longest x1 1.66 us: gather_by_exchange(): jnp.broadcast_to(block[None], (lax.axis_size(axis),) + block.shape)]
  transfers between devices with their start and end apart: 8 -> 10, of which waited for: 5 -> 5; matrix products, arithmetic and copies ran while one was open for 2% -> 5% of each run, Pallas kernels for 10% -> 9%
where the time goes in v6:
time: 146 us; the launch traced here: 145 us
  starting transfers between devices  45.5 us (31%)
  blocking collectives  27.2 us (19%)
  waiting for transfers between devices  22.7 us (16%)
  Pallas kernels  18.5 us (13%)
  local copies, waits for them, and re-layouts  15.9 us (11%)
  between operations  13.7 us (9%)
  other arithmetic  1.52 us (1%)
    ppermute x7, starting transfers between devices, swap(): lax.ppermute(block, axis, [(i, i ^ d) for i in range(lax.axis_size(axis))])  31 us
    all_to_all x2, blocking collectives, exchange(): return lax.all_to_all(copies, axis, split_axis=0, concat_axis=0, tiled=True)  27.2 us
    all_to_all x2, starting transfers between devices, exchange(): return lax.all_to_all(copies, axis, split_axis=0, concat_axis=0, tiled=True)  14.5 us
    all_to_all x2, waiting for transfers between devices, exchange(): return lax.all_to_all(copies, axis, split_axis=0, concat_axis=0, tiled=True)  14 us
    unnamed x34, local copies, waits for them, and re-layouts  9.46 us
    ppermute x7, waiting for transfers between devices, swap(): lax.ppermute(block, axis, [(i, i ^ d) for i in range(lax.axis_size(axis))])  8.66 us
    pallas_call x1, Pallas kernels, on_device(): pl.pallas_call(far_pool_kernel, out_shape=jax.ShapeDtypeStruct((slices, 2...  4.82 us
    pallas_call x1, Pallas kernels, on_device(): pl.pallas_call(near_pool_kernel, out_shape=jax.ShapeDtypeStruct((2 * PASS...  4.08 us
  transfers between devices with their start and end apart: 10, of which 5 were waited for; matrix products, arithmetic and copies ran while one was open for 5% of the time, Pallas kernels for 9%

profile of v6, /device:TPU:1, one launch (start us, length us, event | category | flops | bytes accessed | tf_op | source)
XLA Modules:
  0.0 145.1 jit_solution(869302528151089147)
XLA Ops:
  6.5 6.8 %collective-permute-start = (bf16[64,768]{1,0:T(8,128)(2,1)}, bf16[64,768]{1,0:T(8,128)(2,1)S(1)}, u32[]{:S(2)}, u32[]{:S(2)}) collective-permute-start(bf16[64,768]{1,0:T(8,128)(2,1)} %bitcast.33), channel_id=1, source_target_pairs={{0,16},{16,0},{32,48},{48,32},{1,17},{17,1},{33,49},{49,33},{2,18}... | collective-permute-start | bytes 294920 | tf_op jit(solution)/shard_map/ppermute | solution.py:304
  13.3 8.8 %collective-permute-start.1 = (bf16[64,768]{1,0:T(8,128)(2,1)}, bf16[64,768]{1,0:T(8,128)(2,1)S(1)}, u32[]{:S(2)}, u32[]{:S(2)}) collective-permute-start(bf16[64,768]{1,0:T(8,128)(2,1)} %bitcast.34), channel_id=1, source_target_pairs={{0,32},{16,48},{32,0},{48,16},{1,33},{17,49},{33,1},{49,17},{2,34}... | collective-permute-start | bytes 294920 | tf_op jit(solution)/shard_map/ppermute | solution.py:304
  22.2 1.9 %collective-permute-start.2 = (bf16[64,768]{1,0:T(8,128)(2,1)}, bf16[64,768]{1,0:T(8,128)(2,1)S(1)}, u32[]{:S(2)}, u32[]{:S(2)}) collective-permute-start(bf16[64,768]{1,0:T(8,128)(2,1)} %bitcast.35), channel_id=1, source_target_pairs={{0,48},{16,32},{32,16},{48,0},{1,49},{17,33},{33,17},{49,1},{2,50}... | collective-permute-start | bytes 294920 | tf_op jit(solution)/shard_map/ppermute | solution.py:304
  24.1 3.9 %attention.1 = bf16[4,480,256]{2,1,0:T(8,128)(2,1)} custom-call(f32[768]{0:T(1024)} %gain_hbm.1, bf16[256,768]{1,0:T(8,128)(2,1)} %bitcast.30, s32[128,256]{1,0:T(8,128)} %segment_ref.1, bf16[3,192,768]{2,1,0:T(8,128)(2,1)} %bitcast.39, bf16[192,256]{1,0:T(8,128)(2,1)} %constant.53.clone.table_hbm, bf16[192,768]{1,0:T(8,128)(2,1)} %out_weight_hbm.1), custom_call_target="tpu_custom_call" | custom-call | flops 1200000000 | bytes 2000000 | tf_op jit(solution)/shard_map/attention/pallas_call | solution.py:360
  28.0 4.2 %collective-permute-done.2 = bf16[64,768]{1,0:T(8,128)(2,1)S(1)} collective-permute-done((bf16[64,768]{1,0:T(8,128)(2,1)}, bf16[64,768]{1,0:T(8,128)(2,1)S(1)}, u32[]{:S(2)}, u32[]{:S(2)}) %collective-permute-start.2) | collective-permute-done | bytes 98336 | tf_op jit(solution)/shard_map/ppermute | solution.py:304
  32.2 0.8 pad_maximum_fusion
  33.0 17.7 %all_to_all.20.merged_ref = bf16[4,480,256]{2,1,0:T(8,128)(2,1)S(1)} all-to-all(bf16[4,480,256]{2,1,0:T(8,128)(2,1)} %attention.1), channel_id=1, replica_groups=mesh['y'=8,'zh'=4,'zl'=2,'core'=2,'term'=4] {'term'}, dimensions={0} | all-to-all | bytes 1966080 | tf_op jit(solution)/shard_map/all_to_all | solution.py:300
  50.7 0.9 slice.4
  51.6 3.6 %collective-permute-start.3 = (bf16[4,288,256]{2,1,0:T(8,128)(2,1)}, bf16[4,288,256]{2,1,0:T(8,128)(2,1)S(1)}, u32[]{:S(2)}, u32[]{:S(2)}) collective-permute-start(bf16[4,288,256]{2,1,0:T(8,128)(2,1)} %slice.4), channel_id=1, source_target_pairs={{0,4},{4,0},{1,5},{5,1},{2,6},{6,2},{3,7},{7,3},{8,12},{12,8},{9,1... | collective-permute-start | bytes 1769480 | tf_op jit(solution)/shard_map/ppermute | solution.py:304
  55.2 1.3 broadcast_in_dim.12.gain_ref
  57.1 1.2 concatenate.11.ids_ref
  59.6 2.9 %ffn.1 = (f32[64,768]{1,0:T(8,128)S(1)}, bf16[256,768]{1,0:T(8,128)(2,1)}) custom-call(s32[9]{0:T(128)S(1)} %copy-done.6, bf16[256,768]{1,0:T(8,128)(2,1)S(1)} %bitcast.31, bf16[4,480,256]{2,1,0:T(8,128)(2,1)S(1)} %all_to_all.20.merged_ref, bf16[4,288,256]{2,1,0:T(8,128)(2,1)S(1)} %collective-permute-done.3.other_ref, f32[1,768]{1,0:T(1,128)S(1)} %copy-done.5, ...), custom_call_target="tpu_custom_call" | custom-call | flops 700000000 | bytes 4000000 | tf_op jit(solution)/shard_map/ffn/pallas_call | solution.py:383
  63.2 3.6 %all-to-all-start.1 = ((bf16[4,64,768]{2,1,0:T(8,128)(2,1)}), bf16[4,64,768]{2,1,0:T(8,128)(2,1)S(1)}, u32[]{:S(2)}, u32[]{:S(2)}) async-start(bf16[4,64,768]{2,1,0:T(8,128)(2,1)} %bitcast.12), calls=%async_computation.1 | async-start | bytes 786432 | tf_op jit(solution)/shard_map/all_to_all | solution.py:300
  66.8 0.8 copy.23.docs_ref
  69.1 0.9 copy-done.4
  70.6 1.0 prep.1
  71.6 3.5 %all-to-all-done.1.partial_ref = bf16[4,64,768]{2,1,0:T(8,128)(2,1)S(1)} async-done(((bf16[4,64,768]{2,1,0:T(8,128)(2,1)}), bf16[4,64,768]{2,1,0:T(8,128)(2,1)S(1)}, u32[]{:S(2)}, u32[]{:S(2)}) %all-to-all-start.1) | async-done | bytes 393248 | tf_op jit(solution)/shard_map/all_to_all | solution.py:300
  75.0 1.3 copy-done.11
  76.3 0.9 copy-done.13
  78.0 9.5 %all_to_all.21 = bf16[4,64,768]{2,1,0:T(8,128)(2,1)S(1)} all-to-all(bf16[4,64,768]{2,1,0:T(8,128)(2,1)S(1)} %head.1), channel_id=1, replica_groups=mesh['y'=8,'zh'=4,'zl'=2,'core'=2,'term'=4] {'term'}, dimensions={0} | all-to-all | bytes 786432 | tf_op jit(solution)/shard_map/all_to_all | solution.py:300
  87.5 3.8 %collective-permute-start.5 = (bf16[256,768]{1,0:T(8,128)(2,1)S(1)}, bf16[256,768]{1,0:T(8,128)(2,1)S(1)}, u32[]{:S(2)}, u32[]{:S(2)}) collective-permute-start(bf16[256,768]{1,0:T(8,128)(2,1)S(1)} %bitcast.27), channel_id=1, source_target_pairs={{0,4},{4,0},{1,5},{5,1},{2,6},{6,2},{3,7},{7,3},{8,12},{12,8},{9,1... | collective-permute-start | bytes 1179656 | tf_op jit(solution)/shard_map/ppermute | solution.py:304
  91.3 3.5 %collective-permute-start.4 = (bf16[256,768]{1,0:T(8,128)(2,1)S(1)}, bf16[256,768]{1,0:T(8,128)(2,1)S(1)}, u32[]{:S(2)}, u32[]{:S(2)}) collective-permute-start(bf16[256,768]{1,0:T(8,128)(2,1)S(1)} %bitcast.28), channel_id=1, source_target_pairs={{0,8},{8,0},{1,9},{9,1},{2,10},{10,2},{3,11},{11,3},{4,12},{12,4},... | collective-permute-start | bytes 1179656 | tf_op jit(solution)/shard_map/ppermute | solution.py:304
  94.9 1.9 %copy-done.9 = bf16[2048,768]{1,0:T(8,128)(2,1)S(1)} copy-done((bf16[2048,768]{1,0:T(8,128)(2,1)S(1)}, bf16[2048,768]{1,0:T(8,128)(2,1)}, u32[]{:S(2)}) %copy-start.9) | copy-done | bytes 3145752
  96.8 4.1 %near_pool.1.low_ref = f32[8,2048]{1,0:T(8,128)S(1)} custom-call(s32[9]{0:T(128)S(1)} %copy-done.8, s32[128,8]{1,0:T(8,128)S(1)} %get-tuple-element.22.bounds_ref, bf16[256,768]{1,0:T(8,128)(2,1)S(1)} %bitcast.29, bf16[256,768]{1,0:T(8,128)(2,1)S(1)} %collective-permute-done.5.core_ref, bf16[2048,768]{1,0:T(8,128)(2,1)S(1)} %copy-done.9), custom_call_target="tpu_custom_call" | custom-call | flops 1600000000 | bytes 4000000 | tf_op jit(solution)/shard_map/near_pool/pallas_call | solution.py:429
  100.9 3.3 %collective-permute-done.4.far_ref = bf16[256,768]{1,0:T(8,128)(2,1)S(1)} collective-permute-done((bf16[256,768]{1,0:T(8,128)(2,1)S(1)}, bf16[256,768]{1,0:T(8,128)(2,1)S(1)}, u32[]{:S(2)}, u32[]{:S(2)}) %collective-permute-start.4) | collective-permute-done | bytes 393248 | tf_op jit(solution)/shard_map/ppermute | solution.py:304
  104.2 2.6 %collective-permute-start.6 = (bf16[256,768]{1,0:T(8,128)(2,1)S(1)}, bf16[256,768]{1,0:T(8,128)(2,1)S(1)}, u32[]{:S(2)}, u32[]{:S(2)}) collective-permute-start(bf16[256,768]{1,0:T(8,128)(2,1)S(1)} %collective-permute-done.4.far_ref), channel_id=1, source_target_pairs={{0,4},{4,0},{1,5},{5,1},{2,6},{6,2},{3,7},{7,3},{8,12},{12,8},{9,1... | collective-permute-start | bytes 1179656 | tf_op jit(solution)/shard_map/ppermute | solution.py:304
  107.0 1.1 collective-permute-done.6.far_core_ref
  108.1 1.9 %copy-done.10 = bf16[2048,768]{1,0:T(8,128)(2,1)S(1)} copy-done((bf16[2048,768]{1,0:T(8,128)(2,1)S(1)}, bf16[2048,768]{1,0:T(8,128)(2,1)}, u32[]{:S(2)}) %copy-start.10) | copy-done | bytes 3145752
  110.0 4.8 %far_pool.1 = f32[32,8,128]{2,1,0:T(8,128)} custom-call(s32[9]{0:T(128)S(1)} %copy-done.8, s32[128,8]{1,0:T(8,128)S(1)} %get-tuple-element.22.bounds_ref, bf16[256,768]{1,0:T(8,128)(2,1)S(1)} %collective-permute-done.4.far_ref, bf16[256,768]{1,0:T(8,128)(2,1)S(1)} %collective-permute-done.6.far_core_ref, bf16[2048,768]{1,0:T(8,128)(2,1)S(1)} %copy-done.10, ...), custom_call_target="tpu_custom_call" | custom-call | flops 1600000000 | bytes 4000000 | tf_op jit(solution)/shard_map/far_pool/pallas_call | solution.py:441
  114.8 10.9 %all-to-all-start.3 = ((f32[32,8,128]{2,1,0:T(8,128)}), f32[32,8,128]{2,1,0:T(8,128)S(1)}, u32[]{:S(2)}, u32[]{:S(2)}) async-start(f32[32,8,128]{2,1,0:T(8,128)} %far_pool.1), calls=%async_computation.3 | async-start | bytes 262144 | tf_op jit(solution)/shard_map/all_to_all | solution.py:300
  126.6 10.5 %all-to-all-done.3 = f32[32,8,128]{2,1,0:T(8,128)S(1)} async-done(((f32[32,8,128]{2,1,0:T(8,128)}), f32[32,8,128]{2,1,0:T(8,128)S(1)}, u32[]{:S(2)}, u32[]{:S(2)}) %all-to-all-start.3) | async-done | bytes 131104 | tf_op jit(solution)/shard_map/all_to_all | solution.py:300
  137.1 1.2 place.1
  (51 shorter events, 6.3 us)
Async XLA Ops:
  6.5 25.6 %copy-start.14 = (bf16[1,8,1,8,768]{4,3,2,1,0:T(8,128)(2,1)S(1)}, bf16[1,8,1,8,768]{4,3,2,1,0:T(8,128)(2,1)}, u32[]{:S(2)}) copy-start(bf16[1,8,1,8,768]{4,3,2,1,0:T(8,128)(2,1)} %param.29) | copy-start | bytes 294916
  6.5 88.3 %all-gather.2.cloned.1.call-start = ((), (), s32[]{:S(2)}) async-start(), calls=%async_computation.4 | async-start | bytes 3538944 | tf_op jit(solution)/shard_map/all_gather | solution.py:380
  6.5 21.5 %collective-permute-start = (bf16[64,768]{1,0:T(8,128)(2,1)}, bf16[64,768]{1,0:T(8,128)(2,1)S(1)}, u32[]{:S(2)}, u32[]{:S(2)}) collective-permute-start(bf16[64,768]{1,0:T(8,128)(2,1)} %bitcast.33), channel_id=1, source_target_pairs={{0,16},{16,0},{32,48},{48,32},{1,17},{17,1},{33,49},{49,33},{2,18}... | collective-permute-start | bytes 294920 | tf_op jit(solution)/shard_map/ppermute | solution.py:304
  13.3 14.7 %collective-permute-start.1 = (bf16[64,768]{1,0:T(8,128)(2,1)}, bf16[64,768]{1,0:T(8,128)(2,1)S(1)}, u32[]{:S(2)}, u32[]{:S(2)}) collective-permute-start(bf16[64,768]{1,0:T(8,128)(2,1)} %bitcast.34), channel_id=1, source_target_pairs={{0,32},{16,48},{32,0},{48,16},{1,33},{17,49},{33,1},{49,17},{2,34}... | collective-permute-start | bytes 294920 | tf_op jit(solution)/shard_map/ppermute | solution.py:304
  22.2 10.0 %collective-permute-start.2 = (bf16[64,768]{1,0:T(8,128)(2,1)}, bf16[64,768]{1,0:T(8,128)(2,1)S(1)}, u32[]{:S(2)}, u32[]{:S(2)}) collective-permute-start(bf16[64,768]{1,0:T(8,128)(2,1)} %bitcast.35), channel_id=1, source_target_pairs={{0,48},{16,32},{32,16},{48,0},{1,49},{17,33},{33,17},{49,1},{2,50}... | collective-permute-start | bytes 294920 | tf_op jit(solution)/shard_map/ppermute | solution.py:304
  28.0 30.4 %copy-start = (bf16[2,768,288]{1,2,0:T(8,128)(2,1)S(1)}, bf16[2,768,288]{1,2,0:T(8,128)(2,1)}, u32[]{:S(2)}) copy-start(bf16[2,768,288]{1,2,0:T(8,128)(2,1)} %param.24) | copy-start | bytes 2654212
  28.0 30.4 %copy-start.1 = (bf16[288,768]{1,0:T(8,128)(2,1)S(1)}, bf16[288,768]{1,0:T(8,128)(2,1)}, u32[]{:S(2)}) copy-start(bf16[288,768]{1,0:T(8,128)(2,1)} %down_ref.1) | copy-start | bytes 1327108
  28.0 30.4 %copy-start.2 = (bf16[1,256,768]{2,1,0:T(8,128)(2,1)S(1)}, bf16[1,256,768]{2,1,0:T(8,128)(2,1)}, u32[]{:S(2)}) copy-start(bf16[1,256,768]{2,1,0:T(8,128)(2,1)} %param.16) | copy-start | bytes 1179652
  50.7 18.4 %copy-start.3 = (s32[512,128]{1,0:T(8,128)S(1)}, s32[512,128]{1,0:T(8,128)}, u32[]{:S(2)}) copy-start(s32[512,128]{1,0:T(8,128)} %list_ref.1) | copy-start | bytes 786436
  51.6 6.8 %collective-permute-start.3 = (bf16[4,288,256]{2,1,0:T(8,128)(2,1)}, bf16[4,288,256]{2,1,0:T(8,128)(2,1)S(1)}, u32[]{:S(2)}, u32[]{:S(2)}) collective-permute-start(bf16[4,288,256]{2,1,0:T(8,128)(2,1)} %slice.4), channel_id=1, source_target_pairs={{0,4},{4,0},{1,5},{5,1},{2,6},{6,2},{3,7},{7,3},{8,12},{12,8},{9,1... | collective-permute-start | bytes 1769480 | tf_op jit(solution)/shard_map/ppermute | solution.py:304
  58.4 0.7 copy-start.5
  59.0 0.6 copy-start.6
  62.6 0.7 copy-start.12
  63.2 31.6 %copy-start.8 = (s32[9]{0:T(128)S(1)}, s32[9]{0:T(128)}, u32[]{:S(2)}) copy-start(s32[9]{0:T(128)} %concatenate.11.ids_ref) | copy-start | bytes 112
  63.2 11.8 %all-to-all-start.1 = ((bf16[4,64,768]{2,1,0:T(8,128)(2,1)}), bf16[4,64,768]{2,1,0:T(8,128)(2,1)S(1)}, u32[]{:S(2)}, u32[]{:S(2)}) async-start(bf16[4,64,768]{2,1,0:T(8,128)(2,1)} %bitcast.12), calls=%async_computation.1 | async-start | bytes 786432 | tf_op jit(solution)/shard_map/all_to_all | solution.py:300
  69.1 0.9 copy-start.4
  70.0 0.6 copy-start.7
  75.0 1.3 copy-start.11
  76.3 0.9 copy-start.13
  77.9 28.9 %copy-start.15 = (s32[512]{0:T(512)S(1)}, s32[512]{0:T(512)}, u32[]{:S(2)}) copy-start(s32[512]{0:T(512)} %param.19) | copy-start | bytes 6148
  87.5 7.4 %collective-permute-start.5 = (bf16[256,768]{1,0:T(8,128)(2,1)S(1)}, bf16[256,768]{1,0:T(8,128)(2,1)S(1)}, u32[]{:S(2)}, u32[]{:S(2)}) collective-permute-start(bf16[256,768]{1,0:T(8,128)(2,1)S(1)} %bitcast.27), channel_id=1, source_target_pairs={{0,4},{4,0},{1,5},{5,1},{2,6},{6,2},{3,7},{7,3},{8,12},{12,8},{9,1... | collective-permute-start | bytes 1179656 | tf_op jit(solution)/shard_map/ppermute | solution.py:304
  91.3 12.9 %collective-permute-start.4 = (bf16[256,768]{1,0:T(8,128)(2,1)S(1)}, bf16[256,768]{1,0:T(8,128)(2,1)S(1)}, u32[]{:S(2)}, u32[]{:S(2)}) collective-permute-start(bf16[256,768]{1,0:T(8,128)(2,1)S(1)} %bitcast.28), channel_id=1, source_target_pairs={{0,8},{8,0},{1,9},{9,1},{2,10},{10,2},{3,11},{11,3},{4,12},{12,4},... | collective-permute-start | bytes 1179656 | tf_op jit(solution)/shard_map/ppermute | solution.py:304
  94.9 1.9 %copy-start.9 = (bf16[2048,768]{1,0:T(8,128)(2,1)S(1)}, bf16[2048,768]{1,0:T(8,128)(2,1)}, u32[]{:S(2)}) copy-start(bf16[2048,768]{1,0:T(8,128)(2,1)} %all-gather.2.cloned.1.call-done.table_ref) | copy-start | bytes 9437188
  104.2 3.9 %collective-permute-start.6 = (bf16[256,768]{1,0:T(8,128)(2,1)S(1)}, bf16[256,768]{1,0:T(8,128)(2,1)S(1)}, u32[]{:S(2)}, u32[]{:S(2)}) collective-permute-start(bf16[256,768]{1,0:T(8,128)(2,1)S(1)} %collective-permute-done.4.far_ref), channel_id=1, source_target_pairs={{0,4},{4,0},{1,5},{5,1},{2,6},{6,2},{3,7},{7,3},{8,12},{12,8},{9,1... | collective-permute-start | bytes 1179656 | tf_op jit(solution)/shard_map/ppermute | solution.py:304
  108.1 1.9 %copy-start.10 = (bf16[2048,768]{1,0:T(8,128)(2,1)S(1)}, bf16[2048,768]{1,0:T(8,128)(2,1)}, u32[]{:S(2)}) copy-start(bf16[2048,768]{1,0:T(8,128)(2,1)} %all-gather.2.cloned.1.call-done.table_ref) | copy-start | bytes 9437188
  110.0 16.4 %copy-start.16 = (bf16[1,8,1,8]{3,1,2,0:T(8,128)(2,1)S(1)}, bf16[1,8,1,8]{3,1,2,0:T(8,128)(2,1)}, u32[]{:S(2)}) copy-start(bf16[1,8,1,8]{3,1,2,0:T(8,128)(2,1)} %param.30) | copy-start | bytes 388
  114.8 22.3 %all-to-all-start.3 = ((f32[32,8,128]{2,1,0:T(8,128)}), f32[32,8,128]{2,1,0:T(8,128)S(1)}, u32[]{:S(2)}, u32[]{:S(2)}) async-start(f32[32,8,128]{2,1,0:T(8,128)} %far_pool.1), calls=%async_computation.3 | async-start | bytes 262144 | tf_op jit(solution)/shard_map/all_to_all | solution.py:300
Sparse Core Ops, SparseCore 0:
  33.1 46.7 all-gather.1

commit v7 on v6

--- a/solution.py
+++ b/solution.py
@@ -17,7 +17,6 @@
 SPAN = 8
 NEAR = 4
 LOWEST = -3.0e38
-TERM_AT, BLOCK_AT, STRIDE_AT, CORE_AT, NEAR_AT = 4, 5, 6, 7, 8
 
 NT = (((1,), (1,)), ((), ()))
 TN = (((0,), (0,)), ((), ()))
@@ -49,6 +48,12 @@
 
 def matmul(left, right, dims):
     return lax.dot_general(left, right, dims, preferred_element_type=jnp.float32)
+
+
+def row_index(d=0):
+    near = lax.axis_index("zl") * lax.axis_size("core") + lax.axis_index("core")
+    own = lax.axis_index("y") * lax.axis_size("zh") + lax.axis_index("zh")
+    return own * lax.axis_size("zl") * lax.axis_size("core") + jnp.bitwise_xor(near, d)
 
 
 def attention_kernel(
@@ -68,9 +73,7 @@
     sems,
 ):
     length = hidden_ref.shape[0]
-    row = lax.axis_index("y")
-    for axis in ("zh", "zl", "core"):
-        row = row * lax.axis_size(axis) + lax.axis_index(axis)
+    row = row_index()
     tile = pl.multiple_of(lax.shift_left(lax.shift_right_logical(row, 3), 3), 8)
     copies = [
         pltpu.make_async_copy(hidden_hbm, hidden_ref, sems.at[0]),
@@ -144,7 +147,7 @@
 
 
 def ffn_kernel(
-    ids_ref, hidden_ref, merged_ref, other_ref, gain_ref, in_ref, down_ref, after_ref, out_ref, weight_ref, all_ref
+    hidden_ref, merged_ref, other_ref, gain_ref, in_ref, down_ref, after_ref, out_ref, weight_ref, all_ref
 ):
     length, width = hidden_ref.shape
     shards = merged_ref.shape[0]
@@ -156,8 +159,8 @@
             at = slice(column * half, (column + 1) * half)
             mine = merged_ref[shard, head_width + column * half : head_width + (column + 1) * half]
             for core, block in (
-                (ids_ref[CORE_AT], mine),
-                (1 - ids_ref[CORE_AT], other_ref[shard, at, :]),
+                (lax.axis_index("core"), mine),
+                (1 - lax.axis_index("core"), other_ref[shard, at, :]),
             ):
                 first = pl.multiple_of(shard * head_width + core * half, half)
                 weight_ref[pl.ds(first, half), to] = block
@@ -165,8 +168,8 @@
     after_attn = hidden_ref[...].astype(jnp.float32) + matmul(context, weight_ref[...], TN)
     all_ref[...] = after_attn
     share = after_ref.shape[0]
-    after_ref[...] = all_ref[pl.ds(pl.multiple_of(ids_ref[TERM_AT] * share, share), share), :]
-    mixed = layer_norm(after_attn, gain_ref[...]).astype(jnp.bfloat16)
+    after_ref[...] = all_ref[pl.ds(pl.multiple_of(lax.axis_index("term") * share, share), share), :]
+    mixed = layer_norm(after_attn, gain_ref[...].reshape(1, -1)).astype(jnp.bfloat16)
     inner_up = matmul(in_ref[0], mixed, NT)
     gate_part = matmul(in_ref[1], mixed, NT)
     activated = (gelu(inner_up) * gate_part).astype(jnp.bfloat16)
@@ -177,14 +180,14 @@
     after_ffn = after_ref[...]
     for shard in range(partial_ref.shape[0]):
         after_ffn = after_ffn + partial_ref[shard].astype(jnp.float32)
-    normed = layer_norm(after_ffn, final_ref[...]).astype(jnp.bfloat16)
+    normed = layer_norm(after_ffn, final_ref[...].reshape(1, -1)).astype(jnp.bfloat16)
     dense = matmul(normed, dense_ref[...], (((1,), (0,)), ((), ())))
-    headed = layer_norm(gelu(dense), head_ref[...]).astype(jnp.bfloat16)
+    headed = layer_norm(gelu(dense), head_ref[...].reshape(1, -1)).astype(jnp.bfloat16)
     for copy in range(out_ref.shape[0]):
         out_ref[copy] = headed
 
 
-def prep_kernel(ids_ref, segment_ref, list_ref, docs_ref, bounds_ref, mask_ref):
+def prep_kernel(segment_ref, list_ref, docs_ref, bounds_ref, mask_ref):
     segments = segment_ref[...]
     slot = lax.broadcasted_iota(jnp.int32, bounds_ref.shape, 1)
     bounds = jnp.zeros(bounds_ref.shape, jnp.int32)
@@ -194,8 +197,9 @@
     bounds_ref[...] = bounds
     own_terms, passages = mask_ref.shape
     groups = own_terms // SPAN
-    stride = ids_ref[STRIDE_AT]
-    blocks = list_ref[...] - ids_ref[BLOCK_AT]
+    stride = segment_ref.shape[0] * SPAN // BLOCK
+    first_block = lax.axis_index("term") * groups * stride + row_index() * SPAN // BLOCK
+    blocks = list_ref[...] - first_block
     bits = jnp.zeros(blocks.shape, jnp.float32)
     for group in range(groups):
         bits = jnp.where(blocks == group * stride, np.float32(2**group), bits)
@@ -209,7 +213,7 @@
         mask_ref[group * SPAN : (group + 1) * SPAN, :] = held.astype(jnp.float32)
 
 
-def passage_maxima(ids_ref, bounds_ref, first_row, rows, table_ref, logits_ref):
+def passage_maxima(bounds_ref, first_row, rows, table_ref, logits_ref):
     length = rows[0].shape[0]
     stacked = jnp.concatenate([row[...] for row in rows], axis=0)
     logits_ref[...] = matmul(stacked, table_ref[...], NT)
@@ -217,7 +221,7 @@
     sublane = lax.broadcasted_iota(jnp.int32, (tile, logits_ref.shape[1]), 0)
     maxima = []
     for r in range(len(rows)):
-        row = ids_ref[first_row + r]
+        row = row_index(first_row + r)
         for passage in range(PASS_DEV):
             first = bounds_ref[row, passage]
             end = bounds_ref[row, passage + 1]
@@ -239,21 +243,21 @@
     return jnp.concatenate(maxima, axis=0)
 
 
-def near_pool_kernel(ids_ref, bounds_ref, own_ref, core_ref, table_ref, low_ref, logits_ref):
+def near_pool_kernel(bounds_ref, own_ref, core_ref, table_ref, low_ref, logits_ref):
     rows = (own_ref, core_ref)
-    low_ref[...] = passage_maxima(ids_ref, bounds_ref, 0, rows, table_ref, logits_ref)
+    low_ref[...] = passage_maxima(bounds_ref, 0, rows, table_ref, logits_ref)
 
 
 def far_pool_kernel(
-    ids_ref, bounds_ref, far_ref, far_core_ref, table_ref, low_ref, out_ref, logits_ref
+    bounds_ref, far_ref, far_core_ref, table_ref, low_ref, out_ref, logits_ref
 ):
     rows = (far_ref, far_core_ref)
-    high = passage_maxima(ids_ref, bounds_ref, len(rows), rows, table_ref, logits_ref)
+    high = passage_maxima(bounds_ref, len(rows), rows, table_ref, logits_ref)
     low = low_ref[...]
     own_terms = out_ref.shape[2] // 2
     for slot in range(out_ref.shape[0]):
         at = slice(slot * own_terms, (slot + 1) * own_terms)
-        to = slot - slot % NEAR + jnp.bitwise_xor(ids_ref[NEAR_AT], slot % NEAR)
+        to = slot - slot % NEAR + jnp.bitwise_xor(lax.axis_index("zh"), slot % NEAR)
         out_ref[to] = jnp.concatenate([low[:, at], high[:, at]], axis=1)
 
 
@@ -327,10 +331,8 @@
 ):
     near = ("y", "zh")
     slices = lax.axis_size(near)
-    slice_index = lax.axis_index(near)
     near_row = lax.axis_index(("zl", "core"))
     rows_here = lax.axis_size(("zl", "core"))
-    row_index = slice_index * rows_here + near_row
     tensor = lax.axis_size("term")
     tokens = hidden[0]
     length, width = tokens.shape
@@ -339,21 +341,8 @@
     head_width = qkv_weight.shape[2]
     passages = block_lists.shape[0]
     near_rows = jnp.stack([jnp.bitwise_xor(near_row, d) for d in range(rows_here)])
-    row_ids = slice_index * rows_here + near_rows
-
-    dp_count = slices * rows_here
-    first_block = (lax.axis_index("term") * groups * dp_count * span + row_index * span) // BLOCK
-    scalars = [
-        lax.axis_index("term"),
-        first_block,
-        jnp.int32(dp_count * span // BLOCK),
-        lax.axis_index("core"),
-        lax.axis_index("zh"),
-    ]
-    ids = jnp.concatenate([row_ids, jnp.stack(scalars)])
 
     own_slice = decoder.reshape(own_terms, width)
-    pieces = others(own_slice, "zh")
     rotary = jnp.asarray(rotary_table(length))
     half = head_width // 2
     chunk = head_width + half * width // length
@@ -375,10 +364,10 @@
         cost_estimate=cost(1200000000, 2000000),
         name="attention",
     )(attn_gain, tokens, segment_ids, jnp.swapaxes(qkv_weight, 1, 2), rotary, attn_out)
-    pieces, merged = lax.optimization_barrier((pieces, merged))
-    part = jnp.concatenate([own_slice] + pieces, axis=0)
+    own_slice, merged = lax.optimization_barrier((own_slice, merged))
+    part = jnp.concatenate([own_slice] + others(own_slice, "zh"), axis=0)
+    merged, part = lax.optimization_barrier((exchange(merged, "term"), part))
     table = lax.all_gather(part, "y", axis=0, tiled=True)
-    merged = exchange(merged, "term")
     other = swap(merged[:, head_width:], "core")
     after_attn, partial = pl.pallas_call(
         ffn_kernel,
@@ -386,7 +375,7 @@
             jax.ShapeDtypeStruct((length // tensor, width), jnp.float32),
             jax.ShapeDtypeStruct((length, width), jnp.bfloat16),
         ),
-        in_specs=[smem()] + [vmem()] * 6,
+        in_specs=[vmem()] * 6,
         out_specs=(vmem(), vmem()),
         scratch_shapes=[
             pltpu.VMEM((width, width), jnp.bfloat16),
@@ -395,19 +384,19 @@
         compiler_params=grant(20),
         cost_estimate=cost(700000000, 4000000),
         name="ffn",
-    )(ids, tokens, merged, other, mlp_gain[None], jnp.swapaxes(ffn_in, 1, 2), ffn_out)
+    )(tokens, merged, other, mlp_gain, jnp.swapaxes(ffn_in, 1, 2), ffn_out)
     bounds, mask = pl.pallas_call(
         prep_kernel,
         out_shape=(
             jax.ShapeDtypeStruct((segment_ids.shape[0], 2 * PASS_DEV), jnp.int32),
             jax.ShapeDtypeStruct((own_terms, passages), jnp.float32),
         ),
-        in_specs=[smem()] + [vmem()] * 3,
+        in_specs=[vmem()] * 3,
         out_specs=(vmem(), vmem()),
         compiler_params=grant(20),
         cost_estimate=cost(1000000, 1000000),
         name="prep",
-    )(ids, segment_ids, block_lists, doc_ids[:, None])
+    )(segment_ids, block_lists, doc_ids[:, None])
     partials = exchange(partial.reshape(tensor, -1, width), "term")
     partials, bounds, mask = lax.optimization_barrier((partials, bounds, mask))
     headed = pl.pallas_call(
@@ -418,7 +407,7 @@
         compiler_params=grant(20),
         cost_estimate=cost(800000000, 5000000),
         name="head",
-    )(after_attn, partials, final_gain[None], head_dense, head_gain[None])
+    )(after_attn, partials, final_gain, head_dense, head_gain)
 
     headed = exchange(headed, "term").reshape(length, width)
 
@@ -429,25 +418,24 @@
     low = pl.pallas_call(
         near_pool_kernel,
         out_shape=jax.ShapeDtypeStruct((2 * PASS_DEV, terms_here), jnp.float32),
-        in_specs=[smem(), smem()] + [vmem()] * 3,
+        in_specs=[smem()] + [vmem()] * 3,
         out_specs=vmem(),
         scratch_shapes=[logits],
         compiler_params=grant(20),
         cost_estimate=cost(1600000000, 4000000),
         name="near_pool",
-    )(ids, bounds, headed, core, table)
-    far, low = lax.optimization_barrier((far, low))
+    )(bounds, headed, core, table)
     far_core = swap(far, "core")
     pooled = pl.pallas_call(
         far_pool_kernel,
         out_shape=jax.ShapeDtypeStruct((slices, 2 * PASS_DEV, 2 * own_terms), jnp.float32),
-        in_specs=[smem(), smem()] + [vmem()] * 4,
+        in_specs=[smem()] + [vmem()] * 4,
         out_specs=vmem(),
         scratch_shapes=[logits],
         compiler_params=grant(20),
         cost_estimate=cost(1600000000, 4000000),
         name="far_pool",
-    )(ids, bounds, far, far_core, table, low)
+    )(bounds, far, far_core, table, low)
     received = exchange(pooled, near)
 
     bias = decoder_bias.reshape(1, own_terms).astype(jnp.float32)

time: 146 us -> 130 us (0.89)
  blocking collectives: 27.2 us -> 8.67 us
  local copies, waits for them, and re-layouts: 15.9 us -> 4.22 us
  starting transfers between devices: 45.5 us -> 53.7 us
  waiting for transfers between devices: 22.7 us -> 29.9 us
    all_to_all x2 -> x1, blocking collectives: 27.2 us -> 8.67 us  [exchange(): return lax.all_to_all(copies, axis, split_axis=0, concat_axis=0, tiled=True)]
    unnamed x34 -> x28, local copies, waits for them, and re-layouts: 9.46 us -> 3.22 us
    all_to_all x2 -> x3, starting transfers between devices: 14.5 us -> 20.1 us  [exchange(): return lax.all_to_all(copies, axis, split_axis=0, concat_axis=0, tiled=True)]
    all_to_all x2 -> x3, waiting for transfers between devices: 14 us -> 17.1 us  [exchange(): return lax.all_to_all(copies, axis, split_axis=0, concat_axis=0, tiled=True)]
    broadcast_in_dim x3 -> x0, local copies, waits for them, and re-layouts: 2.66 us -> none  [the longest x1 1.27 us: on_device(): mlp_gain[None]]
    ppermute x7, starting transfers between devices: 31 us -> 33.6 us  [swap(): lax.ppermute(block, axis, [(i, i ^ d) for i in range(lax.axis_size(axis))])]
    ppermute x7, waiting for transfers between devices: 8.66 us -> 10.9 us  [swap(): lax.ppermute(block, axis, [(i, i ^ d) for i in range(lax.axis_size(axis))])]
    all_gather x1, waiting for transfers between devices: 0.02 us -> 1.92 us  [on_device(): table = lax.all_gather(part, 'y', axis=0, tiled=True)]
  transfers between devices with their start and end apart: 10 -> 11, of which waited for: 5 -> 7; matrix products, arithmetic and copies ran while one was open for 5% -> 1% of each run, Pallas kernels for 9% -> 6%
where the time goes in v7:
time: 130 us; the launch traced here: 129 us
  starting transfers between devices  53.7 us (41%)
  waiting for transfers between devices  29.9 us (23%)
  Pallas kernels  17.6 us (14%)
  between operations  13.7 us (11%)
  blocking collectives  8.67 us (7%)
  local copies, waits for them, and re-layouts  4.22 us (3%)
    ppermute x7, starting transfers between devices, swap(): lax.ppermute(block, axis, [(i, i ^ d) for i in range(lax.axis_size(axis))])  33.6 us
    all_to_all x3, starting transfers between devices, exchange(): return lax.all_to_all(copies, axis, split_axis=0, concat_axis=0, tiled=True)  20.1 us
    all_to_all x3, waiting for transfers between devices, exchange(): return lax.all_to_all(copies, axis, split_axis=0, concat_axis=0, tiled=True)  17.1 us
    ppermute x7, waiting for transfers between devices, swap(): lax.ppermute(block, axis, [(i, i ^ d) for i in range(lax.axis_size(axis))])  10.9 us
    all_to_all x1, blocking collectives, exchange(): return lax.all_to_all(copies, axis, split_axis=0, concat_axis=0, tiled=True)  8.67 us
    pallas_call x1, Pallas kernels, on_device(): pl.pallas_call(far_pool_kernel, out_shape=jax.ShapeDtypeStruct((slices, 2...  4.79 us
    pallas_call x1, Pallas kernels, on_device(): pl.pallas_call(near_pool_kernel, out_shape=jax.ShapeDtypeStruct((2 * PASS...  4.07 us
    pallas_call x1, Pallas kernels, on_device(): pl.pallas_call(attention_kernel, out_shape=jax.ShapeDtypeStruct((tensor,...  3.94 us
  transfers between devices with their start and end apart: 11, of which 7 were waited for; matrix products, arithmetic and copies ran while one was open for 1% of the time, Pallas kernels for 6%

profile of v7, /device:TPU:1, one launch (start us, length us, event | category | flops | bytes accessed | tf_op | source)
XLA Modules:
  0.0 128.7 jit_solution(6374783160727238506)
XLA Ops:
  6.5 3.9 %attention.1 = bf16[4,480,256]{2,1,0:T(8,128)(2,1)} custom-call(f32[768]{0:T(1024)} %gain_hbm.1, bf16[256,768]{1,0:T(8,128)(2,1)} %bitcast.19, s32[128,256]{1,0:T(8,128)} %segment_ref.1, bf16[3,192,768]{2,1,0:T(8,128)(2,1)} %bitcast.31, bf16[192,256]{1,0:T(8,128)(2,1)} %constant.22.clone.table_hbm, bf16[192,768]{1,0:T(8,128)(2,1)} %out_weight_hbm.1), custom_call_target="tpu_custom_call" | custom-call | flops 1200000000 | bytes 2000000 | tf_op jit(solution)/shard_map/attention/pallas_call | solution.py:349
  10.5 5.0 %all-to-all-start = ((bf16[4,480,256]{2,1,0:T(8,128)(2,1)}), bf16[4,480,256]{2,1,0:T(8,128)(2,1)S(1)}, u32[]{:S(2)}, u32[]{:S(2)}) async-start(bf16[4,480,256]{2,1,0:T(8,128)(2,1)} %attention.1), calls=%async_computation | async-start | bytes 1966080 | tf_op jit(solution)/shard_map/all_to_all | solution.py:304
  15.5 5.8 %collective-permute-start = (bf16[64,768]{1,0:T(8,128)(2,1)S(1)}, bf16[64,768]{1,0:T(8,128)(2,1)S(1)}, u32[]{:S(2)}, u32[]{:S(2)}) collective-permute-start(bf16[64,768]{1,0:T(8,128)(2,1)S(1)} %bitcast.25), channel_id=1, source_target_pairs={{0,16},{16,0},{32,48},{48,32},{1,17},{17,1},{33,49},{49,33},{2,18}... | collective-permute-start | bytes 294920 | tf_op jit(solution)/shard_map/ppermute | solution.py:308
  21.3 8.8 %collective-permute-start.1 = (bf16[64,768]{1,0:T(8,128)(2,1)S(1)}, bf16[64,768]{1,0:T(8,128)(2,1)S(1)}, u32[]{:S(2)}, u32[]{:S(2)}) collective-permute-start(bf16[64,768]{1,0:T(8,128)(2,1)S(1)} %bitcast.26), channel_id=1, source_target_pairs={{0,32},{16,48},{32,0},{48,16},{1,33},{17,49},{33,1},{49,17},{2,34}... | collective-permute-start | bytes 294920 | tf_op jit(solution)/shard_map/ppermute | solution.py:308
  30.2 1.9 %collective-permute-start.2 = (bf16[64,768]{1,0:T(8,128)(2,1)S(1)}, bf16[64,768]{1,0:T(8,128)(2,1)S(1)}, u32[]{:S(2)}, u32[]{:S(2)}) collective-permute-start(bf16[64,768]{1,0:T(8,128)(2,1)S(1)} %bitcast.27), channel_id=1, source_target_pairs={{0,48},{16,32},{32,16},{48,0},{1,49},{17,33},{33,17},{49,1},{2,50}... | collective-permute-start | bytes 294920 | tf_op jit(solution)/shard_map/ppermute | solution.py:308
  32.1 1.0 collective-permute-done.1
  33.1 6.8 %collective-permute-done.2 = bf16[64,768]{1,0:T(8,128)(2,1)S(1)} collective-permute-done((bf16[64,768]{1,0:T(8,128)(2,1)S(1)}, bf16[64,768]{1,0:T(8,128)(2,1)S(1)}, u32[]{:S(2)}, u32[]{:S(2)}) %collective-permute-start.2) | collective-permute-done | bytes 98336 | tf_op jit(solution)/shard_map/ppermute | solution.py:308
  39.9 0.8 pad_maximum_fusion
  40.8 2.5 %collective-permute-start.3 = (bf16[4,288,256]{2,1,0:T(8,128)(2,1)S(1)}, bf16[4,288,256]{2,1,0:T(8,128)(2,1)S(1)}, u32[]{:S(2)}, u32[]{:S(2)}) collective-permute-start(bf16[4,288,256]{2,1,0:T(8,128)(2,1)S(1)} %slice.3), channel_id=1, source_target_pairs={{0,4},{4,0},{1,5},{5,1},{2,6},{6,2},{3,7},{7,3},{8,12},{12,8},{9,1... | collective-permute-start | bytes 1769480 | tf_op jit(solution)/shard_map/ppermute | solution.py:308
  43.3 1.6 %collective-permute-done.3.other_ref = bf16[4,288,256]{2,1,0:T(8,128)(2,1)S(1)} collective-permute-done((bf16[4,288,256]{2,1,0:T(8,128)(2,1)S(1)}, bf16[4,288,256]{2,1,0:T(8,128)(2,1)S(1)}, u32[]{:S(2)}, u32[]{:S(2)}) %collective-permute-start.3) | collective-permute-done | bytes 589856 | tf_op jit(solution)/shard_map/ppermute | solution.py:308
  44.9 2.5 %ffn.1 = (f32[64,768]{1,0:T(8,128)S(1)}, bf16[256,768]{1,0:T(8,128)(2,1)}) custom-call(bf16[256,768]{1,0:T(8,128)(2,1)S(1)} %bitcast.20, bf16[4,480,256]{2,1,0:T(8,128)(2,1)S(1)} %all-to-all-done.merged_ref, bf16[4,288,256]{2,1,0:T(8,128)(2,1)S(1)} %collective-permute-done.3.other_ref, f32[768]{0:T(1024)S(1)} %copy-done.5, ...), custom_call_target="tpu_custom_call" | custom-call | flops 700000000 | bytes 4000000 | tf_op jit(solution)/shard_map/ffn/pallas_call | solution.py:372
  47.4 4.5 %all-to-all-start.1 = ((bf16[4,64,768]{2,1,0:T(8,128)(2,1)}), bf16[4,64,768]{2,1,0:T(8,128)(2,1)S(1)}, u32[]{:S(2)}, u32[]{:S(2)}) async-start(bf16[4,64,768]{2,1,0:T(8,128)(2,1)} %bitcast.4), calls=%async_computation.1 | async-start | bytes 786432 | tf_op jit(solution)/shard_map/all_to_all | solution.py:304
  52.0 0.1 copy.23.docs_ref
  52.2 0.4 prep.1
  52.6 6.6 %all-to-all-done.1.partial_ref = bf16[4,64,768]{2,1,0:T(8,128)(2,1)S(1)} async-done(((bf16[4,64,768]{2,1,0:T(8,128)(2,1)}), bf16[4,64,768]{2,1,0:T(8,128)(2,1)S(1)}, u32[]{:S(2)}, u32[]{:S(2)}) %all-to-all-start.1) | async-done | bytes 393248 | tf_op jit(solution)/shard_map/all_to_all | solution.py:304
  59.2 1.3 copy-done.8
  60.5 0.7 head.1
  61.2 8.7 %all_to_all.20 = bf16[4,64,768]{2,1,0:T(8,128)(2,1)S(1)} all-to-all(bf16[4,64,768]{2,1,0:T(8,128)(2,1)S(1)} %head.1), channel_id=1, replica_groups=mesh['y'=8,'zh'=4,'zl'=2,'core'=2,'term'=4] {'term'}, dimensions={0} | all-to-all | bytes 786432 | tf_op jit(solution)/shard_map/all_to_all | solution.py:304
  69.8 4.1 %collective-permute-start.4 = (bf16[256,768]{1,0:T(8,128)(2,1)S(1)}, bf16[256,768]{1,0:T(8,128)(2,1)S(1)}, u32[]{:S(2)}, u32[]{:S(2)}) collective-permute-start(bf16[256,768]{1,0:T(8,128)(2,1)S(1)} %bitcast.21), channel_id=1, source_target_pairs={{0,8},{8,0},{1,9},{9,1},{2,10},{10,2},{3,11},{11,3},{4,12},{12,4},... | collective-permute-start | bytes 1179656 | tf_op jit(solution)/shard_map/ppermute | solution.py:308
  73.9 5.1 %collective-permute-start.6 = (bf16[256,768]{1,0:T(8,128)(2,1)S(1)}, bf16[256,768]{1,0:T(8,128)(2,1)S(1)}, u32[]{:S(2)}, u32[]{:S(2)}) collective-permute-start(bf16[256,768]{1,0:T(8,128)(2,1)S(1)} %bitcast.22), channel_id=1, source_target_pairs={{0,4},{4,0},{1,5},{5,1},{2,6},{6,2},{3,7},{7,3},{8,12},{12,8},{9,1... | collective-permute-start | bytes 1179656 | tf_op jit(solution)/shard_map/ppermute | solution.py:308
  79.0 1.5 %collective-permute-done.4.far_ref = bf16[256,768]{1,0:T(8,128)(2,1)S(1)} collective-permute-done((bf16[256,768]{1,0:T(8,128)(2,1)S(1)}, bf16[256,768]{1,0:T(8,128)(2,1)S(1)}, u32[]{:S(2)}, u32[]{:S(2)}) %collective-permute-start.4) | collective-permute-done | bytes 393248 | tf_op jit(solution)/shard_map/ppermute | solution.py:308
  80.5 5.4 %collective-permute-start.5 = (bf16[256,768]{1,0:T(8,128)(2,1)S(1)}, bf16[256,768]{1,0:T(8,128)(2,1)S(1)}, u32[]{:S(2)}, u32[]{:S(2)}) collective-permute-start(bf16[256,768]{1,0:T(8,128)(2,1)S(1)} %collective-permute-done.4.far_ref), channel_id=1, source_target_pairs={{0,4},{4,0},{1,5},{5,1},{2,6},{6,2},{3,7},{7,3},{8,12},{12,8},{9,1... | collective-permute-start | bytes 1179656 | tf_op jit(solution)/shard_map/ppermute | solution.py:308
  85.9 0.1 reshape.43
  86.0 1.9 %all-gather.2.cloned.1.call-done.table_ref = bf16[2048,768]{1,0:T(8,128)(2,1)} async-done(((bf16[256,768]{1,0:T(8,128)(2,1)}), bf16[2048,768]{1,0:T(8,128)(2,1)}) %all-gather.2.cloned.1.call-update) | async-done | bytes 3145744 | tf_op jit(solution)/shard_map/all_gather | solution.py:370
  88.0 1.9 %copy-done.6 = bf16[2048,768]{1,0:T(8,128)(2,1)S(1)} copy-done((bf16[2048,768]{1,0:T(8,128)(2,1)S(1)}, bf16[2048,768]{1,0:T(8,128)(2,1)}, u32[]{:S(2)}) %copy-start.6) | copy-done | bytes 3145752
  89.9 4.1 %near_pool.1.low_ref = f32[8,2048]{1,0:T(8,128)S(1)} custom-call(s32[128,8]{1,0:T(8,128)S(1)} %get-tuple-element.22.bounds_ref, bf16[256,768]{1,0:T(8,128)(2,1)S(1)} %bitcast.23, bf16[256,768]{1,0:T(8,128)(2,1)S(1)} %collective-permute-done.6.core_ref, bf16[2048,768]{1,0:T(8,128)(2,1)S(1)} %copy-done.6), custom_call_target="tpu_custom_call" | custom-call | flops 1600000000 | bytes 4000000 | tf_op jit(solution)/shard_map/near_pool/pallas_call | solution.py:418
  94.0 4.8 %far_pool.1 = f32[32,8,128]{2,1,0:T(8,128)} custom-call(s32[128,8]{1,0:T(8,128)S(1)} %get-tuple-element.22.bounds_ref, bf16[256,768]{1,0:T(8,128)(2,1)S(1)} %collective-permute-done.4.far_ref, bf16[256,768]{1,0:T(8,128)(2,1)S(1)} %collective-permute-done.5.far_core_ref, bf16[2048,768]{1,0:T(8,128)(2,1)S(1)} %copy-done.7, f32[8,2048]{1,0:T(8,128)S(1)} %near_pool.1.low_ref), custom_call_target="tpu_custom_call" | custom-call | flops 1600000000 | bytes 4000000 | tf_op jit(solution)/shard_map/far_pool/pallas_call | solution.py:429
  98.8 10.6 %all-to-all-start.3 = ((f32[32,8,128]{2,1,0:T(8,128)}), f32[32,8,128]{2,1,0:T(8,128)S(1)}, u32[]{:S(2)}, u32[]{:S(2)}) async-start(f32[32,8,128]{2,1,0:T(8,128)} %far_pool.1), calls=%async_computation.3 | async-start | bytes 262144 | tf_op jit(solution)/shard_map/all_to_all | solution.py:304
  109.8 0.1 reshape.47.docs_ref
  110.0 0.1 convert_element_type.12
  110.1 10.6 %all-to-all-done.3 = f32[32,8,128]{2,1,0:T(8,128)S(1)} async-done(((f32[32,8,128]{2,1,0:T(8,128)}), f32[32,8,128]{2,1,0:T(8,128)S(1)}, u32[]{:S(2)}, u32[]{:S(2)}) %all-to-all-start.3) | async-done | bytes 131104 | tf_op jit(solution)/shard_map/all_to_all | solution.py:304
  120.7 1.2 place.1
  (41 shorter events, 0.7 us)
Async XLA Ops:
  6.5 9.0 %copy-start.11 = (bf16[1,8,1,8,768]{4,3,2,1,0:T(8,128)(2,1)S(1)}, bf16[1,8,1,8,768]{4,3,2,1,0:T(8,128)(2,1)}, u32[]{:S(2)}) copy-start(bf16[1,8,1,8,768]{4,3,2,1,0:T(8,128)(2,1)} %param.29) | copy-start | bytes 294916
  10.5 34.4 %copy-start = (bf16[2,768,288]{1,2,0:T(8,128)(2,1)S(1)}, bf16[2,768,288]{1,2,0:T(8,128)(2,1)}, u32[]{:S(2)}) copy-start(bf16[2,768,288]{1,2,0:T(8,128)(2,1)} %param.24) | copy-start | bytes 2654212
  10.5 34.4 %copy-start.1 = (bf16[288,768]{1,0:T(8,128)(2,1)S(1)}, bf16[288,768]{1,0:T(8,128)(2,1)}, u32[]{:S(2)}) copy-start(bf16[288,768]{1,0:T(8,128)(2,1)} %down_ref.1) | copy-start | bytes 1327108
  10.5 34.4 %copy-start.2 = (bf16[1,256,768]{2,1,0:T(8,128)(2,1)S(1)}, bf16[1,256,768]{2,1,0:T(8,128)(2,1)}, u32[]{:S(2)}) copy-start(bf16[1,256,768]{2,1,0:T(8,128)(2,1)} %param.16) | copy-start | bytes 1179652
  10.5 34.4 %copy-start.5 = (f32[768]{0:T(1024)S(1)}, f32[768]{0:T(1024)}, u32[]{:S(2)}) copy-start(f32[768]{0:T(1024)} %gain_ref.1) | copy-start | bytes 9220
  10.5 30.1 %all-to-all-start = ((bf16[4,480,256]{2,1,0:T(8,128)(2,1)}), bf16[4,480,256]{2,1,0:T(8,128)(2,1)S(1)}, u32[]{:S(2)}, u32[]{:S(2)}) async-start(bf16[4,480,256]{2,1,0:T(8,128)(2,1)} %attention.1), calls=%async_computation | async-start | bytes 1966080 | tf_op jit(solution)/shard_map/all_to_all | solution.py:304
  15.5 36.5 %copy-start.12 = (s32[512]{0:T(512)S(1)}, s32[512]{0:T(512)}, u32[]{:S(2)}) copy-start(s32[512]{0:T(512)} %param.19) | copy-start | bytes 6148
  15.5 72.4 %all-gather.2.cloned.1.call-start = ((), (), s32[]{:S(2)}) async-start(), calls=%async_computation.4 | async-start | bytes 3538944 | tf_op jit(solution)/shard_map/all_gather | solution.py:370
  15.5 16.6 %collective-permute-start = (bf16[64,768]{1,0:T(8,128)(2,1)S(1)}, bf16[64,768]{1,0:T(8,128)(2,1)S(1)}, u32[]{:S(2)}, u32[]{:S(2)}) collective-permute-start(bf16[64,768]{1,0:T(8,128)(2,1)S(1)} %bitcast.25), channel_id=1, source_target_pairs={{0,16},{16,0},{32,48},{48,32},{1,17},{17,1},{33,49},{49,33},{2,18}... | collective-permute-start | bytes 294920 | tf_op jit(solution)/shard_map/ppermute | solution.py:308
  21.3 11.8 %collective-permute-start.1 = (bf16[64,768]{1,0:T(8,128)(2,1)S(1)}, bf16[64,768]{1,0:T(8,128)(2,1)S(1)}, u32[]{:S(2)}, u32[]{:S(2)}) collective-permute-start(bf16[64,768]{1,0:T(8,128)(2,1)S(1)} %bitcast.26), channel_id=1, source_target_pairs={{0,32},{16,48},{32,0},{48,16},{1,33},{17,49},{33,1},{49,17},{2,34}... | collective-permute-start | bytes 294920 | tf_op jit(solution)/shard_map/ppermute | solution.py:308
  30.2 9.7 %collective-permute-start.2 = (bf16[64,768]{1,0:T(8,128)(2,1)S(1)}, bf16[64,768]{1,0:T(8,128)(2,1)S(1)}, u32[]{:S(2)}, u32[]{:S(2)}) collective-permute-start(bf16[64,768]{1,0:T(8,128)(2,1)S(1)} %bitcast.27), channel_id=1, source_target_pairs={{0,48},{16,32},{32,16},{48,0},{1,49},{17,33},{33,17},{49,1},{2,50}... | collective-permute-start | bytes 294920 | tf_op jit(solution)/shard_map/ppermute | solution.py:308
  40.7 11.5 %copy-start.3 = (s32[512,128]{1,0:T(8,128)S(1)}, s32[512,128]{1,0:T(8,128)}, u32[]{:S(2)}) copy-start(s32[512,128]{1,0:T(8,128)} %list_ref.1) | copy-start | bytes 786436
  40.7 11.5 %copy-start.4 = (s32[128,256]{1,0:T(8,128)S(1)}, s32[128,256]{1,0:T(8,128)}, u32[]{:S(2)}) copy-start(s32[128,256]{1,0:T(8,128)} %segment_ref.1) | copy-start | bytes 393220
  40.7 18.5 %copy-start.9 = (f32[768]{0:T(1024)S(1)}, f32[768]{0:T(1024)}, u32[]{:S(2)}) copy-start(f32[768]{0:T(1024)} %final_ref.1) | copy-start | bytes 9220
  40.7 18.5 %copy-start.10 = (f32[768]{0:T(1024)S(1)}, f32[768]{0:T(1024)}, u32[]{:S(2)}) copy-start(f32[768]{0:T(1024)} %head_ref.1) | copy-start | bytes 9220
  40.8 4.1 %collective-permute-start.3 = (bf16[4,288,256]{2,1,0:T(8,128)(2,1)S(1)}, bf16[4,288,256]{2,1,0:T(8,128)(2,1)S(1)}, u32[]{:S(2)}, u32[]{:S(2)}) collective-permute-start(bf16[4,288,256]{2,1,0:T(8,128)(2,1)S(1)} %slice.3), channel_id=1, source_target_pairs={{0,4},{4,0},{1,5},{5,1},{2,6},{6,2},{3,7},{7,3},{8,12},{12,8},{9,1... | collective-permute-start | bytes 1769480 | tf_op jit(solution)/shard_map/ppermute | solution.py:308
  47.4 11.7 %all-to-all-start.1 = ((bf16[4,64,768]{2,1,0:T(8,128)(2,1)}), bf16[4,64,768]{2,1,0:T(8,128)(2,1)S(1)}, u32[]{:S(2)}, u32[]{:S(2)}) async-start(bf16[4,64,768]{2,1,0:T(8,128)(2,1)} %bitcast.4), calls=%async_computation.1 | async-start | bytes 786432 | tf_op jit(solution)/shard_map/all_to_all | solution.py:304
  59.2 1.3 copy-start.8
  69.8 10.7 %collective-permute-start.4 = (bf16[256,768]{1,0:T(8,128)(2,1)S(1)}, bf16[256,768]{1,0:T(8,128)(2,1)S(1)}, u32[]{:S(2)}, u32[]{:S(2)}) collective-permute-start(bf16[256,768]{1,0:T(8,128)(2,1)S(1)} %bitcast.21), channel_id=1, source_target_pairs={{0,8},{8,0},{1,9},{9,1},{2,10},{10,2},{3,11},{11,3},{4,12},{12,4},... | collective-permute-start | bytes 1179656 | tf_op jit(solution)/shard_map/ppermute | solution.py:308
  73.9 12.1 %collective-permute-start.6 = (bf16[256,768]{1,0:T(8,128)(2,1)S(1)}, bf16[256,768]{1,0:T(8,128)(2,1)S(1)}, u32[]{:S(2)}, u32[]{:S(2)}) collective-permute-start(bf16[256,768]{1,0:T(8,128)(2,1)S(1)} %bitcast.22), channel_id=1, source_target_pairs={{0,4},{4,0},{1,5},{5,1},{2,6},{6,2},{3,7},{7,3},{8,12},{12,8},{9,1... | collective-permute-start | bytes 1179656 | tf_op jit(solution)/shard_map/ppermute | solution.py:308
  80.5 13.5 %collective-permute-start.5 = (bf16[256,768]{1,0:T(8,128)(2,1)S(1)}, bf16[256,768]{1,0:T(8,128)(2,1)S(1)}, u32[]{:S(2)}, u32[]{:S(2)}) collective-permute-start(bf16[256,768]{1,0:T(8,128)(2,1)S(1)} %collective-permute-done.4.far_ref), channel_id=1, source_target_pairs={{0,4},{4,0},{1,5},{5,1},{2,6},{6,2},{3,7},{7,3},{8,12},{12,8},{9,1... | collective-permute-start | bytes 1179656 | tf_op jit(solution)/shard_map/ppermute | solution.py:308
  88.0 1.9 %copy-start.6 = (bf16[2048,768]{1,0:T(8,128)(2,1)S(1)}, bf16[2048,768]{1,0:T(8,128)(2,1)}, u32[]{:S(2)}) copy-start(bf16[2048,768]{1,0:T(8,128)(2,1)} %all-gather.2.cloned.1.call-done.table_ref) | copy-start | bytes 9437188
  89.9 4.1 %copy-start.7 = (bf16[2048,768]{1,0:T(8,128)(2,1)S(1)}, bf16[2048,768]{1,0:T(8,128)(2,1)}, u32[]{:S(2)}) copy-start(bf16[2048,768]{1,0:T(8,128)(2,1)} %all-gather.2.cloned.1.call-done.table_ref) | copy-start | bytes 9437188
  93.9 16.0 %copy-start.13 = (bf16[1,8,1,8]{3,1,2,0:T(8,128)(2,1)S(1)}, bf16[1,8,1,8]{3,1,2,0:T(8,128)(2,1)}, u32[]{:S(2)}) copy-start(bf16[1,8,1,8]{3,1,2,0:T(8,128)(2,1)} %param.30) | copy-start | bytes 388
  98.8 21.9 %all-to-all-start.3 = ((f32[32,8,128]{2,1,0:T(8,128)}), f32[32,8,128]{2,1,0:T(8,128)S(1)}, u32[]{:S(2)}, u32[]{:S(2)}) async-start(f32[32,8,128]{2,1,0:T(8,128)} %far_pool.1), calls=%async_computation.3 | async-start | bytes 262144 | tf_op jit(solution)/shard_map/all_to_all | solution.py:304
Sparse Core Ops, SparseCore 0:
  40.8 47.0 all-gather.1

commit v8 on v7

--- a/solution.py
+++ b/solution.py
@@ -63,7 +63,10 @@
     weight_hbm,
     table_hbm,
     out_weight_hbm,
+    in_hbm,
+    down_hbm,
     out_ref,
+    shard_ref,
     gain_ref,
     hidden_ref,
     segment_ref,
@@ -87,6 +90,11 @@
     own_rows = pl.ds(pl.multiple_of(lax.axis_index("core") * half, half), half)
     copies.append(pltpu.make_async_copy(out_weight_hbm.at[own_rows, :], half_ref, sems.at[6]))
     copies.append(pltpu.make_async_copy(gain_hbm, gain_ref, sems.at[7]))
+    units = shard_ref.shape[0] // 3
+    own_units = pl.ds(pl.multiple_of(lax.axis_index("core") * units, units), units)
+    for slot, source in enumerate((in_hbm.at[0], in_hbm.at[1], down_hbm)):
+        to = shard_ref.at[slot * units : (slot + 1) * units, :]
+        copies.append(pltpu.make_async_copy(source.at[own_units, :], to, sems.at[8 + slot]))
     for copy in copies:
         copy.start()
     copies[1].wait()
@@ -144,10 +152,23 @@
         at = slice(head_width + column * half, head_width + (column + 1) * half)
         for copy in range(out_ref.shape[0]):
             out_ref[copy, at, :] = block
+    for copy in copies[8:]:
+        copy.wait()
 
 
 def ffn_kernel(
-    hidden_ref, merged_ref, other_ref, gain_ref, in_ref, down_ref, after_ref, out_ref, weight_ref, all_ref
+    hidden_ref,
+    merged_ref,
+    other_ref,
+    gain_ref,
+    in_ref,
+    down_ref,
+    near_half_ref,
+    far_half_ref,
+    after_ref,
+    out_ref,
+    weight_ref,
+    shards_ref,
 ):
     length, width = hidden_ref.shape
     shards = merged_ref.shape[0]
@@ -166,25 +187,27 @@
                 weight_ref[pl.ds(first, half), to] = block
     context = jnp.concatenate([merged_ref[shard, :head_width] for shard in range(shards)], axis=0)
     after_attn = hidden_ref[...].astype(jnp.float32) + matmul(context, weight_ref[...], TN)
-    all_ref[...] = after_attn
-    share = after_ref.shape[0]
-    after_ref[...] = all_ref[pl.ds(pl.multiple_of(lax.axis_index("term") * share, share), share), :]
+    units = near_half_ref.shape[0] // 3
+    for slot in range(3):
+        at = slice(slot * units, (slot + 1) * units)
+        own = down_ref[...] if slot == 2 else in_ref[slot]
+        parts = [own, near_half_ref[at, :], far_half_ref[at, :]]
+        shards_ref[slot] = jnp.concatenate(parts, axis=0)
     mixed = layer_norm(after_attn, gain_ref[...].reshape(1, -1)).astype(jnp.bfloat16)
-    inner_up = matmul(in_ref[0], mixed, NT)
-    gate_part = matmul(in_ref[1], mixed, NT)
+    inner_up = matmul(shards_ref[0], mixed, NT)
+    gate_part = matmul(shards_ref[1], mixed, NT)
     activated = (gelu(inner_up) * gate_part).astype(jnp.bfloat16)
-    out_ref[...] = matmul(activated, down_ref[...], TN).astype(jnp.bfloat16)
+    partial = matmul(activated, shards_ref[2], TN)
+    after_ref[...] = after_attn + partial
+    out_ref[...] = partial.astype(jnp.bfloat16)
 
 
 def head_kernel(after_ref, partial_ref, final_ref, dense_ref, head_ref, out_ref):
-    after_ffn = after_ref[...]
-    for shard in range(partial_ref.shape[0]):
-        after_ffn = after_ffn + partial_ref[shard].astype(jnp.float32)
+    after_ffn = after_ref[...] + partial_ref[...].astype(jnp.float32)
     normed = layer_norm(after_ffn, final_ref[...].reshape(1, -1)).astype(jnp.bfloat16)
     dense = matmul(normed, dense_ref[...], (((1,), (0,)), ((), ())))
-    headed = layer_norm(gelu(dense), head_ref[...].reshape(1, -1)).astype(jnp.bfloat16)
-    for copy in range(out_ref.shape[0]):
-        out_ref[copy] = headed
+    headed = layer_norm(gelu(dense), head_ref[...].reshape(1, -1))
+    out_ref[...] = headed.astype(jnp.bfloat16)
 
 
 def prep_kernel(segment_ref, list_ref, docs_ref, bounds_ref, mask_ref):
@@ -346,11 +369,17 @@
     rotary = jnp.asarray(rotary_table(length))
     half = head_width // 2
     chunk = head_width + half * width // length
-    merged = pl.pallas_call(
+    pieces = others(own_slice, "zh")
+    ffn_in_rows = jnp.swapaxes(ffn_in, 1, 2)
+    units = ffn_out.shape[0] // 2
+    merged, shard = pl.pallas_call(
         attention_kernel,
-        out_shape=jax.ShapeDtypeStruct((tensor, chunk, length), jnp.bfloat16),
-        in_specs=[hbm()] * 6,
-        out_specs=vmem(),
+        out_shape=(
+            jax.ShapeDtypeStruct((tensor, chunk, length), jnp.bfloat16),
+            jax.ShapeDtypeStruct((3 * units, width), jnp.bfloat16),
+        ),
+        in_specs=[hbm()] * 8,
+        out_specs=(vmem(), vmem()),
         scratch_shapes=[
             pltpu.VMEM((width,), jnp.float32),
             pltpu.VMEM((length, width), jnp.bfloat16),
@@ -358,33 +387,45 @@
             pltpu.VMEM((3, head_width, width), jnp.bfloat16),
             pltpu.VMEM(rotary.shape, jnp.bfloat16),
             pltpu.VMEM((half, width), jnp.bfloat16),
-            pltpu.SemaphoreType.DMA((8,)),
+            pltpu.SemaphoreType.DMA((11,)),
         ],
         compiler_params=grant(60),
         cost_estimate=cost(1200000000, 2000000),
         name="attention",
-    )(attn_gain, tokens, segment_ids, jnp.swapaxes(qkv_weight, 1, 2), rotary, attn_out)
-    own_slice, merged = lax.optimization_barrier((own_slice, merged))
-    part = jnp.concatenate([own_slice] + others(own_slice, "zh"), axis=0)
-    merged, part = lax.optimization_barrier((exchange(merged, "term"), part))
+    )(
+        attn_gain,
+        tokens,
+        segment_ids,
+        jnp.swapaxes(qkv_weight, 1, 2),
+        rotary,
+        attn_out,
+        ffn_in_rows,
+        ffn_out,
+    )
+    pieces, merged, shard = lax.optimization_barrier((pieces, merged, shard))
+    part = jnp.concatenate([own_slice] + pieces, axis=0)
     table = lax.all_gather(part, "y", axis=0, tiled=True)
+    merged, near_half = lax.optimization_barrier(
+        (exchange(merged, "term"), swap(shard, "term", 1))
+    )
     other = swap(merged[:, head_width:], "core")
-    after_attn, partial = pl.pallas_call(
+    far_half = swap(near_half, "core")
+    after_ffn, partial = pl.pallas_call(
         ffn_kernel,
         out_shape=(
-            jax.ShapeDtypeStruct((length // tensor, width), jnp.float32),
+            jax.ShapeDtypeStruct((length, width), jnp.float32),
             jax.ShapeDtypeStruct((length, width), jnp.bfloat16),
         ),
-        in_specs=[vmem()] * 6,
+        in_specs=[vmem()] * 8,
         out_specs=(vmem(), vmem()),
         scratch_shapes=[
             pltpu.VMEM((width, width), jnp.bfloat16),
-            pltpu.VMEM((length, width), jnp.float32),
+            pltpu.VMEM((3, 4 * units, width), jnp.bfloat16),
         ],
         compiler_params=grant(20),
-        cost_estimate=cost(700000000, 4000000),
+        cost_estimate=cost(1200000000, 4000000),
         name="ffn",
-    )(tokens, merged, other, mlp_gain, jnp.swapaxes(ffn_in, 1, 2), ffn_out)
+    )(tokens, merged, other, mlp_gain, ffn_in_rows, ffn_out, near_half, far_half)
     bounds, mask = pl.pallas_call(
         prep_kernel,
         out_shape=(
@@ -397,19 +438,17 @@
         cost_estimate=cost(1000000, 1000000),
         name="prep",
     )(segment_ids, block_lists, doc_ids[:, None])
-    partials = exchange(partial.reshape(tensor, -1, width), "term")
-    partials, bounds, mask = lax.optimization_barrier((partials, bounds, mask))
+    rest = swap(partial, "term", 3)
+    rest, bounds, mask = lax.optimization_barrier((rest, bounds, mask))
     headed = pl.pallas_call(
         head_kernel,
-        out_shape=jax.ShapeDtypeStruct((tensor, length // tensor, width), jnp.bfloat16),
+        out_shape=jax.ShapeDtypeStruct((length, width), jnp.bfloat16),
         in_specs=[vmem()] * 5,
         out_specs=vmem(),
         compiler_params=grant(20),
         cost_estimate=cost(800000000, 5000000),
         name="head",
-    )(after_attn, partials, final_gain, head_dense, head_gain)
-
-    headed = exchange(headed, "term").reshape(length, width)
+    )(after_ffn, rest, final_gain, head_dense, head_gain)
 
     far = swap(headed, "zl")
     core = swap(headed, "core")

time: 130 us -> 150 us (1.15)
  waiting for transfers between devices: 29.9 us -> 53.2 us
  blocking collectives: 8.67 us -> 0 us
  local copies, waits for them, and re-layouts: 4.22 us -> 7.17 us
  starting transfers between devices: 53.7 us -> 55.4 us
    ppermute x7 -> x10, waiting for transfers between devices: 10.9 us -> 42.6 us  [swap(): lax.ppermute(block, axis, [(i, i ^ d) for i in range(lax.axis_size(axis))])]
    all_to_all x1 -> x0, blocking collectives: 8.67 us -> none  [exchange(): return lax.all_to_all(copies, axis, split_axis=0, concat_axis=0, tiled=True)]
    ppermute x7 -> x10, starting transfers between devices: 33.6 us -> 40.4 us  [swap(): lax.ppermute(block, axis, [(i, i ^ d) for i in range(lax.axis_size(axis))])]
    all_to_all x3 -> x2, waiting for transfers between devices: 17.1 us -> 10.5 us  [exchange(): return lax.all_to_all(copies, axis, split_axis=0, concat_axis=0, tiled=True)]
    all_to_all x3 -> x2, starting transfers between devices: 20.1 us -> 15 us  [exchange(): return lax.all_to_all(copies, axis, split_axis=0, concat_axis=0, tiled=True)]
    unnamed x28 -> x32, local copies, waits for them, and re-layouts: 3.22 us -> 6.17 us
    all_gather x1, waiting for transfers between devices: 1.92 us -> 0.02 us  [on_device(): table = lax.all_gather(part, 'y', axis=0, tiled=True)]
  transfers between devices with their start and end apart: 11 -> 13, of which waited for: 7 -> 6; matrix products, arithmetic and copies ran while one was open for 1% -> 1% of each run, Pallas kernels for 6% -> 8%
where the time goes in v8:
time: 150 us; the launch traced here: 149 us
  starting transfers between devices  55.4 us (37%)
  waiting for transfers between devices  53.2 us (35%)
  Pallas kernels  18.3 us (12%)
  between operations  13.8 us (9%)
  local copies, waits for them, and re-layouts  7.17 us (5%)
    ppermute x10, waiting for transfers between devices, swap(): lax.ppermute(block, axis, [(i, i ^ d) for i in range(lax.axis_size(axis))])  42.6 us
    ppermute x10, starting transfers between devices, swap(): lax.ppermute(block, axis, [(i, i ^ d) for i in range(lax.axis_size(axis))])  40.4 us
    all_to_all x2, starting transfers between devices, exchange(): return lax.all_to_all(copies, axis, split_axis=0, concat_axis=0, tiled=True)  15 us
    all_to_all x2, waiting for transfers between devices, exchange(): return lax.all_to_all(copies, axis, split_axis=0, concat_axis=0, tiled=True)  10.5 us
    unnamed x32, local copies, waits for them, and re-layouts  6.17 us
    pallas_call x1, Pallas kernels, on_device(): pl.pallas_call(far_pool_kernel, out_shape=jax.ShapeDtypeStruct((slices, 2...  4.8 us
    pallas_call x1, Pallas kernels, on_device(): pl.pallas_call(attention_kernel, out_shape=(jax.ShapeDtypeStruct((tensor,...  4.16 us
    pallas_call x1, Pallas kernels, on_device(): pl.pallas_call(near_pool_kernel, out_shape=jax.ShapeDtypeStruct((2 * PASS...  4.07 us
  transfers between devices with their start and end apart: 13, of which 6 were waited for; matrix products, arithmetic and copies ran while one was open for 1% of the time, Pallas kernels for 8%

profile of v8, /device:TPU:1, one launch (start us, length us, event | category | flops | bytes accessed | tf_op | source)
XLA Modules:
  0.0 148.6 jit_solution(1671289023074193305)
XLA Ops:
  6.5 6.8 %collective-permute-start = (bf16[64,768]{1,0:T(8,128)(2,1)}, bf16[64,768]{1,0:T(8,128)(2,1)S(1)}, u32[]{:S(2)}, u32[]{:S(2)}) collective-permute-start(bf16[64,768]{1,0:T(8,128)(2,1)} %bitcast.21), channel_id=1, source_target_pairs={{0,16},{16,0},{32,48},{48,32},{1,17},{17,1},{33,49},{49,33},{2,18}... | collective-permute-start | bytes 294920 | tf_op jit(solution)/shard_map/ppermute | solution.py:331
  13.3 8.8 %collective-permute-start.1 = (bf16[64,768]{1,0:T(8,128)(2,1)}, bf16[64,768]{1,0:T(8,128)(2,1)S(1)}, u32[]{:S(2)}, u32[]{:S(2)}) collective-permute-start(bf16[64,768]{1,0:T(8,128)(2,1)} %bitcast.22), channel_id=1, source_target_pairs={{0,32},{16,48},{32,0},{48,16},{1,33},{17,49},{33,1},{49,17},{2,34}... | collective-permute-start | bytes 294920 | tf_op jit(solution)/shard_map/ppermute | solution.py:331
  22.2 1.9 %collective-permute-start.2 = (bf16[64,768]{1,0:T(8,128)(2,1)}, bf16[64,768]{1,0:T(8,128)(2,1)S(1)}, u32[]{:S(2)}, u32[]{:S(2)}) collective-permute-start(bf16[64,768]{1,0:T(8,128)(2,1)} %bitcast.23), channel_id=1, source_target_pairs={{0,48},{16,32},{32,16},{48,0},{1,49},{17,33},{33,17},{49,1},{2,50}... | collective-permute-start | bytes 294920 | tf_op jit(solution)/shard_map/ppermute | solution.py:331
  24.1 4.2 %attention.1 = (bf16[4,480,256]{2,1,0:T(8,128)(2,1)}, bf16[432,768]{1,0:T(8,128)(2,1)}) custom-call(f32[768]{0:T(1024)} %gain_hbm.1, bf16[256,768]{1,0:T(8,128)(2,1)} %bitcast.18, s32[128,256]{1,0:T(8,128)} %segment_ref.1, bf16[3,192,768]{2,1,0:T(8,128)(2,1)} %bitcast.27, bf16[192,256]{1,0:T(8,128)(2,1)} %constant.22.clone.table_hbm, ...), custom_call_target="tpu_custom_call" | custom-call | flops 1200000000 | bytes 2000000 | tf_op jit(solution)/shard_map/attention/pallas_call | solution.py:375
  28.3 3.9 %collective-permute-done.2 = bf16[64,768]{1,0:T(8,128)(2,1)S(1)} collective-permute-done((bf16[64,768]{1,0:T(8,128)(2,1)}, bf16[64,768]{1,0:T(8,128)(2,1)S(1)}, u32[]{:S(2)}, u32[]{:S(2)}) %collective-permute-start.2) | collective-permute-done | bytes 98336 | tf_op jit(solution)/shard_map/ppermute | solution.py:331
  32.2 0.8 pad_maximum_fusion
  33.0 4.0 %all-to-all-start = ((bf16[4,480,256]{2,1,0:T(8,128)(2,1)}), bf16[4,480,256]{2,1,0:T(8,128)(2,1)S(1)}, u32[]{:S(2)}, u32[]{:S(2)}) async-start(bf16[4,480,256]{2,1,0:T(8,128)(2,1)} %get-tuple-element.23), calls=%async_computation | async-start | bytes 1966080 | tf_op jit(solution)/shard_map/all_to_all | solution.py:327
  37.0 3.5 %collective-permute-start.3 = (bf16[432,768]{1,0:T(8,128)(2,1)}, bf16[432,768]{1,0:T(8,128)(2,1)S(1)}, u32[]{:S(2)}, u32[]{:S(2)}) collective-permute-start(bf16[432,768]{1,0:T(8,128)(2,1)} %get-tuple-element.24), channel_id=1, source_target_pairs={{0,1},{1,0},{2,3},{3,2},{4,5},{5,4},{6,7},{7,6},{8,9},{9,8},{10,11... | collective-permute-start | bytes 1990664 | tf_op jit(solution)/shard_map/ppermute | solution.py:331
  40.5 23.0 %collective-permute-done.3.near_half_ref = bf16[432,768]{1,0:T(8,128)(2,1)S(1)} collective-permute-done((bf16[432,768]{1,0:T(8,128)(2,1)}, bf16[432,768]{1,0:T(8,128)(2,1)S(1)}, u32[]{:S(2)}, u32[]{:S(2)}) %collective-permute-start.3) | collective-permute-done | bytes 663584 | tf_op jit(solution)/shard_map/ppermute | solution.py:331
  63.5 3.5 %collective-permute-start.5 = (bf16[432,768]{1,0:T(8,128)(2,1)S(1)}, bf16[432,768]{1,0:T(8,128)(2,1)S(1)}, u32[]{:S(2)}, u32[]{:S(2)}) collective-permute-start(bf16[432,768]{1,0:T(8,128)(2,1)S(1)} %collective-permute-done.3.near_half_ref), channel_id=1, source_target_pairs={{0,4},{4,0},{1,5},{5,1},{2,6},{6,2},{3,7},{7,3},{8,12},{12,8},{9,1... | collective-permute-start | bytes 1990664 | tf_op jit(solution)/shard_map/ppermute | solution.py:331
  67.0 1.9 %collective-permute-start.4 = (bf16[4,288,256]{2,1,0:T(8,128)(2,1)S(1)}, bf16[4,288,256]{2,1,0:T(8,128)(2,1)S(1)}, u32[]{:S(2)}, u32[]{:S(2)}) collective-permute-start(bf16[4,288,256]{2,1,0:T(8,128)(2,1)S(1)} %slice.3), channel_id=1, source_target_pairs={{0,4},{4,0},{1,5},{5,1},{2,6},{6,2},{3,7},{7,3},{8,12},{12,8},{9,1... | collective-permute-start | bytes 1769480 | tf_op jit(solution)/shard_map/ppermute | solution.py:331
  69.0 2.0 %collective-permute-done.4.other_ref = bf16[4,288,256]{2,1,0:T(8,128)(2,1)S(1)} collective-permute-done((bf16[4,288,256]{2,1,0:T(8,128)(2,1)S(1)}, bf16[4,288,256]{2,1,0:T(8,128)(2,1)S(1)}, u32[]{:S(2)}, u32[]{:S(2)}) %collective-permute-start.4) | collective-permute-done | bytes 589856 | tf_op jit(solution)/shard_map/ppermute | solution.py:331
  71.0 2.7 %ffn.1 = (f32[256,768]{1,0:T(8,128)S(1)}, bf16[256,768]{1,0:T(8,128)(2,1)}) custom-call(bf16[256,768]{1,0:T(8,128)(2,1)S(1)} %bitcast.19, bf16[4,480,256]{2,1,0:T(8,128)(2,1)S(1)} %all-to-all-done.merged_ref, bf16[4,288,256]{2,1,0:T(8,128)(2,1)S(1)} %collective-permute-done.4.other_ref, f32[768]{0:T(1024)S(1)} %copy-done.5, ...), custom_call_target="tpu_custom_call" | custom-call | flops 1200000000 | bytes 4000000 | tf_op jit(solution)/shard_map/ffn/pallas_call | solution.py:413
  73.7 0.9 copy-done.9
  74.6 3.7 %collective-permute-start.6 = (bf16[256,768]{1,0:T(8,128)(2,1)}, bf16[256,768]{1,0:T(8,128)(2,1)S(1)}, u32[]{:S(2)}, u32[]{:S(2)}) collective-permute-start(bf16[256,768]{1,0:T(8,128)(2,1)} %get-tuple-element.27), channel_id=1, source_target_pairs={{0,3},{1,2},{2,1},{3,0},{4,7},{5,6},{6,5},{7,4},{8,11},{9,10},{10,... | collective-permute-start | bytes 1179656 | tf_op jit(solution)/shard_map/ppermute | solution.py:331
  78.5 0.9 copy-done.3
  79.5 0.4 prep.1
  79.9 8.6 %collective-permute-done.6.partial_ref = bf16[256,768]{1,0:T(8,128)(2,1)S(1)} collective-permute-done((bf16[256,768]{1,0:T(8,128)(2,1)}, bf16[256,768]{1,0:T(8,128)(2,1)S(1)}, u32[]{:S(2)}, u32[]{:S(2)}) %collective-permute-start.6) | collective-permute-done | bytes 393248 | tf_op jit(solution)/shard_map/ppermute | solution.py:331
  88.5 1.3 copy-done.8
  89.8 1.1 copy-done.10
  90.9 0.9 head.1.own_ref
  91.8 3.5 %collective-permute-start.7 = (bf16[256,768]{1,0:T(8,128)(2,1)S(1)}, bf16[256,768]{1,0:T(8,128)(2,1)S(1)}, u32[]{:S(2)}, u32[]{:S(2)}) collective-permute-start(bf16[256,768]{1,0:T(8,128)(2,1)S(1)} %head.1.own_ref), channel_id=1, source_target_pairs={{0,8},{8,0},{1,9},{9,1},{2,10},{10,2},{3,11},{11,3},{4,12},{12,4},... | collective-permute-start | bytes 1179656 | tf_op jit(solution)/shard_map/ppermute | solution.py:331
  95.3 3.1 %collective-permute-start.9 = (bf16[256,768]{1,0:T(8,128)(2,1)S(1)}, bf16[256,768]{1,0:T(8,128)(2,1)S(1)}, u32[]{:S(2)}, u32[]{:S(2)}) collective-permute-start(bf16[256,768]{1,0:T(8,128)(2,1)S(1)} %head.1.own_ref), channel_id=1, source_target_pairs={{0,4},{4,0},{1,5},{5,1},{2,6},{6,2},{3,7},{7,3},{8,12},{12,8},{9,1... | collective-permute-start | bytes 1179656 | tf_op jit(solution)/shard_map/ppermute | solution.py:331
  98.4 5.2 %collective-permute-done.7.far_ref = bf16[256,768]{1,0:T(8,128)(2,1)S(1)} collective-permute-done((bf16[256,768]{1,0:T(8,128)(2,1)S(1)}, bf16[256,768]{1,0:T(8,128)(2,1)S(1)}, u32[]{:S(2)}, u32[]{:S(2)}) %collective-permute-start.7) | collective-permute-done | bytes 393248 | tf_op jit(solution)/shard_map/ppermute | solution.py:331
  103.7 3.6 %collective-permute-start.8 = (bf16[256,768]{1,0:T(8,128)(2,1)S(1)}, bf16[256,768]{1,0:T(8,128)(2,1)S(1)}, u32[]{:S(2)}, u32[]{:S(2)}) collective-permute-start(bf16[256,768]{1,0:T(8,128)(2,1)S(1)} %collective-permute-done.7.far_ref), channel_id=1, source_target_pairs={{0,4},{4,0},{1,5},{5,1},{2,6},{6,2},{3,7},{7,3},{8,12},{12,8},{9,1... | collective-permute-start | bytes 1179656 | tf_op jit(solution)/shard_map/ppermute | solution.py:331
  107.5 1.9 %copy-done.6 = bf16[2048,768]{1,0:T(8,128)(2,1)S(1)} copy-done((bf16[2048,768]{1,0:T(8,128)(2,1)S(1)}, bf16[2048,768]{1,0:T(8,128)(2,1)}, u32[]{:S(2)}) %copy-start.6) | copy-done | bytes 3145752
  109.4 4.1 %near_pool.1.low_ref = f32[8,2048]{1,0:T(8,128)S(1)} custom-call(s32[128,8]{1,0:T(8,128)S(1)} %get-tuple-element.30.bounds_ref, bf16[256,768]{1,0:T(8,128)(2,1)S(1)} %head.1.own_ref, bf16[256,768]{1,0:T(8,128)(2,1)S(1)} %collective-permute-done.9.core_ref, bf16[2048,768]{1,0:T(8,128)(2,1)S(1)} %copy-done.6), custom_call_target="tpu_custom_call" | custom-call | flops 1600000000 | bytes 4000000 | tf_op jit(solution)/shard_map/near_pool/pallas_call | solution.py:457
  113.5 4.8 %far_pool.1 = f32[32,8,128]{2,1,0:T(8,128)} custom-call(s32[128,8]{1,0:T(8,128)S(1)} %get-tuple-element.30.bounds_ref, bf16[256,768]{1,0:T(8,128)(2,1)S(1)} %collective-permute-done.7.far_ref, bf16[256,768]{1,0:T(8,128)(2,1)S(1)} %collective-permute-done.8.far_core_ref, bf16[2048,768]{1,0:T(8,128)(2,1)S(1)} %copy-done.7, f32[8,2048]{1,0:T(8,128)S(1)} %near_pool.1.low_ref), custom_call_target="tpu_custom_call" | custom-call | flops 1600000000 | bytes 4000000 | tf_op jit(solution)/shard_map/far_pool/pallas_call | solution.py:468
  118.3 11.0 %all-to-all-start.1 = ((f32[32,8,128]{2,1,0:T(8,128)}), f32[32,8,128]{2,1,0:T(8,128)S(1)}, u32[]{:S(2)}, u32[]{:S(2)}) async-start(f32[32,8,128]{2,1,0:T(8,128)} %far_pool.1), calls=%async_computation.1 | async-start | bytes 262144 | tf_op jit(solution)/shard_map/all_to_all | solution.py:327
  129.8 0.1 reshape.39.docs_ref
  130.1 10.5 %all-to-all-done.1 = f32[32,8,128]{2,1,0:T(8,128)S(1)} async-done(((f32[32,8,128]{2,1,0:T(8,128)}), f32[32,8,128]{2,1,0:T(8,128)S(1)}, u32[]{:S(2)}, u32[]{:S(2)}) %all-to-all-start.1) | async-done | bytes 131104 | tf_op jit(solution)/shard_map/all_to_all | solution.py:327
  140.6 1.2 place.1
  (48 shorter events, 1.1 us)
Async XLA Ops:
  6.5 25.6 %copy-start.13 = (bf16[1,8,1,8,768]{4,3,2,1,0:T(8,128)(2,1)S(1)}, bf16[1,8,1,8,768]{4,3,2,1,0:T(8,128)(2,1)}, u32[]{:S(2)}) copy-start(bf16[1,8,1,8,768]{4,3,2,1,0:T(8,128)(2,1)} %param.29) | copy-start | bytes 294916
  6.5 100.9 %all-gather.2.cloned.1.call-start = ((), (), s32[]{:S(2)}) async-start(), calls=%async_computation.2 | async-start | bytes 3538944 | tf_op jit(solution)/shard_map/all_gather | solution.py:407
  6.5 21.8 %collective-permute-start = (bf16[64,768]{1,0:T(8,128)(2,1)}, bf16[64,768]{1,0:T(8,128)(2,1)S(1)}, u32[]{:S(2)}, u32[]{:S(2)}) collective-permute-start(bf16[64,768]{1,0:T(8,128)(2,1)} %bitcast.21), channel_id=1, source_target_pairs={{0,16},{16,0},{32,48},{48,32},{1,17},{17,1},{33,49},{49,33},{2,18}... | collective-permute-start | bytes 294920 | tf_op jit(solution)/shard_map/ppermute | solution.py:331
  13.3 15.0 %collective-permute-start.1 = (bf16[64,768]{1,0:T(8,128)(2,1)}, bf16[64,768]{1,0:T(8,128)(2,1)S(1)}, u32[]{:S(2)}, u32[]{:S(2)}) collective-permute-start(bf16[64,768]{1,0:T(8,128)(2,1)} %bitcast.22), channel_id=1, source_target_pairs={{0,32},{16,48},{32,0},{48,16},{1,33},{17,49},{33,1},{49,17},{2,34}... | collective-permute-start | bytes 294920 | tf_op jit(solution)/shard_map/ppermute | solution.py:331
  22.2 10.0 %collective-permute-start.2 = (bf16[64,768]{1,0:T(8,128)(2,1)}, bf16[64,768]{1,0:T(8,128)(2,1)S(1)}, u32[]{:S(2)}, u32[]{:S(2)}) collective-permute-start(bf16[64,768]{1,0:T(8,128)(2,1)} %bitcast.23), channel_id=1, source_target_pairs={{0,48},{16,32},{32,16},{48,0},{1,49},{17,33},{33,17},{49,1},{2,50}... | collective-permute-start | bytes 294920 | tf_op jit(solution)/shard_map/ppermute | solution.py:331
  28.2 42.7 %copy-start = (bf16[2,768,288]{1,2,0:T(8,128)(2,1)S(1)}, bf16[2,768,288]{1,2,0:T(8,128)(2,1)}, u32[]{:S(2)}) copy-start(bf16[2,768,288]{1,2,0:T(8,128)(2,1)} %param.24) | copy-start | bytes 2654212
  28.3 42.7 %copy-start.1 = (bf16[288,768]{1,0:T(8,128)(2,1)S(1)}, bf16[288,768]{1,0:T(8,128)(2,1)}, u32[]{:S(2)}) copy-start(bf16[288,768]{1,0:T(8,128)(2,1)} %down_ref.1) | copy-start | bytes 1327108
  28.3 42.7 %copy-start.2 = (bf16[1,256,768]{2,1,0:T(8,128)(2,1)S(1)}, bf16[1,256,768]{2,1,0:T(8,128)(2,1)}, u32[]{:S(2)}) copy-start(bf16[1,256,768]{2,1,0:T(8,128)(2,1)} %param.16) | copy-start | bytes 1179652
  28.3 42.7 %copy-start.5 = (f32[768]{0:T(1024)S(1)}, f32[768]{0:T(1024)}, u32[]{:S(2)}) copy-start(f32[768]{0:T(1024)} %gain_ref.1) | copy-start | bytes 9220
  33.0 30.5 %all-to-all-start = ((bf16[4,480,256]{2,1,0:T(8,128)(2,1)}), bf16[4,480,256]{2,1,0:T(8,128)(2,1)S(1)}, u32[]{:S(2)}, u32[]{:S(2)}) async-start(bf16[4,480,256]{2,1,0:T(8,128)(2,1)} %get-tuple-element.23), calls=%async_computation | async-start | bytes 1966080 | tf_op jit(solution)/shard_map/all_to_all | solution.py:327
  37.0 41.3 %copy-start.14 = (s32[512]{0:T(512)S(1)}, s32[512]{0:T(512)}, u32[]{:S(2)}) copy-start(s32[512]{0:T(512)} %param.19) | copy-start | bytes 6148
  37.0 41.5 %copy-start.4 = (s32[128,256]{1,0:T(8,128)S(1)}, s32[128,256]{1,0:T(8,128)}, u32[]{:S(2)}) copy-start(s32[128,256]{1,0:T(8,128)} %segment_ref.1) | copy-start | bytes 393220
  37.0 51.5 %copy-start.11 = (f32[768]{0:T(1024)S(1)}, f32[768]{0:T(1024)}, u32[]{:S(2)}) copy-start(f32[768]{0:T(1024)} %final_ref.1) | copy-start | bytes 9220
  37.0 51.5 %copy-start.12 = (f32[768]{0:T(1024)S(1)}, f32[768]{0:T(1024)}, u32[]{:S(2)}) copy-start(f32[768]{0:T(1024)} %head_ref.1) | copy-start | bytes 9220
  37.0 26.5 %collective-permute-start.3 = (bf16[432,768]{1,0:T(8,128)(2,1)}, bf16[432,768]{1,0:T(8,128)(2,1)S(1)}, u32[]{:S(2)}, u32[]{:S(2)}) collective-permute-start(bf16[432,768]{1,0:T(8,128)(2,1)} %get-tuple-element.24), channel_id=1, source_target_pairs={{0,1},{1,0},{2,3},{3,2},{4,5},{5,4},{6,7},{7,6},{8,9},{9,8},{10,11... | collective-permute-start | bytes 1990664 | tf_op jit(solution)/shard_map/ppermute | solution.py:331
  63.5 7.4 %collective-permute-start.5 = (bf16[432,768]{1,0:T(8,128)(2,1)S(1)}, bf16[432,768]{1,0:T(8,128)(2,1)S(1)}, u32[]{:S(2)}, u32[]{:S(2)}) collective-permute-start(bf16[432,768]{1,0:T(8,128)(2,1)S(1)} %collective-permute-done.3.near_half_ref), channel_id=1, source_target_pairs={{0,4},{4,0},{1,5},{5,1},{2,6},{6,2},{3,7},{7,3},{8,12},{12,8},{9,1... | collective-permute-start | bytes 1990664 | tf_op jit(solution)/shard_map/ppermute | solution.py:331
  67.0 3.9 %collective-permute-start.4 = (bf16[4,288,256]{2,1,0:T(8,128)(2,1)S(1)}, bf16[4,288,256]{2,1,0:T(8,128)(2,1)S(1)}, u32[]{:S(2)}, u32[]{:S(2)}) collective-permute-start(bf16[4,288,256]{2,1,0:T(8,128)(2,1)S(1)} %slice.3), channel_id=1, source_target_pairs={{0,4},{4,0},{1,5},{5,1},{2,6},{6,2},{3,7},{7,3},{8,12},{12,8},{9,1... | collective-permute-start | bytes 1769480 | tf_op jit(solution)/shard_map/ppermute | solution.py:331
  73.7 0.9 copy-start.9
  74.6 13.9 %collective-permute-start.6 = (bf16[256,768]{1,0:T(8,128)(2,1)}, bf16[256,768]{1,0:T(8,128)(2,1)S(1)}, u32[]{:S(2)}, u32[]{:S(2)}) collective-permute-start(bf16[256,768]{1,0:T(8,128)(2,1)} %get-tuple-element.27), channel_id=1, source_target_pairs={{0,3},{1,2},{2,1},{3,0},{4,7},{5,6},{6,5},{7,4},{8,11},{9,10},{10,... | collective-permute-start | bytes 1179656 | tf_op jit(solution)/shard_map/ppermute | solution.py:331
  78.5 1.0 copy-start.3
  88.5 1.3 copy-start.8
  89.8 1.1 copy-start.10
  91.8 11.9 %collective-permute-start.7 = (bf16[256,768]{1,0:T(8,128)(2,1)S(1)}, bf16[256,768]{1,0:T(8,128)(2,1)S(1)}, u32[]{:S(2)}, u32[]{:S(2)}) collective-permute-start(bf16[256,768]{1,0:T(8,128)(2,1)S(1)} %head.1.own_ref), channel_id=1, source_target_pairs={{0,8},{8,0},{1,9},{9,1},{2,10},{10,2},{3,11},{11,3},{4,12},{12,4},... | collective-permute-start | bytes 1179656 | tf_op jit(solution)/shard_map/ppermute | solution.py:331
  95.3 12.1 %collective-permute-start.9 = (bf16[256,768]{1,0:T(8,128)(2,1)S(1)}, bf16[256,768]{1,0:T(8,128)(2,1)S(1)}, u32[]{:S(2)}, u32[]{:S(2)}) collective-permute-start(bf16[256,768]{1,0:T(8,128)(2,1)S(1)} %head.1.own_ref), channel_id=1, source_target_pairs={{0,4},{4,0},{1,5},{5,1},{2,6},{6,2},{3,7},{7,3},{8,12},{12,8},{9,1... | collective-permute-start | bytes 1179656 | tf_op jit(solution)/shard_map/ppermute | solution.py:331
  103.7 9.8 %collective-permute-start.8 = (bf16[256,768]{1,0:T(8,128)(2,1)S(1)}, bf16[256,768]{1,0:T(8,128)(2,1)S(1)}, u32[]{:S(2)}, u32[]{:S(2)}) collective-permute-start(bf16[256,768]{1,0:T(8,128)(2,1)S(1)} %collective-permute-done.7.far_ref), channel_id=1, source_target_pairs={{0,4},{4,0},{1,5},{5,1},{2,6},{6,2},{3,7},{7,3},{8,12},{12,8},{9,1... | collective-permute-start | bytes 1179656 | tf_op jit(solution)/shard_map/ppermute | solution.py:331
  107.5 1.9 %copy-start.6 = (bf16[2048,768]{1,0:T(8,128)(2,1)S(1)}, bf16[2048,768]{1,0:T(8,128)(2,1)}, u32[]{:S(2)}) copy-start(bf16[2048,768]{1,0:T(8,128)(2,1)} %all-gather.2.cloned.1.call-done.table_ref) | copy-start | bytes 9437188
  109.4 4.1 %copy-start.7 = (bf16[2048,768]{1,0:T(8,128)(2,1)S(1)}, bf16[2048,768]{1,0:T(8,128)(2,1)}, u32[]{:S(2)}) copy-start(bf16[2048,768]{1,0:T(8,128)(2,1)} %all-gather.2.cloned.1.call-done.table_ref) | copy-start | bytes 9437188
  113.4 16.5 %copy-start.15 = (bf16[1,8,1,8]{3,1,2,0:T(8,128)(2,1)S(1)}, bf16[1,8,1,8]{3,1,2,0:T(8,128)(2,1)}, u32[]{:S(2)}) copy-start(bf16[1,8,1,8]{3,1,2,0:T(8,128)(2,1)} %param.30) | copy-start | bytes 388
  118.3 22.3 %all-to-all-start.1 = ((f32[32,8,128]{2,1,0:T(8,128)}), f32[32,8,128]{2,1,0:T(8,128)S(1)}, u32[]{:S(2)}, u32[]{:S(2)}) async-start(f32[32,8,128]{2,1,0:T(8,128)} %far_pool.1), calls=%async_computation.1 | async-start | bytes 262144 | tf_op jit(solution)/shard_map/all_to_all | solution.py:327
Sparse Core Ops, SparseCore 0:
  33.1 46.7 all-gather.1

commit v9 on v7

--- a/solution.py
+++ b/solution.py
@@ -75,21 +75,29 @@
     length = hidden_ref.shape[0]
     row = row_index()
     tile = pl.multiple_of(lax.shift_left(lax.shift_right_logical(row, 3), 3), 8)
-    copies = [
-        pltpu.make_async_copy(hidden_hbm, hidden_ref, sems.at[0]),
-        pltpu.make_async_copy(segment_hbm.at[pl.ds(tile, 8), :], segment_ref, sems.at[1]),
-        pltpu.make_async_copy(table_hbm, table_ref, sems.at[2]),
-    ] + [
-        pltpu.make_async_copy(weight_hbm.at[slot], weight_ref.at[slot], sems.at[3 + slot])
+    sem = iter(range(sems.shape[0]))
+
+    def fetch(source, to):
+        return pltpu.make_async_copy(source, to, sems.at[next(sem)])
+
+    share = length // 4
+    cuts = [slice(i * share, (i + 1) * share) for i in range(4)]
+    hidden_copies = [fetch(hidden_hbm.at[cut, :], hidden_ref.at[cut, :]) for cut in cuts]
+    hidden_copies.append(fetch(gain_hbm, gain_ref))
+    segment_copy = fetch(segment_hbm.at[pl.ds(tile, 8), :], segment_ref)
+    table_copy = fetch(table_hbm, table_ref)
+    half = half_ref.shape[0]
+    weight_copies = [
+        fetch(weight_hbm.at[slot, cut, :], weight_ref.at[slot, cut, :])
         for slot in range(3)
+        for cut in (slice(0, half), slice(half, 2 * half))
     ]
-    half = half_ref.shape[0]
     own_rows = pl.ds(pl.multiple_of(lax.axis_index("core") * half, half), half)
-    copies.append(pltpu.make_async_copy(out_weight_hbm.at[own_rows, :], half_ref, sems.at[6]))
-    copies.append(pltpu.make_async_copy(gain_hbm, gain_ref, sems.at[7]))
+    half_copy = fetch(out_weight_hbm.at[own_rows, :], half_ref)
+    copies = hidden_copies + [segment_copy, table_copy] + weight_copies + [half_copy]
     for copy in copies:
         copy.start()
-    copies[1].wait()
+    segment_copy.wait()
     head_width = weight_ref.shape[1]
     segments = segment_ref[pl.ds(row - tile, 1), :]
     starts = jnp.zeros_like(segments)
@@ -99,7 +107,7 @@
     lane = lax.broadcasted_iota(jnp.int32, (1, length), 1)
     positions = lane - starts
     sublane = lax.broadcasted_iota(jnp.int32, (length, length), 0)
-    copies[2].wait()
+    table_copy.wait()
     chosen = (sublane == positions).astype(jnp.float32).astype(jnp.bfloat16)
     parts = matmul(table_ref[...], chosen, (((1,), (0,)), ((), ())))
     part = [parts[i * HALF_HEAD : (i + 1) * HALF_HEAD] for i in range(6)]
@@ -113,11 +121,11 @@
     high = jnp.minimum(starts + lengths - 1, lane + HALF_WIN)
     allowed = (sublane >= low) & (sublane <= high)
 
-    copies[0].wait()
-    copies[7].wait()
+    for copy in hidden_copies:
+        copy.wait()
     gain = gain_ref[...].reshape(1, -1)
     normed = layer_norm(hidden_ref[...].astype(jnp.float32), gain).astype(jnp.bfloat16)
-    for copy in copies[3:6]:
+    for copy in weight_copies:
         copy.wait()
     queries = matmul(weight_ref[0], normed, NT)
     key_cols = matmul(weight_ref[1], normed, NT)
@@ -138,7 +146,7 @@
         context = matmul(values[at], probabilities, (((1,), (0,)), ((), ()))).astype(jnp.bfloat16)
         for copy in range(out_ref.shape[0]):
             out_ref[copy, at, :] = context
-    copies[6].wait()
+    half_copy.wait()
     for column in range(half_ref.shape[1] // length):
         block = half_ref[:, column * length : (column + 1) * length]
         at = slice(head_width + column * half, head_width + (column + 1) * half)
@@ -213,15 +221,12 @@
         mask_ref[group * SPAN : (group + 1) * SPAN, :] = held.astype(jnp.float32)
 
 
-def passage_maxima(bounds_ref, first_row, rows, table_ref, logits_ref):
-    length = rows[0].shape[0]
-    stacked = jnp.concatenate([row[...] for row in rows], axis=0)
-    logits_ref[...] = matmul(stacked, table_ref[...], NT)
+def passage_maxima(bounds_ref, rows, length, logits_ref):
     tile = 8
     sublane = lax.broadcasted_iota(jnp.int32, (tile, logits_ref.shape[1]), 0)
     maxima = []
-    for r in range(len(rows)):
-        row = row_index(first_row + r)
+    for r in range(rows):
+        row = row_index(r)
         for passage in range(PASS_DEV):
             first = bounds_ref[row, passage]
             end = bounds_ref[row, passage + 1]
@@ -243,22 +248,25 @@
     return jnp.concatenate(maxima, axis=0)
 
 
-def near_pool_kernel(bounds_ref, own_ref, core_ref, table_ref, low_ref, logits_ref):
-    rows = (own_ref, core_ref)
-    low_ref[...] = passage_maxima(bounds_ref, 0, rows, table_ref, logits_ref)
-
-
-def far_pool_kernel(
-    bounds_ref, far_ref, far_core_ref, table_ref, low_ref, out_ref, logits_ref
+def pool_kernel(
+    bounds_ref, own_ref, core_ref, far_ref, far_core_ref, table_ref, out_ref, rows_ref, logits_ref
 ):
-    rows = (far_ref, far_core_ref)
-    high = passage_maxima(bounds_ref, len(rows), rows, table_ref, logits_ref)
-    low = low_ref[...]
+    rows = (own_ref, core_ref, far_ref, far_core_ref)
+    length = own_ref.shape[0]
+
+    @pl.when(pl.program_id(0) == 0)
+    def _():
+        for r, row in enumerate(rows):
+            rows_ref[r * length : (r + 1) * length, :] = row[...]
+
+    logits_ref[...] = matmul(rows_ref[...], table_ref[...], NT)
+    maxima = passage_maxima(bounds_ref, len(rows), length, logits_ref)
+    half = maxima.shape[0] // 2
     own_terms = out_ref.shape[2] // 2
     for slot in range(out_ref.shape[0]):
         at = slice(slot * own_terms, (slot + 1) * own_terms)
         to = slot - slot % NEAR + jnp.bitwise_xor(lax.axis_index("zh"), slot % NEAR)
-        out_ref[to] = jnp.concatenate([low[:, at], high[:, at]], axis=1)
+        out_ref[to] = jnp.concatenate([maxima[:half, at], maxima[half:, at]], axis=1)
 
 
 def place_kernel(maxima_ref, bias_ref, mask_ref, docs_ref, out_ref):
@@ -358,7 +366,7 @@
             pltpu.VMEM((3, head_width, width), jnp.bfloat16),
             pltpu.VMEM(rotary.shape, jnp.bfloat16),
             pltpu.VMEM((half, width), jnp.bfloat16),
-            pltpu.SemaphoreType.DMA((8,)),
+            pltpu.SemaphoreType.DMA((14,)),
         ],
         compiler_params=grant(60),
         cost_estimate=cost(1200000000, 2000000),
@@ -413,29 +421,27 @@
 
     far = swap(headed, "zl")
     core = swap(headed, "core")
+    far_core = swap(far, "core")
     terms_here = slices * own_terms
-    logits = pltpu.VMEM((2 * length, terms_here), jnp.float32)
-    low = pl.pallas_call(
-        near_pool_kernel,
-        out_shape=jax.ShapeDtypeStruct((2 * PASS_DEV, terms_here), jnp.float32),
-        in_specs=[smem()] + [vmem()] * 3,
-        out_specs=vmem(),
-        scratch_shapes=[logits],
-        compiler_params=grant(20),
-        cost_estimate=cost(1600000000, 4000000),
-        name="near_pool",
-    )(bounds, headed, core, table)
-    far_core = swap(far, "core")
+    step = terms_here // 2
     pooled = pl.pallas_call(
-        far_pool_kernel,
+        pool_kernel,
         out_shape=jax.ShapeDtypeStruct((slices, 2 * PASS_DEV, 2 * own_terms), jnp.float32),
-        in_specs=[smem()] + [vmem()] * 4,
-        out_specs=vmem(),
-        scratch_shapes=[logits],
-        compiler_params=grant(20),
-        cost_estimate=cost(1600000000, 4000000),
-        name="far_pool",
-    )(bounds, far, far_core, table, low)
+        grid=(terms_here // step,),
+        in_specs=[smem()]
+        + [pl.BlockSpec((length, width), lambda j: (0, 0))] * rows_here
+        + [pl.BlockSpec((step, width), lambda j: (j, 0))],
+        out_specs=pl.BlockSpec(
+            (step // own_terms, 2 * PASS_DEV, 2 * own_terms), lambda j: (j, 0, 0)
+        ),
+        scratch_shapes=[
+            pltpu.VMEM((rows_here * length, width), jnp.bfloat16),
+            pltpu.VMEM((rows_here * length, step), jnp.float32),
+        ],
+        compiler_params=grant(56),
+        cost_estimate=cost(3300000000, 6000000),
+        name="pool",
+    )(bounds, headed, core, far, far_core, table)
     received = exchange(pooled, near)
 
     bias = decoder_bias.reshape(1, own_terms).astype(jnp.float32)

time: 130 us -> 127 us (0.977)
  local copies, waits for them, and re-layouts: 4.22 us -> 2.35 us
    unnamed x28 -> x34, local copies, waits for them, and re-layouts: 3.22 us -> 1.35 us
    pallas_call x2 -> x1, Pallas kernels: 8.86 us -> 8.19 us  [on_device(): pl.pallas_call(pool_kernel, out_shape=jax.ShapeDtypeStruct((slices, 2 * P...]
  transfers between devices with their start and end apart: 11 -> 11, of which waited for: 7 -> 8; matrix products, arithmetic and copies ran while one was open for 1% -> 1% of each run, Pallas kernels for 6% -> 3%
where the time goes in v9:
time: 127 us; the launch traced here: 126 us
  starting transfers between devices  53.8 us (42%)
  waiting for transfers between devices  29.9 us (24%)
  Pallas kernels  17.1 us (13%)
  between operations  13.7 us (11%)
  blocking collectives  8.65 us (7%)
  local copies, waits for them, and re-layouts  2.35 us (2%)
    ppermute x7, starting transfers between devices, swap(): lax.ppermute(block, axis, [(i, i ^ d) for i in range(lax.axis_size(axis))])  33.7 us
    all_to_all x3, starting transfers between devices, exchange(): return lax.all_to_all(copies, axis, split_axis=0, concat_axis=0, tiled=True)  20.1 us
    all_to_all x3, waiting for transfers between devices, exchange(): return lax.all_to_all(copies, axis, split_axis=0, concat_axis=0, tiled=True)  17.1 us
    ppermute x7, waiting for transfers between devices, swap(): lax.ppermute(block, axis, [(i, i ^ d) for i in range(lax.axis_size(axis))])  12 us
    all_to_all x1, blocking collectives, exchange(): return lax.all_to_all(copies, axis, split_axis=0, concat_axis=0, tiled=True)  8.65 us
    pallas_call x1, Pallas kernels, on_device(): pl.pallas_call(pool_kernel, out_shape=jax.ShapeDtypeStruct((slices, 2 * P...  8.19 us
    pallas_call x1, Pallas kernels, on_device(): pl.pallas_call(attention_kernel, out_shape=jax.ShapeDtypeStruct((tensor,...  4.08 us
  transfers between devices with their start and end apart: 11, of which 8 were waited for; matrix products, arithmetic and copies ran while one was open for 1% of the time, Pallas kernels for 3%

profile of v9, /device:TPU:1, one launch (start us, length us, event | category | flops | bytes accessed | tf_op | source)
XLA Modules:
  0.0 126.3 jit_solution(17358883897327343514)
XLA Ops:
  6.5 4.1 %attention.1 = bf16[4,480,256]{2,1,0:T(8,128)(2,1)} custom-call(f32[768]{0:T(1024)} %gain_hbm.1, bf16[256,768]{1,0:T(8,128)(2,1)} %bitcast.19, s32[128,256]{1,0:T(8,128)} %segment_ref.1, bf16[3,192,768]{2,1,0:T(8,128)(2,1)} %bitcast.31, bf16[192,256]{1,0:T(8,128)(2,1)} %constant.22.clone.table_hbm, bf16[192,768]{1,0:T(8,128)(2,1)} %out_weight_hbm.1), custom_call_target="tpu_custom_call" | custom-call | flops 1200000000 | bytes 2000000 | tf_op jit(solution)/shard_map/attention/pallas_call | solution.py:357
  10.7 5.0 %all-to-all-start = ((bf16[4,480,256]{2,1,0:T(8,128)(2,1)}), bf16[4,480,256]{2,1,0:T(8,128)(2,1)S(1)}, u32[]{:S(2)}, u32[]{:S(2)}) async-start(bf16[4,480,256]{2,1,0:T(8,128)(2,1)} %attention.1), calls=%async_computation | async-start | bytes 1966080 | tf_op jit(solution)/shard_map/all_to_all | solution.py:312
  15.7 5.8 %collective-permute-start = (bf16[64,768]{1,0:T(8,128)(2,1)S(1)}, bf16[64,768]{1,0:T(8,128)(2,1)S(1)}, u32[]{:S(2)}, u32[]{:S(2)}) collective-permute-start(bf16[64,768]{1,0:T(8,128)(2,1)S(1)} %bitcast.25), channel_id=1, source_target_pairs={{0,16},{16,0},{32,48},{48,32},{1,17},{17,1},{33,49},{49,33},{2,18}... | collective-permute-start | bytes 294920 | tf_op jit(solution)/shard_map/ppermute | solution.py:316
  21.5 8.8 %collective-permute-start.1 = (bf16[64,768]{1,0:T(8,128)(2,1)S(1)}, bf16[64,768]{1,0:T(8,128)(2,1)S(1)}, u32[]{:S(2)}, u32[]{:S(2)}) collective-permute-start(bf16[64,768]{1,0:T(8,128)(2,1)S(1)} %bitcast.26), channel_id=1, source_target_pairs={{0,32},{16,48},{32,0},{48,16},{1,33},{17,49},{33,1},{49,17},{2,34}... | collective-permute-start | bytes 294920 | tf_op jit(solution)/shard_map/ppermute | solution.py:316
  30.3 1.9 %collective-permute-start.2 = (bf16[64,768]{1,0:T(8,128)(2,1)S(1)}, bf16[64,768]{1,0:T(8,128)(2,1)S(1)}, u32[]{:S(2)}, u32[]{:S(2)}) collective-permute-start(bf16[64,768]{1,0:T(8,128)(2,1)S(1)} %bitcast.27), channel_id=1, source_target_pairs={{0,48},{16,32},{32,16},{48,0},{1,49},{17,33},{33,17},{49,1},{2,50}... | collective-permute-start | bytes 294920 | tf_op jit(solution)/shard_map/ppermute | solution.py:316
  32.3 1.0 collective-permute-done.1
  33.3 6.8 %collective-permute-done.2 = bf16[64,768]{1,0:T(8,128)(2,1)S(1)} collective-permute-done((bf16[64,768]{1,0:T(8,128)(2,1)S(1)}, bf16[64,768]{1,0:T(8,128)(2,1)S(1)}, u32[]{:S(2)}, u32[]{:S(2)}) %collective-permute-start.2) | collective-permute-done | bytes 98336 | tf_op jit(solution)/shard_map/ppermute | solution.py:316
  40.0 0.8 pad_maximum_fusion
  40.9 2.5 %collective-permute-start.3 = (bf16[4,288,256]{2,1,0:T(8,128)(2,1)S(1)}, bf16[4,288,256]{2,1,0:T(8,128)(2,1)S(1)}, u32[]{:S(2)}, u32[]{:S(2)}) collective-permute-start(bf16[4,288,256]{2,1,0:T(8,128)(2,1)S(1)} %slice.3), channel_id=1, source_target_pairs={{0,4},{4,0},{1,5},{5,1},{2,6},{6,2},{3,7},{7,3},{8,12},{12,8},{9,1... | collective-permute-start | bytes 1769480 | tf_op jit(solution)/shard_map/ppermute | solution.py:316
  43.5 1.6 %collective-permute-done.3.other_ref = bf16[4,288,256]{2,1,0:T(8,128)(2,1)S(1)} collective-permute-done((bf16[4,288,256]{2,1,0:T(8,128)(2,1)S(1)}, bf16[4,288,256]{2,1,0:T(8,128)(2,1)S(1)}, u32[]{:S(2)}, u32[]{:S(2)}) %collective-permute-start.3) | collective-permute-done | bytes 589856 | tf_op jit(solution)/shard_map/ppermute | solution.py:316
  45.1 2.5 %ffn.1 = (f32[64,768]{1,0:T(8,128)S(1)}, bf16[256,768]{1,0:T(8,128)(2,1)}) custom-call(bf16[256,768]{1,0:T(8,128)(2,1)S(1)} %bitcast.20, bf16[4,480,256]{2,1,0:T(8,128)(2,1)S(1)} %all-to-all-done.merged_ref, bf16[4,288,256]{2,1,0:T(8,128)(2,1)S(1)} %collective-permute-done.3.other_ref, f32[768]{0:T(1024)S(1)} %copy-done.5, ...), custom_call_target="tpu_custom_call" | custom-call | flops 700000000 | bytes 4000000 | tf_op jit(solution)/shard_map/ffn/pallas_call | solution.py:380
  47.6 4.5 %all-to-all-start.1 = ((bf16[4,64,768]{2,1,0:T(8,128)(2,1)}), bf16[4,64,768]{2,1,0:T(8,128)(2,1)S(1)}, u32[]{:S(2)}, u32[]{:S(2)}) async-start(bf16[4,64,768]{2,1,0:T(8,128)(2,1)} %bitcast.4), calls=%async_computation.1 | async-start | bytes 786432 | tf_op jit(solution)/shard_map/all_to_all | solution.py:312
  52.1 0.1 copy.23.docs_ref
  52.3 0.4 prep.1
  52.8 6.6 %all-to-all-done.1.partial_ref = bf16[4,64,768]{2,1,0:T(8,128)(2,1)S(1)} async-done(((bf16[4,64,768]{2,1,0:T(8,128)(2,1)}), bf16[4,64,768]{2,1,0:T(8,128)(2,1)S(1)}, u32[]{:S(2)}, u32[]{:S(2)}) %all-to-all-start.1) | async-done | bytes 393248 | tf_op jit(solution)/shard_map/all_to_all | solution.py:312
  59.3 1.3 %copy-done.6 = bf16[768,768]{1,0:T(8,128)(2,1)S(1)} copy-done((bf16[768,768]{1,0:T(8,128)(2,1)S(1)}, bf16[768,768]{1,0:T(8,128)(2,1)}, u32[]{:S(2)}) %copy-start.6) | copy-done | bytes 1179672
  60.6 0.7 head.1
  61.3 8.7 %all_to_all.20 = bf16[4,64,768]{2,1,0:T(8,128)(2,1)S(1)} all-to-all(bf16[4,64,768]{2,1,0:T(8,128)(2,1)S(1)} %head.1), channel_id=1, replica_groups=mesh['y'=8,'zh'=4,'zl'=2,'core'=2,'term'=4] {'term'}, dimensions={0} | all-to-all | bytes 786432 | tf_op jit(solution)/shard_map/all_to_all | solution.py:312
  70.0 4.1 %collective-permute-start.5 = (bf16[256,768]{1,0:T(8,128)(2,1)S(1)}, bf16[256,768]{1,0:T(8,128)(2,1)S(1)}, u32[]{:S(2)}, u32[]{:S(2)}) collective-permute-start(bf16[256,768]{1,0:T(8,128)(2,1)S(1)} %bitcast.22), channel_id=1, source_target_pairs={{0,8},{8,0},{1,9},{9,1},{2,10},{10,2},{3,11},{11,3},{4,12},{12,4},... | collective-permute-start | bytes 1179656 | tf_op jit(solution)/shard_map/ppermute | solution.py:316
  74.1 5.1 %collective-permute-start.4 = (bf16[256,768]{1,0:T(8,128)(2,1)S(1)}, bf16[256,768]{1,0:T(8,128)(2,1)S(1)}, u32[]{:S(2)}, u32[]{:S(2)}) collective-permute-start(bf16[256,768]{1,0:T(8,128)(2,1)S(1)} %bitcast.23), channel_id=1, source_target_pairs={{0,4},{4,0},{1,5},{5,1},{2,6},{6,2},{3,7},{7,3},{8,12},{12,8},{9,1... | collective-permute-start | bytes 1179656 | tf_op jit(solution)/shard_map/ppermute | solution.py:316
  79.2 1.5 %collective-permute-done.5.far_ref = bf16[256,768]{1,0:T(8,128)(2,1)S(1)} collective-permute-done((bf16[256,768]{1,0:T(8,128)(2,1)S(1)}, bf16[256,768]{1,0:T(8,128)(2,1)S(1)}, u32[]{:S(2)}, u32[]{:S(2)}) %collective-permute-start.5) | collective-permute-done | bytes 393248 | tf_op jit(solution)/shard_map/ppermute | solution.py:316
  80.6 5.4 %collective-permute-start.6 = (bf16[256,768]{1,0:T(8,128)(2,1)S(1)}, bf16[256,768]{1,0:T(8,128)(2,1)S(1)}, u32[]{:S(2)}, u32[]{:S(2)}) collective-permute-start(bf16[256,768]{1,0:T(8,128)(2,1)S(1)} %collective-permute-done.5.far_ref), channel_id=1, source_target_pairs={{0,4},{4,0},{1,5},{5,1},{2,6},{6,2},{3,7},{7,3},{8,12},{12,8},{9,1... | collective-permute-start | bytes 1179656 | tf_op jit(solution)/shard_map/ppermute | solution.py:316
  86.0 0.1 reshape.43
  86.2 1.1 collective-permute-done.6.far_core_ref
  87.3 0.8 all-gather.2.cloned.1.call-done.table_ref
  88.1 8.2 %pool.1 = f32[32,8,128]{2,1,0:T(8,128)} custom-call(s32[128,8]{1,0:T(8,128)} %copy-done.7, bf16[256,768]{1,0:T(8,128)(2,1)} %bitcast.24, bf16[256,768]{1,0:T(8,128)(2,1)} %copy-done.15, bf16[256,768]{1,0:T(8,128)(2,1)} %copy-done.14, bf16[256,768]{1,0:T(8,128)(2,1)} %copy-done.16, bf16[2048,768]{1,0:T(8,128)(2,1)} %all-gather.2.cloned.1.call-done.table_ref), custom_call_target="tpu_custom_call" | custom-call | flops 3300000000 | bytes 6000000 | tf_op jit(solution)/shard_map/pool/pallas_call | solution.py:427
  96.3 10.6 %all-to-all-start.3 = ((f32[32,8,128]{2,1,0:T(8,128)}), f32[32,8,128]{2,1,0:T(8,128)S(1)}, u32[]{:S(2)}, u32[]{:S(2)}) async-start(f32[32,8,128]{2,1,0:T(8,128)} %pool.1), calls=%async_computation.3 | async-start | bytes 262144 | tf_op jit(solution)/shard_map/all_to_all | solution.py:312
  107.3 0.1 copy.28
  107.4 0.1 reshape.47.docs_ref
  107.6 0.1 convert_element_type.12
  107.7 10.6 %all-to-all-done.3 = f32[32,8,128]{2,1,0:T(8,128)S(1)} async-done(((f32[32,8,128]{2,1,0:T(8,128)}), f32[32,8,128]{2,1,0:T(8,128)S(1)}, u32[]{:S(2)}, u32[]{:S(2)}) %all-to-all-start.3) | async-done | bytes 131104 | tf_op jit(solution)/shard_map/all_to_all | solution.py:312
  118.3 1.2 place.1
  (46 shorter events, 0.6 us)
Async XLA Ops:
  6.5 9.1 %copy-start.11 = (bf16[1,8,1,8,768]{4,3,2,1,0:T(8,128)(2,1)S(1)}, bf16[1,8,1,8,768]{4,3,2,1,0:T(8,128)(2,1)}, u32[]{:S(2)}) copy-start(bf16[1,8,1,8,768]{4,3,2,1,0:T(8,128)(2,1)} %param.29) | copy-start | bytes 294916
  10.6 34.5 %copy-start = (bf16[2,768,288]{1,2,0:T(8,128)(2,1)S(1)}, bf16[2,768,288]{1,2,0:T(8,128)(2,1)}, u32[]{:S(2)}) copy-start(bf16[2,768,288]{1,2,0:T(8,128)(2,1)} %param.24) | copy-start | bytes 2654212
  10.6 34.4 %copy-start.1 = (bf16[288,768]{1,0:T(8,128)(2,1)S(1)}, bf16[288,768]{1,0:T(8,128)(2,1)}, u32[]{:S(2)}) copy-start(bf16[288,768]{1,0:T(8,128)(2,1)} %down_ref.1) | copy-start | bytes 1327108
  10.6 34.4 %copy-start.2 = (bf16[1,256,768]{2,1,0:T(8,128)(2,1)S(1)}, bf16[1,256,768]{2,1,0:T(8,128)(2,1)}, u32[]{:S(2)}) copy-start(bf16[1,256,768]{2,1,0:T(8,128)(2,1)} %param.16) | copy-start | bytes 1179652
  10.7 34.4 %copy-start.5 = (f32[768]{0:T(1024)S(1)}, f32[768]{0:T(1024)}, u32[]{:S(2)}) copy-start(f32[768]{0:T(1024)} %gain_ref.1) | copy-start | bytes 9220
  10.7 30.2 %all-to-all-start = ((bf16[4,480,256]{2,1,0:T(8,128)(2,1)}), bf16[4,480,256]{2,1,0:T(8,128)(2,1)S(1)}, u32[]{:S(2)}, u32[]{:S(2)}) async-start(bf16[4,480,256]{2,1,0:T(8,128)(2,1)} %attention.1), calls=%async_computation | async-start | bytes 1966080 | tf_op jit(solution)/shard_map/all_to_all | solution.py:312
  15.7 36.5 %copy-start.12 = (s32[512]{0:T(512)S(1)}, s32[512]{0:T(512)}, u32[]{:S(2)}) copy-start(s32[512]{0:T(512)} %param.19) | copy-start | bytes 6148
  15.7 72.5 %all-gather.2.cloned.1.call-start = ((), (), s32[]{:S(2)}) async-start(), calls=%async_computation.4 | async-start | bytes 3538944 | tf_op jit(solution)/shard_map/all_gather | solution.py:378
  15.7 16.6 %collective-permute-start = (bf16[64,768]{1,0:T(8,128)(2,1)S(1)}, bf16[64,768]{1,0:T(8,128)(2,1)S(1)}, u32[]{:S(2)}, u32[]{:S(2)}) collective-permute-start(bf16[64,768]{1,0:T(8,128)(2,1)S(1)} %bitcast.25), channel_id=1, source_target_pairs={{0,16},{16,0},{32,48},{48,32},{1,17},{17,1},{33,49},{49,33},{2,18}... | collective-permute-start | bytes 294920 | tf_op jit(solution)/shard_map/ppermute | solution.py:316
  21.5 11.8 %collective-permute-start.1 = (bf16[64,768]{1,0:T(8,128)(2,1)S(1)}, bf16[64,768]{1,0:T(8,128)(2,1)S(1)}, u32[]{:S(2)}, u32[]{:S(2)}) collective-permute-start(bf16[64,768]{1,0:T(8,128)(2,1)S(1)} %bitcast.26), channel_id=1, source_target_pairs={{0,32},{16,48},{32,0},{48,16},{1,33},{17,49},{33,1},{49,17},{2,34}... | collective-permute-start | bytes 294920 | tf_op jit(solution)/shard_map/ppermute | solution.py:316
  30.3 9.7 %collective-permute-start.2 = (bf16[64,768]{1,0:T(8,128)(2,1)S(1)}, bf16[64,768]{1,0:T(8,128)(2,1)S(1)}, u32[]{:S(2)}, u32[]{:S(2)}) collective-permute-start(bf16[64,768]{1,0:T(8,128)(2,1)S(1)} %bitcast.27), channel_id=1, source_target_pairs={{0,48},{16,32},{32,16},{48,0},{1,49},{17,33},{33,17},{49,1},{2,50}... | collective-permute-start | bytes 294920 | tf_op jit(solution)/shard_map/ppermute | solution.py:316
  40.8 11.5 %copy-start.3 = (s32[512,128]{1,0:T(8,128)S(1)}, s32[512,128]{1,0:T(8,128)}, u32[]{:S(2)}) copy-start(s32[512,128]{1,0:T(8,128)} %list_ref.1) | copy-start | bytes 786436
  40.8 11.5 %copy-start.4 = (s32[128,256]{1,0:T(8,128)S(1)}, s32[128,256]{1,0:T(8,128)}, u32[]{:S(2)}) copy-start(s32[128,256]{1,0:T(8,128)} %segment_ref.1) | copy-start | bytes 393220
  40.9 18.5 %copy-start.8 = (f32[768]{0:T(1024)S(1)}, f32[768]{0:T(1024)}, u32[]{:S(2)}) copy-start(f32[768]{0:T(1024)} %final_ref.1) | copy-start | bytes 9220
  40.9 18.5 %copy-start.9 = (f32[768]{0:T(1024)S(1)}, f32[768]{0:T(1024)}, u32[]{:S(2)}) copy-start(f32[768]{0:T(1024)} %head_ref.1) | copy-start | bytes 9220
  40.9 4.1 %collective-permute-start.3 = (bf16[4,288,256]{2,1,0:T(8,128)(2,1)S(1)}, bf16[4,288,256]{2,1,0:T(8,128)(2,1)S(1)}, u32[]{:S(2)}, u32[]{:S(2)}) collective-permute-start(bf16[4,288,256]{2,1,0:T(8,128)(2,1)S(1)} %slice.3), channel_id=1, source_target_pairs={{0,4},{4,0},{1,5},{5,1},{2,6},{6,2},{3,7},{7,3},{8,12},{12,8},{9,1... | collective-permute-start | bytes 1769480 | tf_op jit(solution)/shard_map/ppermute | solution.py:316
  47.6 11.7 %all-to-all-start.1 = ((bf16[4,64,768]{2,1,0:T(8,128)(2,1)}), bf16[4,64,768]{2,1,0:T(8,128)(2,1)S(1)}, u32[]{:S(2)}, u32[]{:S(2)}) async-start(bf16[4,64,768]{2,1,0:T(8,128)(2,1)} %bitcast.4), calls=%async_computation.1 | async-start | bytes 786432 | tf_op jit(solution)/shard_map/all_to_all | solution.py:312
  52.8 35.4 %copy-start.7 = (s32[128,8]{1,0:T(8,128)}, s32[128,8]{1,0:T(8,128)S(1)}, u32[]{:S(2)}) copy-start(s32[128,8]{1,0:T(8,128)S(1)} %get-tuple-element.22.bounds_ref) | copy-start | bytes 12292
  59.3 1.3 %copy-start.6 = (bf16[768,768]{1,0:T(8,128)(2,1)S(1)}, bf16[768,768]{1,0:T(8,128)(2,1)}, u32[]{:S(2)}) copy-start(bf16[768,768]{1,0:T(8,128)(2,1)} %dense_ref.1) | copy-start | bytes 3538948
  70.0 18.2 %copy-start.10 = (bf16[4,64,768]{2,1,0:T(8,128)(2,1)}, bf16[4,64,768]{2,1,0:T(8,128)(2,1)S(1)}, u32[]{:S(2)}) copy-start(bf16[4,64,768]{2,1,0:T(8,128)(2,1)S(1)} %all_to_all.20) | copy-start | bytes 1179652
  70.0 10.7 %collective-permute-start.5 = (bf16[256,768]{1,0:T(8,128)(2,1)S(1)}, bf16[256,768]{1,0:T(8,128)(2,1)S(1)}, u32[]{:S(2)}, u32[]{:S(2)}) collective-permute-start(bf16[256,768]{1,0:T(8,128)(2,1)S(1)} %bitcast.22), channel_id=1, source_target_pairs={{0,8},{8,0},{1,9},{9,1},{2,10},{10,2},{3,11},{11,3},{4,12},{12,4},... | collective-permute-start | bytes 1179656 | tf_op jit(solution)/shard_map/ppermute | solution.py:316
  74.1 12.2 %collective-permute-start.4 = (bf16[256,768]{1,0:T(8,128)(2,1)S(1)}, bf16[256,768]{1,0:T(8,128)(2,1)S(1)}, u32[]{:S(2)}, u32[]{:S(2)}) collective-permute-start(bf16[256,768]{1,0:T(8,128)(2,1)S(1)} %bitcast.23), channel_id=1, source_target_pairs={{0,4},{4,0},{1,5},{5,1},{2,6},{6,2},{3,7},{7,3},{8,12},{12,8},{9,1... | collective-permute-start | bytes 1179656 | tf_op jit(solution)/shard_map/ppermute | solution.py:316
  80.6 7.5 %copy-start.14 = (bf16[256,768]{1,0:T(8,128)(2,1)}, bf16[256,768]{1,0:T(8,128)(2,1)S(1)}, u32[]{:S(2)}) copy-start(bf16[256,768]{1,0:T(8,128)(2,1)S(1)} %collective-permute-done.5.far_ref) | copy-start | bytes 1179652
  80.6 6.7 %collective-permute-start.6 = (bf16[256,768]{1,0:T(8,128)(2,1)S(1)}, bf16[256,768]{1,0:T(8,128)(2,1)S(1)}, u32[]{:S(2)}, u32[]{:S(2)}) collective-permute-start(bf16[256,768]{1,0:T(8,128)(2,1)S(1)} %collective-permute-done.5.far_ref), channel_id=1, source_target_pairs={{0,4},{4,0},{1,5},{5,1},{2,6},{6,2},{3,7},{7,3},{8,12},{12,8},{9,1... | collective-permute-start | bytes 1179656 | tf_op jit(solution)/shard_map/ppermute | solution.py:316
  86.2 21.4 %copy-start.13 = (bf16[1,8,1,8]{3,1,2,0:T(8,128)(2,1)S(1)}, bf16[1,8,1,8]{3,1,2,0:T(8,128)(2,1)}, u32[]{:S(2)}) copy-start(bf16[1,8,1,8]{3,1,2,0:T(8,128)(2,1)} %param.30) | copy-start | bytes 388
  86.2 1.9 %copy-start.15 = (bf16[256,768]{1,0:T(8,128)(2,1)}, bf16[256,768]{1,0:T(8,128)(2,1)S(1)}, u32[]{:S(2)}) copy-start(bf16[256,768]{1,0:T(8,128)(2,1)S(1)} %collective-permute-done.4.core_ref) | copy-start | bytes 1179652
  87.3 0.8 copy-start.16
  96.3 22.0 %all-to-all-start.3 = ((f32[32,8,128]{2,1,0:T(8,128)}), f32[32,8,128]{2,1,0:T(8,128)S(1)}, u32[]{:S(2)}, u32[]{:S(2)}) async-start(f32[32,8,128]{2,1,0:T(8,128)} %pool.1), calls=%async_computation.3 | async-start | bytes 262144 | tf_op jit(solution)/shard_map/all_to_all | solution.py:312
Sparse Core Ops, SparseCore 0:
  41.0 47.0 all-gather.1

commit v10 on v9

--- a/solution.py
+++ b/solution.py
@@ -372,8 +372,10 @@
         cost_estimate=cost(1200000000, 2000000),
         name="attention",
     )(attn_gain, tokens, segment_ids, jnp.swapaxes(qkv_weight, 1, 2), rotary, attn_out)
-    own_slice, merged = lax.optimization_barrier((own_slice, merged))
-    part = jnp.concatenate([own_slice] + others(own_slice, "zh"), axis=0)
+    across = swap(own_slice, "zh", 2)
+    late_slice, merged = lax.optimization_barrier((own_slice, merged))
+    pieces = [own_slice, swap(late_slice, "zh", 1), across, swap(late_slice, "zh", 3)]
+    part = jnp.concatenate(pieces, axis=0)
     merged, part = lax.optimization_barrier((exchange(merged, "term"), part))
     table = lax.all_gather(part, "y", axis=0, tiled=True)
     other = swap(merged[:, head_width:], "core")

time: 127 us -> 128 us (level)
  transfers between devices with their start and end apart: 11 -> 11, of which waited for: 8 -> 7; matrix products, arithmetic and copies ran while one was open for 1% -> 1% of each run, Pallas kernels for 3% -> 3%
where the time goes in v10:
time: 128 us; the launch traced here: 126 us
  starting transfers between devices  54.2 us (42%)
  waiting for transfers between devices  29.4 us (23%)
  Pallas kernels  17.1 us (13%)
  between operations  13.7 us (11%)
  blocking collectives  8.67 us (7%)
  local copies, waits for them, and re-layouts  2.37 us (2%)
    ppermute x7, starting transfers between devices, swap(): lax.ppermute(block, axis, [(i, i ^ d) for i in range(lax.axis_size(axis))])  33.9 us
    all_to_all x3, starting transfers between devices, exchange(): return lax.all_to_all(copies, axis, split_axis=0, concat_axis=0, tiled=True)  20.3 us
    all_to_all x3, waiting for transfers between devices, exchange(): return lax.all_to_all(copies, axis, split_axis=0, concat_axis=0, tiled=True)  17.1 us
    ppermute x7, waiting for transfers between devices, swap(): lax.ppermute(block, axis, [(i, i ^ d) for i in range(lax.axis_size(axis))])  11.5 us
    all_to_all x1, blocking collectives, exchange(): return lax.all_to_all(copies, axis, split_axis=0, concat_axis=0, tiled=True)  8.67 us
    pallas_call x1, Pallas kernels, on_device(): pl.pallas_call(pool_kernel, out_shape=jax.ShapeDtypeStruct((slices, 2 * P...  8.19 us
    pallas_call x1, Pallas kernels, on_device(): pl.pallas_call(attention_kernel, out_shape=jax.ShapeDtypeStruct((tensor,...  4.08 us
  transfers between devices with their start and end apart: 11, of which 7 were waited for; matrix products, arithmetic and copies ran while one was open for 1% of the time, Pallas kernels for 3%

profile of v10, /device:TPU:1, one launch (start us, length us, event | category | flops | bytes accessed | tf_op | source)
XLA Modules:
  0.0 126.4 jit_solution(4579461520651491717)
XLA Ops:
  6.5 4.1 %attention.1 = bf16[4,480,256]{2,1,0:T(8,128)(2,1)} custom-call(f32[768]{0:T(1024)} %gain_hbm.1, bf16[256,768]{1,0:T(8,128)(2,1)} %bitcast.19, s32[128,256]{1,0:T(8,128)} %segment_ref.1, bf16[3,192,768]{2,1,0:T(8,128)(2,1)} %bitcast.31, bf16[192,256]{1,0:T(8,128)(2,1)} %constant.22.clone.table_hbm, bf16[192,768]{1,0:T(8,128)(2,1)} %out_weight_hbm.1), custom_call_target="tpu_custom_call" | custom-call | flops 1200000000 | bytes 2000000 | tf_op jit(solution)/shard_map/attention/pallas_call | solution.py:357
  10.7 5.0 %all-to-all-start = ((bf16[4,480,256]{2,1,0:T(8,128)(2,1)}), bf16[4,480,256]{2,1,0:T(8,128)(2,1)S(1)}, u32[]{:S(2)}, u32[]{:S(2)}) async-start(bf16[4,480,256]{2,1,0:T(8,128)(2,1)} %attention.1), calls=%async_computation | async-start | bytes 1966080 | tf_op jit(solution)/shard_map/all_to_all | solution.py:312
  15.7 5.8 %collective-permute-start = (bf16[64,768]{1,0:T(8,128)(2,1)S(1)}, bf16[64,768]{1,0:T(8,128)(2,1)S(1)}, u32[]{:S(2)}, u32[]{:S(2)}) collective-permute-start(bf16[64,768]{1,0:T(8,128)(2,1)S(1)} %bitcast.25), channel_id=1, source_target_pairs={{0,16},{16,0},{32,48},{48,32},{1,17},{17,1},{33,49},{49,33},{2,18}... | collective-permute-start | bytes 294920 | tf_op jit(solution)/shard_map/ppermute | solution.py:316
  21.5 7.0 %collective-permute-start.2 = (bf16[64,768]{1,0:T(8,128)(2,1)S(1)}, bf16[64,768]{1,0:T(8,128)(2,1)S(1)}, u32[]{:S(2)}, u32[]{:S(2)}) collective-permute-start(bf16[64,768]{1,0:T(8,128)(2,1)S(1)} %bitcast.26), channel_id=1, source_target_pairs={{0,48},{16,32},{32,16},{48,0},{1,49},{17,33},{33,17},{49,1},{2,50}... | collective-permute-start | bytes 294920 | tf_op jit(solution)/shard_map/ppermute | solution.py:316
  28.5 3.7 %collective-permute-start.1 = (bf16[64,768]{1,0:T(8,128)(2,1)S(1)}, bf16[64,768]{1,0:T(8,128)(2,1)S(1)}, u32[]{:S(2)}, u32[]{:S(2)}) collective-permute-start(bf16[64,768]{1,0:T(8,128)(2,1)S(1)} %bitcast.27), channel_id=1, source_target_pairs={{0,32},{16,48},{32,0},{48,16},{1,33},{17,49},{33,1},{49,17},{2,34}... | collective-permute-start | bytes 294920 | tf_op jit(solution)/shard_map/ppermute | solution.py:316
  32.3 7.1 %collective-permute-done.1 = bf16[64,768]{1,0:T(8,128)(2,1)S(1)} collective-permute-done((bf16[64,768]{1,0:T(8,128)(2,1)S(1)}, bf16[64,768]{1,0:T(8,128)(2,1)S(1)}, u32[]{:S(2)}, u32[]{:S(2)}) %collective-permute-start.1) | collective-permute-done | bytes 98336 | tf_op jit(solution)/shard_map/ppermute | solution.py:316
  39.4 0.8 pad_maximum_fusion
  40.3 3.7 %collective-permute-start.3 = (bf16[4,288,256]{2,1,0:T(8,128)(2,1)S(1)}, bf16[4,288,256]{2,1,0:T(8,128)(2,1)S(1)}, u32[]{:S(2)}, u32[]{:S(2)}) collective-permute-start(bf16[4,288,256]{2,1,0:T(8,128)(2,1)S(1)} %slice.3), channel_id=1, source_target_pairs={{0,4},{4,0},{1,5},{5,1},{2,6},{6,2},{3,7},{7,3},{8,12},{12,8},{9,1... | collective-permute-start | bytes 1769480 | tf_op jit(solution)/shard_map/ppermute | solution.py:316
  44.0 1.6 %collective-permute-done.3.other_ref = bf16[4,288,256]{2,1,0:T(8,128)(2,1)S(1)} collective-permute-done((bf16[4,288,256]{2,1,0:T(8,128)(2,1)S(1)}, bf16[4,288,256]{2,1,0:T(8,128)(2,1)S(1)}, u32[]{:S(2)}, u32[]{:S(2)}) %collective-permute-start.3) | collective-permute-done | bytes 589856 | tf_op jit(solution)/shard_map/ppermute | solution.py:316
  45.6 2.5 %ffn.1 = (f32[64,768]{1,0:T(8,128)S(1)}, bf16[256,768]{1,0:T(8,128)(2,1)}) custom-call(bf16[256,768]{1,0:T(8,128)(2,1)S(1)} %bitcast.20, bf16[4,480,256]{2,1,0:T(8,128)(2,1)S(1)} %all-to-all-done.merged_ref, bf16[4,288,256]{2,1,0:T(8,128)(2,1)S(1)} %collective-permute-done.3.other_ref, f32[768]{0:T(1024)S(1)} %copy-done.5, ...), custom_call_target="tpu_custom_call" | custom-call | flops 700000000 | bytes 4000000 | tf_op jit(solution)/shard_map/ffn/pallas_call | solution.py:382
  48.1 4.8 %all-to-all-start.1 = ((bf16[4,64,768]{2,1,0:T(8,128)(2,1)}), bf16[4,64,768]{2,1,0:T(8,128)(2,1)S(1)}, u32[]{:S(2)}, u32[]{:S(2)}) async-start(bf16[4,64,768]{2,1,0:T(8,128)(2,1)} %bitcast.4), calls=%async_computation.1 | async-start | bytes 786432 | tf_op jit(solution)/shard_map/all_to_all | solution.py:312
  52.8 0.1 copy.23.docs_ref
  53.0 0.4 prep.1
  53.5 6.6 %all-to-all-done.1.partial_ref = bf16[4,64,768]{2,1,0:T(8,128)(2,1)S(1)} async-done(((bf16[4,64,768]{2,1,0:T(8,128)(2,1)}), bf16[4,64,768]{2,1,0:T(8,128)(2,1)S(1)}, u32[]{:S(2)}, u32[]{:S(2)}) %all-to-all-start.1) | async-done | bytes 393248 | tf_op jit(solution)/shard_map/all_to_all | solution.py:312
  60.0 1.3 %copy-done.6 = bf16[768,768]{1,0:T(8,128)(2,1)S(1)} copy-done((bf16[768,768]{1,0:T(8,128)(2,1)S(1)}, bf16[768,768]{1,0:T(8,128)(2,1)}, u32[]{:S(2)}) %copy-start.6) | copy-done | bytes 1179672
  61.3 0.7 head.1
  62.0 8.7 %all_to_all.20 = bf16[4,64,768]{2,1,0:T(8,128)(2,1)S(1)} all-to-all(bf16[4,64,768]{2,1,0:T(8,128)(2,1)S(1)} %head.1), channel_id=1, replica_groups=mesh['y'=8,'zh'=4,'zl'=2,'core'=2,'term'=4] {'term'}, dimensions={0} | all-to-all | bytes 786432 | tf_op jit(solution)/shard_map/all_to_all | solution.py:312
  70.7 2.9 %collective-permute-start.5 = (bf16[256,768]{1,0:T(8,128)(2,1)S(1)}, bf16[256,768]{1,0:T(8,128)(2,1)S(1)}, u32[]{:S(2)}, u32[]{:S(2)}) collective-permute-start(bf16[256,768]{1,0:T(8,128)(2,1)S(1)} %bitcast.22), channel_id=1, source_target_pairs={{0,8},{8,0},{1,9},{9,1},{2,10},{10,2},{3,11},{11,3},{4,12},{12,4},... | collective-permute-start | bytes 1179656 | tf_op jit(solution)/shard_map/ppermute | solution.py:316
  73.6 5.1 %collective-permute-start.4 = (bf16[256,768]{1,0:T(8,128)(2,1)S(1)}, bf16[256,768]{1,0:T(8,128)(2,1)S(1)}, u32[]{:S(2)}, u32[]{:S(2)}) collective-permute-start(bf16[256,768]{1,0:T(8,128)(2,1)S(1)} %bitcast.23), channel_id=1, source_target_pairs={{0,4},{4,0},{1,5},{5,1},{2,6},{6,2},{3,7},{7,3},{8,12},{12,8},{9,1... | collective-permute-start | bytes 1179656 | tf_op jit(solution)/shard_map/ppermute | solution.py:316
  78.8 1.6 %collective-permute-done.5.far_ref = bf16[256,768]{1,0:T(8,128)(2,1)S(1)} collective-permute-done((bf16[256,768]{1,0:T(8,128)(2,1)S(1)}, bf16[256,768]{1,0:T(8,128)(2,1)S(1)}, u32[]{:S(2)}, u32[]{:S(2)}) %collective-permute-start.5) | collective-permute-done | bytes 393248 | tf_op jit(solution)/shard_map/ppermute | solution.py:316
  80.4 5.6 %collective-permute-start.6 = (bf16[256,768]{1,0:T(8,128)(2,1)S(1)}, bf16[256,768]{1,0:T(8,128)(2,1)S(1)}, u32[]{:S(2)}, u32[]{:S(2)}) collective-permute-start(bf16[256,768]{1,0:T(8,128)(2,1)S(1)} %collective-permute-done.5.far_ref), channel_id=1, source_target_pairs={{0,4},{4,0},{1,5},{5,1},{2,6},{6,2},{3,7},{7,3},{8,12},{12,8},{9,1... | collective-permute-start | bytes 1179656 | tf_op jit(solution)/shard_map/ppermute | solution.py:316
  86.1 0.1 reshape.43
  86.2 1.1 collective-permute-done.6.far_core_ref
  87.4 0.8 all-gather.2.cloned.1.call-done.table_ref
  88.2 8.2 %pool.1 = f32[32,8,128]{2,1,0:T(8,128)} custom-call(s32[128,8]{1,0:T(8,128)} %copy-done.7, bf16[256,768]{1,0:T(8,128)(2,1)} %bitcast.24, bf16[256,768]{1,0:T(8,128)(2,1)} %copy-done.15, bf16[256,768]{1,0:T(8,128)(2,1)} %copy-done.14, bf16[256,768]{1,0:T(8,128)(2,1)} %copy-done.16, bf16[2048,768]{1,0:T(8,128)(2,1)} %all-gather.2.cloned.1.call-done.table_ref), custom_call_target="tpu_custom_call" | custom-call | flops 3300000000 | bytes 6000000 | tf_op jit(solution)/shard_map/pool/pallas_call | solution.py:429
  96.4 10.6 %all-to-all-start.3 = ((f32[32,8,128]{2,1,0:T(8,128)}), f32[32,8,128]{2,1,0:T(8,128)S(1)}, u32[]{:S(2)}, u32[]{:S(2)}) async-start(f32[32,8,128]{2,1,0:T(8,128)} %pool.1), calls=%async_computation.3 | async-start | bytes 262144 | tf_op jit(solution)/shard_map/all_to_all | solution.py:312
  107.4 0.1 copy.28
  107.5 0.1 reshape.47.docs_ref
  107.6 0.1 convert_element_type.12
  107.7 0.1 maximum_convert_fusion.bias_ref
  107.8 10.6 %all-to-all-done.3 = f32[32,8,128]{2,1,0:T(8,128)S(1)} async-done(((f32[32,8,128]{2,1,0:T(8,128)}), f32[32,8,128]{2,1,0:T(8,128)S(1)}, u32[]{:S(2)}, u32[]{:S(2)}) %all-to-all-start.3) | async-done | bytes 131104 | tf_op jit(solution)/shard_map/all_to_all | solution.py:312
  118.4 1.2 place.1
  (46 shorter events, 0.5 us)
Async XLA Ops:
  6.5 9.1 %copy-start.11 = (bf16[1,8,1,8,768]{4,3,2,1,0:T(8,128)(2,1)S(1)}, bf16[1,8,1,8,768]{4,3,2,1,0:T(8,128)(2,1)}, u32[]{:S(2)}) copy-start(bf16[1,8,1,8,768]{4,3,2,1,0:T(8,128)(2,1)} %param.29) | copy-start | bytes 294916
  10.6 34.9 %copy-start = (bf16[2,768,288]{1,2,0:T(8,128)(2,1)S(1)}, bf16[2,768,288]{1,2,0:T(8,128)(2,1)}, u32[]{:S(2)}) copy-start(bf16[2,768,288]{1,2,0:T(8,128)(2,1)} %param.24) | copy-start | bytes 2654212
  10.6 34.9 %copy-start.1 = (bf16[288,768]{1,0:T(8,128)(2,1)S(1)}, bf16[288,768]{1,0:T(8,128)(2,1)}, u32[]{:S(2)}) copy-start(bf16[288,768]{1,0:T(8,128)(2,1)} %down_ref.1) | copy-start | bytes 1327108
  10.6 34.9 %copy-start.2 = (bf16[1,256,768]{2,1,0:T(8,128)(2,1)S(1)}, bf16[1,256,768]{2,1,0:T(8,128)(2,1)}, u32[]{:S(2)}) copy-start(bf16[1,256,768]{2,1,0:T(8,128)(2,1)} %param.16) | copy-start | bytes 1179652
  10.7 34.9 %copy-start.5 = (f32[768]{0:T(1024)S(1)}, f32[768]{0:T(1024)}, u32[]{:S(2)}) copy-start(f32[768]{0:T(1024)} %gain_ref.1) | copy-start | bytes 9220
  10.7 29.5 %all-to-all-start = ((bf16[4,480,256]{2,1,0:T(8,128)(2,1)}), bf16[4,480,256]{2,1,0:T(8,128)(2,1)S(1)}, u32[]{:S(2)}, u32[]{:S(2)}) async-start(bf16[4,480,256]{2,1,0:T(8,128)(2,1)} %attention.1), calls=%async_computation | async-start | bytes 1966080 | tf_op jit(solution)/shard_map/all_to_all | solution.py:312
  15.7 37.2 %copy-start.12 = (s32[512]{0:T(512)S(1)}, s32[512]{0:T(512)}, u32[]{:S(2)}) copy-start(s32[512]{0:T(512)} %param.19) | copy-start | bytes 6148
  15.7 72.5 %all-gather.2.cloned.1.call-start = ((), (), s32[]{:S(2)}) async-start(), calls=%async_computation.4 | async-start | bytes 3538944 | tf_op jit(solution)/shard_map/all_gather | solution.py:380
  15.7 16.6 %collective-permute-start = (bf16[64,768]{1,0:T(8,128)(2,1)S(1)}, bf16[64,768]{1,0:T(8,128)(2,1)S(1)}, u32[]{:S(2)}, u32[]{:S(2)}) collective-permute-start(bf16[64,768]{1,0:T(8,128)(2,1)S(1)} %bitcast.25), channel_id=1, source_target_pairs={{0,16},{16,0},{32,48},{48,32},{1,17},{17,1},{33,49},{49,33},{2,18}... | collective-permute-start | bytes 294920 | tf_op jit(solution)/shard_map/ppermute | solution.py:316
  21.5 10.8 %collective-permute-start.2 = (bf16[64,768]{1,0:T(8,128)(2,1)S(1)}, bf16[64,768]{1,0:T(8,128)(2,1)S(1)}, u32[]{:S(2)}, u32[]{:S(2)}) collective-permute-start(bf16[64,768]{1,0:T(8,128)(2,1)S(1)} %bitcast.26), channel_id=1, source_target_pairs={{0,48},{16,32},{32,16},{48,0},{1,49},{17,33},{33,17},{49,1},{2,50}... | collective-permute-start | bytes 294920 | tf_op jit(solution)/shard_map/ppermute | solution.py:316
  28.5 10.9 %collective-permute-start.1 = (bf16[64,768]{1,0:T(8,128)(2,1)S(1)}, bf16[64,768]{1,0:T(8,128)(2,1)S(1)}, u32[]{:S(2)}, u32[]{:S(2)}) collective-permute-start(bf16[64,768]{1,0:T(8,128)(2,1)S(1)} %bitcast.27), channel_id=1, source_target_pairs={{0,32},{16,48},{32,0},{48,16},{1,33},{17,49},{33,1},{49,17},{2,34}... | collective-permute-start | bytes 294920 | tf_op jit(solution)/shard_map/ppermute | solution.py:316
  40.2 12.8 %copy-start.3 = (s32[512,128]{1,0:T(8,128)S(1)}, s32[512,128]{1,0:T(8,128)}, u32[]{:S(2)}) copy-start(s32[512,128]{1,0:T(8,128)} %list_ref.1) | copy-start | bytes 786436
  40.2 12.8 %copy-start.4 = (s32[128,256]{1,0:T(8,128)S(1)}, s32[128,256]{1,0:T(8,128)}, u32[]{:S(2)}) copy-start(s32[128,256]{1,0:T(8,128)} %segment_ref.1) | copy-start | bytes 393220
  40.2 19.9 %copy-start.8 = (f32[768]{0:T(1024)S(1)}, f32[768]{0:T(1024)}, u32[]{:S(2)}) copy-start(f32[768]{0:T(1024)} %final_ref.1) | copy-start | bytes 9220
  40.2 19.8 %copy-start.9 = (f32[768]{0:T(1024)S(1)}, f32[768]{0:T(1024)}, u32[]{:S(2)}) copy-start(f32[768]{0:T(1024)} %head_ref.1) | copy-start | bytes 9220
  40.3 5.3 %collective-permute-start.3 = (bf16[4,288,256]{2,1,0:T(8,128)(2,1)S(1)}, bf16[4,288,256]{2,1,0:T(8,128)(2,1)S(1)}, u32[]{:S(2)}, u32[]{:S(2)}) collective-permute-start(bf16[4,288,256]{2,1,0:T(8,128)(2,1)S(1)} %slice.3), channel_id=1, source_target_pairs={{0,4},{4,0},{1,5},{5,1},{2,6},{6,2},{3,7},{7,3},{8,12},{12,8},{9,1... | collective-permute-start | bytes 1769480 | tf_op jit(solution)/shard_map/ppermute | solution.py:316
  48.1 12.0 %all-to-all-start.1 = ((bf16[4,64,768]{2,1,0:T(8,128)(2,1)}), bf16[4,64,768]{2,1,0:T(8,128)(2,1)S(1)}, u32[]{:S(2)}, u32[]{:S(2)}) async-start(bf16[4,64,768]{2,1,0:T(8,128)(2,1)} %bitcast.4), calls=%async_computation.1 | async-start | bytes 786432 | tf_op jit(solution)/shard_map/all_to_all | solution.py:312
  53.5 34.7 %copy-start.7 = (s32[128,8]{1,0:T(8,128)}, s32[128,8]{1,0:T(8,128)S(1)}, u32[]{:S(2)}) copy-start(s32[128,8]{1,0:T(8,128)S(1)} %get-tuple-element.22.bounds_ref) | copy-start | bytes 12292
  60.0 1.3 %copy-start.6 = (bf16[768,768]{1,0:T(8,128)(2,1)S(1)}, bf16[768,768]{1,0:T(8,128)(2,1)}, u32[]{:S(2)}) copy-start(bf16[768,768]{1,0:T(8,128)(2,1)} %dense_ref.1) | copy-start | bytes 3538948
  70.7 17.5 %copy-start.10 = (bf16[4,64,768]{2,1,0:T(8,128)(2,1)}, bf16[4,64,768]{2,1,0:T(8,128)(2,1)S(1)}, u32[]{:S(2)}) copy-start(bf16[4,64,768]{2,1,0:T(8,128)(2,1)S(1)} %all_to_all.20) | copy-start | bytes 1179652
  70.7 9.7 %collective-permute-start.5 = (bf16[256,768]{1,0:T(8,128)(2,1)S(1)}, bf16[256,768]{1,0:T(8,128)(2,1)S(1)}, u32[]{:S(2)}, u32[]{:S(2)}) collective-permute-start(bf16[256,768]{1,0:T(8,128)(2,1)S(1)} %bitcast.22), channel_id=1, source_target_pairs={{0,8},{8,0},{1,9},{9,1},{2,10},{10,2},{3,11},{11,3},{4,12},{12,4},... | collective-permute-start | bytes 1179656 | tf_op jit(solution)/shard_map/ppermute | solution.py:316
  73.6 12.6 %collective-permute-start.4 = (bf16[256,768]{1,0:T(8,128)(2,1)S(1)}, bf16[256,768]{1,0:T(8,128)(2,1)S(1)}, u32[]{:S(2)}, u32[]{:S(2)}) collective-permute-start(bf16[256,768]{1,0:T(8,128)(2,1)S(1)} %bitcast.23), channel_id=1, source_target_pairs={{0,4},{4,0},{1,5},{5,1},{2,6},{6,2},{3,7},{7,3},{8,12},{12,8},{9,1... | collective-permute-start | bytes 1179656 | tf_op jit(solution)/shard_map/ppermute | solution.py:316
  80.4 7.8 %copy-start.14 = (bf16[256,768]{1,0:T(8,128)(2,1)}, bf16[256,768]{1,0:T(8,128)(2,1)S(1)}, u32[]{:S(2)}) copy-start(bf16[256,768]{1,0:T(8,128)(2,1)S(1)} %collective-permute-done.5.far_ref) | copy-start | bytes 1179652
  80.4 7.0 %collective-permute-start.6 = (bf16[256,768]{1,0:T(8,128)(2,1)S(1)}, bf16[256,768]{1,0:T(8,128)(2,1)S(1)}, u32[]{:S(2)}, u32[]{:S(2)}) collective-permute-start(bf16[256,768]{1,0:T(8,128)(2,1)S(1)} %collective-permute-done.5.far_ref), channel_id=1, source_target_pairs={{0,4},{4,0},{1,5},{5,1},{2,6},{6,2},{3,7},{7,3},{8,12},{12,8},{9,1... | collective-permute-start | bytes 1179656 | tf_op jit(solution)/shard_map/ppermute | solution.py:316
  86.2 21.4 %copy-start.13 = (bf16[1,8,1,8]{3,1,2,0:T(8,128)(2,1)S(1)}, bf16[1,8,1,8]{3,1,2,0:T(8,128)(2,1)}, u32[]{:S(2)}) copy-start(bf16[1,8,1,8]{3,1,2,0:T(8,128)(2,1)} %param.30) | copy-start | bytes 388
  86.2 2.0 %copy-start.15 = (bf16[256,768]{1,0:T(8,128)(2,1)}, bf16[256,768]{1,0:T(8,128)(2,1)S(1)}, u32[]{:S(2)}) copy-start(bf16[256,768]{1,0:T(8,128)(2,1)S(1)} %collective-permute-done.4.core_ref) | copy-start | bytes 1179652
  87.4 0.8 copy-start.16
  96.4 22.0 %all-to-all-start.3 = ((f32[32,8,128]{2,1,0:T(8,128)}), f32[32,8,128]{2,1,0:T(8,128)S(1)}, u32[]{:S(2)}, u32[]{:S(2)}) async-start(f32[32,8,128]{2,1,0:T(8,128)} %pool.1), calls=%async_computation.3 | async-start | bytes 262144 | tf_op jit(solution)/shard_map/all_to_all | solution.py:312
Sparse Core Ops, SparseCore 0:
  40.3 47.8 all-gather.1

commit v11 on v10

--- a/solution.py
+++ b/solution.py
@@ -63,13 +63,13 @@
     weight_hbm,
     table_hbm,
     out_weight_hbm,
-    out_ref,
+    out_hbm,
     gain_ref,
     hidden_ref,
     segment_ref,
     weight_ref,
     table_ref,
-    half_ref,
+    context_ref,
     sems,
 ):
     length = hidden_ref.shape[0]
@@ -86,19 +86,26 @@
     hidden_copies.append(fetch(gain_hbm, gain_ref))
     segment_copy = fetch(segment_hbm.at[pl.ds(tile, 8), :], segment_ref)
     table_copy = fetch(table_hbm, table_ref)
-    half = half_ref.shape[0]
+    head_width, length = context_ref.shape
+    half = head_width // 2
     weight_copies = [
         fetch(weight_hbm.at[slot, cut, :], weight_ref.at[slot, cut, :])
         for slot in range(3)
         for cut in (slice(0, half), slice(half, 2 * half))
     ]
     own_rows = pl.ds(pl.multiple_of(lax.axis_index("core") * half, half), half)
-    half_copy = fetch(out_weight_hbm.at[own_rows, :], half_ref)
-    copies = hidden_copies + [segment_copy, table_copy] + weight_copies + [half_copy]
+    half_copies = [
+        fetch(
+            out_weight_hbm.at[own_rows, column * length : (column + 1) * length],
+            out_hbm.at[place, head_width + column * half : head_width + (column + 1) * half, :],
+        )
+        for column in range(out_weight_hbm.shape[1] // length)
+        for place in range(out_hbm.shape[0])
+    ]
+    copies = hidden_copies + [segment_copy, table_copy] + weight_copies + half_copies
     for copy in copies:
         copy.start()
     segment_copy.wait()
-    head_width = weight_ref.shape[1]
     segments = segment_ref[pl.ds(row - tile, 1), :]
     starts = jnp.zeros_like(segments)
     for passage in range(PASS_DEV - 1):
@@ -144,14 +151,13 @@
         raised = jnp.where(allowed, jnp.exp(scores), 0.0)
         probabilities = (raised / jnp.sum(raised, axis=0, keepdims=True)).astype(jnp.bfloat16)
         context = matmul(values[at], probabilities, (((1,), (0,)), ((), ()))).astype(jnp.bfloat16)
-        for copy in range(out_ref.shape[0]):
-            out_ref[copy, at, :] = context
-    half_copy.wait()
-    for column in range(half_ref.shape[1] // length):
-        block = half_ref[:, column * length : (column + 1) * length]
-        at = slice(head_width + column * half, head_width + (column + 1) * half)
-        for copy in range(out_ref.shape[0]):
-            out_ref[copy, at, :] = block
+        context_ref[at, :] = context
+        for place in range(out_hbm.shape[0]):
+            sent = fetch(context_ref.at[at, :], out_hbm.at[place, at, :])
+            sent.start()
+            half_copies.append(sent)
+    for copy in half_copies:
+        copy.wait()
 
 
 def ffn_kernel(
@@ -358,15 +364,15 @@
         attention_kernel,
         out_shape=jax.ShapeDtypeStruct((tensor, chunk, length), jnp.bfloat16),
         in_specs=[hbm()] * 6,
-        out_specs=vmem(),
+        out_specs=hbm(),
         scratch_shapes=[
             pltpu.VMEM((width,), jnp.float32),
             pltpu.VMEM((length, width), jnp.bfloat16),
             pltpu.VMEM((8, length), jnp.int32),
             pltpu.VMEM((3, head_width, width), jnp.bfloat16),
             pltpu.VMEM(rotary.shape, jnp.bfloat16),
-            pltpu.VMEM((half, width), jnp.bfloat16),
-            pltpu.SemaphoreType.DMA((14,)),
+            pltpu.VMEM((head_width, length), jnp.bfloat16),
+            pltpu.SemaphoreType.DMA((37,)),
         ],
         compiler_params=grant(60),
         cost_estimate=cost(1200000000, 2000000),

time: 128 us -> 143 us (1.12)
  Pallas kernels: 17.1 us -> 32.3 us
    pallas_call x1, Pallas kernels: 4.08 us -> 19.3 us  [on_device(): pl.pallas_call(attention_kernel, out_shape=jax.ShapeDtypeStruct((tensor,...]
where the time goes in v11:
time: 143 us; the launch traced here: 142 us
  starting transfers between devices  54.2 us (38%)
  Pallas kernels  32.3 us (23%)
  waiting for transfers between devices  29.4 us (21%)
  between operations  13.7 us (10%)
  blocking collectives  8.67 us (6%)
  local copies, waits for them, and re-layouts  2.37 us (2%)
    ppermute x7, starting transfers between devices, swap(): lax.ppermute(block, axis, [(i, i ^ d) for i in range(lax.axis_size(axis))])  33.9 us
    all_to_all x3, starting transfers between devices, exchange(): return lax.all_to_all(copies, axis, split_axis=0, concat_axis=0, tiled=True)  20.3 us
    pallas_call x1, Pallas kernels, on_device(): pl.pallas_call(attention_kernel, out_shape=jax.ShapeDtypeStruct((tensor,...  19.3 us
    all_to_all x3, waiting for transfers between devices, exchange(): return lax.all_to_all(copies, axis, split_axis=0, concat_axis=0, tiled=True)  17.1 us
    ppermute x7, waiting for transfers between devices, swap(): lax.ppermute(block, axis, [(i, i ^ d) for i in range(lax.axis_size(axis))])  11.4 us
    all_to_all x1, blocking collectives, exchange(): return lax.all_to_all(copies, axis, split_axis=0, concat_axis=0, tiled=True)  8.67 us
    pallas_call x1, Pallas kernels, on_device(): pl.pallas_call(pool_kernel, out_shape=jax.ShapeDtypeStruct((slices, 2 * P...  8.19 us
  transfers between devices with their start and end apart: 11, of which 7 were waited for; matrix products, arithmetic and copies ran while one was open for 1% of the time, Pallas kernels for 3%

profile of v11, /device:TPU:1, one launch (start us, length us, event | category | flops | bytes accessed | tf_op | source)
XLA Modules:
  0.0 141.6 jit_solution(17575420848601192426)
XLA Ops:
  6.5 19.3 %attention.1 = bf16[4,480,256]{2,1,0:T(8,128)(2,1)} custom-call(f32[768]{0:T(1024)} %gain_hbm.1, bf16[256,768]{1,0:T(8,128)(2,1)} %bitcast.19, s32[128,256]{1,0:T(8,128)} %segment_ref.1, bf16[3,192,768]{2,1,0:T(8,128)(2,1)} %bitcast.31, bf16[192,256]{1,0:T(8,128)(2,1)} %constant.22.clone.table_hbm, bf16[192,768]{1,0:T(8,128)(2,1)} %out_weight_hbm.1), custom_call_target="tpu_custom_call" | custom-call | flops 1200000000 | bytes 2000000 | tf_op jit(solution)/shard_map/attention/pallas_call | solution.py:363
  25.9 5.0 %all-to-all-start = ((bf16[4,480,256]{2,1,0:T(8,128)(2,1)}), bf16[4,480,256]{2,1,0:T(8,128)(2,1)S(1)}, u32[]{:S(2)}, u32[]{:S(2)}) async-start(bf16[4,480,256]{2,1,0:T(8,128)(2,1)} %attention.1), calls=%async_computation | async-start | bytes 1966080 | tf_op jit(solution)/shard_map/all_to_all | solution.py:318
  30.9 5.8 %collective-permute-start = (bf16[64,768]{1,0:T(8,128)(2,1)S(1)}, bf16[64,768]{1,0:T(8,128)(2,1)S(1)}, u32[]{:S(2)}, u32[]{:S(2)}) collective-permute-start(bf16[64,768]{1,0:T(8,128)(2,1)S(1)} %bitcast.25), channel_id=1, source_target_pairs={{0,16},{16,0},{32,48},{48,32},{1,17},{17,1},{33,49},{49,33},{2,18}... | collective-permute-start | bytes 294920 | tf_op jit(solution)/shard_map/ppermute | solution.py:322
  36.7 7.0 %collective-permute-start.2 = (bf16[64,768]{1,0:T(8,128)(2,1)S(1)}, bf16[64,768]{1,0:T(8,128)(2,1)S(1)}, u32[]{:S(2)}, u32[]{:S(2)}) collective-permute-start(bf16[64,768]{1,0:T(8,128)(2,1)S(1)} %bitcast.26), channel_id=1, source_target_pairs={{0,48},{16,32},{32,16},{48,0},{1,49},{17,33},{33,17},{49,1},{2,50}... | collective-permute-start | bytes 294920 | tf_op jit(solution)/shard_map/ppermute | solution.py:322
  43.8 3.7 %collective-permute-start.1 = (bf16[64,768]{1,0:T(8,128)(2,1)S(1)}, bf16[64,768]{1,0:T(8,128)(2,1)S(1)}, u32[]{:S(2)}, u32[]{:S(2)}) collective-permute-start(bf16[64,768]{1,0:T(8,128)(2,1)S(1)} %bitcast.27), channel_id=1, source_target_pairs={{0,32},{16,48},{32,0},{48,16},{1,33},{17,49},{33,1},{49,17},{2,34}... | collective-permute-start | bytes 294920 | tf_op jit(solution)/shard_map/ppermute | solution.py:322
  47.5 7.1 %collective-permute-done.1 = bf16[64,768]{1,0:T(8,128)(2,1)S(1)} collective-permute-done((bf16[64,768]{1,0:T(8,128)(2,1)S(1)}, bf16[64,768]{1,0:T(8,128)(2,1)S(1)}, u32[]{:S(2)}, u32[]{:S(2)}) %collective-permute-start.1) | collective-permute-done | bytes 98336 | tf_op jit(solution)/shard_map/ppermute | solution.py:322
  54.6 0.8 pad_maximum_fusion
  55.5 3.7 %collective-permute-start.3 = (bf16[4,288,256]{2,1,0:T(8,128)(2,1)S(1)}, bf16[4,288,256]{2,1,0:T(8,128)(2,1)S(1)}, u32[]{:S(2)}, u32[]{:S(2)}) collective-permute-start(bf16[4,288,256]{2,1,0:T(8,128)(2,1)S(1)} %slice.3), channel_id=1, source_target_pairs={{0,4},{4,0},{1,5},{5,1},{2,6},{6,2},{3,7},{7,3},{8,12},{12,8},{9,1... | collective-permute-start | bytes 1769480 | tf_op jit(solution)/shard_map/ppermute | solution.py:322
  59.2 1.6 %collective-permute-done.3.other_ref = bf16[4,288,256]{2,1,0:T(8,128)(2,1)S(1)} collective-permute-done((bf16[4,288,256]{2,1,0:T(8,128)(2,1)S(1)}, bf16[4,288,256]{2,1,0:T(8,128)(2,1)S(1)}, u32[]{:S(2)}, u32[]{:S(2)}) %collective-permute-start.3) | collective-permute-done | bytes 589856 | tf_op jit(solution)/shard_map/ppermute | solution.py:322
  60.8 2.5 %ffn.1 = (f32[64,768]{1,0:T(8,128)S(1)}, bf16[256,768]{1,0:T(8,128)(2,1)}) custom-call(bf16[256,768]{1,0:T(8,128)(2,1)S(1)} %bitcast.20, bf16[4,480,256]{2,1,0:T(8,128)(2,1)S(1)} %all-to-all-done.merged_ref, bf16[4,288,256]{2,1,0:T(8,128)(2,1)S(1)} %collective-permute-done.3.other_ref, f32[768]{0:T(1024)S(1)} %copy-done.5, ...), custom_call_target="tpu_custom_call" | custom-call | flops 700000000 | bytes 4000000 | tf_op jit(solution)/shard_map/ffn/pallas_call | solution.py:388
  63.3 4.7 %all-to-all-start.1 = ((bf16[4,64,768]{2,1,0:T(8,128)(2,1)}), bf16[4,64,768]{2,1,0:T(8,128)(2,1)S(1)}, u32[]{:S(2)}, u32[]{:S(2)}) async-start(bf16[4,64,768]{2,1,0:T(8,128)(2,1)} %bitcast.4), calls=%async_computation.1 | async-start | bytes 786432 | tf_op jit(solution)/shard_map/all_to_all | solution.py:318
  68.1 0.1 copy.23.docs_ref
  68.2 0.4 prep.1
  68.7 6.6 %all-to-all-done.1.partial_ref = bf16[4,64,768]{2,1,0:T(8,128)(2,1)S(1)} async-done(((bf16[4,64,768]{2,1,0:T(8,128)(2,1)}), bf16[4,64,768]{2,1,0:T(8,128)(2,1)S(1)}, u32[]{:S(2)}, u32[]{:S(2)}) %all-to-all-start.1) | async-done | bytes 393248 | tf_op jit(solution)/shard_map/all_to_all | solution.py:318
  75.3 1.3 copy-done.6
  76.6 0.7 head.1
  77.3 8.7 %all_to_all.20 = bf16[4,64,768]{2,1,0:T(8,128)(2,1)S(1)} all-to-all(bf16[4,64,768]{2,1,0:T(8,128)(2,1)S(1)} %head.1), channel_id=1, replica_groups=mesh['y'=8,'zh'=4,'zl'=2,'core'=2,'term'=4] {'term'}, dimensions={0} | all-to-all | bytes 786432 | tf_op jit(solution)/shard_map/all_to_all | solution.py:318
  85.9 2.9 %collective-permute-start.5 = (bf16[256,768]{1,0:T(8,128)(2,1)S(1)}, bf16[256,768]{1,0:T(8,128)(2,1)S(1)}, u32[]{:S(2)}, u32[]{:S(2)}) collective-permute-start(bf16[256,768]{1,0:T(8,128)(2,1)S(1)} %bitcast.22), channel_id=1, source_target_pairs={{0,8},{8,0},{1,9},{9,1},{2,10},{10,2},{3,11},{11,3},{4,12},{12,4},... | collective-permute-start | bytes 1179656 | tf_op jit(solution)/shard_map/ppermute | solution.py:322
  88.9 5.1 %collective-permute-start.4 = (bf16[256,768]{1,0:T(8,128)(2,1)S(1)}, bf16[256,768]{1,0:T(8,128)(2,1)S(1)}, u32[]{:S(2)}, u32[]{:S(2)}) collective-permute-start(bf16[256,768]{1,0:T(8,128)(2,1)S(1)} %bitcast.23), channel_id=1, source_target_pairs={{0,4},{4,0},{1,5},{5,1},{2,6},{6,2},{3,7},{7,3},{8,12},{12,8},{9,1... | collective-permute-start | bytes 1179656 | tf_op jit(solution)/shard_map/ppermute | solution.py:322
  94.0 1.6 %collective-permute-done.5.far_ref = bf16[256,768]{1,0:T(8,128)(2,1)S(1)} collective-permute-done((bf16[256,768]{1,0:T(8,128)(2,1)S(1)}, bf16[256,768]{1,0:T(8,128)(2,1)S(1)}, u32[]{:S(2)}, u32[]{:S(2)}) %collective-permute-start.5) | collective-permute-done | bytes 393248 | tf_op jit(solution)/shard_map/ppermute | solution.py:322
  95.6 5.6 %collective-permute-start.6 = (bf16[256,768]{1,0:T(8,128)(2,1)S(1)}, bf16[256,768]{1,0:T(8,128)(2,1)S(1)}, u32[]{:S(2)}, u32[]{:S(2)}) collective-permute-start(bf16[256,768]{1,0:T(8,128)(2,1)S(1)} %collective-permute-done.5.far_ref), channel_id=1, source_target_pairs={{0,4},{4,0},{1,5},{5,1},{2,6},{6,2},{3,7},{7,3},{8,12},{12,8},{9,1... | collective-permute-start | bytes 1179656 | tf_op jit(solution)/shard_map/ppermute | solution.py:322
  101.3 0.1 reshape.43
  101.5 1.1 collective-permute-done.6.far_core_ref
  102.6 0.8 all-gather.2.cloned.1.call-done.table_ref
  103.5 8.2 %pool.1 = f32[32,8,128]{2,1,0:T(8,128)} custom-call(s32[128,8]{1,0:T(8,128)} %copy-done.7, bf16[256,768]{1,0:T(8,128)(2,1)} %bitcast.24, bf16[256,768]{1,0:T(8,128)(2,1)} %copy-done.15, bf16[256,768]{1,0:T(8,128)(2,1)} %copy-done.14, bf16[256,768]{1,0:T(8,128)(2,1)} %copy-done.16, bf16[2048,768]{1,0:T(8,128)(2,1)} %all-gather.2.cloned.1.call-done.table_ref), custom_call_target="tpu_custom_call" | custom-call | flops 3300000000 | bytes 6000000 | tf_op jit(solution)/shard_map/pool/pallas_call | solution.py:435
  111.6 10.6 %all-to-all-start.3 = ((f32[32,8,128]{2,1,0:T(8,128)}), f32[32,8,128]{2,1,0:T(8,128)S(1)}, u32[]{:S(2)}, u32[]{:S(2)}) async-start(f32[32,8,128]{2,1,0:T(8,128)} %pool.1), calls=%async_computation.3 | async-start | bytes 262144 | tf_op jit(solution)/shard_map/all_to_all | solution.py:318
  122.6 0.1 copy.28
  122.7 0.1 reshape.47.docs_ref
  122.8 0.1 convert_element_type.12
  122.9 0.1 maximum_convert_fusion.bias_ref
  123.0 10.6 %all-to-all-done.3 = f32[32,8,128]{2,1,0:T(8,128)S(1)} async-done(((f32[32,8,128]{2,1,0:T(8,128)}), f32[32,8,128]{2,1,0:T(8,128)S(1)}, u32[]{:S(2)}, u32[]{:S(2)}) %all-to-all-start.3) | async-done | bytes 131104 | tf_op jit(solution)/shard_map/all_to_all | solution.py:318
  133.6 1.2 place.1
  (46 shorter events, 0.5 us)
Async XLA Ops:
  6.5 24.4 %copy-start.11 = (bf16[1,8,1,8,768]{4,3,2,1,0:T(8,128)(2,1)S(1)}, bf16[1,8,1,8,768]{4,3,2,1,0:T(8,128)(2,1)}, u32[]{:S(2)}) copy-start(bf16[1,8,1,8,768]{4,3,2,1,0:T(8,128)(2,1)} %param.29) | copy-start | bytes 294916
  25.9 34.9 %copy-start = (bf16[2,768,288]{1,2,0:T(8,128)(2,1)S(1)}, bf16[2,768,288]{1,2,0:T(8,128)(2,1)}, u32[]{:S(2)}) copy-start(bf16[2,768,288]{1,2,0:T(8,128)(2,1)} %param.24) | copy-start | bytes 2654212
  25.9 34.9 %copy-start.1 = (bf16[288,768]{1,0:T(8,128)(2,1)S(1)}, bf16[288,768]{1,0:T(8,128)(2,1)}, u32[]{:S(2)}) copy-start(bf16[288,768]{1,0:T(8,128)(2,1)} %down_ref.1) | copy-start | bytes 1327108
  25.9 34.9 %copy-start.2 = (bf16[1,256,768]{2,1,0:T(8,128)(2,1)S(1)}, bf16[1,256,768]{2,1,0:T(8,128)(2,1)}, u32[]{:S(2)}) copy-start(bf16[1,256,768]{2,1,0:T(8,128)(2,1)} %param.16) | copy-start | bytes 1179652
  25.9 34.9 %copy-start.5 = (f32[768]{0:T(1024)S(1)}, f32[768]{0:T(1024)}, u32[]{:S(2)}) copy-start(f32[768]{0:T(1024)} %gain_ref.1) | copy-start | bytes 9220
  25.9 29.5 %all-to-all-start = ((bf16[4,480,256]{2,1,0:T(8,128)(2,1)}), bf16[4,480,256]{2,1,0:T(8,128)(2,1)S(1)}, u32[]{:S(2)}, u32[]{:S(2)}) async-start(bf16[4,480,256]{2,1,0:T(8,128)(2,1)} %attention.1), calls=%async_computation | async-start | bytes 1966080 | tf_op jit(solution)/shard_map/all_to_all | solution.py:318
  30.9 37.2 %copy-start.12 = (s32[512]{0:T(512)S(1)}, s32[512]{0:T(512)}, u32[]{:S(2)}) copy-start(s32[512]{0:T(512)} %param.19) | copy-start | bytes 6148
  30.9 72.5 %all-gather.2.cloned.1.call-start = ((), (), s32[]{:S(2)}) async-start(), calls=%async_computation.4 | async-start | bytes 3538944 | tf_op jit(solution)/shard_map/all_gather | solution.py:386
  30.9 16.6 %collective-permute-start = (bf16[64,768]{1,0:T(8,128)(2,1)S(1)}, bf16[64,768]{1,0:T(8,128)(2,1)S(1)}, u32[]{:S(2)}, u32[]{:S(2)}) collective-permute-start(bf16[64,768]{1,0:T(8,128)(2,1)S(1)} %bitcast.25), channel_id=1, source_target_pairs={{0,16},{16,0},{32,48},{48,32},{1,17},{17,1},{33,49},{49,33},{2,18}... | collective-permute-start | bytes 294920 | tf_op jit(solution)/shard_map/ppermute | solution.py:322
  36.7 10.8 %collective-permute-start.2 = (bf16[64,768]{1,0:T(8,128)(2,1)S(1)}, bf16[64,768]{1,0:T(8,128)(2,1)S(1)}, u32[]{:S(2)}, u32[]{:S(2)}) collective-permute-start(bf16[64,768]{1,0:T(8,128)(2,1)S(1)} %bitcast.26), channel_id=1, source_target_pairs={{0,48},{16,32},{32,16},{48,0},{1,49},{17,33},{33,17},{49,1},{2,50}... | collective-permute-start | bytes 294920 | tf_op jit(solution)/shard_map/ppermute | solution.py:322
  43.8 10.9 %collective-permute-start.1 = (bf16[64,768]{1,0:T(8,128)(2,1)S(1)}, bf16[64,768]{1,0:T(8,128)(2,1)S(1)}, u32[]{:S(2)}, u32[]{:S(2)}) collective-permute-start(bf16[64,768]{1,0:T(8,128)(2,1)S(1)} %bitcast.27), channel_id=1, source_target_pairs={{0,32},{16,48},{32,0},{48,16},{1,33},{17,49},{33,1},{49,17},{2,34}... | collective-permute-start | bytes 294920 | tf_op jit(solution)/shard_map/ppermute | solution.py:322
  55.4 12.8 %copy-start.3 = (s32[512,128]{1,0:T(8,128)S(1)}, s32[512,128]{1,0:T(8,128)}, u32[]{:S(2)}) copy-start(s32[512,128]{1,0:T(8,128)} %list_ref.1) | copy-start | bytes 786436
  55.4 12.8 %copy-start.4 = (s32[128,256]{1,0:T(8,128)S(1)}, s32[128,256]{1,0:T(8,128)}, u32[]{:S(2)}) copy-start(s32[128,256]{1,0:T(8,128)} %segment_ref.1) | copy-start | bytes 393220
  55.4 19.8 %copy-start.8 = (f32[768]{0:T(1024)S(1)}, f32[768]{0:T(1024)}, u32[]{:S(2)}) copy-start(f32[768]{0:T(1024)} %final_ref.1) | copy-start | bytes 9220
  55.4 19.8 %copy-start.9 = (f32[768]{0:T(1024)S(1)}, f32[768]{0:T(1024)}, u32[]{:S(2)}) copy-start(f32[768]{0:T(1024)} %head_ref.1) | copy-start | bytes 9220
  55.5 5.3 %collective-permute-start.3 = (bf16[4,288,256]{2,1,0:T(8,128)(2,1)S(1)}, bf16[4,288,256]{2,1,0:T(8,128)(2,1)S(1)}, u32[]{:S(2)}, u32[]{:S(2)}) collective-permute-start(bf16[4,288,256]{2,1,0:T(8,128)(2,1)S(1)} %slice.3), channel_id=1, source_target_pairs={{0,4},{4,0},{1,5},{5,1},{2,6},{6,2},{3,7},{7,3},{8,12},{12,8},{9,1... | collective-permute-start | bytes 1769480 | tf_op jit(solution)/shard_map/ppermute | solution.py:322
  63.3 11.9 %all-to-all-start.1 = ((bf16[4,64,768]{2,1,0:T(8,128)(2,1)}), bf16[4,64,768]{2,1,0:T(8,128)(2,1)S(1)}, u32[]{:S(2)}, u32[]{:S(2)}) async-start(bf16[4,64,768]{2,1,0:T(8,128)(2,1)} %bitcast.4), calls=%async_computation.1 | async-start | bytes 786432 | tf_op jit(solution)/shard_map/all_to_all | solution.py:318
  68.7 34.7 %copy-start.7 = (s32[128,8]{1,0:T(8,128)}, s32[128,8]{1,0:T(8,128)S(1)}, u32[]{:S(2)}) copy-start(s32[128,8]{1,0:T(8,128)S(1)} %get-tuple-element.22.bounds_ref) | copy-start | bytes 12292
  75.3 1.3 copy-start.6
  85.9 17.5 %copy-start.10 = (bf16[4,64,768]{2,1,0:T(8,128)(2,1)}, bf16[4,64,768]{2,1,0:T(8,128)(2,1)S(1)}, u32[]{:S(2)}) copy-start(bf16[4,64,768]{2,1,0:T(8,128)(2,1)S(1)} %all_to_all.20) | copy-start | bytes 1179652
  85.9 9.7 %collective-permute-start.5 = (bf16[256,768]{1,0:T(8,128)(2,1)S(1)}, bf16[256,768]{1,0:T(8,128)(2,1)S(1)}, u32[]{:S(2)}, u32[]{:S(2)}) collective-permute-start(bf16[256,768]{1,0:T(8,128)(2,1)S(1)} %bitcast.22), channel_id=1, source_target_pairs={{0,8},{8,0},{1,9},{9,1},{2,10},{10,2},{3,11},{11,3},{4,12},{12,4},... | collective-permute-start | bytes 1179656 | tf_op jit(solution)/shard_map/ppermute | solution.py:322
  88.9 12.6 %collective-permute-start.4 = (bf16[256,768]{1,0:T(8,128)(2,1)S(1)}, bf16[256,768]{1,0:T(8,128)(2,1)S(1)}, u32[]{:S(2)}, u32[]{:S(2)}) collective-permute-start(bf16[256,768]{1,0:T(8,128)(2,1)S(1)} %bitcast.23), channel_id=1, source_target_pairs={{0,4},{4,0},{1,5},{5,1},{2,6},{6,2},{3,7},{7,3},{8,12},{12,8},{9,1... | collective-permute-start | bytes 1179656 | tf_op jit(solution)/shard_map/ppermute | solution.py:322
  95.6 7.8 %copy-start.14 = (bf16[256,768]{1,0:T(8,128)(2,1)}, bf16[256,768]{1,0:T(8,128)(2,1)S(1)}, u32[]{:S(2)}) copy-start(bf16[256,768]{1,0:T(8,128)(2,1)S(1)} %collective-permute-done.5.far_ref) | copy-start | bytes 1179652
  95.6 7.0 %collective-permute-start.6 = (bf16[256,768]{1,0:T(8,128)(2,1)S(1)}, bf16[256,768]{1,0:T(8,128)(2,1)S(1)}, u32[]{:S(2)}, u32[]{:S(2)}) collective-permute-start(bf16[256,768]{1,0:T(8,128)(2,1)S(1)} %collective-permute-done.5.far_ref), channel_id=1, source_target_pairs={{0,4},{4,0},{1,5},{5,1},{2,6},{6,2},{3,7},{7,3},{8,12},{12,8},{9,1... | collective-permute-start | bytes 1179656 | tf_op jit(solution)/shard_map/ppermute | solution.py:322
  101.4 21.4 %copy-start.13 = (bf16[1,8,1,8]{3,1,2,0:T(8,128)(2,1)S(1)}, bf16[1,8,1,8]{3,1,2,0:T(8,128)(2,1)}, u32[]{:S(2)}) copy-start(bf16[1,8,1,8]{3,1,2,0:T(8,128)(2,1)} %param.30) | copy-start | bytes 388
  101.5 2.0 %copy-start.15 = (bf16[256,768]{1,0:T(8,128)(2,1)}, bf16[256,768]{1,0:T(8,128)(2,1)S(1)}, u32[]{:S(2)}) copy-start(bf16[256,768]{1,0:T(8,128)(2,1)S(1)} %collective-permute-done.4.core_ref) | copy-start | bytes 1179652
  102.6 0.9 copy-start.16
  111.6 21.9 %all-to-all-start.3 = ((f32[32,8,128]{2,1,0:T(8,128)}), f32[32,8,128]{2,1,0:T(8,128)S(1)}, u32[]{:S(2)}, u32[]{:S(2)}) async-start(f32[32,8,128]{2,1,0:T(8,128)} %pool.1), calls=%async_computation.3 | async-start | bytes 262144 | tf_op jit(solution)/shard_map/all_to_all | solution.py:318
Sparse Core Ops, SparseCore 0:
  55.6 47.8 all-gather.1

commit v12 on v11

--- a/solution.py
+++ b/solution.py
@@ -69,6 +69,7 @@
     segment_ref,
     weight_ref,
     table_ref,
+    half_ref,
     context_ref,
     sems,
 ):
@@ -94,15 +95,8 @@
         for cut in (slice(0, half), slice(half, 2 * half))
     ]
     own_rows = pl.ds(pl.multiple_of(lax.axis_index("core") * half, half), half)
-    half_copies = [
-        fetch(
-            out_weight_hbm.at[own_rows, column * length : (column + 1) * length],
-            out_hbm.at[place, head_width + column * half : head_width + (column + 1) * half, :],
-        )
-        for column in range(out_weight_hbm.shape[1] // length)
-        for place in range(out_hbm.shape[0])
-    ]
-    copies = hidden_copies + [segment_copy, table_copy] + weight_copies + half_copies
+    half_copy = fetch(out_weight_hbm.at[own_rows, :], half_ref)
+    copies = hidden_copies + [segment_copy, table_copy] + weight_copies + [half_copy]
     for copy in copies:
         copy.start()
     segment_copy.wait()
@@ -134,6 +128,17 @@
     normed = layer_norm(hidden_ref[...].astype(jnp.float32), gain).astype(jnp.bfloat16)
     for copy in weight_copies:
         copy.wait()
+    half_copy.wait()
+    sent_copies = [
+        fetch(
+            half_ref.at[:, column * length : (column + 1) * length],
+            out_hbm.at[place, head_width + column * half : head_width + (column + 1) * half, :],
+        )
+        for column in range(half_ref.shape[1] // length)
+        for place in range(out_hbm.shape[0])
+    ]
+    for copy in sent_copies:
+        copy.start()
     queries = matmul(weight_ref[0], normed, NT)
     key_cols = matmul(weight_ref[1], normed, NT)
     values = matmul(weight_ref[2], normed, NT).astype(jnp.bfloat16)
@@ -155,8 +160,8 @@
         for place in range(out_hbm.shape[0]):
             sent = fetch(context_ref.at[at, :], out_hbm.at[place, at, :])
             sent.start()
-            half_copies.append(sent)
-    for copy in half_copies:
+            sent_copies.append(sent)
+    for copy in sent_copies:
         copy.wait()
 
 
@@ -371,8 +376,9 @@
             pltpu.VMEM((8, length), jnp.int32),
             pltpu.VMEM((3, head_width, width), jnp.bfloat16),
             pltpu.VMEM(rotary.shape, jnp.bfloat16),
+            pltpu.VMEM((half, width), jnp.bfloat16),
             pltpu.VMEM((head_width, length), jnp.bfloat16),
-            pltpu.SemaphoreType.DMA((37,)),
+            pltpu.SemaphoreType.DMA((38,)),
         ],
         compiler_params=grant(60),
         cost_estimate=cost(1200000000, 2000000),

time: 143 us -> 127 us (0.89)
  Pallas kernels: 32.3 us -> 17 us
    pallas_call x1, Pallas kernels: 19.3 us -> 3.94 us  [on_device(): pl.pallas_call(attention_kernel, out_shape=jax.ShapeDtypeStruct((tensor,...]
where the time goes in v12:
time: 127 us; the launch traced here: 126 us
  starting transfers between devices  54.2 us (43%)
  waiting for transfers between devices  29.4 us (23%)
  Pallas kernels  17 us (13%)
  between operations  13.7 us (11%)
  blocking collectives  8.67 us (7%)
  local copies, waits for them, and re-layouts  2.37 us (2%)
    ppermute x7, starting transfers between devices, swap(): lax.ppermute(block, axis, [(i, i ^ d) for i in range(lax.axis_size(axis))])  34 us
    all_to_all x3, starting transfers between devices, exchange(): return lax.all_to_all(copies, axis, split_axis=0, concat_axis=0, tiled=True)  20.3 us
    all_to_all x3, waiting for transfers between devices, exchange(): return lax.all_to_all(copies, axis, split_axis=0, concat_axis=0, tiled=True)  17.1 us
    ppermute x7, waiting for transfers between devices, swap(): lax.ppermute(block, axis, [(i, i ^ d) for i in range(lax.axis_size(axis))])  11.4 us
    all_to_all x1, blocking collectives, exchange(): return lax.all_to_all(copies, axis, split_axis=0, concat_axis=0, tiled=True)  8.67 us
    pallas_call x1, Pallas kernels, on_device(): pl.pallas_call(pool_kernel, out_shape=jax.ShapeDtypeStruct((slices, 2 * P...  8.22 us
    pallas_call x1, Pallas kernels, on_device(): pl.pallas_call(attention_kernel, out_shape=jax.ShapeDtypeStruct((tensor,...  3.94 us
  transfers between devices with their start and end apart: 11, of which 7 were waited for; matrix products, arithmetic and copies ran while one was open for 1% of the time, Pallas kernels for 3%

profile of v12, /device:TPU:1, one launch (start us, length us, event | category | flops | bytes accessed | tf_op | source)
XLA Modules:
  0.0 126.2 jit_solution(5656176554093093610)
XLA Ops:
  6.5 3.9 %attention.1 = bf16[4,480,256]{2,1,0:T(8,128)(2,1)} custom-call(f32[768]{0:T(1024)} %gain_hbm.1, bf16[256,768]{1,0:T(8,128)(2,1)} %bitcast.19, s32[128,256]{1,0:T(8,128)} %segment_ref.1, bf16[3,192,768]{2,1,0:T(8,128)(2,1)} %bitcast.31, bf16[192,256]{1,0:T(8,128)(2,1)} %constant.22.clone.table_hbm, bf16[192,768]{1,0:T(8,128)(2,1)} %out_weight_hbm.1), custom_call_target="tpu_custom_call" | custom-call | flops 1200000000 | bytes 2000000 | tf_op jit(solution)/shard_map/attention/pallas_call | solution.py:368
  10.5 5.0 %all-to-all-start = ((bf16[4,480,256]{2,1,0:T(8,128)(2,1)}), bf16[4,480,256]{2,1,0:T(8,128)(2,1)S(1)}, u32[]{:S(2)}, u32[]{:S(2)}) async-start(bf16[4,480,256]{2,1,0:T(8,128)(2,1)} %attention.1), calls=%async_computation | async-start | bytes 1966080 | tf_op jit(solution)/shard_map/all_to_all | solution.py:323
  15.5 5.8 %collective-permute-start = (bf16[64,768]{1,0:T(8,128)(2,1)S(1)}, bf16[64,768]{1,0:T(8,128)(2,1)S(1)}, u32[]{:S(2)}, u32[]{:S(2)}) collective-permute-start(bf16[64,768]{1,0:T(8,128)(2,1)S(1)} %bitcast.25), channel_id=1, source_target_pairs={{0,16},{16,0},{32,48},{48,32},{1,17},{17,1},{33,49},{49,33},{2,18}... | collective-permute-start | bytes 294920 | tf_op jit(solution)/shard_map/ppermute | solution.py:327
  21.4 7.0 %collective-permute-start.2 = (bf16[64,768]{1,0:T(8,128)(2,1)S(1)}, bf16[64,768]{1,0:T(8,128)(2,1)S(1)}, u32[]{:S(2)}, u32[]{:S(2)}) collective-permute-start(bf16[64,768]{1,0:T(8,128)(2,1)S(1)} %bitcast.26), channel_id=1, source_target_pairs={{0,48},{16,32},{32,16},{48,0},{1,49},{17,33},{33,17},{49,1},{2,50}... | collective-permute-start | bytes 294920 | tf_op jit(solution)/shard_map/ppermute | solution.py:327
  28.4 3.7 %collective-permute-start.1 = (bf16[64,768]{1,0:T(8,128)(2,1)S(1)}, bf16[64,768]{1,0:T(8,128)(2,1)S(1)}, u32[]{:S(2)}, u32[]{:S(2)}) collective-permute-start(bf16[64,768]{1,0:T(8,128)(2,1)S(1)} %bitcast.27), channel_id=1, source_target_pairs={{0,32},{16,48},{32,0},{48,16},{1,33},{17,49},{33,1},{49,17},{2,34}... | collective-permute-start | bytes 294920 | tf_op jit(solution)/shard_map/ppermute | solution.py:327
  32.1 7.1 %collective-permute-done.1 = bf16[64,768]{1,0:T(8,128)(2,1)S(1)} collective-permute-done((bf16[64,768]{1,0:T(8,128)(2,1)S(1)}, bf16[64,768]{1,0:T(8,128)(2,1)S(1)}, u32[]{:S(2)}, u32[]{:S(2)}) %collective-permute-start.1) | collective-permute-done | bytes 98336 | tf_op jit(solution)/shard_map/ppermute | solution.py:327
  39.2 0.8 pad_maximum_fusion
  40.1 3.7 %collective-permute-start.3 = (bf16[4,288,256]{2,1,0:T(8,128)(2,1)S(1)}, bf16[4,288,256]{2,1,0:T(8,128)(2,1)S(1)}, u32[]{:S(2)}, u32[]{:S(2)}) collective-permute-start(bf16[4,288,256]{2,1,0:T(8,128)(2,1)S(1)} %slice.3), channel_id=1, source_target_pairs={{0,4},{4,0},{1,5},{5,1},{2,6},{6,2},{3,7},{7,3},{8,12},{12,8},{9,1... | collective-permute-start | bytes 1769480 | tf_op jit(solution)/shard_map/ppermute | solution.py:327
  43.8 1.6 %collective-permute-done.3.other_ref = bf16[4,288,256]{2,1,0:T(8,128)(2,1)S(1)} collective-permute-done((bf16[4,288,256]{2,1,0:T(8,128)(2,1)S(1)}, bf16[4,288,256]{2,1,0:T(8,128)(2,1)S(1)}, u32[]{:S(2)}, u32[]{:S(2)}) %collective-permute-start.3) | collective-permute-done | bytes 589856 | tf_op jit(solution)/shard_map/ppermute | solution.py:327
  45.4 2.5 %ffn.1 = (f32[64,768]{1,0:T(8,128)S(1)}, bf16[256,768]{1,0:T(8,128)(2,1)}) custom-call(bf16[256,768]{1,0:T(8,128)(2,1)S(1)} %bitcast.20, bf16[4,480,256]{2,1,0:T(8,128)(2,1)S(1)} %all-to-all-done.merged_ref, bf16[4,288,256]{2,1,0:T(8,128)(2,1)S(1)} %collective-permute-done.3.other_ref, f32[768]{0:T(1024)S(1)} %copy-done.5, ...), custom_call_target="tpu_custom_call" | custom-call | flops 700000000 | bytes 4000000 | tf_op jit(solution)/shard_map/ffn/pallas_call | solution.py:394
  47.9 4.7 %all-to-all-start.1 = ((bf16[4,64,768]{2,1,0:T(8,128)(2,1)}), bf16[4,64,768]{2,1,0:T(8,128)(2,1)S(1)}, u32[]{:S(2)}, u32[]{:S(2)}) async-start(bf16[4,64,768]{2,1,0:T(8,128)(2,1)} %bitcast.4), calls=%async_computation.1 | async-start | bytes 786432 | tf_op jit(solution)/shard_map/all_to_all | solution.py:323
  52.7 0.1 copy.23.docs_ref
  52.9 0.4 prep.1
  53.3 6.6 %all-to-all-done.1.partial_ref = bf16[4,64,768]{2,1,0:T(8,128)(2,1)S(1)} async-done(((bf16[4,64,768]{2,1,0:T(8,128)(2,1)}), bf16[4,64,768]{2,1,0:T(8,128)(2,1)S(1)}, u32[]{:S(2)}, u32[]{:S(2)}) %all-to-all-start.1) | async-done | bytes 393248 | tf_op jit(solution)/shard_map/all_to_all | solution.py:323
  59.9 1.3 %copy-done.6 = bf16[768,768]{1,0:T(8,128)(2,1)S(1)} copy-done((bf16[768,768]{1,0:T(8,128)(2,1)S(1)}, bf16[768,768]{1,0:T(8,128)(2,1)}, u32[]{:S(2)}) %copy-start.6) | copy-done | bytes 1179672
  61.2 0.7 head.1
  61.9 8.7 %all_to_all.20 = bf16[4,64,768]{2,1,0:T(8,128)(2,1)S(1)} all-to-all(bf16[4,64,768]{2,1,0:T(8,128)(2,1)S(1)} %head.1), channel_id=1, replica_groups=mesh['y'=8,'zh'=4,'zl'=2,'core'=2,'term'=4] {'term'}, dimensions={0} | all-to-all | bytes 786432 | tf_op jit(solution)/shard_map/all_to_all | solution.py:323
  70.6 2.9 %collective-permute-start.5 = (bf16[256,768]{1,0:T(8,128)(2,1)S(1)}, bf16[256,768]{1,0:T(8,128)(2,1)S(1)}, u32[]{:S(2)}, u32[]{:S(2)}) collective-permute-start(bf16[256,768]{1,0:T(8,128)(2,1)S(1)} %bitcast.22), channel_id=1, source_target_pairs={{0,8},{8,0},{1,9},{9,1},{2,10},{10,2},{3,11},{11,3},{4,12},{12,4},... | collective-permute-start | bytes 1179656 | tf_op jit(solution)/shard_map/ppermute | solution.py:327
  73.5 5.1 %collective-permute-start.4 = (bf16[256,768]{1,0:T(8,128)(2,1)S(1)}, bf16[256,768]{1,0:T(8,128)(2,1)S(1)}, u32[]{:S(2)}, u32[]{:S(2)}) collective-permute-start(bf16[256,768]{1,0:T(8,128)(2,1)S(1)} %bitcast.23), channel_id=1, source_target_pairs={{0,4},{4,0},{1,5},{5,1},{2,6},{6,2},{3,7},{7,3},{8,12},{12,8},{9,1... | collective-permute-start | bytes 1179656 | tf_op jit(solution)/shard_map/ppermute | solution.py:327
  78.6 1.6 %collective-permute-done.5.far_ref = bf16[256,768]{1,0:T(8,128)(2,1)S(1)} collective-permute-done((bf16[256,768]{1,0:T(8,128)(2,1)S(1)}, bf16[256,768]{1,0:T(8,128)(2,1)S(1)}, u32[]{:S(2)}, u32[]{:S(2)}) %collective-permute-start.5) | collective-permute-done | bytes 393248 | tf_op jit(solution)/shard_map/ppermute | solution.py:327
  80.2 5.6 %collective-permute-start.6 = (bf16[256,768]{1,0:T(8,128)(2,1)S(1)}, bf16[256,768]{1,0:T(8,128)(2,1)S(1)}, u32[]{:S(2)}, u32[]{:S(2)}) collective-permute-start(bf16[256,768]{1,0:T(8,128)(2,1)S(1)} %collective-permute-done.5.far_ref), channel_id=1, source_target_pairs={{0,4},{4,0},{1,5},{5,1},{2,6},{6,2},{3,7},{7,3},{8,12},{12,8},{9,1... | collective-permute-start | bytes 1179656 | tf_op jit(solution)/shard_map/ppermute | solution.py:327
  85.9 0.1 reshape.43
  86.1 1.1 collective-permute-done.6.far_core_ref
  87.2 0.8 all-gather.2.cloned.1.call-done.table_ref
  88.1 8.2 %pool.1 = f32[32,8,128]{2,1,0:T(8,128)} custom-call(s32[128,8]{1,0:T(8,128)} %copy-done.7, bf16[256,768]{1,0:T(8,128)(2,1)} %bitcast.24, bf16[256,768]{1,0:T(8,128)(2,1)} %copy-done.15, bf16[256,768]{1,0:T(8,128)(2,1)} %copy-done.14, bf16[256,768]{1,0:T(8,128)(2,1)} %copy-done.16, bf16[2048,768]{1,0:T(8,128)(2,1)} %all-gather.2.cloned.1.call-done.table_ref), custom_call_target="tpu_custom_call" | custom-call | flops 3300000000 | bytes 6000000 | tf_op jit(solution)/shard_map/pool/pallas_call | solution.py:441
  96.3 10.5 %all-to-all-start.3 = ((f32[32,8,128]{2,1,0:T(8,128)}), f32[32,8,128]{2,1,0:T(8,128)S(1)}, u32[]{:S(2)}, u32[]{:S(2)}) async-start(f32[32,8,128]{2,1,0:T(8,128)} %pool.1), calls=%async_computation.3 | async-start | bytes 262144 | tf_op jit(solution)/shard_map/all_to_all | solution.py:323
  107.2 0.1 copy.28
  107.3 0.1 reshape.47.docs_ref
  107.5 0.1 convert_element_type.12
  107.6 0.1 maximum_convert_fusion.bias_ref
  107.7 10.6 %all-to-all-done.3 = f32[32,8,128]{2,1,0:T(8,128)S(1)} async-done(((f32[32,8,128]{2,1,0:T(8,128)}), f32[32,8,128]{2,1,0:T(8,128)S(1)}, u32[]{:S(2)}, u32[]{:S(2)}) %all-to-all-start.3) | async-done | bytes 131104 | tf_op jit(solution)/shard_map/all_to_all | solution.py:323
  118.2 1.2 place.1
  (46 shorter events, 0.5 us)
Async XLA Ops:
  6.5 9.0 %copy-start.11 = (bf16[1,8,1,8,768]{4,3,2,1,0:T(8,128)(2,1)S(1)}, bf16[1,8,1,8,768]{4,3,2,1,0:T(8,128)(2,1)}, u32[]{:S(2)}) copy-start(bf16[1,8,1,8,768]{4,3,2,1,0:T(8,128)(2,1)} %param.29) | copy-start | bytes 294916
  10.5 34.9 %copy-start = (bf16[2,768,288]{1,2,0:T(8,128)(2,1)S(1)}, bf16[2,768,288]{1,2,0:T(8,128)(2,1)}, u32[]{:S(2)}) copy-start(bf16[2,768,288]{1,2,0:T(8,128)(2,1)} %param.24) | copy-start | bytes 2654212
  10.5 34.9 %copy-start.1 = (bf16[288,768]{1,0:T(8,128)(2,1)S(1)}, bf16[288,768]{1,0:T(8,128)(2,1)}, u32[]{:S(2)}) copy-start(bf16[288,768]{1,0:T(8,128)(2,1)} %down_ref.1) | copy-start | bytes 1327108
  10.5 34.9 %copy-start.2 = (bf16[1,256,768]{2,1,0:T(8,128)(2,1)S(1)}, bf16[1,256,768]{2,1,0:T(8,128)(2,1)}, u32[]{:S(2)}) copy-start(bf16[1,256,768]{2,1,0:T(8,128)(2,1)} %param.16) | copy-start | bytes 1179652
  10.5 34.9 %copy-start.5 = (f32[768]{0:T(1024)S(1)}, f32[768]{0:T(1024)}, u32[]{:S(2)}) copy-start(f32[768]{0:T(1024)} %gain_ref.1) | copy-start | bytes 9220
  10.5 29.5 %all-to-all-start = ((bf16[4,480,256]{2,1,0:T(8,128)(2,1)}), bf16[4,480,256]{2,1,0:T(8,128)(2,1)S(1)}, u32[]{:S(2)}, u32[]{:S(2)}) async-start(bf16[4,480,256]{2,1,0:T(8,128)(2,1)} %attention.1), calls=%async_computation | async-start | bytes 1966080 | tf_op jit(solution)/shard_map/all_to_all | solution.py:323
  15.5 37.2 %copy-start.12 = (s32[512]{0:T(512)S(1)}, s32[512]{0:T(512)}, u32[]{:S(2)}) copy-start(s32[512]{0:T(512)} %param.19) | copy-start | bytes 6148
  15.5 72.5 %all-gather.2.cloned.1.call-start = ((), (), s32[]{:S(2)}) async-start(), calls=%async_computation.4 | async-start | bytes 3538944 | tf_op jit(solution)/shard_map/all_gather | solution.py:392
  15.5 16.6 %collective-permute-start = (bf16[64,768]{1,0:T(8,128)(2,1)S(1)}, bf16[64,768]{1,0:T(8,128)(2,1)S(1)}, u32[]{:S(2)}, u32[]{:S(2)}) collective-permute-start(bf16[64,768]{1,0:T(8,128)(2,1)S(1)} %bitcast.25), channel_id=1, source_target_pairs={{0,16},{16,0},{32,48},{48,32},{1,17},{17,1},{33,49},{49,33},{2,18}... | collective-permute-start | bytes 294920 | tf_op jit(solution)/shard_map/ppermute | solution.py:327
  21.4 10.8 %collective-permute-start.2 = (bf16[64,768]{1,0:T(8,128)(2,1)S(1)}, bf16[64,768]{1,0:T(8,128)(2,1)S(1)}, u32[]{:S(2)}, u32[]{:S(2)}) collective-permute-start(bf16[64,768]{1,0:T(8,128)(2,1)S(1)} %bitcast.26), channel_id=1, source_target_pairs={{0,48},{16,32},{32,16},{48,0},{1,49},{17,33},{33,17},{49,1},{2,50}... | collective-permute-start | bytes 294920 | tf_op jit(solution)/shard_map/ppermute | solution.py:327
  28.4 10.9 %collective-permute-start.1 = (bf16[64,768]{1,0:T(8,128)(2,1)S(1)}, bf16[64,768]{1,0:T(8,128)(2,1)S(1)}, u32[]{:S(2)}, u32[]{:S(2)}) collective-permute-start(bf16[64,768]{1,0:T(8,128)(2,1)S(1)} %bitcast.27), channel_id=1, source_target_pairs={{0,32},{16,48},{32,0},{48,16},{1,33},{17,49},{33,1},{49,17},{2,34}... | collective-permute-start | bytes 294920 | tf_op jit(solution)/shard_map/ppermute | solution.py:327
  40.0 12.8 %copy-start.3 = (s32[512,128]{1,0:T(8,128)S(1)}, s32[512,128]{1,0:T(8,128)}, u32[]{:S(2)}) copy-start(s32[512,128]{1,0:T(8,128)} %list_ref.1) | copy-start | bytes 786436
  40.0 12.8 %copy-start.4 = (s32[128,256]{1,0:T(8,128)S(1)}, s32[128,256]{1,0:T(8,128)}, u32[]{:S(2)}) copy-start(s32[128,256]{1,0:T(8,128)} %segment_ref.1) | copy-start | bytes 393220
  40.0 19.8 %copy-start.8 = (f32[768]{0:T(1024)S(1)}, f32[768]{0:T(1024)}, u32[]{:S(2)}) copy-start(f32[768]{0:T(1024)} %final_ref.1) | copy-start | bytes 9220
  40.0 19.8 %copy-start.9 = (f32[768]{0:T(1024)S(1)}, f32[768]{0:T(1024)}, u32[]{:S(2)}) copy-start(f32[768]{0:T(1024)} %head_ref.1) | copy-start | bytes 9220
  40.1 5.3 %collective-permute-start.3 = (bf16[4,288,256]{2,1,0:T(8,128)(2,1)S(1)}, bf16[4,288,256]{2,1,0:T(8,128)(2,1)S(1)}, u32[]{:S(2)}, u32[]{:S(2)}) collective-permute-start(bf16[4,288,256]{2,1,0:T(8,128)(2,1)S(1)} %slice.3), channel_id=1, source_target_pairs={{0,4},{4,0},{1,5},{5,1},{2,6},{6,2},{3,7},{7,3},{8,12},{12,8},{9,1... | collective-permute-start | bytes 1769480 | tf_op jit(solution)/shard_map/ppermute | solution.py:327
  47.9 11.9 %all-to-all-start.1 = ((bf16[4,64,768]{2,1,0:T(8,128)(2,1)}), bf16[4,64,768]{2,1,0:T(8,128)(2,1)S(1)}, u32[]{:S(2)}, u32[]{:S(2)}) async-start(bf16[4,64,768]{2,1,0:T(8,128)(2,1)} %bitcast.4), calls=%async_computation.1 | async-start | bytes 786432 | tf_op jit(solution)/shard_map/all_to_all | solution.py:323
  53.3 34.7 %copy-start.7 = (s32[128,8]{1,0:T(8,128)}, s32[128,8]{1,0:T(8,128)S(1)}, u32[]{:S(2)}) copy-start(s32[128,8]{1,0:T(8,128)S(1)} %get-tuple-element.22.bounds_ref) | copy-start | bytes 12292
  59.9 1.3 %copy-start.6 = (bf16[768,768]{1,0:T(8,128)(2,1)S(1)}, bf16[768,768]{1,0:T(8,128)(2,1)}, u32[]{:S(2)}) copy-start(bf16[768,768]{1,0:T(8,128)(2,1)} %dense_ref.1) | copy-start | bytes 3538948
  70.6 17.5 %copy-start.10 = (bf16[4,64,768]{2,1,0:T(8,128)(2,1)}, bf16[4,64,768]{2,1,0:T(8,128)(2,1)S(1)}, u32[]{:S(2)}) copy-start(bf16[4,64,768]{2,1,0:T(8,128)(2,1)S(1)} %all_to_all.20) | copy-start | bytes 1179652
  70.6 9.7 %collective-permute-start.5 = (bf16[256,768]{1,0:T(8,128)(2,1)S(1)}, bf16[256,768]{1,0:T(8,128)(2,1)S(1)}, u32[]{:S(2)}, u32[]{:S(2)}) collective-permute-start(bf16[256,768]{1,0:T(8,128)(2,1)S(1)} %bitcast.22), channel_id=1, source_target_pairs={{0,8},{8,0},{1,9},{9,1},{2,10},{10,2},{3,11},{11,3},{4,12},{12,4},... | collective-permute-start | bytes 1179656 | tf_op jit(solution)/shard_map/ppermute | solution.py:327
  73.5 12.6 %collective-permute-start.4 = (bf16[256,768]{1,0:T(8,128)(2,1)S(1)}, bf16[256,768]{1,0:T(8,128)(2,1)S(1)}, u32[]{:S(2)}, u32[]{:S(2)}) collective-permute-start(bf16[256,768]{1,0:T(8,128)(2,1)S(1)} %bitcast.23), channel_id=1, source_target_pairs={{0,4},{4,0},{1,5},{5,1},{2,6},{6,2},{3,7},{7,3},{8,12},{12,8},{9,1... | collective-permute-start | bytes 1179656 | tf_op jit(solution)/shard_map/ppermute | solution.py:327
  80.2 7.8 %copy-start.14 = (bf16[256,768]{1,0:T(8,128)(2,1)}, bf16[256,768]{1,0:T(8,128)(2,1)S(1)}, u32[]{:S(2)}) copy-start(bf16[256,768]{1,0:T(8,128)(2,1)S(1)} %collective-permute-done.5.far_ref) | copy-start | bytes 1179652
  80.2 7.0 %collective-permute-start.6 = (bf16[256,768]{1,0:T(8,128)(2,1)S(1)}, bf16[256,768]{1,0:T(8,128)(2,1)S(1)}, u32[]{:S(2)}, u32[]{:S(2)}) collective-permute-start(bf16[256,768]{1,0:T(8,128)(2,1)S(1)} %collective-permute-done.5.far_ref), channel_id=1, source_target_pairs={{0,4},{4,0},{1,5},{5,1},{2,6},{6,2},{3,7},{7,3},{8,12},{12,8},{9,1... | collective-permute-start | bytes 1179656 | tf_op jit(solution)/shard_map/ppermute | solution.py:327
  86.1 21.4 %copy-start.13 = (bf16[1,8,1,8]{3,1,2,0:T(8,128)(2,1)S(1)}, bf16[1,8,1,8]{3,1,2,0:T(8,128)(2,1)}, u32[]{:S(2)}) copy-start(bf16[1,8,1,8]{3,1,2,0:T(8,128)(2,1)} %param.30) | copy-start | bytes 388
  86.1 2.0 %copy-start.15 = (bf16[256,768]{1,0:T(8,128)(2,1)}, bf16[256,768]{1,0:T(8,128)(2,1)S(1)}, u32[]{:S(2)}) copy-start(bf16[256,768]{1,0:T(8,128)(2,1)S(1)} %collective-permute-done.4.core_ref) | copy-start | bytes 1179652
  87.2 0.9 copy-start.16
  96.3 21.9 %all-to-all-start.3 = ((f32[32,8,128]{2,1,0:T(8,128)}), f32[32,8,128]{2,1,0:T(8,128)S(1)}, u32[]{:S(2)}, u32[]{:S(2)}) async-start(f32[32,8,128]{2,1,0:T(8,128)} %pool.1), calls=%async_computation.3 | async-start | bytes 262144 | tf_op jit(solution)/shard_map/all_to_all | solution.py:323
Sparse Core Ops, SparseCore 0:
  40.2 47.8 all-gather.1
